TPU v7x, 32 devices: a whole 2x2x4 slice. The times are simulated.
32 devices in a mesh: parts: 2 (over y), leaf: 4 (over z), top: 4 (over x, core).
Axes of the slice: x: 2, y: 2, z: 4, core: 2. Of those that a mesh axis runs over, the one named last changes fastest.
Arguments:
- right_side: float32 [8, 2560, 256], P(('parts', 'top'), 'leaf'), parts along dimension 0, may hold values from -6 to 6
- leaf_inverse: bfloat16 [8, 2560, 640], P(('parts', 'top'), 'leaf'), parts along dimension 0, as said below
- left_basis: bfloat16 [2, 8, 2560, 128], P(None, ('parts', 'top'), 'leaf'), parts along dimension 1, may hold values from -0.1875 to 0.1875
- right_basis: bfloat16 [2, 8, 2560, 128], P(None, ('parts', 'top'), 'leaf'), parts along dimension 1, may hold values from -6 to 6
- level_caps: bfloat16 [2, 8, 512, 256], P(None, ('parts', 'top'), 'leaf'), parts along dimension 1, may hold values from -0.375 to 0.375
- top_left: bfloat16 [8, 2560, 128], P(('parts', 'top'), 'leaf'), parts along dimension 0, may hold values from -0.1875 to 0.1875
- top_right: bfloat16 [8, 2560, 128], P(('parts', 'top'), 'leaf'), parts along dimension 0, may hold values from -6 to 6
- top_caps: bfloat16 [1024, 512], P(('parts', 'top')), parts along dimension 0, may hold values from -0.25 to 0.25
Outputs:
- solution: float32 [8, 2560, 256], P(('parts', 'top'), 'leaf'), parts along dimension 0
There are 2 independent parts, one for each index of `parts`. A program takes and returns all parts, laid end to end along the dimension named above; each array names one. Nothing has to cross between parts.
Inputs may be any that keep to these rules, and one draw needn't show every extreme that they name: Each leaf block of leaf_inverse is lower triangular with a positive diagonal.
All inputs are finite; a program needn't handle non-finite values.
Results may differ from a plain program's by a relative error of at most 0.0075.
Values may be sent and summed in bfloat16 or wider, within the bound.
No kernel may reach another device: no remote copies, remote signals or barrier semaphores. Data moves between devices by JAX's collectives and lax.ppermute only.
A program may use at most 64 MiB of HBM per device.

v0:
```python
import math

import jax
import jax.numpy as jnp
from jax import lax
from jax.sharding import PartitionSpec as P


def from_partner(value, axis, distance):
    mask = 2**distance
    pairs = [(source, source ^ mask) for source in range(lax.axis_size(axis))]
    return lax.ppermute(value, axis, pairs)


def project_rows(basis, current):
    return lax.dot_general(
        basis,
        current.astype(jnp.bfloat16),
        (((0,), (0,)), ((), ())),
        preferred_element_type=jnp.float32,
    )


def pair_swaps(partial_value, shift_bits):
    position = lax.axis_index("leaf") >> shift_bits
    for bit_index in range(shift_bits):
        partial_value = partial_value + from_partner(partial_value, "leaf", bit_index)
    sibling_sum = from_partner(partial_value.astype(jnp.bfloat16), "leaf", shift_bits).astype(
        partial_value.dtype
    )
    lower_side = position & 1 == 0
    return jnp.where(
        lower_side,
        jnp.concatenate([partial_value, sibling_sum], 0),
        jnp.concatenate([sibling_sum, partial_value], 0),
    )


def level_update(current, project_basis, update_basis, caps_rows, level_num):
    leaf_rows = current.shape[0]
    shift_bits = level_num - 1
    partial_value = project_rows(project_basis, current) * (
        1.0 / math.sqrt(leaf_rows * 2**shift_bits)
    )
    stacked = pair_swaps(partial_value, shift_bits)
    weights = jnp.dot(
        caps_rows, stacked.astype(jnp.bfloat16), preferred_element_type=jnp.float32
    ).astype(jnp.bfloat16)
    return current - jnp.dot(update_basis, weights, preferred_element_type=jnp.float32)


def top_update(current, project_basis, update_basis, caps_rows):
    leaf_count = lax.axis_size("leaf")
    partial_value = project_rows(project_basis, current) * (
        1.0 / math.sqrt(leaf_count * current.shape[0])
    )
    column_total = lax.psum(partial_value, "leaf")
    stacked = lax.all_gather(column_total.astype(jnp.bfloat16), "top", axis=0, tiled=True)
    weights = jnp.dot(caps_rows, stacked, preferred_element_type=jnp.float32).astype(jnp.bfloat16)
    return current - jnp.dot(update_basis, weights, preferred_element_type=jnp.float32)


def on_device(
    right_side, leaf_inverse, left_basis, right_basis, level_caps, top_left, top_right, top_caps
):
    levels = left_basis.shape[0]
    inverse_block = leaf_inverse[0]
    current = jnp.dot(
        inverse_block, right_side[0].astype(jnp.bfloat16), preferred_element_type=jnp.float32
    )
    for level_num in range(1, levels + 1):
        current = level_update(
            current,
            right_basis[level_num - 1, 0],
            left_basis[level_num - 1, 0],
            level_caps[level_num - 1, 0],
            level_num,
        )
    current = top_update(current, top_right[0], top_left[0], top_caps)
    current = top_update(current, top_left[0], top_right[0], top_caps)
    for level_num in range(levels, 0, -1):
        current = level_update(
            current,
            left_basis[level_num - 1, 0],
            right_basis[level_num - 1, 0],
            level_caps[level_num - 1, 0],
            level_num,
        )
    current = project_rows(inverse_block, current)
    return current[None]


def solution(mesh):
    return jax.shard_map(
        on_device,
        mesh=mesh,
        in_specs=(
            P(("parts", "top"), "leaf", None),
            P(("parts", "top"), "leaf", None),
            P(None, ("parts", "top"), "leaf", None),
            P(None, ("parts", "top"), "leaf", None),
            P(None, ("parts", "top"), "leaf", None),
            P(("parts", "top"), "leaf", None),
            P(("parts", "top"), "leaf", None),
            P(("parts", "top"), None),
        ),
        out_specs=P(("parts", "top"), "leaf", None),
        check_vma=False,
    )
```

profile of v0, /device:TPU:0, one launch (start us, length us, event | category | flops | bytes accessed | tf_op | source)
XLA Modules:
  0.0 93.3 jit_solution(5820424412641615513)
XLA Ops:
  0.0 1.1 %copy-done = bf16[1,640,640]{2,1,0:T(8,128)(2,1)S(1)} copy-done((bf16[1,640,640]{2,1,0:T(8,128)(2,1)S(1)}, bf16[1,640,640]{2,1,0:T(8,128)(2,1)}, u32[]{:S(2)}) %copy-start) | copy-done | bytes 819224
  1.1 1.5 %fusion.14 = f32[640,256]{1,0:T(8,128)S(1)} fusion(bf16[1,640,640]{2,1,0:T(8,128)(2,1)S(1)} %copy-done, f32[1,640,256]{2,1,0:T(8,128)} %param.8), kind=kOutput, calls=%fused_computation.33 | convolution fusion | flops 209879040 | bytes 2129920 | tf_op jit(solution)/shard_map/dot_general | solution.py:68
  3.0 3.1 %collective-permute-start = (bf16[128,256]{1,0:T(8,128)(2,1)S(1)}, bf16[128,256]{1,0:T(8,128)(2,1)S(1)}, u32[]{:S(2)}, u32[]{:S(2)}) collective-permute-start(bf16[128,256]{1,0:T(8,128)(2,1)S(1)} %fusion.12), channel_id=1, source_target_pairs={{0,4},{4,0},{8,12},{12,8},{1,5},{5,1},{9,13},{13,9},{2,6},{6,2},{1... | collective-permute-start | bytes 196616 | tf_op jit(solution)/shard_map/ppermute | solution.py:12
  6.1 2.2 %collective-permute-done = bf16[128,256]{1,0:T(8,128)(2,1)S(1)} collective-permute-done((bf16[128,256]{1,0:T(8,128)(2,1)S(1)}, bf16[128,256]{1,0:T(8,128)(2,1)S(1)}, u32[]{:S(2)}, u32[]{:S(2)}) %collective-permute-start) | collective-permute-done | bytes 65568 | tf_op jit(solution)/shard_map/ppermute | solution.py:12
  8.3 0.5 fusion.5
  9.1 2.1 %collective-permute-start.1 = (f32[128,256]{1,0:T(8,128)S(1)}, f32[128,256]{1,0:T(8,128)S(1)}, u32[]{:S(2)}, u32[]{:S(2)}) collective-permute-start(f32[128,256]{1,0:T(8,128)S(1)} %fusion.11), channel_id=1, source_target_pairs={{0,4},{4,0},{8,12},{12,8},{1,5},{5,1},{9,13},{13,9},{2,6},{6,2},{1... | collective-permute-start | bytes 393224 | tf_op jit(solution)/shard_map/ppermute | solution.py:12
  11.1 3.0 %collective-permute-done.1 = f32[128,256]{1,0:T(8,128)S(1)} collective-permute-done((f32[128,256]{1,0:T(8,128)S(1)}, f32[128,256]{1,0:T(8,128)S(1)}, u32[]{:S(2)}, u32[]{:S(2)}) %collective-permute-start.1) | collective-permute-done | bytes 131104 | tf_op jit(solution)/shard_map/ppermute | solution.py:12
  14.1 3.1 %collective-permute-start.2 = (bf16[128,256]{1,0:T(8,128)(2,1)S(1)}, bf16[128,256]{1,0:T(8,128)(2,1)S(1)}, u32[]{:S(2)}, u32[]{:S(2)}) collective-permute-start(bf16[128,256]{1,0:T(8,128)(2,1)S(1)} %add.10), channel_id=1, source_target_pairs={{0,8},{4,12},{8,0},{12,4},{1,9},{5,13},{9,1},{13,5},{2,10},{6,14},... | collective-permute-start | bytes 196616 | tf_op jit(solution)/shard_map/ppermute | solution.py:12
  17.2 2.2 %collective-permute-done.2 = bf16[128,256]{1,0:T(8,128)(2,1)S(1)} collective-permute-done((bf16[128,256]{1,0:T(8,128)(2,1)S(1)}, bf16[128,256]{1,0:T(8,128)(2,1)S(1)}, u32[]{:S(2)}, u32[]{:S(2)}) %collective-permute-start.2) | collective-permute-done | bytes 65568 | tf_op jit(solution)/shard_map/ppermute | solution.py:12
  19.5 0.5 fusion.4
  20.3 22.1 %all-reduce.2 = bf16[128,256]{0,1:T(8,128)(2,1)S(1)} all-reduce(f32[128,256]{0,1:T(8,128)S(1)} %fusion.10), channel_id=1, replica_groups=mesh['parts'=2,'leaf'=4,'top'=4] {'leaf'}, use_global_device_ids=true, to_apply=%region_0.1 | all-reduce | flops 32768 | bytes 196608 | tf_op jit(solution)/shard_map/psum | solution.py:57
  42.4 5.9 %all_gather.6 = bf16[512,256]{0,1:T(8,128)(2,1)S(1)} all-gather(bf16[128,256]{0,1:T(8,128)(2,1)S(1)} %all-reduce.2), channel_id=1, replica_groups=mesh['parts'=2,'leaf'=4,'top'=4] {'top'}, dimensions={0}, use_global_device_ids=true | all-gather | bytes 327680 | tf_op jit(solution)/shard_map/all_gather | solution.py:58
  48.3 0.6 fusion.3
  48.9 0.3 fusion.9
  49.2 18.4 %all-reduce.3 = bf16[128,256]{0,1:T(8,128)(2,1)S(1)} all-reduce(f32[128,256]{0,1:T(8,128)S(1)} %fusion.9), channel_id=1, replica_groups=mesh['parts'=2,'leaf'=4,'top'=4] {'leaf'}, use_global_device_ids=true, to_apply=%region_1.2 | all-reduce | flops 32768 | bytes 196608 | tf_op jit(solution)/shard_map/psum | solution.py:57
  67.7 5.9 %all_gather.7 = bf16[512,256]{0,1:T(8,128)(2,1)S(1)} all-gather(bf16[128,256]{0,1:T(8,128)(2,1)S(1)} %all-reduce.3), channel_id=1, replica_groups=mesh['parts'=2,'leaf'=4,'top'=4] {'top'}, dimensions={0}, use_global_device_ids=true | all-gather | bytes 327680 | tf_op jit(solution)/shard_map/all_gather | solution.py:58
  73.6 0.6 fusion.2
  74.6 5.7 %collective-permute-done.3 = f32[128,256]{1,0:T(8,128)S(1)} collective-permute-done((f32[128,256]{1,0:T(8,128)S(1)}, f32[128,256]{1,0:T(8,128)S(1)}, u32[]{:S(2)}, u32[]{:S(2)}) %collective-permute-start.3) | collective-permute-done | bytes 131104 | tf_op jit(solution)/shard_map/ppermute | solution.py:12
  80.3 0.8 collective-permute-start.4
  81.1 5.1 %collective-permute-done.4 = bf16[128,256]{1,0:T(8,128)(2,1)S(1)} collective-permute-done((bf16[128,256]{1,0:T(8,128)(2,1)S(1)}, bf16[128,256]{1,0:T(8,128)(2,1)S(1)}, u32[]{:S(2)}, u32[]{:S(2)}) %collective-permute-start.4) | collective-permute-done | bytes 65568 | tf_op jit(solution)/shard_map/ppermute | solution.py:12
  86.2 0.5 fusion.1
  87.0 4.3 %collective-permute-done.5 = bf16[128,256]{1,0:T(8,128)(2,1)S(1)} collective-permute-done((bf16[128,256]{1,0:T(8,128)(2,1)S(1)}, bf16[128,256]{1,0:T(8,128)(2,1)S(1)}, u32[]{:S(2)}, u32[]{:S(2)}) %collective-permute-start.5) | collective-permute-done | bytes 65568 | tf_op jit(solution)/shard_map/ppermute | solution.py:12
  91.5 0.8 convolution_bitcast_fusion
  92.3 1.1 %copy.14 = f32[1,640,256]{2,1,0:T(8,128)} copy(f32[1,640,256]{1,2,0:T(8,128)S(1)} %convolution_bitcast_fusion) | data formatting | bytes 1310720 | tf_op jit(solution)/shard_map/broadcast_in_dim | solution.py:90
  (29 shorter events, 1.8 us)
Async XLA Ops:
  0.0 1.1 %copy-start = (bf16[1,640,640]{2,1,0:T(8,128)(2,1)S(1)}, bf16[1,640,640]{2,1,0:T(8,128)(2,1)}, u32[]{:S(2)}) copy-start(bf16[1,640,640]{2,1,0:T(8,128)(2,1)} %param.9) | copy-start | bytes 2457604
  0.0 2.7 %copy-start.1 = (bf16[2,1,640,128]{3,2,1,0:T(8,128)(2,1)S(1)}, bf16[2,1,640,128]{3,2,1,0:T(8,128)(2,1)}, u32[]{:S(2)}) copy-start(bf16[2,1,640,128]{3,2,1,0:T(8,128)(2,1)} %param.11) | copy-start | bytes 983044
  2.7 5.6 %copy-start.2 = (bf16[2,1,640,128]{3,2,1,0:T(8,128)(2,1)S(1)}, bf16[2,1,640,128]{3,2,1,0:T(8,128)(2,1)}, u32[]{:S(2)}) copy-start(bf16[2,1,640,128]{3,2,1,0:T(8,128)(2,1)} %param.10) | copy-start | bytes 983044
  2.7 5.6 %copy-start.8 = (bf16[2,1,128,256]{3,2,1,0:T(8,128)(2,1)S(1)}, bf16[2,1,128,256]{3,2,1,0:T(8,128)(2,1)}, u32[]{:S(2)}) copy-start(bf16[2,1,128,256]{3,2,1,0:T(8,128)(2,1)} %param.12) | copy-start | bytes 393220
  3.0 5.3 %collective-permute-start = (bf16[128,256]{1,0:T(8,128)(2,1)S(1)}, bf16[128,256]{1,0:T(8,128)(2,1)S(1)}, u32[]{:S(2)}, u32[]{:S(2)}) collective-permute-start(bf16[128,256]{1,0:T(8,128)(2,1)S(1)} %fusion.12), channel_id=1, source_target_pairs={{0,4},{4,0},{8,12},{12,8},{1,5},{5,1},{9,13},{13,9},{2,6},{6,2},{1... | collective-permute-start | bytes 196616 | tf_op jit(solution)/shard_map/ppermute | solution.py:12
  9.1 5.0 %collective-permute-start.1 = (f32[128,256]{1,0:T(8,128)S(1)}, f32[128,256]{1,0:T(8,128)S(1)}, u32[]{:S(2)}, u32[]{:S(2)}) collective-permute-start(f32[128,256]{1,0:T(8,128)S(1)} %fusion.11), channel_id=1, source_target_pairs={{0,4},{4,0},{8,12},{12,8},{1,5},{5,1},{9,13},{13,9},{2,6},{6,2},{1... | collective-permute-start | bytes 393224 | tf_op jit(solution)/shard_map/ppermute | solution.py:12
  14.1 5.3 %collective-permute-start.2 = (bf16[128,256]{1,0:T(8,128)(2,1)S(1)}, bf16[128,256]{1,0:T(8,128)(2,1)S(1)}, u32[]{:S(2)}, u32[]{:S(2)}) collective-permute-start(bf16[128,256]{1,0:T(8,128)(2,1)S(1)} %add.10), channel_id=1, source_target_pairs={{0,8},{4,12},{8,0},{12,4},{1,9},{5,13},{9,1},{13,5},{2,10},{6,14},... | collective-permute-start | bytes 196616 | tf_op jit(solution)/shard_map/ppermute | solution.py:12
  17.2 2.7 %copy-start.4 = (bf16[1,640,128]{2,1,0:T(8,128)(2,1)S(1)}, bf16[1,640,128]{2,1,0:T(8,128)(2,1)}, u32[]{:S(2)}) copy-start(bf16[1,640,128]{2,1,0:T(8,128)(2,1)} %param.14) | copy-start | bytes 491524
  42.4 6.0 %copy-start.3 = (bf16[1,640,128]{2,1,0:T(8,128)(2,1)S(1)}, bf16[1,640,128]{2,1,0:T(8,128)(2,1)}, u32[]{:S(2)}) copy-start(bf16[1,640,128]{2,1,0:T(8,128)(2,1)} %param.13) | copy-start | bytes 491524
  42.4 6.0 %copy-start.6 = (bf16[128,512]{1,0:T(8,128)(2,1)S(1)}, bf16[128,512]{1,0:T(8,128)(2,1)}, u32[]{:S(2)}) copy-start(bf16[128,512]{1,0:T(8,128)(2,1)} %param.15) | copy-start | bytes 393220
  67.7 6.0 %copy-start.5 = (bf16[1,640,128]{2,1,0:T(8,128)(2,1)S(1)}, bf16[1,640,128]{2,1,0:T(8,128)(2,1)}, u32[]{:S(2)}) copy-start(bf16[1,640,128]{2,1,0:T(8,128)(2,1)} %param.14) | copy-start | bytes 491524
  67.7 6.0 %copy-start.7 = (bf16[128,512]{1,0:T(8,128)(2,1)S(1)}, bf16[128,512]{1,0:T(8,128)(2,1)}, u32[]{:S(2)}) copy-start(bf16[128,512]{1,0:T(8,128)(2,1)} %param.15) | copy-start | bytes 393220
  74.5 11.7 %copy-start.9 = (bf16[2,1,128,256]{3,2,1,0:T(8,128)(2,1)S(1)}, bf16[2,1,128,256]{3,2,1,0:T(8,128)(2,1)}, u32[]{:S(2)}) copy-start(bf16[2,1,128,256]{3,2,1,0:T(8,128)(2,1)} %param.12) | copy-start | bytes 393220
  74.5 5.8 %collective-permute-start.3 = (f32[128,256]{1,0:T(8,128)S(1)}, f32[128,256]{1,0:T(8,128)S(1)}, u32[]{:S(2)}, u32[]{:S(2)}) collective-permute-start(f32[128,256]{1,0:T(8,128)S(1)} %fusion.8), channel_id=1, source_target_pairs={{0,4},{4,0},{8,12},{12,8},{1,5},{5,1},{9,13},{13,9},{2,6},{6,2},{1... | collective-permute-start | bytes 393224 | tf_op jit(solution)/shard_map/ppermute | solution.py:12
  80.3 5.9 %collective-permute-start.4 = (bf16[128,256]{1,0:T(8,128)(2,1)S(1)}, bf16[128,256]{1,0:T(8,128)(2,1)S(1)}, u32[]{:S(2)}, u32[]{:S(2)}) collective-permute-start(bf16[128,256]{1,0:T(8,128)(2,1)S(1)} %add.11), channel_id=1, source_target_pairs={{0,8},{4,12},{8,0},{12,4},{1,9},{5,13},{9,1},{13,5},{2,10},{6,14},... | collective-permute-start | bytes 196616 | tf_op jit(solution)/shard_map/ppermute | solution.py:12
  86.9 4.3 %collective-permute-start.5 = (bf16[128,256]{1,0:T(8,128)(2,1)S(1)}, bf16[128,256]{1,0:T(8,128)(2,1)S(1)}, u32[]{:S(2)}, u32[]{:S(2)}) collective-permute-start(bf16[128,256]{1,0:T(8,128)(2,1)S(1)} %fusion.7), channel_id=1, source_target_pairs={{0,4},{4,0},{8,12},{12,8},{1,5},{5,1},{9,13},{13,9},{2,6},{6,2},{1... | collective-permute-start | bytes 196616 | tf_op jit(solution)/shard_map/ppermute | solution.py:12
where the time goes:
time: 93.6 us; the launch traced here: 93.3 us
  blocking collectives  52.4 us (56%)
  waiting for transfers between devices  22.5 us (24%)
  starting transfers between devices  9.21 us (10%)
  matrix products  6.72 us (7%)
  local copies, waits for them, and re-layouts  2.27 us (2%)
    psum x2, blocking collectives, top_update(): column_total = lax.psum(partial_value, 'leaf')  40.5 us
    ppermute x6, waiting for transfers between devices, from_partner(): return lax.ppermute(value, axis, pairs)  22.5 us
    all_gather x2, blocking collectives, top_update(): lax.all_gather(column_total.astype(jnp.bfloat16), 'top', axis=0, tiled=True)  11.9 us
    ppermute x6, starting transfers between devices, from_partner(): return lax.ppermute(value, axis, pairs)  9.21 us
    dot_general x7, matrix products, project_rows(): lax.dot_general(basis, current.astype(jnp.bfloat16), (((0,), (0,)), ((),...  2.41 us
  transfers between devices with their start and end apart: 6, of which 6 were waited for; matrix products, arithmetic and copies ran while one was open for 0% of the time, Pallas kernels for 0%

commit v1 on v0

v1 whole, which is shorter than its diff:
```python
import math

import jax
import jax.numpy as jnp
from jax import lax
from jax.sharding import PartitionSpec as P

BF = jnp.bfloat16


def swap(value, axis, mask):
    pairs = [(source, source ^ mask) for source in range(lax.axis_size(axis))]
    return lax.ppermute(value, axis, pairs)


def dot(a, b):
    return jnp.dot(a, b, preferred_element_type=jnp.float32)


def dot_t(a, b):
    return lax.dot_general(a, b, (((0,), (0,)), ((), ())), preferred_element_type=jnp.float32)


def level_step(current, project_basis, update_basis, caps_rows, level_num):
    leaf_rows = current.shape[0]
    shift_bits = level_num - 1
    partial_value = dot_t(project_basis, current.astype(BF)) * (
        1.0 / math.sqrt(leaf_rows * 2**shift_bits)
    )
    for bit_index in range(shift_bits):
        partial_value = partial_value + swap(partial_value, "leaf", 2**bit_index)
    own = partial_value.astype(BF)
    other = swap(own, "leaf", 2**shift_bits)
    upper_side = (lax.axis_index("leaf") >> shift_bits) & 1 == 1
    stacked = ordered(upper_side, own, other)
    weights = dot(caps_rows, stacked).astype(BF)
    return current - dot(update_basis, weights)


def top_step(current, project_basis, update_basis, caps_rows):
    leaf_count = lax.axis_size("leaf")
    partial_value = dot_t(project_basis, current.astype(BF)) * (
        1.0 / math.sqrt(leaf_count * current.shape[0])
    )
    column_total = lax.psum(partial_value, "leaf")
    stacked = lax.all_gather(column_total.astype(BF), "top", axis=0, tiled=True)
    weights = dot(caps_rows, stacked).astype(BF)
    return current - dot(update_basis, weights)


def step_by_step(rhs, inverse, lefts, rights, caps, top_left, top_right, top_caps):
    levels = len(lefts)
    current = dot(inverse, rhs.astype(BF))
    for k in range(levels):
        current = level_step(current, rights[k], lefts[k], caps[k], k + 1)
    current = top_step(current, top_right, top_left, top_caps)
    current = top_step(current, top_left, top_right, top_caps)
    for k in reversed(range(levels)):
        current = level_step(current, lefts[k], rights[k], caps[k], k + 1)
    return dot_t(inverse, current.astype(BF))


def ordered(upper_side, own, other):
    return jnp.where(
        upper_side, jnp.concatenate([other, own], 0), jnp.concatenate([own, other], 0)
    )


def halves(upper_side, value):
    width = value.shape[1] // 2
    low, high = value[:, :width], value[:, width:]
    return jnp.where(upper_side, high, low), jnp.where(upper_side, low, high)


def gather_top(value):
    count = lax.axis_size("top")
    if count != 4:
        return lax.all_gather(value, "top")
    index = lax.axis_index("top")
    far = swap(value, "top", 2)
    near = swap(value, "top", 1)
    far_near = swap(far, "top", 1)
    odd, high = index & 1 == 1, index & 2 == 2
    pair = jnp.where(odd, jnp.stack([near, value]), jnp.stack([value, near]))
    far_pair = jnp.where(odd, jnp.stack([far_near, far]), jnp.stack([far, far_near]))
    return jnp.where(
        high, jnp.concatenate([far_pair, pair], 0), jnp.concatenate([pair, far_pair], 0)
    )


def two_levels(rhs, inverse, lefts, rights, caps, top_left, top_right, top_caps):
    leaf_rows = rhs.shape[0]
    rank = top_left.shape[1]
    s1 = 1.0 / math.sqrt(leaf_rows)
    s2 = 1.0 / math.sqrt(leaf_rows * 2)
    st = 1.0 / math.sqrt(leaf_rows * 4)
    leaf = lax.axis_index("leaf")
    odd, high = leaf & 1 == 1, leaf & 2 == 2
    left1, left2 = lefts
    right1, right2 = rights
    caps1, caps2 = caps

    def cat(*values):
        return jnp.concatenate([v.astype(BF) for v in values], 1)

    def cut(value, *widths):
        out, at = [], 0
        for w in widths:
            out.append(value[:, at * rank : (at + w) * rank])
            at += w
        return out

    start = dot(inverse, rhs.astype(BF))
    proj1 = (dot_t(right1, start.astype(BF)) * s1).astype(BF)
    proj1_sib = swap(proj1, "leaf", 1)

    gram_rl = (dot_t(top_right, left2) * st).astype(BF)
    gram_ll = (dot_t(top_left, left2) * st).astype(BF)
    gram_top = dot_t(top_left, top_left) * st
    next3, next4 = dot(gram_rl, caps2), dot(gram_ll, caps2)
    down5 = cat(dot_t(left2, top_left) * s2, dot_t(left2, top_right) * s2)
    down6 = cat(
        dot_t(left1, top_left) * s1, dot_t(left1, top_right) * s1, dot_t(left1, right2) * s1
    )
    early = swap(cat(next3, next4, gram_top), "leaf", 1)
    all_caps = gather_top(top_caps)
    next3_sib, next4_sib, gram_sib = cut(early, 2, 2, 1)
    next3, next4, gram_top = next3 + next3_sib, next4 + next4_sib, gram_top + gram_sib
    next3_own, next3_send = halves(high, next3)
    next4_own, next4_send = halves(high, next4)
    cross = swap(cat(next3_send, next4_send, gram_top), "leaf", 2)
    next3_far, next4_far, gram_far = cut(cross, 1, 1, 1)
    gram_top = gram_top + gram_far

    coef1 = dot(caps1, ordered(odd, proj1, proj1_sib)).astype(BF)
    state1 = start - dot(left1, coef1)
    state1_b = state1.astype(BF)
    proj2 = dot_t(right2, state1_b) * s2
    proj3 = dot_t(top_right, state1_b) * st
    proj4 = dot_t(top_left, state1_b) * st
    keep3, send3 = halves(odd, proj3)
    keep4, send4 = halves(odd, proj4)
    pair_in = swap(cat(proj2, send3, send4), "leaf", 1)
    in2, in3, in4 = cut(pair_in, 2, 1, 1)
    half2 = (proj2 + in2).astype(BF)
    half2_keep, _ = halves(odd, half2)
    half3 = keep3 + in3 - dot(next3_own.astype(BF), half2_keep)
    half4 = keep4 + in4 - dot(next4_own.astype(BF), half2_keep)
    cross_in = swap(cat(half2, half3, half4), "leaf", 2)
    far2, far3, far4 = cut(cross_in, 2, 1, 1)
    far2_keep, _ = halves(odd, far2)
    column3 = (
        half3 + far3 - dot(next3_send.astype(BF), far2_keep) - dot(next3_far, half2_keep)
    )
    column4 = (
        half4 + far4 - dot(next4_send.astype(BF), far2_keep) - dot(next4_far, half2_keep)
    )
    top_in = gather_top(cat(column3, column4, gram_top))

    late = swap(cat(down5, down6, caps2), "leaf", 1)
    down5_sib, down6_sib, caps2_sib = cut(late, 2, 3, 2)
    down5 = (down5.astype(jnp.float32) + down5_sib).astype(BF)
    down5_far = swap(down5, "leaf", 2)

    coef2 = dot(caps2, ordered(high, half2, far2)).astype(BF)
    state2 = state1 - dot(left2, coef2)
    state2_b = state2.astype(BF)
    down_proj5 = dot_t(left2, state2_b) * s2
    down_proj6 = dot_t(left1, state2_b) * s1
    down_in = swap(cat(down_proj5, down_proj6), "leaf", 1)
    down5_in, down6_in = cut(down_in, 2, 2)
    down_half5 = down_proj5 + down5_in
    down_far5 = swap(down_half5.astype(BF), "leaf", 2)

    stack3 = top_in[:, :, :rank].reshape(-1, rank)
    top_coef_all = dot(all_caps.reshape(-1, all_caps.shape[-1]), stack3).astype(BF)
    turn = lax.dot_general(
        top_in[:, :, 2 * rank :],
        top_coef_all.reshape(-1, rank, rank),
        (((2,), (1,)), ((0,), (0,))),
        preferred_element_type=jnp.float32,
    )
    stack4 = (top_in[:, :, rank : 2 * rank] - turn).astype(BF).reshape(-1, rank)
    up_coef = dot(top_caps, stack3).astype(BF)
    down_coef = dot(top_caps, stack4).astype(BF)
    back = swap(cat(up_coef, down_coef), "leaf", 1)
    up_sib, down_sib = cut(back, 1, 1)

    def columns(own, other):
        return jnp.where(
            odd, jnp.concatenate([other, own], 1), jnp.concatenate([own, other], 1)
        )

    up_coef, down_coef = columns(up_coef, up_sib), columns(down_coef, down_sib)
    both = jnp.concatenate([up_coef, down_coef], 0)
    state4 = state2 - dot(jnp.concatenate([top_left, top_right], 1), both)
    half5 = (down_half5 - dot(down5, both)).astype(BF)
    far5 = (down_far5 - dot(down5_far, both)).astype(BF)
    stack5 = ordered(high, half5, far5)
    coef5 = dot(caps2, stack5).astype(BF)
    coef5_sib = dot(caps2_sib, stack5).astype(BF)
    state5 = state4 - dot(right2, coef5)
    proj6 = (dot_t(left1, state5.astype(BF)) * s1).astype(BF)
    proj6_sib = (down6_in - dot(down6_sib, jnp.concatenate([both, coef5_sib], 0))).astype(BF)
    coef6 = dot(caps1, ordered(odd, proj6, proj6_sib)).astype(BF)
    state6 = state5 - dot(right1, coef6)
    return dot_t(inverse, state6.astype(BF))


def on_device(
    right_side, leaf_inverse, left_basis, right_basis, level_caps, top_left, top_right, top_caps
):
    levels = left_basis.shape[0]
    run = two_levels if levels == 2 and lax.axis_size("leaf") == 4 else step_by_step
    out = run(
        right_side[0],
        leaf_inverse[0],
        [left_basis[k, 0] for k in range(levels)],
        [right_basis[k, 0] for k in range(levels)],
        [level_caps[k, 0] for k in range(levels)],
        top_left[0],
        top_right[0],
        top_caps,
    )
    return out[None]


def solution(mesh):
    rows = P(("parts", "top"), "leaf", None)
    level_rows = P(None, ("parts", "top"), "leaf", None)
    return jax.shard_map(
        on_device,
        mesh=mesh,
        in_specs=(
            rows,
            rows,
            level_rows,
            level_rows,
            level_rows,
            rows,
            rows,
            P(("parts", "top"), None),
        ),
        out_specs=rows,
        check_vma=False,
    )
```

time: 93.6 us -> 63.8 us (0.68)
  blocking collectives: 52.4 us -> 0 us
  matrix products: 6.72 us -> 20 us
  waiting for transfers between devices: 22.5 us -> 9.94 us
  other arithmetic: 0.03 us -> 9.69 us
  starting transfers between devices: 9.21 us -> 18.6 us
  local copies, waits for them, and re-layouts: 2.27 us -> 4.15 us
    psum x2 -> x0, blocking collectives: 40.5 us -> none  [top_update(): column_total = lax.psum(partial_value, 'leaf')]
    dot_general x14 -> x36, matrix products: 6.72 us -> 20 us  [the longest x21 12.6 us: dot(): return jnp.dot(a, b, preferred_element_type=jnp.float32)]
    ppermute x6 -> x16, waiting for transfers between devices: 22.5 us -> 9.94 us  [swap(): return lax.ppermute(value, axis, pairs)]
    all_gather x2 -> x0, blocking collectives: 11.9 us -> none  [top_update(): lax.all_gather(column_total.astype(jnp.bfloat16), 'top', axis=0, tiled=True)]
    ppermute x6 -> x16, starting transfers between devices: 9.21 us -> 18.6 us  [swap(): return lax.ppermute(value, axis, pairs)]
    select_n x0 -> x8, other arithmetic: none -> 4.26 us  [the longest x2 2.04 us: gather_top(): pair = jnp.where(odd, jnp.stack([near, value]), jnp.stack([value, near]))]
    convert_element_type x0 -> x9, other arithmetic: none -> 3.09 us  [the longest x5 1.57 us: cat(): return jnp.concatenate([v.astype(BF) for v in values], 1)]
    concatenate x0 -> x7, other arithmetic: none -> 1.44 us  [cat(): return jnp.concatenate([v.astype(BF) for v in values], 1)]
  transfers between devices with their start and end apart: 6 -> 16, of which waited for: 6 -> 7; matrix products, arithmetic and copies ran while one was open for 0% -> 41% of each run, Pallas kernels for 0% -> 0%
where the time goes in v1:
time: 63.8 us; the launch traced here: 63 us
  matrix products  20 us (31%)
  starting transfers between devices  18.6 us (29%)
  waiting for transfers between devices  9.94 us (16%)
  other arithmetic  9.69 us (15%)
  local copies, waits for them, and re-layouts  4.15 us (7%)
    ppermute x16, starting transfers between devices, swap(): return lax.ppermute(value, axis, pairs)  18.6 us
    dot_general x21, matrix products, dot(): return jnp.dot(a, b, preferred_element_type=jnp.float32)  12.6 us
    ppermute x16, waiting for transfers between devices, swap(): return lax.ppermute(value, axis, pairs)  9.94 us
    dot_general x14, matrix products, dot_t(): lax.dot_general(a, b, (((0,), (0,)), ((), ())), preferred_element_type=jn...  7.26 us
    select_n x2, other arithmetic, gather_top(): pair = jnp.where(odd, jnp.stack([near, value]), jnp.stack([value, near]))  2.04 us
    select_n x2, other arithmetic, gather_top(): jnp.where(odd, jnp.stack([far_near, far]), jnp.stack([far, far_near]))  2.02 us
    unnamed x39, local copies, waits for them, and re-layouts  1.78 us
    convert_element_type x5, other arithmetic, cat(): return jnp.concatenate([v.astype(BF) for v in values], 1)  1.57 us
  transfers between devices with their start and end apart: 16, of which 7 were waited for; matrix products, arithmetic and copies ran while one was open for 41% of the time, Pallas kernels for 0%

profile of v1, /device:TPU:0, one launch (start us, length us, event | category | flops | bytes accessed | tf_op | source)
XLA Modules:
  0.0 63.0 jit_solution(18137320871729837001)
XLA Ops:
  0.5 2.6 %collective-permute-start.8 = (bf16[128,512]{1,0:T(8,128)(2,1)}, bf16[128,512]{1,0:T(8,128)(2,1)}, u32[]{:S(2)}, u32[]{:S(2)}) collective-permute-start(bf16[128,512]{1,0:T(8,128)(2,1)} %param.15), channel_id=1, source_target_pairs={{0,2},{1,3},{2,0},{3,1},{4,6},{5,7},{6,4},{7,5},{8,10},{9,11},{10,... | collective-permute-start | bytes 393224 | tf_op jit(solution)/shard_map/ppermute | solution.py:13
  3.0 1.5 %fusion.32 = f32[640,256]{1,0:T(8,128)S(1)} fusion(bf16[1,640,640]{2,1,0:T(8,128)(2,1)S(1)} %copy-done, f32[1,640,256]{2,1,0:T(8,128)} %param.8), kind=kOutput, calls=%fused_computation.63 | convolution fusion | flops 209879040 | bytes 2129920 | tf_op jit(solution)/shard_map/dot_general | solution.py:17
  4.9 1.6 %collective-permute-start = (bf16[128,256]{1,0:T(8,128)(2,1)S(1)}, bf16[128,256]{1,0:T(8,128)(2,1)}, u32[]{:S(2)}, u32[]{:S(2)}) collective-permute-start(bf16[128,256]{1,0:T(8,128)(2,1)S(1)} %fusion.16), channel_id=1, source_target_pairs={{0,4},{4,0},{8,12},{12,8},{1,5},{5,1},{9,13},{13,9},{2,6},{6,2},{1... | collective-permute-start | bytes 196616 | tf_op jit(solution)/shard_map/ppermute | solution.py:13
  7.7 1.0 %fusion.202 = (bf16[128,256]{1,0:T(8,128)(2,1)S(1)}, f32[128,256]{1,0:T(8,128)}) fusion(bf16[2,1,128,256]{3,2,1,0:T(8,128)(2,1)S(1)} %copy-done.6, bf16[2,1,640,128]{3,2,1,0:T(8,128)(2,1)S(1)} %copy-done.1, bf16[1,640,128]{2,1,0:T(8,128)(2,1)S(1)} %copy-done.3), kind=kOutput, calls=%fused_computation.236 | convolution fusion | flops 29425664 | bytes 589824 | tf_op jit(solution)/shard_map/dot_general | solution.py:17
  15.2 1.4 %collective-permute-start.14 = (bf16[128,896]{0,1:T(8,128)(2,1)}, bf16[128,896]{0,1:T(8,128)(2,1)}, u32[]{:S(2)}, u32[]{:S(2)}) collective-permute-start(bf16[128,896]{0,1:T(8,128)(2,1)} %bitcast_dynamic-update-slice_fusion), channel_id=1, source_target_pairs={{0,4},{4,0},{8,12},{12,8},{1,5},{5,1},{9,13},{13,9},{2,6},{6,2},{1... | collective-permute-start | bytes 688136 | tf_op jit(solution)/shard_map/ppermute | solution.py:13
  16.6 1.4 %fusion.3 = f32[640,256]{1,0:T(8,128)S(1)} fusion(f32[640,256]{1,0:T(8,128)S(1)} %fusion.32, bf16[128,256]{1,0:T(8,128)(2,1)S(1)} %copy-done.15, bf16[128,256]{1,0:T(8,128)(2,1)} %collective-permute-done, pred[]{:T(512)S(6)} %eq.14, bf16[2,1,640,128]{3,2,1,0:T(8,128)(2,1)S(1)} %copy-done.1, bf16[2,1,128,256]{3,2,1,0:T(8,128)(2,1)S(1)} %copy-done.6), kind=kOutput, calls=%fused_computation.9 | convolution fusion | flops 59506688 | bytes 1671169 | tf_op jit(solution)/shard_map/dot_general | solution.py:17
  19.8 1.0 %maximum_select_fusion.3 = bf16[2,128,512]{2,1,0:T(8,128)(2,1)S(1)} fusion(bf16[1,128,512]{2,1,0:T(8,128)(2,1)S(1)} %bitcast.193, bf16[1,128,512]{2,1,0:T(8,128)(2,1)} %bitcast.24, pred[]{:T(512)S(6)} %eq.17), kind=kLoop, calls=%fused_computation.75 | loop fusion | flops 393216 | bytes 524289 | tf_op jit(solution)/shard_map/jit(_where)/select_n | solution.py:84
  22.6 2.7 %collective-permute-start.4 = (bf16[128,384]{1,0:T(8,128)(2,1)S(1)}, bf16[128,384]{1,0:T(8,128)(2,1)S(1)}, u32[]{:S(2)}, u32[]{:S(2)}) collective-permute-start(bf16[128,384]{1,0:T(8,128)(2,1)S(1)} %pad_maximum_fusion.5), channel_id=1, source_target_pairs={{0,8},{4,12},{8,0},{12,4},{1,9},{5,13},{9,1},{13,5},{2,10},{6,14},... | collective-permute-start | bytes 294920 | tf_op jit(solution)/shard_map/ppermute | solution.py:13
  26.0 2.9 %collective-permute-start.3 = (bf16[128,512]{1,0:T(8,128)(2,1)S(1)}, bf16[128,512]{1,0:T(8,128)(2,1)S(1)}, u32[]{:S(2)}, u32[]{:S(2)}) collective-permute-start(bf16[128,512]{1,0:T(8,128)(2,1)S(1)} %pad_maximum_fusion.2), channel_id=1, source_target_pairs={{0,8},{4,12},{8,0},{12,4},{1,9},{5,13},{9,1},{13,5},{2,10},{6,14},... | collective-permute-start | bytes 393224 | tf_op jit(solution)/shard_map/ppermute | solution.py:13
  28.9 1.5 %add_convert_fusion = bf16[128,256]{0,1:T(8,128)(2,1)} fusion(bf16[128,896]{0,1:T(8,128)(2,1)} %collective-permute-done.14, bf16[128,128]{0,1:T(8,128)(2,1)S(1)} %copy-done.18, bf16[128,128]{0,1:T(8,128)(2,1)S(1)} %get-tuple-element.24), kind=kLoop, calls=%fused_computation.132 | loop fusion | flops 229376 | bytes 196608 | tf_op jit(solution)/shard_map/convert_element_type | solution.py:162
  31.0 3.7 %collective-permute-done.4 = bf16[128,384]{1,0:T(8,128)(2,1)S(1)} collective-permute-done((bf16[128,384]{1,0:T(8,128)(2,1)S(1)}, bf16[128,384]{1,0:T(8,128)(2,1)S(1)}, u32[]{:S(2)}, u32[]{:S(2)}) %collective-permute-start.4) | collective-permute-done | bytes 98336 | tf_op jit(solution)/shard_map/ppermute | solution.py:13
  35.6 1.0 %maximum_select_fusion.2 = bf16[2,128,512]{2,1,0:T(8,128)(2,1)S(1)} fusion(bf16[1,128,512]{2,1,0:T(8,128)(2,1)} %bitcast.23, bf16[1,128,512]{2,1,0:T(8,128)(2,1)S(1)} %bitcast.196, pred[]{:T(512)S(6)} %eq.17), kind=kLoop, calls=%fused_computation.74 | loop fusion | flops 393216 | bytes 524289 | tf_op jit(solution)/shard_map/jit(_where)/select_n | solution.py:85
  36.7 1.6 %collective-permute-done.3 = bf16[128,512]{1,0:T(8,128)(2,1)S(1)} collective-permute-done((bf16[128,512]{1,0:T(8,128)(2,1)S(1)}, bf16[128,512]{1,0:T(8,128)(2,1)S(1)}, u32[]{:S(2)}, u32[]{:S(2)}) %collective-permute-start.3) | collective-permute-done | bytes 131104 | tf_op jit(solution)/shard_map/ppermute | solution.py:13
  39.5 1.1 %collective-permute-start.5 = (bf16[128,384]{1,0:T(8,128)(2,1)}, bf16[128,384]{1,0:T(8,128)(2,1)}, u32[]{:S(2)}, u32[]{:S(2)}) collective-permute-start(bf16[128,384]{1,0:T(8,128)(2,1)} %get-tuple-element.7), channel_id=1, source_target_pairs={{0,2},{1,3},{2,0},{3,1},{4,6},{5,7},{6,4},{7,5},{8,10},{9,11},{10,... | collective-permute-start | bytes 294920 | tf_op jit(solution)/shard_map/ppermute | solution.py:13
  41.2 1.4 %fusion.2 = f32[640,256]{1,0:T(8,128)S(1)} fusion(f32[640,256]{1,0:T(8,128)S(1)} %fusion.3, bf16[128,256]{1,0:T(8,128)(2,1)S(1)} %add_convert_fusion.1, bf16[128,256]{1,0:T(8,128)(2,1)} %slice.177, pred[]{:T(512)S(6)} %eq.15, bf16[2,1,640,128]{3,2,1,0:T(8,128)(2,1)S(1)} %copy-done.1, bf16[2,1,128,256]{3,2,1,0:T(8,128)(2,1)S(1)} %copy-done.6), kind=kOutput, calls=%fused_computation.7 | convolution fusion | flops 59506688 | bytes 1671169 | tf_op jit(solution)/shard_map/dot_general | solution.py:17
  43.4 1.6 %collective-permute-done.5 = bf16[128,384]{1,0:T(8,128)(2,1)} collective-permute-done((bf16[128,384]{1,0:T(8,128)(2,1)}, bf16[128,384]{1,0:T(8,128)(2,1)}, u32[]{:S(2)}, u32[]{:S(2)}) %collective-permute-start.5) | collective-permute-done | bytes 98336 | tf_op jit(solution)/shard_map/ppermute | solution.py:13
  45.1 1.0 %maximum_select_fusion.5 = bf16[2,128,384]{2,1,0:T(8,128)(2,1)S(1)} fusion(bf16[1,128,384]{2,1,0:T(8,128)(2,1)S(1)} %copy-done.13, bf16[1,128,384]{2,1,0:T(8,128)(2,1)} %bitcast.18, pred[]{:T(512)S(6)} %eq.17), kind=kLoop, calls=%fused_computation.77 | loop fusion | flops 294912 | bytes 393217 | tf_op jit(solution)/shard_map/jit(_where)/select_n | solution.py:84
  49.9 3.4 %collective-permute-start.13 = (bf16[128,256]{1,0:T(8,128)(2,1)S(1)}, bf16[128,256]{1,0:T(8,128)(2,1)S(1)}, u32[]{:S(2)}, u32[]{:S(2)}) collective-permute-start(bf16[128,256]{1,0:T(8,128)(2,1)S(1)} %fusion.111), channel_id=1, source_target_pairs={{0,8},{4,12},{8,0},{12,4},{1,9},{5,13},{9,1},{13,5},{2,10},{6,14},... | collective-permute-start | bytes 196616 | tf_op jit(solution)/shard_map/ppermute | solution.py:13
  54.2 1.1 %fusion.13 = bf16[128,256]{1,0:T(8,128)(2,1)S(1)} fusion(bf16[128,256]{0,1:T(8,128)(2,1)} %add_convert_fusion, f32[128,256]{1,0:T(8,128)S(1)} %get-tuple-element.28, bf16[128,512]{1,0:T(8,128)(2,1)S(1)} %collective-permute-done.12, bf16[128,256]{0,1:T(8,128)(2,1)S(1)} %get-tuple-element.30, bf16[128,256]{0,1:T(8,128)(2,1)S(1)} %get-tuple-element.29), kind=kOutput, calls=%fused_computation.29 | convolution fusion | flops 17170432 | bytes 458752 | tf_op jit(solution)/shard_map/dot_general | solution.py:17
  55.3 1.5 %collective-permute-done.13 = bf16[128,256]{1,0:T(8,128)(2,1)S(1)} collective-permute-done((bf16[128,256]{1,0:T(8,128)(2,1)S(1)}, bf16[128,256]{1,0:T(8,128)(2,1)S(1)}, u32[]{:S(2)}, u32[]{:S(2)}) %collective-permute-start.13) | collective-permute-done | bytes 65568 | tf_op jit(solution)/shard_map/ppermute | solution.py:13
  56.8 1.0 %subtract_convert_fusion.1 = bf16[128,256]{1,0:T(8,128)(2,1)S(1)} fusion(bf16[128,256]{1,0:T(8,128)(2,1)S(1)} %collective-permute-done.13, bf16[128,256]{0,1:T(8,128)(2,1)} %collective-permute-done.15, bf16[128,256]{0,1:T(8,128)(2,1)S(1)} %get-tuple-element.30, bf16[128,256]{0,1:T(8,128)(2,1)S(1)} %get-tuple-element.29), kind=kOutput, calls=%fused_computation.131 | convolution fusion | flops 17137664 | bytes 327680 | tf_op jit(solution)/shard_map/dot_general | solution.py:17
  58.6 1.1 %convolution_convert_fusion.2 = bf16[128,256]{0,1:T(8,128)(2,1)S(1)} fusion(bf16[128,896]{0,1:T(8,128)(2,1)} %collective-permute-done.14, bf16[128,256]{1,0:T(8,128)(2,1)S(1)} %fusion.13, bf16[128,256]{1,0:T(8,128)(2,1)S(1)} %subtract_convert_fusion.1, pred[]{:T(512)S(6)} %eq.15), kind=kOutput, calls=%fused_computation.31 | convolution fusion | flops 17399808 | bytes 262145 | tf_op jit(solution)/shard_map/dot_general | solution.py:17
  59.8 1.1 %subtract_convert_fusion = bf16[128,256]{1,0:T(8,128)(2,1)S(1)} fusion(bf16[128,256]{0,1:T(8,128)(2,1)S(1)} %convolution_convert_fusion.2, bf16[128,256]{0,1:T(8,128)(2,1)S(1)} %copy-done.11, bf16[128,256]{0,1:T(8,128)(2,1)S(1)} %get-tuple-element.29, bf16[128,896]{0,1:T(8,128)(2,1)} %collective-permute-done.14, bf16[128,512]{1,0:T(8,128)(2,1)S(1)} %copy-done.17), kind=kOutput, calls=%fused_computation.130 | convolution fusion | flops 25853952 | bytes 425984 | tf_op jit(solution)/shard_map/dot_general | solution.py:17
  61.9 1.1 %copy.24 = f32[1,640,256]{2,1,0:T(8,128)} copy(f32[1,640,256]{1,2,0:T(8,128)S(1)} %convolution_bitcast_fusion) | data formatting | bytes 1310720 | tf_op jit(solution)/shard_map/broadcast_in_dim | solution.py:225
  (115 shorter events, 23.1 us)
Async XLA Ops:
  0.0 3.0 %copy-start = (bf16[1,640,640]{2,1,0:T(8,128)(2,1)S(1)}, bf16[1,640,640]{2,1,0:T(8,128)(2,1)}, u32[]{:S(2)}) copy-start(bf16[1,640,640]{2,1,0:T(8,128)(2,1)} %param.9) | copy-start | bytes 2457604
  0.0 4.5 %copy-start.4 = (bf16[2,1,640,128]{3,2,1,0:T(8,128)(2,1)S(1)}, bf16[2,1,640,128]{3,2,1,0:T(8,128)(2,1)}, u32[]{:S(2)}) copy-start(bf16[2,1,640,128]{3,2,1,0:T(8,128)(2,1)} %param.11) | copy-start | bytes 983044
  0.0 19.6 %collective-permute-start.10 = (bf16[128,512]{1,0:T(8,128)(2,1)}, bf16[128,512]{1,0:T(8,128)(2,1)}, u32[]{:S(2)}, u32[]{:S(2)}) collective-permute-start(bf16[128,512]{1,0:T(8,128)(2,1)} %param.15), channel_id=1, source_target_pairs={{0,1},{1,0},{2,3},{3,2},{4,5},{5,4},{6,7},{7,6},{8,9},{9,8},{10,11... | collective-permute-start | bytes 393224 | tf_op jit(solution)/shard_map/ppermute | solution.py:13
  0.5 19.1 %collective-permute-start.8 = (bf16[128,512]{1,0:T(8,128)(2,1)}, bf16[128,512]{1,0:T(8,128)(2,1)}, u32[]{:S(2)}, u32[]{:S(2)}) collective-permute-start(bf16[128,512]{1,0:T(8,128)(2,1)} %param.15), channel_id=1, source_target_pairs={{0,2},{1,3},{2,0},{3,1},{4,6},{5,7},{6,4},{7,5},{8,10},{9,11},{10,... | collective-permute-start | bytes 393224 | tf_op jit(solution)/shard_map/ppermute | solution.py:13
  4.6 2.2 %copy-start.1 = (bf16[2,1,640,128]{3,2,1,0:T(8,128)(2,1)S(1)}, bf16[2,1,640,128]{3,2,1,0:T(8,128)(2,1)}, u32[]{:S(2)}) copy-start(bf16[2,1,640,128]{3,2,1,0:T(8,128)(2,1)} %param.10) | copy-start | bytes 983044
  4.9 11.8 %collective-permute-start = (bf16[128,256]{1,0:T(8,128)(2,1)S(1)}, bf16[128,256]{1,0:T(8,128)(2,1)}, u32[]{:S(2)}, u32[]{:S(2)}) collective-permute-start(bf16[128,256]{1,0:T(8,128)(2,1)S(1)} %fusion.16), channel_id=1, source_target_pairs={{0,4},{4,0},{8,12},{12,8},{1,5},{5,1},{9,13},{13,9},{2,6},{6,2},{1... | collective-permute-start | bytes 196616 | tf_op jit(solution)/shard_map/ppermute | solution.py:13
  9.4 11.4 %collective-permute-start.2 = (bf16[128,640]{1,0:T(8,128)(2,1)}, bf16[128,640]{1,0:T(8,128)(2,1)}, u32[]{:S(2)}, u32[]{:S(2)}) collective-permute-start(bf16[128,640]{1,0:T(8,128)(2,1)} %pad_maximum_fusion), channel_id=1, source_target_pairs={{0,4},{4,0},{8,12},{12,8},{1,5},{5,1},{9,13},{13,9},{2,6},{6,2},{1... | collective-permute-start | bytes 491528 | tf_op jit(solution)/shard_map/ppermute | solution.py:13
  15.2 13.7 %collective-permute-start.14 = (bf16[128,896]{0,1:T(8,128)(2,1)}, bf16[128,896]{0,1:T(8,128)(2,1)}, u32[]{:S(2)}, u32[]{:S(2)}) collective-permute-start(bf16[128,896]{0,1:T(8,128)(2,1)} %bitcast_dynamic-update-slice_fusion), channel_id=1, source_target_pairs={{0,4},{4,0},{8,12},{12,8},{1,5},{5,1},{9,13},{13,9},{2,6},{6,2},{1... | collective-permute-start | bytes 688136 | tf_op jit(solution)/shard_map/ppermute | solution.py:13
  18.9 6.7 %collective-permute-start.1 = (bf16[128,512]{1,0:T(8,128)(2,1)S(1)}, bf16[128,512]{1,0:T(8,128)(2,1)S(1)}, u32[]{:S(2)}, u32[]{:S(2)}) collective-permute-start(bf16[128,512]{1,0:T(8,128)(2,1)S(1)} %pad_maximum_fusion.1), channel_id=1, source_target_pairs={{0,4},{4,0},{8,12},{12,8},{1,5},{5,1},{9,13},{13,9},{2,6},{6,2},{1... | collective-permute-start | bytes 393224 | tf_op jit(solution)/shard_map/ppermute | solution.py:13
  19.6 16.0 %collective-permute-start.9 = (bf16[128,512]{1,0:T(8,128)(2,1)}, bf16[128,512]{1,0:T(8,128)(2,1)S(1)}, u32[]{:S(2)}, u32[]{:S(2)}) collective-permute-start(bf16[128,512]{1,0:T(8,128)(2,1)} %collective-permute-done.8), channel_id=1, source_target_pairs={{0,1},{1,0},{2,3},{3,2},{4,5},{5,4},{6,7},{7,6},{8,9},{9,8},{10,11... | collective-permute-start | bytes 393224 | tf_op jit(solution)/shard_map/ppermute | solution.py:13
  22.6 12.2 %collective-permute-start.4 = (bf16[128,384]{1,0:T(8,128)(2,1)S(1)}, bf16[128,384]{1,0:T(8,128)(2,1)S(1)}, u32[]{:S(2)}, u32[]{:S(2)}) collective-permute-start(bf16[128,384]{1,0:T(8,128)(2,1)S(1)} %pad_maximum_fusion.5), channel_id=1, source_target_pairs={{0,8},{4,12},{8,0},{12,4},{1,9},{5,13},{9,1},{13,5},{2,10},{6,14},... | collective-permute-start | bytes 294920 | tf_op jit(solution)/shard_map/ppermute | solution.py:13
  25.9 3.0 %copy-start.18 = (bf16[128,128]{0,1:T(8,128)(2,1)S(1)}, bf16[128,128]{0,1:T(8,128)(2,1)}, u32[]{:S(2)}) copy-start(bf16[128,128]{0,1:T(8,128)(2,1)} %get-tuple-element.26) | copy-start | bytes 98308
  26.0 12.3 %collective-permute-start.3 = (bf16[128,512]{1,0:T(8,128)(2,1)S(1)}, bf16[128,512]{1,0:T(8,128)(2,1)S(1)}, u32[]{:S(2)}, u32[]{:S(2)}) collective-permute-start(bf16[128,512]{1,0:T(8,128)(2,1)S(1)} %pad_maximum_fusion.2), channel_id=1, source_target_pairs={{0,8},{4,12},{8,0},{12,4},{1,9},{5,13},{9,1},{13,5},{2,10},{6,14},... | collective-permute-start | bytes 393224 | tf_op jit(solution)/shard_map/ppermute | solution.py:13
  30.4 24.9 %collective-permute-start.15 = (bf16[128,256]{0,1:T(8,128)(2,1)}, bf16[128,256]{0,1:T(8,128)(2,1)}, u32[]{:S(2)}, u32[]{:S(2)}) collective-permute-start(bf16[128,256]{0,1:T(8,128)(2,1)} %add_convert_fusion), channel_id=1, source_target_pairs={{0,8},{4,12},{8,0},{12,4},{1,9},{5,13},{9,1},{13,5},{2,10},{6,14},... | collective-permute-start | bytes 196616 | tf_op jit(solution)/shard_map/ppermute | solution.py:13
  39.5 5.5 %collective-permute-start.7 = (bf16[128,384]{1,0:T(8,128)(2,1)}, bf16[128,384]{1,0:T(8,128)(2,1)}, u32[]{:S(2)}, u32[]{:S(2)}) collective-permute-start(bf16[128,384]{1,0:T(8,128)(2,1)} %get-tuple-element.7), channel_id=1, source_target_pairs={{0,1},{1,0},{2,3},{3,2},{4,5},{5,4},{6,7},{7,6},{8,9},{9,8},{10,11... | collective-permute-start | bytes 294920 | tf_op jit(solution)/shard_map/ppermute | solution.py:13
  39.5 5.5 %collective-permute-start.5 = (bf16[128,384]{1,0:T(8,128)(2,1)}, bf16[128,384]{1,0:T(8,128)(2,1)}, u32[]{:S(2)}, u32[]{:S(2)}) collective-permute-start(bf16[128,384]{1,0:T(8,128)(2,1)} %get-tuple-element.7), channel_id=1, source_target_pairs={{0,2},{1,3},{2,0},{3,1},{4,6},{5,7},{6,4},{7,5},{8,10},{9,11},{10,... | collective-permute-start | bytes 294920 | tf_op jit(solution)/shard_map/ppermute | solution.py:13
  43.2 6.6 %collective-permute-start.12 = (bf16[128,512]{1,0:T(8,128)(2,1)S(1)}, bf16[128,512]{1,0:T(8,128)(2,1)S(1)}, u32[]{:S(2)}, u32[]{:S(2)}) collective-permute-start(bf16[128,512]{1,0:T(8,128)(2,1)S(1)} %pad_maximum_fusion.4), channel_id=1, source_target_pairs={{0,4},{4,0},{8,12},{12,8},{1,5},{5,1},{9,13},{13,9},{2,6},{6,2},{1... | collective-permute-start | bytes 393224 | tf_op jit(solution)/shard_map/ppermute | solution.py:13
  45.1 1.5 %collective-permute-start.6 = (bf16[128,384]{1,0:T(8,128)(2,1)}, bf16[128,384]{1,0:T(8,128)(2,1)S(1)}, u32[]{:S(2)}, u32[]{:S(2)}) collective-permute-start(bf16[128,384]{1,0:T(8,128)(2,1)} %collective-permute-done.5), channel_id=1, source_target_pairs={{0,1},{1,0},{2,3},{3,2},{4,5},{5,4},{6,7},{7,6},{8,9},{9,8},{10,11... | collective-permute-start | bytes 294920 | tf_op jit(solution)/shard_map/ppermute | solution.py:13
  49.5 4.3 %collective-permute-start.11 = (bf16[128,256]{0,1:T(8,128)(2,1)S(1)}, bf16[128,256]{0,1:T(8,128)(2,1)S(1)}, u32[]{:S(2)}, u32[]{:S(2)}) collective-permute-start(bf16[128,256]{0,1:T(8,128)(2,1)S(1)} %pad_maximum_fusion.8), channel_id=1, source_target_pairs={{0,4},{4,0},{8,12},{12,8},{1,5},{5,1},{9,13},{13,9},{2,6},{6,2},{1... | collective-permute-start | bytes 196616 | tf_op jit(solution)/shard_map/ppermute | solution.py:13
  49.8 4.4 %copy-start.16 = (bf16[128,512]{1,0:T(8,128)(2,1)}, bf16[128,512]{1,0:T(8,128)(2,1)S(1)}, u32[]{:S(2)}) copy-start(bf16[128,512]{1,0:T(8,128)(2,1)S(1)} %collective-permute-done.12) | copy-start | bytes 393220
  49.9 6.9 %collective-permute-start.13 = (bf16[128,256]{1,0:T(8,128)(2,1)S(1)}, bf16[128,256]{1,0:T(8,128)(2,1)S(1)}, u32[]{:S(2)}, u32[]{:S(2)}) collective-permute-start(bf16[128,256]{1,0:T(8,128)(2,1)S(1)} %fusion.111), channel_id=1, source_target_pairs={{0,8},{4,12},{8,0},{12,4},{1,9},{5,13},{9,1},{13,5},{2,10},{6,14},... | collective-permute-start | bytes 196616 | tf_op jit(solution)/shard_map/ppermute | solution.py:13
  53.9 2.9 %copy-start.10 = (bf16[128,256]{0,1:T(8,128)(2,1)}, bf16[128,256]{0,1:T(8,128)(2,1)S(1)}, u32[]{:S(2)}) copy-start(bf16[128,256]{0,1:T(8,128)(2,1)S(1)} %get-tuple-element.30) | copy-start | bytes 196612
  54.2 3.6 %copy-start.5 = (bf16[2,1,640,128]{3,2,1,0:T(8,128)(2,1)S(1)}, bf16[2,1,640,128]{3,2,1,0:T(8,128)(2,1)}, u32[]{:S(2)}) copy-start(bf16[2,1,640,128]{3,2,1,0:T(8,128)(2,1)} %param.11) | copy-start | bytes 983044
  55.3 2.5 %copy-start.7 = (bf16[2,1,128,256]{3,2,1,0:T(8,128)(2,1)S(1)}, bf16[2,1,128,256]{3,2,1,0:T(8,128)(2,1)}, u32[]{:S(2)}) copy-start(bf16[2,1,128,256]{3,2,1,0:T(8,128)(2,1)} %param.12) | copy-start | bytes 393220
  (12 other events, 16.7 us)

commit v2 on v0

v2 whole, which is shorter than its diff:
```python
import math

import jax
import jax.numpy as jnp
from jax import lax
from jax.experimental import pallas as pl
from jax.experimental.pallas import tpu as pltpu
from jax.sharding import PartitionSpec as P

BF = jnp.bfloat16


def swap(value, axis, mask):
    pairs = [(source, source ^ mask) for source in range(lax.axis_size(axis))]
    return lax.ppermute(value, axis, pairs)


def dot(a, b):
    return jnp.dot(a, b, preferred_element_type=jnp.float32)


def dot_t(a, b):
    return lax.dot_general(a, b, (((0,), (0,)), ((), ())), preferred_element_type=jnp.float32)


def ordered(upper_side, own, other):
    return jnp.where(
        upper_side, jnp.concatenate([other, own], 0), jnp.concatenate([own, other], 0)
    )


def level_step(current, project_basis, update_basis, caps_rows, level_num):
    leaf_rows = current.shape[0]
    shift_bits = level_num - 1
    partial_value = dot_t(project_basis, current.astype(BF)) * (
        1.0 / math.sqrt(leaf_rows * 2**shift_bits)
    )
    for bit_index in range(shift_bits):
        partial_value = partial_value + swap(partial_value, "leaf", 2**bit_index)
    own = partial_value.astype(BF)
    other = swap(own, "leaf", 2**shift_bits)
    upper_side = (lax.axis_index("leaf") >> shift_bits) & 1 == 1
    stacked = ordered(upper_side, own, other)
    weights = dot(caps_rows, stacked).astype(BF)
    return current - dot(update_basis, weights)


def top_step(current, project_basis, update_basis, caps_rows):
    leaf_count = lax.axis_size("leaf")
    partial_value = dot_t(project_basis, current.astype(BF)) * (
        1.0 / math.sqrt(leaf_count * current.shape[0])
    )
    column_total = lax.psum(partial_value, "leaf")
    stacked = lax.all_gather(column_total.astype(BF), "top", axis=0, tiled=True)
    weights = dot(caps_rows, stacked).astype(BF)
    return current - dot(update_basis, weights)


def step_by_step(
    right_side, leaf_inverse, left_basis, right_basis, level_caps, top_left, top_right, top_caps
):
    levels = left_basis.shape[0]
    lefts = [left_basis[k, 0] for k in range(levels)]
    rights = [right_basis[k, 0] for k in range(levels)]
    current = dot(leaf_inverse[0], right_side[0].astype(BF))
    for k in range(levels):
        current = level_step(current, rights[k], lefts[k], level_caps[k, 0], k + 1)
    current = top_step(current, top_right[0], top_left[0], top_caps)
    current = top_step(current, top_left[0], top_right[0], top_caps)
    for k in reversed(range(levels)):
        current = level_step(current, lefts[k], rights[k], level_caps[k, 0], k + 1)
    return dot_t(leaf_inverse[0], current.astype(BF))[None]


def call(body, outs, *args, scratch=(), hbm=()):
    vmem = pl.BlockSpec(memory_space=pltpu.VMEM)
    anywhere = pl.BlockSpec(memory_space=pl.ANY)
    return pl.pallas_call(
        body,
        out_shape=[jax.ShapeDtypeStruct(shape, dtype) for shape, dtype in outs],
        in_specs=[anywhere if i in hbm else vmem for i in range(len(args))],
        out_specs=[vmem] * len(outs),
        scratch_shapes=list(scratch),
    )(*args)


def side(bit):
    return (lax.axis_index("leaf") >> bit) & 1


def block(index, width):
    return pl.ds(pl.multiple_of(index * width, width), width)


def put_ordered(scratch, upper, own, other):
    rows = own.shape[0]
    scratch[block(upper, rows), :] = own
    scratch[block(1 - upper, rows), :] = other


def two_levels(
    right_side, leaf_inverse, left_basis, right_basis, level_caps, top_left, top_right, top_caps
):
    rows, cols = right_side.shape[1:]
    rank = top_left.shape[2]
    half = cols // 2
    f32 = jnp.float32
    s1 = 1.0 / math.sqrt(rows)
    s2 = 1.0 / math.sqrt(rows * 2)
    st = 1.0 / math.sqrt(rows * 4)
    blocks = rows // rank
    square, wide = (rank, rank), (rank, cols)

    def span(i, n=1):
        return slice(i * rank, (i + n) * rank)

    def start_body(rhs_hbm, inv_hbm, rb_hbm, x_ref, inv_ref, p_ref, rhs_v, rb_v, sems):
        copies = []
        for i in range(blocks):
            copies.append(
                (
                    pltpu.make_async_copy(
                        rhs_hbm.at[0, span(i), :], rhs_v.at[span(i), :], sems.at[0, i]
                    ),
                    pltpu.make_async_copy(
                        inv_hbm.at[0, span(i), span(0, i + 1)],
                        inv_ref.at[span(i), span(0, i + 1)],
                        sems.at[1, i],
                    ),
                )
            )
            copies[i][0].start()
            copies[i][1].start()
        basis = pltpu.make_async_copy(rb_hbm.at[0, 0], rb_v, sems.at[2, 0])
        basis.start()
        for i in range(blocks):
            copies[i][0].wait()
            copies[i][1].wait()
            x_ref[span(i), :] = dot(
                inv_ref[span(i), span(0, i + 1)], rhs_v[span(0, i + 1), :].astype(BF)
            )
        basis.wait()
        p_ref[...] = (dot_t(rb_v[...], x_ref[...].astype(BF)) * s1).astype(BF)

    state0, inverse, proj1 = call(
        start_body,
        [((rows, cols), f32), ((rows, rows), BF), (wide, BF)],
        right_side,
        leaf_inverse,
        right_basis,
        hbm=(0, 1, 2),
        scratch=[
            pltpu.VMEM((rows, cols), f32),
            pltpu.VMEM((rows, rank), BF),
            pltpu.SemaphoreType.DMA((3, blocks)),
        ],
    )
    proj1_sib = swap(proj1, "leaf", 1)

    def early_body(lb, caps, tl, tr, out):
        for i, basis in enumerate((tr, tl)):
            gram = (dot_t(basis[0], lb[1, 0]) * st).astype(BF)
            out[:, span(2 * i, 2)] = dot(gram, caps[1, 0]).astype(BF)
        out[:, span(4)] = (dot_t(tl[0], tl[0]) * st).astype(BF)

    (early,) = call(
        early_body, [((rank, 5 * rank), BF)], left_basis, level_caps, top_left, top_right
    )
    early_sib = swap(early, "leaf", 1)

    def pair_body(own, sib, send, keep, gram, scratch):
        upper = side(1)
        for i in range(2):
            scratch[...] = own[:, span(2 * i, 2)].astype(f32) + sib[:, span(2 * i, 2)]
            send[:, span(i)] = scratch[:, block(1 - upper, rank)].astype(BF)
            keep[:, span(2 * i)] = scratch[:, block(upper, rank)].astype(BF)
            keep[:, span(2 * i + 1)] = send[:, span(i)]
        gram[...] = own[:, span(4)].astype(f32) + sib[:, span(4)]
        send[:, span(2)] = gram[...].astype(BF)

    next_send, next_keep, gram_pair = call(
        pair_body,
        [((rank, 3 * rank), BF), ((rank, 4 * rank), BF), (square, f32)],
        early,
        early_sib,
        scratch=[pltpu.VMEM((rank, 2 * rank), f32)],
    )
    next_far = swap(next_send, "leaf", 2)

    def one_body(x0, p, p_sib, lb, rb, caps, tl, tr, x1, send, keep, stack, scratch):
        odd = side(0)
        put_ordered(stack, odd, p[...], p_sib[...])
        coef = dot(caps[0, 0], stack[...]).astype(BF)
        x1[...] = x0[...] - dot(lb[0, 0], coef)
        state = x1[...].astype(BF)
        keep[:, :cols] = dot_t(rb[1, 0], state) * s2
        send[:, :cols] = keep[:, :cols].astype(BF)
        for i, basis in enumerate((tr, tl)):
            at = slice(cols + i * half, cols + (i + 1) * half)
            scratch[...] = dot_t(basis[0], state) * st
            send[:, at] = scratch[:, block(1 - odd, half)].astype(BF)
            keep[:, at] = scratch[:, block(odd, half)]

    state1, pair_send, pair_keep = call(
        one_body,
        [((rows, cols), f32), ((rank, 2 * cols), BF), ((rank, 2 * cols), f32)],
        state0,
        proj1,
        proj1_sib,
        left_basis,
        right_basis,
        level_caps,
        top_left,
        top_right,
        scratch=[pltpu.VMEM((2 * rank, cols), BF), pltpu.VMEM(wide, f32)],
    )
    pair_in = swap(pair_send, "leaf", 1)

    def half_body(keep, pair, nexts, send, keep2):
        odd = side(0)
        send[:, :cols] = (keep[:, :cols] + pair[:, :cols]).astype(BF)
        own = send[:, block(odd, half)]
        for i in range(2):
            at = slice(cols + i * half, cols + (i + 1) * half)
            keep2[:, i * half : (i + 1) * half] = (
                keep[:, at] + pair[:, at] - dot(nexts[:, span(2 * i)], own)
            )
        send[:, cols:] = keep2[...].astype(BF)

    cross_send, cross_keep = call(
        half_body, [((rank, 2 * cols), BF), (wide, f32)], pair_keep, pair_in, next_keep
    )
    cross_in = swap(cross_send, "leaf", 2)

    def column_body(send, keep2, far, nexts, nexts_far, gram, out):
        odd = side(0)
        own, other = send[:, block(odd, half)], far[:, block(odd, half)]
        for i in range(2):
            at = slice(i * half, (i + 1) * half)
            out[:, at] = (
                keep2[:, at]
                + far[:, cols + i * half : cols + (i + 1) * half]
                - dot(nexts[:, span(2 * i + 1)], other)
                - dot(nexts_far[:, span(i)], own)
            ).astype(BF)
        out[:, 2 * half :] = (gram[...] + nexts_far[:, span(2)]).astype(BF)

    (top_send,) = call(
        column_body,
        [((rank, 2 * half + rank), BF)],
        cross_send,
        cross_keep,
        cross_in,
        next_keep,
        next_far,
        gram_pair,
    )

    def around_top(value):
        far = swap(value, "top", 2)
        near = swap(value, "top", 1)
        return value, near, far, swap(far, "top", 1)

    def two_body(x1, send, far, lb, caps, x2, z5, z, stack):
        put_ordered(stack, side(1), send[:, :cols], far[:, :cols])
        coef = dot(caps[1, 0], stack[...]).astype(BF)
        x2[...] = x1[...] - dot(lb[1, 0], coef)
        state = x2[...].astype(BF)
        z5[...] = dot_t(lb[1, 0], state) * s2
        z[:, :cols] = z5[...].astype(BF)
        z[:, cols:] = (dot_t(lb[0, 0], state) * s1).astype(BF)

    top_parts = around_top(top_send)
    state2, down5, down_send = call(
        two_body,
        [((rows, cols), f32), (wide, f32), ((rank, 2 * cols), BF)],
        state1,
        cross_send,
        cross_in,
        left_basis,
        level_caps,
        scratch=[pltpu.VMEM((2 * rank, cols), BF)],
    )
    down_in = swap(down_send, "leaf", 1)

    def add_body(own, sib, out, out_b):
        out[...] = own[...] + sib[:, :cols]
        out_b[...] = out[...].astype(BF)

    down5, down5_send = call(add_body, [(wide, f32), (wide, BF)], down5, down_in)
    down5_far = swap(down5_send, "leaf", 2)

    def late_body(lb, rb, caps, tl, tr, out):
        for i, basis in enumerate((tl, tr)):
            out[:, span(i)] = (dot_t(lb[1, 0], basis[0]) * s2).astype(BF)
            out[:, span(2 + i)] = (dot_t(lb[0, 0], basis[0]) * s1).astype(BF)
        out[:, span(4)] = (dot_t(lb[0, 0], rb[1, 0]) * s1).astype(BF)
        out[:, span(5, cols // rank)] = caps[1, 0]

    (late,) = call(
        late_body,
        [((rank, 5 * rank + cols), BF)],
        left_basis,
        right_basis,
        level_caps,
        top_left,
        top_right,
    )
    late_sib = swap(late, "leaf", 1)

    def grams_body(own, sib, out):
        out[...] = (own[:, span(0, 2)].astype(f32) + sib[:, span(0, 2)]).astype(BF)

    (gram5,) = call(grams_body, [((rank, 2 * rank), BF)], late, late_sib)
    gram5_far = swap(gram5, "leaf", 2)

    def turn_body(inv, inv_t):
        for r in range(blocks):
            for c in range(r + 1):
                inv_t[span(c), span(r)] = inv[span(r), span(c)].T

    (inverse_t,) = call(turn_body, [((rows, rows), BF)], inverse)

    caps_parts = around_top(top_caps)

    def order_body(a, b, c, d, out):
        here = lax.axis_index("top")
        for i, part in enumerate((a, b, c, d)):
            for k in range(4):
                out[span(i), span(k)] = part[:, block(here ^ k, rank)]

    (caps_all,) = call(order_body, [((4 * rank, 4 * rank), BF)], *caps_parts)

    def top_body(a, b, c, d, caps, out, up, down):
        for i, part in enumerate((a, b, c, d)):
            up[span(i), :] = part[:, :half]
        coef = dot(caps[...], up[...]).astype(BF)
        for i, part in enumerate((a, b, c, d)):
            down[span(i), :] = (
                part[:, half : 2 * half] - dot(part[:, 2 * half :], coef[span(i), :])
            ).astype(BF)
        out[:, :half] = coef[:rank, :]
        out[:, half:] = dot(caps[:rank, :], down[...]).astype(BF)

    (back_send,) = call(
        top_body,
        [(wide, BF)],
        *top_parts,
        caps_all,
        scratch=[pltpu.VMEM((4 * rank, half), BF)] * 2,
    )
    back_in = swap(back_send, "leaf", 1)

    def last_body(
        x2, back, back_sib, down5, down5_far, gram5, gram5_far, late, late_sib,
        z, z_sib, lb, rb, caps, tl, tr, inv_t, out, both, stack, coefs, x6, out_v, sems,
    ):
        odd, high = side(0), side(1)
        for i in range(2):
            at = slice(i * half, (i + 1) * half)
            both[span(i), block(odd, half)] = back[:, at]
            both[span(i), block(1 - odd, half)] = back_sib[:, at]
        put_ordered(
            stack,
            high,
            (down5[...] - dot(gram5[...], both[...])).astype(BF),
            (down5_far[...] - dot(gram5_far[...], both[...])).astype(BF),
        )
        coef5 = dot(caps[1, 0], stack[...]).astype(BF)
        coef5_sib = dot(late_sib[:, span(5, cols // rank)], stack[...]).astype(BF)

        def proj(zs, grams, coef):
            return (
                zs[:, cols:]
                - dot(grams[:, span(2, 2)], both[...])
                - dot(grams[:, span(4)], coef)
            ).astype(BF)

        put_ordered(coefs, odd, proj(z, late, coef5), proj(z_sib, late_sib, coef5_sib))
        coef6 = dot(caps[0, 0], coefs[...]).astype(BF)
        x6[...] = (
            x2[...]
            - dot(tl[0], both[span(0), :])
            - dot(tr[0], both[span(1), :])
            - dot(rb[1, 0], coef5)
            - dot(rb[0, 0], coef6)
        ).astype(BF)
        copies = []
        for c in reversed(range(blocks)):
            out_v[span(c), :] = dot(inv_t[span(c), c * rank :], x6[c * rank :, :])
            copy = pltpu.make_async_copy(out_v.at[span(c), :], out.at[0, span(c), :], sems.at[c])
            copy.start()
            copies.append(copy)
        for copy in copies:
            copy.wait()

    args = (
        state2, back_send, back_in, down5, down5_far, gram5, gram5_far, late, late_sib,
        down_send, down_in, left_basis, right_basis, level_caps, top_left, top_right, inverse_t,
    )
    return pl.pallas_call(
        last_body,
        out_shape=jax.ShapeDtypeStruct((1, rows, cols), f32),
        in_specs=[pl.BlockSpec(memory_space=pltpu.VMEM)] * len(args),
        out_specs=pl.BlockSpec(memory_space=pl.ANY),
        scratch_shapes=[
            pltpu.VMEM((2 * rank, cols), BF),
            pltpu.VMEM((2 * rank, cols), BF),
            pltpu.VMEM((2 * rank, cols), BF),
            pltpu.VMEM((rows, cols), BF),
            pltpu.VMEM((rows, cols), f32),
            pltpu.SemaphoreType.DMA((blocks,)),
        ],
    )(*args)


def on_device(*args):
    levels = args[2].shape[0]
    sizes = lax.axis_size("leaf"), lax.axis_size("top")
    if levels == 2 and sizes == (4, 4):
        return two_levels(*args)
    return step_by_step(*args)


def solution(mesh):
    rows = P(("parts", "top"), "leaf", None)
    level_rows = P(None, ("parts", "top"), "leaf", None)
    return jax.shard_map(
        on_device,
        mesh=mesh,
        in_specs=(
            rows,
            rows,
            level_rows,
            level_rows,
            level_rows,
            rows,
            rows,
            P(("parts", "top"), None),
        ),
        out_specs=rows,
        check_vma=False,
    )
```

time: 93.6 us -> 66.6 us (0.71)
  blocking collectives: 52.4 us -> 0 us
  Pallas kernels: 0 us -> 33.9 us
  waiting for transfers between devices: 22.5 us -> 6.35 us
  starting transfers between devices: 9.21 us -> 19.8 us
  matrix products: 6.72 us -> 0 us
  local copies, waits for them, and re-layouts: 2.27 us -> 5.97 us
    psum x2 -> x0, blocking collectives: 40.5 us -> none  [top_update(): column_total = lax.psum(partial_value, 'leaf')]
    pallas_call x0 -> x14, Pallas kernels: none -> 33.9 us  [the longest x13 29.6 us: call(): pl.pallas_call(body, out_shape=[jax.ShapeDtypeStruct(shape, dtype) for sh...]
    ppermute x6 -> x16, waiting for transfers between devices: 22.5 us -> 6.35 us  [swap(): return lax.ppermute(value, axis, pairs)]
    all_gather x2 -> x0, blocking collectives: 11.9 us -> none  [top_update(): lax.all_gather(column_total.astype(jnp.bfloat16), 'top', axis=0, tiled=True)]
    ppermute x6 -> x16, starting transfers between devices: 9.21 us -> 19.8 us  [swap(): return lax.ppermute(value, axis, pairs)]
    dot_general x14 -> x0, matrix products: 6.72 us -> none  [the longest x7 2.41 us: project_rows(): lax.dot_general(basis, current.astype(jnp.bfloat16), (((0,), (0,)), ((),...]
    unnamed x20 -> x38, local copies, waits for them, and re-layouts: 1.19 us -> 5.97 us
    broadcast_in_dim x1 -> x0, local copies, waits for them, and re-layouts: 1.07 us -> none  [on_device(): return current[None]]
  transfers between devices with their start and end apart: 6 -> 16, of which waited for: 6 -> 4; matrix products, arithmetic and copies ran while one was open for 0% -> 0% of each run, Pallas kernels for 0% -> 37%
where the time goes in v2:
time: 66.6 us; the launch traced here: 66.1 us
  Pallas kernels  33.9 us (51%)
  starting transfers between devices  19.8 us (30%)
  waiting for transfers between devices  6.35 us (10%)
  local copies, waits for them, and re-layouts  5.97 us (9%)
    pallas_call x13, Pallas kernels, call(): pl.pallas_call(body, out_shape=[jax.ShapeDtypeStruct(shape, dtype) for sh...  29.6 us
    ppermute x16, starting transfers between devices, swap(): return lax.ppermute(value, axis, pairs)  19.8 us
    ppermute x16, waiting for transfers between devices, swap(): return lax.ppermute(value, axis, pairs)  6.35 us
    unnamed x38, local copies, waits for them, and re-layouts  5.97 us
    pallas_call x1, Pallas kernels, two_levels(): pl.pallas_call(last_body, out_shape=jax.ShapeDtypeStruct((1, rows, cols),...  4.35 us
  transfers between devices with their start and end apart: 16, of which 4 were waited for; matrix products, arithmetic and copies ran while one was open for 0% of the time, Pallas kernels for 37%

profile of v2, /device:TPU:0, one launch (start us, length us, event | category | flops | bytes accessed | tf_op | source)
XLA Modules:
  0.0 66.1 jit_solution(6986695223927969480)
XLA Ops:
  0.0 3.2 %shard_map.82 = (f32[640,256]{1,0:T(8,128)}, bf16[640,640]{1,0:T(8,128)(2,1)}, bf16[128,256]{1,0:T(8,128)(2,1)}) custom-call(f32[1,640,256]{2,1,0:T(8,128)} %rhs_hbm.1, bf16[1,640,640]{2,1,0:T(8,128)(2,1)} %inv_hbm.1, bf16[2,1,640,128]{3,2,1,0:T(8,128)(2,1)} %rb.5), custom_call_target="tpu_custom_call" | custom-call | tf_op jit(solution)/shard_map/pallas_call | solution.py:78
  3.2 3.1 %collective-permute-start = (bf16[128,256]{1,0:T(8,128)(2,1)}, bf16[128,256]{1,0:T(8,128)(2,1)S(1)}, u32[]{:S(2)}, u32[]{:S(2)}) collective-permute-start(bf16[128,256]{1,0:T(8,128)(2,1)} %get-tuple-element.22.p), channel_id=1, source_target_pairs={{0,4},{4,0},{8,12},{12,8},{1,5},{5,1},{9,13},{13,9},{2,6},{6,2},{1... | collective-permute-start | bytes 196616 | tf_op jit(solution)/shard_map/ppermute | solution.py:15
  6.3 2.4 %shard_map.84.own = bf16[128,640]{1,0:T(8,128)(2,1)} custom-call(bf16[2,1,640,128]{3,2,1,0:T(8,128)(2,1)} %lb.9, bf16[2,1,128,256]{3,2,1,0:T(8,128)(2,1)} %caps.9, bf16[1,640,128]{2,1,0:T(8,128)(2,1)} %tl.7, bf16[1,640,128]{2,1,0:T(8,128)(2,1)} %tr.7), custom_call_target="tpu_custom_call" | custom-call | tf_op jit(solution)/shard_map/pallas_call | solution.py:78
  9.4 3.1 %shard_map.83 = (f32[640,256]{1,0:T(8,128)}, bf16[128,512]{1,0:T(8,128)(2,1)}, f32[128,512]{1,0:T(8,128)}) custom-call(f32[640,256]{1,0:T(8,128)} %get-tuple-element.21.x0, bf16[128,256]{1,0:T(8,128)(2,1)} %get-tuple-element.22.p, bf16[128,256]{1,0:T(8,128)(2,1)} %copy-done.17, bf16[2,1,640,128]{3,2,1,0:T(8,128)(2,1)} %lb.9, bf16[2,1,640,128]{3,2,1,0:T(8,128)(2,1)} %rb.5, ...), custom_call_target="tpu_custom_call" | custom-call | tf_op jit(solution)/shard_map/pallas_call | solution.py:78
  12.5 2.0 %collective-permute-start.1 = (bf16[128,512]{1,0:T(8,128)(2,1)}, bf16[128,512]{1,0:T(8,128)(2,1)S(1)}, u32[]{:S(2)}, u32[]{:S(2)}) collective-permute-start(bf16[128,512]{1,0:T(8,128)(2,1)} %get-tuple-element.25), channel_id=1, source_target_pairs={{0,4},{4,0},{8,12},{12,8},{1,5},{5,1},{9,13},{13,9},{2,6},{6,2},{1... | collective-permute-start | bytes 393224 | tf_op jit(solution)/shard_map/ppermute | solution.py:15
  15.2 1.8 %shard_map.85 = (bf16[128,384]{1,0:T(8,128)(2,1)}, bf16[128,512]{1,0:T(8,128)(2,1)}, f32[128,128]{1,0:T(8,128)}) custom-call(bf16[128,640]{1,0:T(8,128)(2,1)} %shard_map.84.own, bf16[128,640]{1,0:T(8,128)(2,1)} %copy-done.4), custom_call_target="tpu_custom_call" | custom-call | tf_op jit(solution)/shard_map/pallas_call | solution.py:78
  18.3 1.9 %shard_map.86 = (bf16[128,512]{1,0:T(8,128)(2,1)}, f32[128,256]{1,0:T(8,128)}) custom-call(f32[128,512]{1,0:T(8,128)} %get-tuple-element.24.keep, bf16[128,512]{1,0:T(8,128)(2,1)} %copy-done.5, bf16[128,512]{1,0:T(8,128)(2,1)} %get-tuple-element.26.nexts), custom_call_target="tpu_custom_call" | custom-call | tf_op jit(solution)/shard_map/pallas_call | solution.py:78
  20.3 3.0 %collective-permute-start.3 = (bf16[128,512]{1,0:T(8,128)(2,1)}, bf16[128,512]{1,0:T(8,128)(2,1)S(1)}, u32[]{:S(2)}, u32[]{:S(2)}) collective-permute-start(bf16[128,512]{1,0:T(8,128)(2,1)} %get-tuple-element.27.send), channel_id=1, source_target_pairs={{0,8},{4,12},{8,0},{12,4},{1,9},{5,13},{9,1},{13,5},{2,10},{6,14},... | collective-permute-start | bytes 393224 | tf_op jit(solution)/shard_map/ppermute | solution.py:15
  23.3 2.4 %shard_map.92.own.late = bf16[128,896]{1,0:T(8,128)(2,1)} custom-call(bf16[2,1,640,128]{3,2,1,0:T(8,128)(2,1)} %lb.9, bf16[2,1,640,128]{3,2,1,0:T(8,128)(2,1)} %rb.5, bf16[2,1,128,256]{3,2,1,0:T(8,128)(2,1)} %caps.9, bf16[1,640,128]{2,1,0:T(8,128)(2,1)} %tl.7, bf16[1,640,128]{2,1,0:T(8,128)(2,1)} %tr.7), custom_call_target="tpu_custom_call" | custom-call | tf_op jit(solution)/shard_map/pallas_call | solution.py:78
  25.7 1.6 %collective-permute-start.14 = (bf16[128,896]{1,0:T(8,128)(2,1)}, bf16[128,896]{1,0:T(8,128)(2,1)S(1)}, u32[]{:S(2)}, u32[]{:S(2)}) collective-permute-start(bf16[128,896]{1,0:T(8,128)(2,1)} %shard_map.92.own.late), channel_id=1, source_target_pairs={{0,4},{4,0},{8,12},{12,8},{1,5},{5,1},{9,13},{13,9},{2,6},{6,2},{1... | collective-permute-start | bytes 688136 | tf_op jit(solution)/shard_map/ppermute | solution.py:15
  27.6 1.5 %collective-permute-start.9 = (bf16[128,512]{1,0:T(8,128)(2,1)S(1)}, bf16[128,512]{1,0:T(8,128)(2,1)S(1)}, u32[]{:S(2)}, u32[]{:S(2)}) collective-permute-start(bf16[128,512]{1,0:T(8,128)(2,1)S(1)} %copy-done.6), channel_id=1, source_target_pairs={{0,2},{1,3},{2,0},{3,1},{4,6},{5,7},{6,4},{7,5},{8,10},{9,11},{10,... | collective-permute-start | bytes 393224 | tf_op jit(solution)/shard_map/ppermute | solution.py:15
  29.1 4.3 %collective-permute-done.4.nexts_far = bf16[128,384]{1,0:T(8,128)(2,1)S(1)} collective-permute-done((bf16[128,384]{1,0:T(8,128)(2,1)S(1)}, bf16[128,384]{1,0:T(8,128)(2,1)S(1)}, u32[]{:S(2)}, u32[]{:S(2)}) %collective-permute-start.4) | collective-permute-done | bytes 98336 | tf_op jit(solution)/shard_map/ppermute | solution.py:15
  34.1 2.0 %shard_map.88.a = bf16[128,384]{1,0:T(8,128)(2,1)} custom-call(bf16[128,512]{1,0:T(8,128)(2,1)} %get-tuple-element.27.send, f32[128,256]{1,0:T(8,128)} %get-tuple-element.29.keep2, bf16[128,512]{1,0:T(8,128)(2,1)} %copy-done.2, bf16[128,512]{1,0:T(8,128)(2,1)} %get-tuple-element.26.nexts, bf16[128,384]{1,0:T(8,128)(2,1)} %copy-done.10, ...), custom_call_target="tpu_custom_call" | custom-call | tf_op jit(solution)/shard_map/pallas_call | solution.py:78
  36.0 1.5 %collective-permute-start.6 = (bf16[128,384]{1,0:T(8,128)(2,1)}, bf16[128,384]{1,0:T(8,128)(2,1)S(1)}, u32[]{:S(2)}, u32[]{:S(2)}) collective-permute-start(bf16[128,384]{1,0:T(8,128)(2,1)} %shard_map.88.a), channel_id=1, source_target_pairs={{0,2},{1,3},{2,0},{3,1},{4,6},{5,7},{6,4},{7,5},{8,10},{9,11},{10,... | collective-permute-start | bytes 294920 | tf_op jit(solution)/shard_map/ppermute | solution.py:15
  38.0 2.8 %shard_map.87 = (f32[640,256]{1,0:T(8,128)}, f32[128,256]{1,0:T(8,128)}, bf16[128,512]{1,0:T(8,128)(2,1)}) custom-call(f32[640,256]{1,0:T(8,128)} %get-tuple-element.23.x1, bf16[128,512]{1,0:T(8,128)(2,1)} %get-tuple-element.27.send, bf16[128,512]{1,0:T(8,128)(2,1)} %copy-done.2, bf16[2,1,640,128]{3,2,1,0:T(8,128)(2,1)} %lb.9, bf16[2,1,128,256]{3,2,1,0:T(8,128)(2,1)} %caps.9), custom_call_target="tpu_custom_call" | custom-call | tf_op jit(solution)/shard_map/pallas_call | solution.py:78
  40.8 1.7 %collective-permute-start.12 = (bf16[128,512]{1,0:T(8,128)(2,1)}, bf16[128,512]{1,0:T(8,128)(2,1)S(1)}, u32[]{:S(2)}, u32[]{:S(2)}) collective-permute-start(bf16[128,512]{1,0:T(8,128)(2,1)} %get-tuple-element.33.z), channel_id=1, source_target_pairs={{0,4},{4,0},{8,12},{12,8},{1,5},{5,1},{9,13},{13,9},{2,6},{6,2},{1... | collective-permute-start | bytes 393224 | tf_op jit(solution)/shard_map/ppermute | solution.py:15
  43.2 1.7 %shard_map.93.gram5 = bf16[128,256]{1,0:T(8,128)(2,1)} custom-call(bf16[128,896]{1,0:T(8,128)(2,1)} %shard_map.92.own.late, bf16[128,896]{1,0:T(8,128)(2,1)} %copy-done), custom_call_target="tpu_custom_call" | custom-call | tf_op jit(solution)/shard_map/pallas_call | solution.py:78
  44.9 1.4 %collective-permute-start.15 = (bf16[128,256]{1,0:T(8,128)(2,1)}, bf16[128,256]{1,0:T(8,128)(2,1)S(1)}, u32[]{:S(2)}, u32[]{:S(2)}) collective-permute-start(bf16[128,256]{1,0:T(8,128)(2,1)} %shard_map.93.gram5), channel_id=1, source_target_pairs={{0,8},{4,12},{8,0},{12,4},{1,9},{5,13},{9,1},{13,5},{2,10},{6,14},... | collective-permute-start | bytes 196616 | tf_op jit(solution)/shard_map/ppermute | solution.py:15
  47.0 2.0 %shard_map.89.caps = bf16[512,512]{1,0:T(8,128)(2,1)} custom-call(bf16[128,512]{1,0:T(8,128)(2,1)} %a.1, bf16[128,512]{1,0:T(8,128)(2,1)} %copy-done.8, bf16[128,512]{1,0:T(8,128)(2,1)} %copy-done.7, bf16[128,512]{1,0:T(8,128)(2,1)} %copy-done.9), custom_call_target="tpu_custom_call" | custom-call | tf_op jit(solution)/shard_map/pallas_call | solution.py:78
  49.6 1.7 %shard_map.91 = (f32[128,256]{1,0:T(8,128)}, bf16[128,256]{1,0:T(8,128)(2,1)}) custom-call(f32[128,256]{1,0:T(8,128)} %get-tuple-element.32.own, bf16[128,512]{1,0:T(8,128)(2,1)} %copy-done.1), custom_call_target="tpu_custom_call" | custom-call | tf_op jit(solution)/shard_map/pallas_call | solution.py:78
  51.3 1.6 %collective-permute-start.13 = (bf16[128,256]{1,0:T(8,128)(2,1)}, bf16[128,256]{1,0:T(8,128)(2,1)S(1)}, u32[]{:S(2)}, u32[]{:S(2)}) collective-permute-start(bf16[128,256]{1,0:T(8,128)(2,1)} %get-tuple-element.35), channel_id=1, source_target_pairs={{0,8},{4,12},{8,0},{12,4},{1,9},{5,13},{9,1},{13,5},{2,10},{6,14},... | collective-permute-start | bytes 196616 | tf_op jit(solution)/shard_map/ppermute | solution.py:15
  54.1 2.5 %shard_map.90.back = bf16[128,256]{1,0:T(8,128)(2,1)} custom-call(bf16[128,384]{1,0:T(8,128)(2,1)} %shard_map.88.a, bf16[128,384]{1,0:T(8,128)(2,1)} %copy-done.12, bf16[128,384]{1,0:T(8,128)(2,1)} %copy-done.11, bf16[128,384]{1,0:T(8,128)(2,1)} %copy-done.13, bf16[512,512]{1,0:T(8,128)(2,1)} %shard_map.89.caps), custom_call_target="tpu_custom_call" | custom-call | tf_op jit(solution)/shard_map/pallas_call | solution.py:78
  57.7 2.2 %shard_map.94.inv_t = bf16[640,640]{1,0:T(8,128)(2,1)} custom-call(bf16[640,640]{1,0:T(8,128)(2,1)} %get-tuple-element.36.inv), custom_call_target="tpu_custom_call" | custom-call | tf_op jit(solution)/shard_map/pallas_call | solution.py:78
  61.8 4.3 %shard_map.95 = f32[1,640,256]{2,1,0:T(8,128)} custom-call(f32[640,256]{1,0:T(8,128)} %get-tuple-element.28.x2, bf16[128,256]{1,0:T(8,128)(2,1)} %shard_map.90.back, bf16[128,256]{1,0:T(8,128)(2,1)} %copy-done.16, f32[128,256]{1,0:T(8,128)} %get-tuple-element.34.down5, bf16[128,256]{1,0:T(8,128)(2,1)} %copy-done.15, bf16[128,256]{1,0:T(8,128)(2,1)} %shard_map.93.gram5, ...), custom_call_target="tpu_custom_call" | custom-call | tf_op jit(solution)/shard_map/pallas_call | solution.py:401
  (60 shorter events, 10.4 us)
Async XLA Ops:
  3.2 5.5 %collective-permute-start = (bf16[128,256]{1,0:T(8,128)(2,1)}, bf16[128,256]{1,0:T(8,128)(2,1)S(1)}, u32[]{:S(2)}, u32[]{:S(2)}) collective-permute-start(bf16[128,256]{1,0:T(8,128)(2,1)} %get-tuple-element.22.p), channel_id=1, source_target_pairs={{0,4},{4,0},{8,12},{12,8},{1,5},{5,1},{9,13},{13,9},{2,6},{6,2},{1... | collective-permute-start | bytes 196616 | tf_op jit(solution)/shard_map/ppermute | solution.py:15
  8.7 5.9 %collective-permute-start.2 = (bf16[128,640]{1,0:T(8,128)(2,1)}, bf16[128,640]{1,0:T(8,128)(2,1)S(1)}, u32[]{:S(2)}, u32[]{:S(2)}) collective-permute-start(bf16[128,640]{1,0:T(8,128)(2,1)} %shard_map.84.own), channel_id=1, source_target_pairs={{0,4},{4,0},{8,12},{12,8},{1,5},{5,1},{9,13},{13,9},{2,6},{6,2},{1... | collective-permute-start | bytes 491528 | tf_op jit(solution)/shard_map/ppermute | solution.py:15
  12.5 5.2 %collective-permute-start.1 = (bf16[128,512]{1,0:T(8,128)(2,1)}, bf16[128,512]{1,0:T(8,128)(2,1)S(1)}, u32[]{:S(2)}, u32[]{:S(2)}) collective-permute-start(bf16[128,512]{1,0:T(8,128)(2,1)} %get-tuple-element.25), channel_id=1, source_target_pairs={{0,4},{4,0},{8,12},{12,8},{1,5},{5,1},{9,13},{13,9},{2,6},{6,2},{1... | collective-permute-start | bytes 393224 | tf_op jit(solution)/shard_map/ppermute | solution.py:15
  20.2 7.0 %copy-start.18 = (bf16[128,384]{1,0:T(8,128)(2,1)S(1)}, bf16[128,384]{1,0:T(8,128)(2,1)}, u32[]{:S(2)}) copy-start(bf16[128,384]{1,0:T(8,128)(2,1)} %get-tuple-element.30) | copy-start | bytes 294916
  20.3 7.3 %copy-start.6 = (bf16[128,512]{1,0:T(8,128)(2,1)S(1)}, bf16[128,512]{1,0:T(8,128)(2,1)}, u32[]{:S(2)}) copy-start(bf16[128,512]{1,0:T(8,128)(2,1)} %a.1) | copy-start | bytes 393220
  20.3 13.1 %collective-permute-start.3 = (bf16[128,512]{1,0:T(8,128)(2,1)}, bf16[128,512]{1,0:T(8,128)(2,1)S(1)}, u32[]{:S(2)}, u32[]{:S(2)}) collective-permute-start(bf16[128,512]{1,0:T(8,128)(2,1)} %get-tuple-element.27.send), channel_id=1, source_target_pairs={{0,8},{4,12},{8,0},{12,4},{1,9},{5,13},{9,1},{13,5},{2,10},{6,14},... | collective-permute-start | bytes 393224 | tf_op jit(solution)/shard_map/ppermute | solution.py:15
  25.7 16.8 %collective-permute-start.14 = (bf16[128,896]{1,0:T(8,128)(2,1)}, bf16[128,896]{1,0:T(8,128)(2,1)S(1)}, u32[]{:S(2)}, u32[]{:S(2)}) collective-permute-start(bf16[128,896]{1,0:T(8,128)(2,1)} %shard_map.92.own.late), channel_id=1, source_target_pairs={{0,4},{4,0},{8,12},{12,8},{1,5},{5,1},{9,13},{13,9},{2,6},{6,2},{1... | collective-permute-start | bytes 688136 | tf_op jit(solution)/shard_map/ppermute | solution.py:15
  27.2 6.1 %collective-permute-start.4 = (bf16[128,384]{1,0:T(8,128)(2,1)S(1)}, bf16[128,384]{1,0:T(8,128)(2,1)S(1)}, u32[]{:S(2)}, u32[]{:S(2)}) collective-permute-start(bf16[128,384]{1,0:T(8,128)(2,1)S(1)} %copy-done.18), channel_id=1, source_target_pairs={{0,8},{4,12},{8,0},{12,4},{1,9},{5,13},{9,1},{13,5},{2,10},{6,14},... | collective-permute-start | bytes 294920 | tf_op jit(solution)/shard_map/ppermute | solution.py:15
  27.6 9.9 %collective-permute-start.9 = (bf16[128,512]{1,0:T(8,128)(2,1)S(1)}, bf16[128,512]{1,0:T(8,128)(2,1)S(1)}, u32[]{:S(2)}, u32[]{:S(2)}) collective-permute-start(bf16[128,512]{1,0:T(8,128)(2,1)S(1)} %copy-done.6), channel_id=1, source_target_pairs={{0,2},{1,3},{2,0},{3,1},{4,6},{5,7},{6,4},{7,5},{8,10},{9,11},{10,... | collective-permute-start | bytes 393224 | tf_op jit(solution)/shard_map/ppermute | solution.py:15
  36.0 6.5 %collective-permute-start.6 = (bf16[128,384]{1,0:T(8,128)(2,1)}, bf16[128,384]{1,0:T(8,128)(2,1)S(1)}, u32[]{:S(2)}, u32[]{:S(2)}) collective-permute-start(bf16[128,384]{1,0:T(8,128)(2,1)} %shard_map.88.a), channel_id=1, source_target_pairs={{0,2},{1,3},{2,0},{3,1},{4,6},{5,7},{6,4},{7,5},{8,10},{9,11},{10,... | collective-permute-start | bytes 294920 | tf_op jit(solution)/shard_map/ppermute | solution.py:15
  37.5 7.4 %collective-permute-start.8 = (bf16[128,512]{1,0:T(8,128)(2,1)S(1)}, bf16[128,512]{1,0:T(8,128)(2,1)S(1)}, u32[]{:S(2)}, u32[]{:S(2)}) collective-permute-start(bf16[128,512]{1,0:T(8,128)(2,1)S(1)} %copy-done.6), channel_id=1, source_target_pairs={{0,1},{1,0},{2,3},{3,2},{4,5},{5,4},{6,7},{7,6},{8,9},{9,8},{10,11... | collective-permute-start | bytes 393224 | tf_op jit(solution)/shard_map/ppermute | solution.py:15
  37.5 3.3 %copy-start.7 = (bf16[128,512]{1,0:T(8,128)(2,1)}, bf16[128,512]{1,0:T(8,128)(2,1)S(1)}, u32[]{:S(2)}) copy-start(bf16[128,512]{1,0:T(8,128)(2,1)S(1)} %collective-permute-done.9.c) | copy-start | bytes 393220
  37.5 8.8 %collective-permute-start.10 = (bf16[128,512]{1,0:T(8,128)(2,1)S(1)}, bf16[128,512]{1,0:T(8,128)(2,1)S(1)}, u32[]{:S(2)}, u32[]{:S(2)}) collective-permute-start(bf16[128,512]{1,0:T(8,128)(2,1)S(1)} %collective-permute-done.9.c), channel_id=1, source_target_pairs={{0,1},{1,0},{2,3},{3,2},{4,5},{5,4},{6,7},{7,6},{8,9},{9,8},{10,11... | collective-permute-start | bytes 393224 | tf_op jit(solution)/shard_map/ppermute | solution.py:15
  38.0 4.5 %copy-start.3 = (bf16[128,384]{1,0:T(8,128)(2,1)S(1)}, bf16[128,384]{1,0:T(8,128)(2,1)}, u32[]{:S(2)}) copy-start(bf16[128,384]{1,0:T(8,128)(2,1)} %shard_map.88.a) | copy-start | bytes 294916
  40.8 8.2 %collective-permute-start.12 = (bf16[128,512]{1,0:T(8,128)(2,1)}, bf16[128,512]{1,0:T(8,128)(2,1)S(1)}, u32[]{:S(2)}, u32[]{:S(2)}) collective-permute-start(bf16[128,512]{1,0:T(8,128)(2,1)} %get-tuple-element.33.z), channel_id=1, source_target_pairs={{0,4},{4,0},{8,12},{12,8},{1,5},{5,1},{9,13},{13,9},{2,6},{6,2},{1... | collective-permute-start | bytes 393224 | tf_op jit(solution)/shard_map/ppermute | solution.py:15
  42.5 10.4 %collective-permute-start.5 = (bf16[128,384]{1,0:T(8,128)(2,1)S(1)}, bf16[128,384]{1,0:T(8,128)(2,1)S(1)}, u32[]{:S(2)}, u32[]{:S(2)}) collective-permute-start(bf16[128,384]{1,0:T(8,128)(2,1)S(1)} %copy-done.3), channel_id=1, source_target_pairs={{0,1},{1,0},{2,3},{3,2},{4,5},{5,4},{6,7},{7,6},{8,9},{9,8},{10,11... | collective-permute-start | bytes 294920 | tf_op jit(solution)/shard_map/ppermute | solution.py:15
  42.6 2.3 %copy-start.11 = (bf16[128,384]{1,0:T(8,128)(2,1)}, bf16[128,384]{1,0:T(8,128)(2,1)S(1)}, u32[]{:S(2)}) copy-start(bf16[128,384]{1,0:T(8,128)(2,1)S(1)} %collective-permute-done.6.c) | copy-start | bytes 294916
  42.6 10.3 %collective-permute-start.7 = (bf16[128,384]{1,0:T(8,128)(2,1)S(1)}, bf16[128,384]{1,0:T(8,128)(2,1)S(1)}, u32[]{:S(2)}, u32[]{:S(2)}) collective-permute-start(bf16[128,384]{1,0:T(8,128)(2,1)S(1)} %collective-permute-done.6.c), channel_id=1, source_target_pairs={{0,1},{1,0},{2,3},{3,2},{4,5},{5,4},{6,7},{7,6},{8,9},{9,8},{10,11... | collective-permute-start | bytes 294920 | tf_op jit(solution)/shard_map/ppermute | solution.py:15
  44.9 1.4 %copy-start.8 = (bf16[128,512]{1,0:T(8,128)(2,1)}, bf16[128,512]{1,0:T(8,128)(2,1)S(1)}, u32[]{:S(2)}) copy-start(bf16[128,512]{1,0:T(8,128)(2,1)S(1)} %collective-permute-done.8.b) | copy-start | bytes 393220
  44.9 15.0 %collective-permute-start.15 = (bf16[128,256]{1,0:T(8,128)(2,1)}, bf16[128,256]{1,0:T(8,128)(2,1)S(1)}, u32[]{:S(2)}, u32[]{:S(2)}) collective-permute-start(bf16[128,256]{1,0:T(8,128)(2,1)} %shard_map.93.gram5), channel_id=1, source_target_pairs={{0,8},{4,12},{8,0},{12,4},{1,9},{5,13},{9,1},{13,5},{2,10},{6,14},... | collective-permute-start | bytes 196616 | tf_op jit(solution)/shard_map/ppermute | solution.py:15
  51.3 8.6 %collective-permute-start.13 = (bf16[128,256]{1,0:T(8,128)(2,1)}, bf16[128,256]{1,0:T(8,128)(2,1)S(1)}, u32[]{:S(2)}, u32[]{:S(2)}) collective-permute-start(bf16[128,256]{1,0:T(8,128)(2,1)} %get-tuple-element.35), channel_id=1, source_target_pairs={{0,8},{4,12},{8,0},{12,4},{1,9},{5,13},{9,1},{13,5},{2,10},{6,14},... | collective-permute-start | bytes 196616 | tf_op jit(solution)/shard_map/ppermute | solution.py:15
  56.7 4.5 %collective-permute-start.11 = (bf16[128,256]{1,0:T(8,128)(2,1)}, bf16[128,256]{1,0:T(8,128)(2,1)S(1)}, u32[]{:S(2)}, u32[]{:S(2)}) collective-permute-start(bf16[128,256]{1,0:T(8,128)(2,1)} %shard_map.90.back), channel_id=1, source_target_pairs={{0,4},{4,0},{8,12},{12,8},{1,5},{5,1},{9,13},{13,9},{2,6},{6,2},{1... | collective-permute-start | bytes 196616 | tf_op jit(solution)/shard_map/ppermute | solution.py:15
  59.9 1.2 %copy-start.14 = (bf16[128,256]{1,0:T(8,128)(2,1)}, bf16[128,256]{1,0:T(8,128)(2,1)S(1)}, u32[]{:S(2)}) copy-start(bf16[128,256]{1,0:T(8,128)(2,1)S(1)} %collective-permute-done.15.gram5_far) | copy-start | bytes 196612
  59.9 1.2 %copy-start.15 = (bf16[128,256]{1,0:T(8,128)(2,1)}, bf16[128,256]{1,0:T(8,128)(2,1)S(1)}, u32[]{:S(2)}) copy-start(bf16[128,256]{1,0:T(8,128)(2,1)S(1)} %collective-permute-done.13.down5_far) | copy-start | bytes 196612
  (11 other events, 7.2 us)

commit v3 on v2

--- a/solution.py
+++ b/solution.py
@@ -8,6 +8,7 @@
 from jax.sharding import PartitionSpec as P
 
 BF = jnp.bfloat16
+VMEM_LIMIT = 8 * 2**20
 
 
 def swap(value, axis, mask):
@@ -77,11 +78,20 @@
     anywhere = pl.BlockSpec(memory_space=pl.ANY)
     return pl.pallas_call(
         body,
-        out_shape=[jax.ShapeDtypeStruct(shape, dtype) for shape, dtype in outs],
+        out_shape=[pltpu.VMEM(shape, dtype) for shape, dtype in outs],
         in_specs=[anywhere if i in hbm else vmem for i in range(len(args))],
         out_specs=[vmem] * len(outs),
         scratch_shapes=list(scratch),
-    )(*args)
+        compiler_params=pltpu.CompilerParams(vmem_limit_bytes=VMEM_LIMIT),
+    )(*[in_hbm(a) if i in hbm else in_vmem(a) for i, a in enumerate(args)])
+
+
+def in_hbm(value):
+    return pltpu.with_memory_space_constraint(value, pltpu.HBM)
+
+
+def in_vmem(value):
+    return pltpu.with_memory_space_constraint(value, pltpu.VMEM)
 
 
 def side(bit):
@@ -411,7 +421,8 @@
             pltpu.VMEM((rows, cols), f32),
             pltpu.SemaphoreType.DMA((blocks,)),
         ],
-    )(*args)
+        compiler_params=pltpu.CompilerParams(vmem_limit_bytes=VMEM_LIMIT),
+    )(*[in_vmem(a) for a in args])
 
 
 def on_device(*args):

time: 66.6 us -> 46.2 us (0.69)
  Pallas kernels: 33.9 us -> 8.58 us
  waiting for transfers between devices: 6.35 us -> 13.7 us
  local copies, waits for them, and re-layouts: 5.97 us -> 0.03 us
  starting transfers between devices: 19.8 us -> 23.6 us
    pallas_call x13, Pallas kernels: 29.6 us -> 6.4 us  [call(): pl.pallas_call(body, out_shape=[pltpu.VMEM(shape, dtype) for shape, dtype...]
    ppermute x16, waiting for transfers between devices: 6.35 us -> 13.7 us  [swap(): return lax.ppermute(value, axis, pairs)]
    unnamed x38 -> x12, local copies, waits for them, and re-layouts: 5.97 us -> 0.03 us
    ppermute x16, starting transfers between devices: 19.8 us -> 23.6 us  [swap(): return lax.ppermute(value, axis, pairs)]
    pallas_call x1, Pallas kernels: 4.35 us -> 2.18 us  [two_levels(): pl.pallas_call(last_body, out_shape=jax.ShapeDtypeStruct((1, rows, cols),...]
  transfers between devices with their start and end apart: 16 -> 16, of which waited for: 4 -> 7; matrix products, arithmetic and copies ran while one was open for 0% -> 0% of each run, Pallas kernels for 37% -> 8%
where the time goes in v3:
time: 46.2 us; the launch traced here: 46 us
  starting transfers between devices  23.6 us (51%)
  waiting for transfers between devices  13.7 us (30%)
  Pallas kernels  8.58 us (19%)
    ppermute x16, starting transfers between devices, swap(): return lax.ppermute(value, axis, pairs)  23.6 us
    ppermute x16, waiting for transfers between devices, swap(): return lax.ppermute(value, axis, pairs)  13.7 us
    pallas_call x13, Pallas kernels, call(): pl.pallas_call(body, out_shape=[pltpu.VMEM(shape, dtype) for shape, dtype...  6.4 us
    pallas_call x1, Pallas kernels, two_levels(): pl.pallas_call(last_body, out_shape=jax.ShapeDtypeStruct((1, rows, cols),...  2.18 us
  transfers between devices with their start and end apart: 16, of which 7 were waited for; matrix products, arithmetic and copies ran while one was open for 0% of the time, Pallas kernels for 8%

profile of v3, /device:TPU:0, one launch (start us, length us, event | category | flops | bytes accessed | tf_op | source)
XLA Modules:
  0.0 46.0 jit_solution(8932708609993174243)
XLA Ops:
  0.0 2.4 %shard_map.82 = (f32[640,256]{1,0:T(8,128)S(1)}, bf16[640,640]{1,0:T(8,128)(2,1)S(1)}, bf16[128,256]{1,0:T(8,128)(2,1)S(1)}) custom-call(f32[1,640,256]{2,1,0:T(8,128)} %rhs_hbm.1, bf16[1,640,640]{2,1,0:T(8,128)(2,1)} %inv_hbm.1, bf16[2,1,640,128]{3,2,1,0:T(8,128)(2,1)} %rb.5), custom_call_target="tpu_custom_call" | custom-call | tf_op jit(solution)/shard_map/pallas_call | solution.py:79
  2.5 3.1 %collective-permute-start = (bf16[128,256]{1,0:T(8,128)(2,1)S(1)}, bf16[128,256]{1,0:T(8,128)(2,1)S(1)}, u32[]{:S(2)}, u32[]{:S(2)}) collective-permute-start(bf16[128,256]{1,0:T(8,128)(2,1)S(1)} %get-tuple-element.22.p), channel_id=1, source_target_pairs={{0,4},{4,0},{8,12},{12,8},{1,5},{5,1},{9,13},{13,9},{2,6},{6,2},{1... | collective-permute-start | bytes 196616 | tf_op jit(solution)/shard_map/ppermute | solution.py:16
  5.6 0.6 %shard_map.84.own = bf16[128,640]{1,0:T(8,128)(2,1)S(1)} custom-call(bf16[2,1,640,128]{3,2,1,0:T(8,128)(2,1)S(1)} %copy-done, bf16[2,1,128,256]{3,2,1,0:T(8,128)(2,1)S(1)} %copy-done.2, bf16[1,640,128]{2,1,0:T(8,128)(2,1)S(1)} %copy-done.3, bf16[1,640,128]{2,1,0:T(8,128)(2,1)S(1)} %copy-done.4), custom_call_target="tpu_custom_call" | custom-call | tf_op jit(solution)/shard_map/pallas_call | solution.py:79
  6.2 1.8 %collective-permute-done.p_sib = bf16[128,256]{1,0:T(8,128)(2,1)S(1)} collective-permute-done((bf16[128,256]{1,0:T(8,128)(2,1)S(1)}, bf16[128,256]{1,0:T(8,128)(2,1)S(1)}, u32[]{:S(2)}, u32[]{:S(2)}) %collective-permute-start) | collective-permute-done | bytes 65568 | tf_op jit(solution)/shard_map/ppermute | solution.py:16
  8.1 0.8 %shard_map.83 = (f32[640,256]{1,0:T(8,128)S(1)}, bf16[128,512]{1,0:T(8,128)(2,1)S(1)}, f32[128,512]{1,0:T(8,128)S(1)}) custom-call(f32[640,256]{1,0:T(8,128)S(1)} %get-tuple-element.21.x0, bf16[128,256]{1,0:T(8,128)(2,1)S(1)} %get-tuple-element.22.p, bf16[128,256]{1,0:T(8,128)(2,1)S(1)} %collective-permute-done.p_sib, bf16[2,1,640,128]{3,2,1,0:T(8,128)(2,1)S(1)} %copy-done, ...), custom_call_target="tpu_custom_call" | custom-call | tf_op jit(solution)/shard_map/pallas_call | solution.py:79
  8.9 2.5 %collective-permute-start.1 = (bf16[128,512]{1,0:T(8,128)(2,1)S(1)}, bf16[128,512]{1,0:T(8,128)(2,1)S(1)}, u32[]{:S(2)}, u32[]{:S(2)}) collective-permute-start(bf16[128,512]{1,0:T(8,128)(2,1)S(1)} %get-tuple-element.25), channel_id=1, source_target_pairs={{0,4},{4,0},{8,12},{12,8},{1,5},{5,1},{9,13},{13,9},{2,6},{6,2},{1... | collective-permute-start | bytes 393224 | tf_op jit(solution)/shard_map/ppermute | solution.py:16
  11.4 1.8 %collective-permute-done.2.sib = bf16[128,640]{1,0:T(8,128)(2,1)S(1)} collective-permute-done((bf16[128,640]{1,0:T(8,128)(2,1)S(1)}, bf16[128,640]{1,0:T(8,128)(2,1)S(1)}, u32[]{:S(2)}, u32[]{:S(2)}) %collective-permute-start.2) | collective-permute-done | bytes 163872 | tf_op jit(solution)/shard_map/ppermute | solution.py:16
  13.3 1.3 %collective-permute-done.1.pair = bf16[128,512]{1,0:T(8,128)(2,1)S(1)} collective-permute-done((bf16[128,512]{1,0:T(8,128)(2,1)S(1)}, bf16[128,512]{1,0:T(8,128)(2,1)S(1)}, u32[]{:S(2)}, u32[]{:S(2)}) %collective-permute-start.1) | collective-permute-done | bytes 131104 | tf_op jit(solution)/shard_map/ppermute | solution.py:16
  14.8 2.6 %collective-permute-start.3 = (bf16[128,512]{1,0:T(8,128)(2,1)S(1)}, bf16[128,512]{1,0:T(8,128)(2,1)S(1)}, u32[]{:S(2)}, u32[]{:S(2)}) collective-permute-start(bf16[128,512]{1,0:T(8,128)(2,1)S(1)} %get-tuple-element.27.send), channel_id=1, source_target_pairs={{0,8},{4,12},{8,0},{12,4},{1,9},{5,13},{9,1},{13,5},{2,10},{6,14},... | collective-permute-start | bytes 393224 | tf_op jit(solution)/shard_map/ppermute | solution.py:16
  17.5 0.4 shard_map.92.own.late
  17.9 1.8 %collective-permute-start.14 = (bf16[128,896]{1,0:T(8,128)(2,1)S(1)}, bf16[128,896]{1,0:T(8,128)(2,1)S(1)}, u32[]{:S(2)}, u32[]{:S(2)}) collective-permute-start(bf16[128,896]{1,0:T(8,128)(2,1)S(1)} %shard_map.92.own.late), channel_id=1, source_target_pairs={{0,4},{4,0},{8,12},{12,8},{1,5},{5,1},{9,13},{13,9},{2,6},{6,2},{1... | collective-permute-start | bytes 688136 | tf_op jit(solution)/shard_map/ppermute | solution.py:16
  20.1 1.5 %collective-permute-start.9 = (bf16[128,512]{1,0:T(8,128)(2,1)S(1)}, bf16[128,512]{1,0:T(8,128)(2,1)S(1)}, u32[]{:S(2)}, u32[]{:S(2)}) collective-permute-start(bf16[128,512]{1,0:T(8,128)(2,1)S(1)} %copy-done.5), channel_id=1, source_target_pairs={{0,2},{1,3},{2,0},{3,1},{4,6},{5,7},{6,4},{7,5},{8,10},{9,11},{10,... | collective-permute-start | bytes 393224 | tf_op jit(solution)/shard_map/ppermute | solution.py:16
  21.6 4.6 %collective-permute-done.4.nexts_far = bf16[128,384]{1,0:T(8,128)(2,1)S(1)} collective-permute-done((bf16[128,384]{1,0:T(8,128)(2,1)S(1)}, bf16[128,384]{1,0:T(8,128)(2,1)S(1)}, u32[]{:S(2)}, u32[]{:S(2)}) %collective-permute-start.4) | collective-permute-done | bytes 98336 | tf_op jit(solution)/shard_map/ppermute | solution.py:16
  26.4 1.6 %collective-permute-start.6 = (bf16[128,384]{1,0:T(8,128)(2,1)S(1)}, bf16[128,384]{1,0:T(8,128)(2,1)S(1)}, u32[]{:S(2)}, u32[]{:S(2)}) collective-permute-start(bf16[128,384]{1,0:T(8,128)(2,1)S(1)} %shard_map.88.a), channel_id=1, source_target_pairs={{0,2},{1,3},{2,0},{3,1},{4,6},{5,7},{6,4},{7,5},{8,10},{9,11},{10,... | collective-permute-start | bytes 294920 | tf_op jit(solution)/shard_map/ppermute | solution.py:16
  27.9 0.5 %collective-permute-start.10 = (bf16[128,512]{1,0:T(8,128)(2,1)S(1)}, bf16[128,512]{1,0:T(8,128)(2,1)S(1)}, u32[]{:S(2)}, u32[]{:S(2)}) collective-permute-start(bf16[128,512]{1,0:T(8,128)(2,1)S(1)} %collective-permute-done.9.c), channel_id=1, source_target_pairs={{0,1},{1,0},{2,3},{3,2},{4,5},{5,4},{6,7},{7,6},{8,9},{9,8},{10,11... | collective-permute-start | bytes 393224 | tf_op jit(solution)/shard_map/ppermute | solution.py:16
  28.4 0.7 %shard_map.87 = (f32[640,256]{1,0:T(8,128)S(1)}, f32[128,256]{1,0:T(8,128)S(1)}, bf16[128,512]{1,0:T(8,128)(2,1)S(1)}) custom-call(f32[640,256]{1,0:T(8,128)S(1)} %get-tuple-element.23.x1, bf16[128,512]{1,0:T(8,128)(2,1)S(1)} %get-tuple-element.27.send, bf16[128,512]{1,0:T(8,128)(2,1)S(1)} %collective-permute-done.3.far, ...), custom_call_target="tpu_custom_call" | custom-call | tf_op jit(solution)/shard_map/pallas_call | solution.py:79
  29.2 1.8 %collective-permute-start.12 = (bf16[128,512]{1,0:T(8,128)(2,1)S(1)}, bf16[128,512]{1,0:T(8,128)(2,1)S(1)}, u32[]{:S(2)}, u32[]{:S(2)}) collective-permute-start(bf16[128,512]{1,0:T(8,128)(2,1)S(1)} %get-tuple-element.33.z), channel_id=1, source_target_pairs={{0,4},{4,0},{8,12},{12,8},{1,5},{5,1},{9,13},{13,9},{2,6},{6,2},{1... | collective-permute-start | bytes 393224 | tf_op jit(solution)/shard_map/ppermute | solution.py:16
  31.1 0.4 collective-permute-start.7
  31.5 3.0 %collective-permute-start.15 = (bf16[128,256]{1,0:T(8,128)(2,1)S(1)}, bf16[128,256]{1,0:T(8,128)(2,1)S(1)}, u32[]{:S(2)}, u32[]{:S(2)}) collective-permute-start(bf16[128,256]{1,0:T(8,128)(2,1)S(1)} %shard_map.93.gram5), channel_id=1, source_target_pairs={{0,8},{4,12},{8,0},{12,4},{1,9},{5,13},{9,1},{13,5},{2,10},{6,14},... | collective-permute-start | bytes 196616 | tf_op jit(solution)/shard_map/ppermute | solution.py:16
  34.7 4.1 %collective-permute-start.13 = (bf16[128,256]{1,0:T(8,128)(2,1)S(1)}, bf16[128,256]{1,0:T(8,128)(2,1)S(1)}, u32[]{:S(2)}, u32[]{:S(2)}) collective-permute-start(bf16[128,256]{1,0:T(8,128)(2,1)S(1)} %get-tuple-element.35), channel_id=1, source_target_pairs={{0,8},{4,12},{8,0},{12,4},{1,9},{5,13},{9,1},{13,5},{2,10},{6,14},... | collective-permute-start | bytes 196616 | tf_op jit(solution)/shard_map/ppermute | solution.py:16
  38.8 0.7 %shard_map.90.back = bf16[128,256]{1,0:T(8,128)(2,1)S(1)} custom-call(bf16[128,384]{1,0:T(8,128)(2,1)S(1)} %shard_map.88.a, bf16[128,384]{1,0:T(8,128)(2,1)S(1)} %collective-permute-done.5.b, bf16[128,384]{1,0:T(8,128)(2,1)S(1)} %collective-permute-done.6.c, bf16[128,384]{1,0:T(8,128)(2,1)S(1)} %collective-permute-done.7.d, bf16[512,512]{1,0:T(8,128)(2,1)S(1)} %shard_map.89.caps), custom_call_target="tpu_custom_call" | custom-call | tf_op jit(solution)/shard_map/pallas_call | solution.py:79
  39.8 2.0 %collective-permute-done.13.down5_far = bf16[128,256]{1,0:T(8,128)(2,1)S(1)} collective-permute-done((bf16[128,256]{1,0:T(8,128)(2,1)S(1)}, bf16[128,256]{1,0:T(8,128)(2,1)S(1)}, u32[]{:S(2)}, u32[]{:S(2)}) %collective-permute-start.13) | collective-permute-done | bytes 65568 | tf_op jit(solution)/shard_map/ppermute | solution.py:16
  41.8 2.1 %collective-permute-done.11.back_sib = bf16[128,256]{1,0:T(8,128)(2,1)S(1)} collective-permute-done((bf16[128,256]{1,0:T(8,128)(2,1)S(1)}, bf16[128,256]{1,0:T(8,128)(2,1)S(1)}, u32[]{:S(2)}, u32[]{:S(2)}) %collective-permute-start.11) | collective-permute-done | bytes 65568 | tf_op jit(solution)/shard_map/ppermute | solution.py:16
  43.9 2.2 %shard_map.95 = f32[1,640,256]{2,1,0:T(8,128)} custom-call(f32[640,256]{1,0:T(8,128)S(1)} %get-tuple-element.28.x2, bf16[128,256]{1,0:T(8,128)(2,1)S(1)} %shard_map.90.back, bf16[128,256]{1,0:T(8,128)(2,1)S(1)} %collective-permute-done.11.back_sib, f32[128,256]{1,0:T(8,128)S(1)} %get-tuple-element.34.down5, ...), custom_call_target="tpu_custom_call" | custom-call | tf_op jit(solution)/shard_map/pallas_call | solution.py:411
  (34 shorter events, 1.4 us)
Async XLA Ops:
  0.0 5.6 %copy-start = (bf16[2,1,640,128]{3,2,1,0:T(8,128)(2,1)S(1)}, bf16[2,1,640,128]{3,2,1,0:T(8,128)(2,1)}, u32[]{:S(2)}) copy-start(bf16[2,1,640,128]{3,2,1,0:T(8,128)(2,1)} %lb.9) | copy-start | bytes 983044
  0.0 5.6 %copy-start.2 = (bf16[2,1,128,256]{3,2,1,0:T(8,128)(2,1)S(1)}, bf16[2,1,128,256]{3,2,1,0:T(8,128)(2,1)}, u32[]{:S(2)}) copy-start(bf16[2,1,128,256]{3,2,1,0:T(8,128)(2,1)} %caps.9) | copy-start | bytes 393220
  0.0 5.6 %copy-start.3 = (bf16[1,640,128]{2,1,0:T(8,128)(2,1)S(1)}, bf16[1,640,128]{2,1,0:T(8,128)(2,1)}, u32[]{:S(2)}) copy-start(bf16[1,640,128]{2,1,0:T(8,128)(2,1)} %tl.7) | copy-start | bytes 491524
  0.0 5.6 %copy-start.4 = (bf16[1,640,128]{2,1,0:T(8,128)(2,1)S(1)}, bf16[1,640,128]{2,1,0:T(8,128)(2,1)}, u32[]{:S(2)}) copy-start(bf16[1,640,128]{2,1,0:T(8,128)(2,1)} %tr.7) | copy-start | bytes 491524
  2.4 5.6 %copy-start.1 = (bf16[2,1,640,128]{3,2,1,0:T(8,128)(2,1)S(1)}, bf16[2,1,640,128]{3,2,1,0:T(8,128)(2,1)}, u32[]{:S(2)}) copy-start(bf16[2,1,640,128]{3,2,1,0:T(8,128)(2,1)} %rb.5) | copy-start | bytes 983044
  2.5 5.6 %collective-permute-start = (bf16[128,256]{1,0:T(8,128)(2,1)S(1)}, bf16[128,256]{1,0:T(8,128)(2,1)S(1)}, u32[]{:S(2)}, u32[]{:S(2)}) collective-permute-start(bf16[128,256]{1,0:T(8,128)(2,1)S(1)} %get-tuple-element.22.p), channel_id=1, source_target_pairs={{0,4},{4,0},{8,12},{12,8},{1,5},{5,1},{9,13},{13,9},{2,6},{6,2},{1... | collective-permute-start | bytes 196616 | tf_op jit(solution)/shard_map/ppermute | solution.py:16
  6.1 7.1 %collective-permute-start.2 = (bf16[128,640]{1,0:T(8,128)(2,1)S(1)}, bf16[128,640]{1,0:T(8,128)(2,1)S(1)}, u32[]{:S(2)}, u32[]{:S(2)}) collective-permute-start(bf16[128,640]{1,0:T(8,128)(2,1)S(1)} %shard_map.84.own), channel_id=1, source_target_pairs={{0,4},{4,0},{8,12},{12,8},{1,5},{5,1},{9,13},{13,9},{2,6},{6,2},{1... | collective-permute-start | bytes 491528 | tf_op jit(solution)/shard_map/ppermute | solution.py:16
  8.9 5.8 %collective-permute-start.1 = (bf16[128,512]{1,0:T(8,128)(2,1)S(1)}, bf16[128,512]{1,0:T(8,128)(2,1)S(1)}, u32[]{:S(2)}, u32[]{:S(2)}) collective-permute-start(bf16[128,512]{1,0:T(8,128)(2,1)S(1)} %get-tuple-element.25), channel_id=1, source_target_pairs={{0,4},{4,0},{8,12},{12,8},{1,5},{5,1},{9,13},{13,9},{2,6},{6,2},{1... | collective-permute-start | bytes 393224 | tf_op jit(solution)/shard_map/ppermute | solution.py:16
  14.8 5.3 %copy-start.5 = (bf16[128,512]{1,0:T(8,128)(2,1)S(1)}, bf16[128,512]{1,0:T(8,128)(2,1)}, u32[]{:S(2)}) copy-start(bf16[128,512]{1,0:T(8,128)(2,1)} %a.1) | copy-start | bytes 393220
  14.8 11.3 %collective-permute-start.3 = (bf16[128,512]{1,0:T(8,128)(2,1)S(1)}, bf16[128,512]{1,0:T(8,128)(2,1)S(1)}, u32[]{:S(2)}, u32[]{:S(2)}) collective-permute-start(bf16[128,512]{1,0:T(8,128)(2,1)S(1)} %get-tuple-element.27.send), channel_id=1, source_target_pairs={{0,8},{4,12},{8,0},{12,4},{1,9},{5,13},{9,1},{13,5},{2,10},{6,14},... | collective-permute-start | bytes 393224 | tf_op jit(solution)/shard_map/ppermute | solution.py:16
  17.9 13.0 %collective-permute-start.14 = (bf16[128,896]{1,0:T(8,128)(2,1)S(1)}, bf16[128,896]{1,0:T(8,128)(2,1)S(1)}, u32[]{:S(2)}, u32[]{:S(2)}) collective-permute-start(bf16[128,896]{1,0:T(8,128)(2,1)S(1)} %shard_map.92.own.late), channel_id=1, source_target_pairs={{0,4},{4,0},{8,12},{12,8},{1,5},{5,1},{9,13},{13,9},{2,6},{6,2},{1... | collective-permute-start | bytes 688136 | tf_op jit(solution)/shard_map/ppermute | solution.py:16
  19.7 6.4 %collective-permute-start.4 = (bf16[128,384]{1,0:T(8,128)(2,1)S(1)}, bf16[128,384]{1,0:T(8,128)(2,1)S(1)}, u32[]{:S(2)}, u32[]{:S(2)}) collective-permute-start(bf16[128,384]{1,0:T(8,128)(2,1)S(1)} %get-tuple-element.30), channel_id=1, source_target_pairs={{0,8},{4,12},{8,0},{12,4},{1,9},{5,13},{9,1},{13,5},{2,10},{6,14},... | collective-permute-start | bytes 294920 | tf_op jit(solution)/shard_map/ppermute | solution.py:16
  20.1 7.8 %collective-permute-start.9 = (bf16[128,512]{1,0:T(8,128)(2,1)S(1)}, bf16[128,512]{1,0:T(8,128)(2,1)S(1)}, u32[]{:S(2)}, u32[]{:S(2)}) collective-permute-start(bf16[128,512]{1,0:T(8,128)(2,1)S(1)} %copy-done.5), channel_id=1, source_target_pairs={{0,2},{1,3},{2,0},{3,1},{4,6},{5,7},{6,4},{7,5},{8,10},{9,11},{10,... | collective-permute-start | bytes 393224 | tf_op jit(solution)/shard_map/ppermute | solution.py:16
  26.4 4.7 %collective-permute-start.6 = (bf16[128,384]{1,0:T(8,128)(2,1)S(1)}, bf16[128,384]{1,0:T(8,128)(2,1)S(1)}, u32[]{:S(2)}, u32[]{:S(2)}) collective-permute-start(bf16[128,384]{1,0:T(8,128)(2,1)S(1)} %shard_map.88.a), channel_id=1, source_target_pairs={{0,2},{1,3},{2,0},{3,1},{4,6},{5,7},{6,4},{7,5},{8,10},{9,11},{10,... | collective-permute-start | bytes 294920 | tf_op jit(solution)/shard_map/ppermute | solution.py:16
  27.9 3.6 %collective-permute-start.8 = (bf16[128,512]{1,0:T(8,128)(2,1)S(1)}, bf16[128,512]{1,0:T(8,128)(2,1)S(1)}, u32[]{:S(2)}, u32[]{:S(2)}) collective-permute-start(bf16[128,512]{1,0:T(8,128)(2,1)S(1)} %copy-done.5), channel_id=1, source_target_pairs={{0,1},{1,0},{2,3},{3,2},{4,5},{5,4},{6,7},{7,6},{8,9},{9,8},{10,11... | collective-permute-start | bytes 393224 | tf_op jit(solution)/shard_map/ppermute | solution.py:16
  27.9 6.6 %collective-permute-start.10 = (bf16[128,512]{1,0:T(8,128)(2,1)S(1)}, bf16[128,512]{1,0:T(8,128)(2,1)S(1)}, u32[]{:S(2)}, u32[]{:S(2)}) collective-permute-start(bf16[128,512]{1,0:T(8,128)(2,1)S(1)} %collective-permute-done.9.c), channel_id=1, source_target_pairs={{0,1},{1,0},{2,3},{3,2},{4,5},{5,4},{6,7},{7,6},{8,9},{9,8},{10,11... | collective-permute-start | bytes 393224 | tf_op jit(solution)/shard_map/ppermute | solution.py:16
  29.2 5.5 %collective-permute-start.12 = (bf16[128,512]{1,0:T(8,128)(2,1)S(1)}, bf16[128,512]{1,0:T(8,128)(2,1)S(1)}, u32[]{:S(2)}, u32[]{:S(2)}) collective-permute-start(bf16[128,512]{1,0:T(8,128)(2,1)S(1)} %get-tuple-element.33.z), channel_id=1, source_target_pairs={{0,4},{4,0},{8,12},{12,8},{1,5},{5,1},{9,13},{13,9},{2,6},{6,2},{1... | collective-permute-start | bytes 393224 | tf_op jit(solution)/shard_map/ppermute | solution.py:16
  31.0 7.9 %collective-permute-start.5 = (bf16[128,384]{1,0:T(8,128)(2,1)S(1)}, bf16[128,384]{1,0:T(8,128)(2,1)S(1)}, u32[]{:S(2)}, u32[]{:S(2)}) collective-permute-start(bf16[128,384]{1,0:T(8,128)(2,1)S(1)} %shard_map.88.a), channel_id=1, source_target_pairs={{0,1},{1,0},{2,3},{3,2},{4,5},{5,4},{6,7},{7,6},{8,9},{9,8},{10,11... | collective-permute-start | bytes 294920 | tf_op jit(solution)/shard_map/ppermute | solution.py:16
  31.1 7.8 %collective-permute-start.7 = (bf16[128,384]{1,0:T(8,128)(2,1)S(1)}, bf16[128,384]{1,0:T(8,128)(2,1)S(1)}, u32[]{:S(2)}, u32[]{:S(2)}) collective-permute-start(bf16[128,384]{1,0:T(8,128)(2,1)S(1)} %collective-permute-done.6.c), channel_id=1, source_target_pairs={{0,1},{1,0},{2,3},{3,2},{4,5},{5,4},{6,7},{7,6},{8,9},{9,8},{10,11... | collective-permute-start | bytes 294920 | tf_op jit(solution)/shard_map/ppermute | solution.py:16
  31.5 8.3 %collective-permute-start.15 = (bf16[128,256]{1,0:T(8,128)(2,1)S(1)}, bf16[128,256]{1,0:T(8,128)(2,1)S(1)}, u32[]{:S(2)}, u32[]{:S(2)}) collective-permute-start(bf16[128,256]{1,0:T(8,128)(2,1)S(1)} %shard_map.93.gram5), channel_id=1, source_target_pairs={{0,8},{4,12},{8,0},{12,4},{1,9},{5,13},{9,1},{13,5},{2,10},{6,14},... | collective-permute-start | bytes 196616 | tf_op jit(solution)/shard_map/ppermute | solution.py:16
  34.7 7.1 %collective-permute-start.13 = (bf16[128,256]{1,0:T(8,128)(2,1)S(1)}, bf16[128,256]{1,0:T(8,128)(2,1)S(1)}, u32[]{:S(2)}, u32[]{:S(2)}) collective-permute-start(bf16[128,256]{1,0:T(8,128)(2,1)S(1)} %get-tuple-element.35), channel_id=1, source_target_pairs={{0,8},{4,12},{8,0},{12,4},{1,9},{5,13},{9,1},{13,5},{2,10},{6,14},... | collective-permute-start | bytes 196616 | tf_op jit(solution)/shard_map/ppermute | solution.py:16
  39.5 4.3 %collective-permute-start.11 = (bf16[128,256]{1,0:T(8,128)(2,1)S(1)}, bf16[128,256]{1,0:T(8,128)(2,1)S(1)}, u32[]{:S(2)}, u32[]{:S(2)}) collective-permute-start(bf16[128,256]{1,0:T(8,128)(2,1)S(1)} %shard_map.90.back), channel_id=1, source_target_pairs={{0,4},{4,0},{8,12},{12,8},{1,5},{5,1},{9,13},{13,9},{2,6},{6,2},{1... | collective-permute-start | bytes 196616 | tf_op jit(solution)/shard_map/ppermute | solution.py:16

commit v4 on v0

v4 whole, which is shorter than its diff:
```python
import math

import jax
import jax.numpy as jnp
from jax import lax
from jax.experimental import pallas as pl
from jax.experimental.pallas import tpu as pltpu
from jax.sharding import PartitionSpec as P

BF = jnp.bfloat16
VMEM_LIMIT = 8 * 2**20
FLOPS_PER_MICRO = 1e9


def swap(value, axis, mask):
    pairs = [(source, source ^ mask) for source in range(lax.axis_size(axis))]
    return lax.ppermute(value, axis, pairs)


def dot(a, b):
    return jnp.dot(a, b, preferred_element_type=jnp.float32)


def dot_t(a, b):
    return lax.dot_general(a, b, (((0,), (0,)), ((), ())), preferred_element_type=jnp.float32)


def ordered(upper_side, own, other):
    return jnp.where(
        upper_side, jnp.concatenate([other, own], 0), jnp.concatenate([own, other], 0)
    )


def level_step(current, project_basis, update_basis, caps_rows, level_num):
    leaf_rows = current.shape[0]
    shift_bits = level_num - 1
    partial_value = dot_t(project_basis, current.astype(BF)) * (
        1.0 / math.sqrt(leaf_rows * 2**shift_bits)
    )
    for bit_index in range(shift_bits):
        partial_value = partial_value + swap(partial_value, "leaf", 2**bit_index)
    own = partial_value.astype(BF)
    other = swap(own, "leaf", 2**shift_bits)
    upper_side = (lax.axis_index("leaf") >> shift_bits) & 1 == 1
    stacked = ordered(upper_side, own, other)
    weights = dot(caps_rows, stacked).astype(BF)
    return current - dot(update_basis, weights)


def top_step(current, project_basis, update_basis, caps_rows):
    leaf_count = lax.axis_size("leaf")
    partial_value = dot_t(project_basis, current.astype(BF)) * (
        1.0 / math.sqrt(leaf_count * current.shape[0])
    )
    column_total = lax.psum(partial_value, "leaf")
    stacked = lax.all_gather(column_total.astype(BF), "top", axis=0, tiled=True)
    weights = dot(caps_rows, stacked).astype(BF)
    return current - dot(update_basis, weights)


def step_by_step(
    right_side, leaf_inverse, left_basis, right_basis, level_caps, top_left, top_right, top_caps
):
    levels = left_basis.shape[0]
    lefts = [left_basis[k, 0] for k in range(levels)]
    rights = [right_basis[k, 0] for k in range(levels)]
    current = dot(leaf_inverse[0], right_side[0].astype(BF))
    for k in range(levels):
        current = level_step(current, rights[k], lefts[k], level_caps[k, 0], k + 1)
    current = top_step(current, top_right[0], top_left[0], top_caps)
    current = top_step(current, top_left[0], top_right[0], top_caps)
    for k in reversed(range(levels)):
        current = level_step(current, lefts[k], rights[k], level_caps[k, 0], k + 1)
    return dot_t(leaf_inverse[0], current.astype(BF))[None]


def in_hbm(value):
    return pltpu.with_memory_space_constraint(value, pltpu.HBM)


def in_vmem(value):
    return pltpu.with_memory_space_constraint(value, pltpu.VMEM)


def call(body, outs, *args, scratch=(), hbm=(), hbm_out=False, micros=1):
    vmem = pl.BlockSpec(memory_space=pltpu.VMEM)
    anywhere = pl.BlockSpec(memory_space=pl.ANY)
    return pl.pallas_call(
        body,
        out_shape=[
            jax.ShapeDtypeStruct(shape, dtype) if hbm_out else pltpu.VMEM(shape, dtype)
            for shape, dtype in outs
        ],
        in_specs=[anywhere if i in hbm else vmem for i in range(len(args))],
        out_specs=[anywhere if hbm_out else vmem] * len(outs),
        scratch_shapes=list(scratch),
        compiler_params=pltpu.CompilerParams(vmem_limit_bytes=VMEM_LIMIT),
        cost_estimate=pl.CostEstimate(
            flops=int(micros * FLOPS_PER_MICRO), bytes_accessed=0, transcendentals=0
        ),
    )(*[in_hbm(a) if i in hbm else in_vmem(a) for i, a in enumerate(args)])


def after(value, *others):
    return lax.optimization_barrier((value, *others))[0]


def side(bit):
    return (lax.axis_index("leaf") >> bit) & 1


def block(index, width):
    return pl.ds(pl.multiple_of(index * width, width), width)


def put_rows(scratch, upper, own, other):
    rows = own.shape[0]
    scratch[block(upper, rows), :] = own
    scratch[block(1 - upper, rows), :] = other


def put_columns(out, upper, own, other):
    width = own.shape[1]
    out[:, block(upper, width)] = own
    out[:, block(1 - upper, width)] = other


def two_levels(
    right_side, leaf_inverse, left_basis, right_basis, level_caps, top_left, top_right, top_caps
):
    rows, cols = right_side.shape[1:]
    rank = top_left.shape[2]
    half = cols // 2
    f32 = jnp.float32
    s1 = 1.0 / math.sqrt(rows)
    s2 = 1.0 / math.sqrt(rows * 2)
    st = 1.0 / math.sqrt(rows * 4)
    blocks = rows // rank
    square, wide, tall = (rank, rank), (rank, cols), (rows, cols)

    def span(i, n=1):
        return slice(i * rank, (i + n) * rank)

    def part(i, n=1):
        return slice(i * half, (i + n) * half)

    def around_top(value):
        far = swap(value, "top", 2)
        return value, swap(value, "top", 1), far, swap(far, "top", 1)

    caps_far = swap(top_caps, "top", 2)

    def start_body(
        rhs_hbm, inv_hbm, lb_hbm, rb_hbm, caps_hbm, tl_hbm, tr_hbm,
        x_ref, p_ref, inv_ref, lb, rb, caps, tl, tr, rhs_v, sems,
    ):
        def load(source, target, *at):
            copy = pltpu.make_async_copy(source, target, sems.at[at])
            copy.start()
            return copy

        copies = []
        for i in range(blocks):
            copies.append(load(rhs_hbm.at[0, span(i), :], rhs_v.at[span(i), :], 0, i))
            copies.append(
                load(
                    inv_hbm.at[0, span(i), span(0, i + 1)],
                    inv_ref.at[span(i), span(0, i + 1)],
                    1,
                    i,
                )
            )
        bases = [
            load(source, target, 2, i)
            for i, (source, target) in enumerate(
                ((rb_hbm, rb), (lb_hbm, lb), (tl_hbm, tl), (tr_hbm, tr), (caps_hbm, caps))
            )
        ]
        for i in range(blocks):
            copies[2 * i].wait()
            copies[2 * i + 1].wait()
            x_ref[span(i), :] = dot(
                inv_ref[span(i), span(0, i + 1)], rhs_v[span(0, i + 1), :].astype(BF)
            )
        bases[0].wait()
        p_ref[...] = (dot_t(rb[0, 0], x_ref[...].astype(BF)) * s1).astype(BF)
        for copy in bases[1:]:
            copy.wait()

    state0, proj1, inverse, lb, rb, caps, tl, tr = call(
        start_body,
        [(tall, f32), (wide, BF), ((rows, rows), BF)]
        + [(a.shape, a.dtype) for a in (left_basis, right_basis, level_caps, top_left, top_right)],
        right_side,
        leaf_inverse,
        left_basis,
        right_basis,
        level_caps,
        top_left,
        top_right,
        hbm=range(7),
        scratch=[pltpu.VMEM(tall, f32), pltpu.SemaphoreType.DMA((3, max(blocks, 5)))],
    )
    proj1_sib = swap(proj1, "leaf", 1)
    caps_near = swap(after(top_caps, proj1), "top", 1)
    caps_parts = top_caps, caps_near, caps_far, swap(after(caps_far, proj1), "top", 1)

    def grams_body(lb, caps, tl, tr, seen, out, send, scratch):
        upper = side(1)
        left2, caps2 = lb[1, 0], caps[1, 0]
        for i, (basis, scale) in enumerate(((tr[0], st), (tl[0], st), (left2, s2))):
            gram = (dot_t(basis, left2) * scale).astype(BF)
            scratch[...] = dot(gram, caps2).astype(BF)
            out[:, span(2 * i, 2)] = scratch[...]
            if i < 2:
                send[:, span(i)] = scratch[:, block(1 - upper, rank)]
        out[:, span(6)] = (dot_t(left2, tl[0]) * s2).astype(BF)
        out[:, span(7)] = (dot_t(left2, tr[0]) * s2).astype(BF)
        out[:, span(8)] = (dot_t(tl[0], tl[0]) * st).astype(BF)
        send[:, span(2)] = out[:, span(8)]

    grams, next_send = call(
        grams_body,
        [((rank, 9 * rank), BF), ((rank, 3 * rank), BF)],
        lb,
        caps,
        tl,
        tr,
        caps_near,
        scratch=[pltpu.VMEM((rank, 2 * rank), BF)],
        micros=10,
    )
    grams_sib = swap(grams, "leaf", 1)
    next_far = swap(next_send, "leaf", 2)

    def one_body(x0, p, p_sib, lb, rb, caps, tl, tr, x1, send, keep, y6, stack, scratch):
        odd = side(0)
        put_rows(stack, odd, p[...], p_sib[...])
        coef = dot(caps[0, 0], stack[...]).astype(BF)
        x1[...] = x0[...] - dot(lb[0, 0], coef)
        state = x1[...].astype(BF)
        bases = ((rb[1, 0], s2), (tr[0], st), (tl[0], st), (lb[1, 0], s2))
        for i, (basis, scale) in enumerate(bases):
            scratch[...] = dot_t(basis, state) * scale
            send[:, part(i)] = scratch[:, block(1 - odd, half)].astype(BF)
            keep[:, part(i)] = scratch[:, block(odd, half)]
        y6[...] = (dot_t(lb[0, 0], state) * s1).astype(BF)

    state1, pair_send, pair_keep, down6 = call(
        one_body,
        [(tall, f32), ((rank, 4 * half), BF), ((rank, 4 * half), f32), (wide, BF)],
        state0,
        proj1,
        proj1_sib,
        lb,
        rb,
        caps,
        tl,
        tr,
        scratch=[pltpu.VMEM((2 * rank, cols), BF), pltpu.VMEM(wide, f32)],
        micros=3,
    )
    pair_in = swap(pair_send, "leaf", 1)
    next_far_sib = swap(after(next_far, state1), "leaf", 1)

    def pair_body(own, sib, keep, gram, late, scratch):
        upper = side(1)
        for i in range(2):
            scratch[...] = (own[:, span(2 * i, 2)].astype(f32) + sib[:, span(2 * i, 2)]).astype(BF)
            keep[:, span(2 * i)] = scratch[:, block(upper, rank)]
            keep[:, span(2 * i + 1)] = scratch[:, block(1 - upper, rank)]
        late[...] = (own[:, span(4, 4)].astype(f32) + sib[:, span(4, 4)]).astype(BF)
        gram[...] = own[:, span(8)].astype(f32) + sib[:, span(8)]

    next_keep, gram_pair, gram5 = call(
        pair_body,
        [((rank, 4 * rank), BF), (square, f32), ((rank, 4 * rank), BF)],
        grams,
        grams_sib,
        scratch=[pltpu.VMEM((rank, 2 * rank), BF)],
    )

    def order_body(a, b, c, d, out):
        here = lax.axis_index("top")
        for i, piece in enumerate((a, b, c, d)):
            for k in range(4):
                out[span(i), span(k)] = piece[:, block(here ^ k, rank)]

    (caps_all,) = call(order_body, [((4 * rank, 4 * rank), BF)], *caps_parts)

    def half_body(keep, pair, nexts, seen, send, keep2):
        keep2[...] = keep[...] + pair[...]
        own = keep2[:, part(0)].astype(BF)
        for i in range(2):
            keep2[:, part(1 + i)] = keep2[:, part(1 + i)] - dot(nexts[:, span(2 * i)], own)
        send[...] = keep2[...].astype(BF)

    cross_send, cross_keep = call(
        half_body,
        [((rank, 4 * half), BF), ((rank, 4 * half), f32)],
        pair_keep,
        pair_in,
        next_keep,
        caps_all,
    )
    cross_in = swap(cross_send, "leaf", 2)
    gram5_far = swap(after(gram5, cross_send), "leaf", 2)

    def late_body(lb, rb, caps, tl, tr, y6, seen, out):
        left1 = lb[0, 0]
        for i, basis in enumerate((lb[1, 0], rb[1, 0])):
            gram = (dot_t(left1, basis) * s1).astype(BF)
            out[:, span(2 * i, 2)] = dot(gram, caps[1, 0]).astype(BF)
        for i, basis in enumerate((tl, tr)):
            out[:, span(4 + i)] = (dot_t(left1, basis[0]) * s1).astype(BF)
        out[:, 6 * rank :] = y6[...]

    (late,) = call(
        late_body, [((rank, 6 * rank + cols), BF)], lb, rb, caps, tl, tr, down6, cross_send
    )

    def column_body(send, keep2, far, nexts, nexts_far, nexts_far_sib, gram, top, halves, total):
        own, other = send[:, part(0)], far[:, part(0)]
        total[...] = nexts_far[...].astype(f32) + nexts_far_sib[...]
        for i in range(2):
            top[:, part(i)] = (
                keep2[:, part(1 + i)]
                + far[:, part(1 + i)]
                - dot(nexts[:, span(2 * i + 1)], other)
                - dot(total[:, span(i)].astype(BF), own)
            ).astype(BF)
        top[:, 2 * half :] = (gram[...] + total[:, span(2)]).astype(BF)
        halves[:, part(0)] = own
        halves[:, part(1)] = other

    top_send, halves_send = call(
        column_body,
        [((rank, 2 * half + rank), BF), (wide, BF)],
        cross_send,
        cross_keep,
        cross_in,
        next_keep,
        next_far,
        next_far_sib,
        gram_pair,
        scratch=[pltpu.VMEM((rank, 3 * rank), f32)],
    )
    top_parts = around_top(top_send)
    halves_in = swap(halves_send, "leaf", 1)
    late_sib = swap(after(late, top_send, halves_in), "leaf", 1)

    def two_body(x1, own, sib, lb, rb, caps, tl, tr, inv, out2, under, both, mine, x2):
        odd, high = side(0), side(1)
        for i in range(2):
            put_columns(mine.at[span(i), :], odd, own[:, part(i)], sib[:, part(i)])
        put_rows(both, high, mine[span(0), :], mine[span(1), :])
        coef = dot(caps[1, 0], both[...]).astype(BF)
        x2[...] = (x1[...] - dot(lb[1, 0], coef)).astype(BF)
        for c in range(blocks):
            column = inv[c * rank :, span(c)]
            out2[span(c), :] = dot_t(column, x2[c * rank :, :])
            for i, basis in enumerate((tl[0], tr[0], rb[1, 0], rb[0, 0])):
                under[span(c), span(i)] = dot_t(column, basis[c * rank :, :]).astype(BF)

    out2, under, stack2 = call(
        two_body,
        [(tall, f32), ((rows, 4 * rank), BF), ((2 * rank, cols), BF)],
        state1,
        halves_send,
        halves_in,
        lb,
        rb,
        caps,
        tl,
        tr,
        inverse,
        scratch=[pltpu.VMEM((2 * rank, cols), BF), pltpu.VMEM(tall, BF)],
    )

    def top_body(
        a, b, c, d, caps, send, keep2, far, gram5, gram5_far, seen, out, up, down, both
    ):
        pieces = (a, b, c, d)
        for i, piece in enumerate(pieces):
            up[span(i), :] = piece[:, part(0)]
        coef = dot(caps[...], up[...]).astype(BF)
        for i, piece in enumerate(pieces):
            down[span(i), :] = (
                piece[:, part(1)] - dot(piece[:, 2 * half :], coef[span(i), :])
            ).astype(BF)
        out[:, part(0)] = coef[:rank, :]
        out[:, part(1)] = dot(caps[:rank, :], down[...]).astype(BF)
        put_rows(both.at[: 2 * rank, :], side(1), send[:, part(0)], far[:, part(0)])
        both[span(2), :] = out[:, part(0)]
        both[span(3), :] = out[:, part(1)]
        out[:, part(2)] = (keep2[:, part(3)] - dot(gram5[...], both[...])).astype(BF)
        out[:, part(3)] = (far[:, part(3)] - dot(gram5_far[...], both[...])).astype(BF)

    (back_send,) = call(
        top_body,
        [((rank, 4 * half), BF)],
        *top_parts,
        caps_all,
        cross_send,
        cross_keep,
        cross_in,
        gram5,
        gram5_far,
        out2,
        scratch=[pltpu.VMEM((4 * rank, half), BF)] * 3,
    )
    back_in = swap(back_send, "leaf", 1)

    def last_body(
        out2, under, stack2, back, back_sib, late, late_sib, caps, out,
        mine, coefs, proj, out_v, sems,
    ):
        odd, high = side(0), side(1)
        for i in range(2):
            put_columns(coefs.at[span(i), :], odd, back[:, part(i)], back_sib[:, part(i)])
            put_columns(mine.at[span(i), :], odd, back[:, part(2 + i)], back_sib[:, part(2 + i)])
        put_rows(proj, high, mine[span(0), :], mine[span(1), :])
        stack5 = proj[...]
        coefs[span(2), :] = dot(caps[1, 0], stack5).astype(BF)

        def down(grams):
            return (
                grams[:, 6 * rank :]
                - dot(grams[:, span(0, 2)], stack2[...])
                - dot(grams[:, span(2, 2)], stack5)
                - dot(grams[:, span(4, 2)], coefs[span(0, 2), :])
            ).astype(BF)

        put_rows(proj, odd, down(late), down(late_sib))
        coefs[span(3), :] = dot(caps[0, 0], proj[...]).astype(BF)
        copies = []
        for c in range(blocks):
            out_v[span(c), :] = out2[span(c), :] - dot(under[span(c), :], coefs[...])
            copy = pltpu.make_async_copy(out_v.at[span(c), :], out.at[0, span(c), :], sems.at[c])
            copy.start()
            copies.append(copy)
        for copy in copies:
            copy.wait()

    (out,) = call(
        last_body,
        [((1, rows, cols), f32)],
        out2,
        under,
        stack2,
        back_send,
        back_in,
        late,
        late_sib,
        caps,
        hbm_out=True,
        scratch=[
            pltpu.VMEM((2 * rank, cols), BF),
            pltpu.VMEM((4 * rank, cols), BF),
            pltpu.VMEM((2 * rank, cols), BF),
            pltpu.VMEM(tall, f32),
            pltpu.SemaphoreType.DMA((blocks,)),
        ],
    )
    return out


def on_device(*args):
    levels = args[2].shape[0]
    sizes = lax.axis_size("leaf"), lax.axis_size("top")
    if levels == 2 and sizes == (4, 4):
        return two_levels(*args)
    return step_by_step(*args)


def solution(mesh):
    rows = P(("parts", "top"), "leaf", None)
    level_rows = P(None, ("parts", "top"), "leaf", None)
    return jax.shard_map(
        on_device,
        mesh=mesh,
        in_specs=(
            rows,
            rows,
            level_rows,
            level_rows,
            level_rows,
            rows,
            rows,
            P(("parts", "top"), None),
        ),
        out_specs=rows,
        check_vma=False,
    )
```

time: 93.6 us -> 49.1 us (0.52)
  blocking collectives: 52.4 us -> 0 us
  Pallas kernels: 0 us -> 9.27 us
  starting transfers between devices: 9.21 us -> 16.6 us
  matrix products: 6.72 us -> 0 us
  local copies, waits for them, and re-layouts: 2.27 us -> 0.01 us
    psum x2 -> x0, blocking collectives: 40.5 us -> none  [top_update(): column_total = lax.psum(partial_value, 'leaf')]
    all_gather x2 -> x0, blocking collectives: 11.9 us -> none  [top_update(): lax.all_gather(column_total.astype(jnp.bfloat16), 'top', axis=0, tiled=True)]
    pallas_call x0 -> x11, Pallas kernels: none -> 9.27 us  [call(): pl.pallas_call(body, out_shape=[jax.ShapeDtypeStruct(shape, dtype) if hbm...]
    ppermute x6 -> x16, starting transfers between devices: 9.21 us -> 16.6 us  [swap(): return lax.ppermute(value, axis, pairs)]
    dot_general x14 -> x0, matrix products: 6.72 us -> none  [the longest x7 2.41 us: project_rows(): lax.dot_general(basis, current.astype(jnp.bfloat16), (((0,), (0,)), ((),...]
    unnamed x20 -> x2, local copies, waits for them, and re-layouts: 1.19 us -> 0.01 us
    broadcast_in_dim x1 -> x0, local copies, waits for them, and re-layouts: 1.07 us -> none  [on_device(): return current[None]]
    ppermute x6 -> x16, waiting for transfers between devices: 22.5 us -> 22.9 us  [swap(): return lax.ppermute(value, axis, pairs)]
  transfers between devices with their start and end apart: 6 -> 16, of which waited for: 6 -> 7; matrix products, arithmetic and copies ran while one was open for 0% -> 0% of each run, Pallas kernels for 0% -> 10%
where the time goes in v4:
time: 49.1 us; the launch traced here: 48.9 us
  waiting for transfers between devices  22.9 us (47%)
  starting transfers between devices  16.6 us (34%)
  Pallas kernels  9.27 us (19%)
    ppermute x16, waiting for transfers between devices, swap(): return lax.ppermute(value, axis, pairs)  22.9 us
    ppermute x16, starting transfers between devices, swap(): return lax.ppermute(value, axis, pairs)  16.6 us
    pallas_call x11, Pallas kernels, call(): pl.pallas_call(body, out_shape=[jax.ShapeDtypeStruct(shape, dtype) if hbm...  9.27 us
  transfers between devices with their start and end apart: 16, of which 7 were waited for; matrix products, arithmetic and copies ran while one was open for 0% of the time, Pallas kernels for 10%

profile of v4, /device:TPU:0, one launch (start us, length us, event | category | flops | bytes accessed | tf_op | source)
XLA Modules:
  0.0 48.9 jit_solution(988085595275879511)
XLA Ops:
  0.0 2.4 %shard_map.82 = (f32[640,256]{1,0:T(8,128)S(1)}, bf16[128,256]{1,0:T(8,128)(2,1)S(1)}, bf16[640,640]{1,0:T(8,128)(2,1)S(1)}, bf16[2,1,640,128]{3,2,1,0:T(8,128)(...) custom-call(f32[1,640,256]{2,1,0:T(8,128)} %rhs_hbm.1, ...), custom_call_target="tpu_custom_call" | custom-call | flops 1000000000 | tf_op jit(solution)/shard_map/pallas_call | solution.py:88
  2.4 0.5 %collective-permute-start.2 = (bf16[128,512]{1,0:T(8,128)(2,1)S(1)}, bf16[128,512]{1,0:T(8,128)(2,1)S(1)}, u32[]{:S(2)}, u32[]{:S(2)}) collective-permute-start(bf16[128,512]{1,0:T(8,128)(2,1)S(1)} %copy-done), channel_id=1, source_target_pairs={{0,1},{1,0},{2,3},{3,2},{4,5},{5,4},{6,7},{7,6},{8,9},{9,8},{10,11... | collective-permute-start | bytes 393224 | tf_op jit(solution)/shard_map/ppermute | solution.py:17
  2.9 2.6 %collective-permute-start = (bf16[128,256]{1,0:T(8,128)(2,1)S(1)}, bf16[128,256]{1,0:T(8,128)(2,1)S(1)}, u32[]{:S(2)}, u32[]{:S(2)}) collective-permute-start(bf16[128,256]{1,0:T(8,128)(2,1)S(1)} %get-tuple-element.35.p), channel_id=1, source_target_pairs={{0,4},{4,0},{8,12},{12,8},{1,5},{5,1},{9,13},{13,9},{2,6},{6,2},{1... | collective-permute-start | bytes 196616 | tf_op jit(solution)/shard_map/ppermute | solution.py:17
  5.6 1.5 %collective-permute-start.4 = (bf16[128,512]{1,0:T(8,128)(2,1)S(1)}, bf16[128,512]{1,0:T(8,128)(2,1)S(1)}, u32[]{:S(2)}, u32[]{:S(2)}) collective-permute-start(bf16[128,512]{1,0:T(8,128)(2,1)S(1)} %copy-done), channel_id=1, source_target_pairs={{0,2},{1,3},{2,0},{3,1},{4,6},{5,7},{6,4},{7,5},{8,10},{9,11},{10,... | collective-permute-start | bytes 393224 | tf_op jit(solution)/shard_map/ppermute | solution.py:17
  7.1 0.9 %shard_map.84 = (bf16[128,1152]{1,0:T(8,128)(2,1)S(1)}, bf16[128,384]{1,0:T(8,128)(2,1)S(1)}) custom-call(bf16[2,1,640,128]{3,2,1,0:T(8,128)(2,1)S(1)} %get-tuple-element.36.lb, bf16[2,1,128,256]{3,2,1,0:T(8,128)(2,1)S(1)} %get-tuple-element.38.caps, bf16[1,640,128]{2,1,0:T(8,128)(2,1)S(1)} %get-tuple-element.39.tl, ...), custom_call_target="tpu_custom_call" | custom-call | flops 10000000000 | tf_op jit(solution)/shard_map/pallas_call | solution.py:88
  8.0 0.5 %collective-permute-start.3 = (bf16[128,1152]{1,0:T(8,128)(2,1)S(1)}, bf16[128,1152]{1,0:T(8,128)(2,1)S(1)}, u32[]{:S(2)}, u32[]{:S(2)}) collective-permute-start(bf16[128,1152]{1,0:T(8,128)(2,1)S(1)} %get-tuple-element.45.own), channel_id=1, source_target_pairs={{0,4},{4,0},{8,12},{12,8},{1,5},{5,1},{9,13},{13,9},{2,6},{6,2},{1... | collective-permute-start | bytes 884744 | tf_op jit(solution)/shard_map/ppermute | solution.py:17
  8.5 2.6 %collective-permute-done.4.c = bf16[128,512]{1,0:T(8,128)(2,1)S(1)} collective-permute-done((bf16[128,512]{1,0:T(8,128)(2,1)S(1)}, bf16[128,512]{1,0:T(8,128)(2,1)S(1)}, u32[]{:S(2)}, u32[]{:S(2)}) %collective-permute-start.4) | collective-permute-done | bytes 131104 | tf_op jit(solution)/shard_map/ppermute | solution.py:17
  11.2 1.0 %shard_map.83 = (f32[640,256]{1,0:T(8,128)S(1)}, bf16[128,512]{1,0:T(8,128)(2,1)S(1)}, f32[128,512]{1,0:T(8,128)S(1)}, bf16[128,256]{1,0:T(8,128)(2,1)S(1)}) custom-call(f32[640,256]{1,0:T(8,128)S(1)} %get-tuple-element.34.x0, bf16[128,256]{1,0:T(8,128)(2,1)S(1)} %get-tuple-element.35.p, bf16[128,256]{1,0:T(8,128)(2,1)S(1)} %collective-permute-done.p_sib, ...), custom_call_target="tpu_custom_call" | custom-call | flops 3000000000 | tf_op jit(solution)/shard_map/pallas_call | solution.py:88
  12.5 2.8 %collective-permute-start.7 = (bf16[128,384]{1,0:T(8,128)(2,1)S(1)}, bf16[128,384]{1,0:T(8,128)(2,1)S(1)}, u32[]{:S(2)}, u32[]{:S(2)}) collective-permute-start(bf16[128,384]{1,0:T(8,128)(2,1)S(1)} %get-tuple-element.50), channel_id=1, source_target_pairs={{0,8},{4,12},{8,0},{12,4},{1,9},{5,13},{9,1},{13,5},{2,10},{6,14},... | collective-permute-start | bytes 294920 | tf_op jit(solution)/shard_map/ppermute | solution.py:17
  15.3 4.7 %collective-permute-done.3.sib = bf16[128,1152]{1,0:T(8,128)(2,1)S(1)} collective-permute-done((bf16[128,1152]{1,0:T(8,128)(2,1)S(1)}, bf16[128,1152]{1,0:T(8,128)(2,1)S(1)}, u32[]{:S(2)}, u32[]{:S(2)}) %collective-permute-start.3) | collective-permute-done | bytes 294944 | tf_op jit(solution)/shard_map/ppermute | solution.py:17
  20.1 1.6 %collective-permute-done.1.pair = bf16[128,512]{1,0:T(8,128)(2,1)S(1)} collective-permute-done((bf16[128,512]{1,0:T(8,128)(2,1)S(1)}, bf16[128,512]{1,0:T(8,128)(2,1)S(1)}, u32[]{:S(2)}, u32[]{:S(2)}) %collective-permute-start.1) | collective-permute-done | bytes 131104 | tf_op jit(solution)/shard_map/ppermute | solution.py:17
  21.9 1.6 %collective-permute-start.6 = (bf16[128,512]{1,0:T(8,128)(2,1)S(1)}, bf16[128,512]{1,0:T(8,128)(2,1)S(1)}, u32[]{:S(2)}, u32[]{:S(2)}) collective-permute-start(bf16[128,512]{1,0:T(8,128)(2,1)S(1)} %get-tuple-element.48.send.seen), channel_id=1, source_target_pairs={{0,8},{4,12},{8,0},{12,4},{1,9},{5,13},{9,1},{13,5},{2,10},{6,14},... | collective-permute-start | bytes 393224 | tf_op jit(solution)/shard_map/ppermute | solution.py:17
  23.5 1.4 %collective-permute-start.8 = (bf16[128,384]{1,0:T(8,128)(2,1)S(1)}, bf16[128,384]{1,0:T(8,128)(2,1)S(1)}, u32[]{:S(2)}, u32[]{:S(2)}) collective-permute-start(bf16[128,384]{1,0:T(8,128)(2,1)S(1)} %collective-permute-done.7.nexts_far), channel_id=1, source_target_pairs={{0,4},{4,0},{8,12},{12,8},{1,5},{5,1},{9,13},{13,9},{2,6},{6,2},{1... | collective-permute-start | bytes 294920 | tf_op jit(solution)/shard_map/ppermute | solution.py:17
  25.0 5.0 %collective-permute-done.8.nexts_far_sib = bf16[128,384]{1,0:T(8,128)(2,1)S(1)} collective-permute-done((bf16[128,384]{1,0:T(8,128)(2,1)S(1)}, bf16[128,384]{1,0:T(8,128)(2,1)S(1)}, u32[]{:S(2)}, u32[]{:S(2)}) %collective-permute-start.8) | collective-permute-done | bytes 98336 | tf_op jit(solution)/shard_map/ppermute | solution.py:17
  30.2 0.9 %collective-permute-start.11 = (bf16[128,384]{1,0:T(8,128)(2,1)S(1)}, bf16[128,384]{1,0:T(8,128)(2,1)S(1)}, u32[]{:S(2)}, u32[]{:S(2)}) collective-permute-start(bf16[128,384]{1,0:T(8,128)(2,1)S(1)} %get-tuple-element.58.a), channel_id=1, source_target_pairs={{0,2},{1,3},{2,0},{3,1},{4,6},{5,7},{6,4},{7,5},{8,10},{9,11},{10,... | collective-permute-start | bytes 294920 | tf_op jit(solution)/shard_map/ppermute | solution.py:17
  31.1 2.3 %collective-permute-start.9 = (bf16[128,256]{1,0:T(8,128)(2,1)S(1)}, bf16[128,256]{1,0:T(8,128)(2,1)S(1)}, u32[]{:S(2)}, u32[]{:S(2)}) collective-permute-start(bf16[128,256]{1,0:T(8,128)(2,1)S(1)} %get-tuple-element.53.own), channel_id=1, source_target_pairs={{0,4},{4,0},{8,12},{12,8},{1,5},{5,1},{9,13},{13,9},{2,6},{6,2},{1... | collective-permute-start | bytes 196616 | tf_op jit(solution)/shard_map/ppermute | solution.py:17
  33.4 1.5 %collective-permute-done.11.c = bf16[128,384]{1,0:T(8,128)(2,1)S(1)} collective-permute-done((bf16[128,384]{1,0:T(8,128)(2,1)S(1)}, bf16[128,384]{1,0:T(8,128)(2,1)S(1)}, u32[]{:S(2)}, u32[]{:S(2)}) %collective-permute-start.11) | collective-permute-done | bytes 98336 | tf_op jit(solution)/shard_map/ppermute | solution.py:17
  34.9 0.6 %shard_map.91.late = bf16[128,1024]{1,0:T(8,128)(2,1)S(1)} custom-call(bf16[2,1,640,128]{3,2,1,0:T(8,128)(2,1)S(1)} %get-tuple-element.36.lb, bf16[2,1,640,128]{3,2,1,0:T(8,128)(2,1)S(1)} %get-tuple-element.37.rb, bf16[2,1,128,256]{3,2,1,0:T(8,128)(2,1)S(1)} %get-tuple-element.38.caps, bf16[1,640,128]{2,1,0:T(8,128)(2,1)S(1)} %get-tuple-element.39.tl, ...), custom_call_target="tpu_custom_call" | custom-call | flops 1000000000 | tf_op jit(solution)/shard_map/pallas_call | solution.py:88
  35.5 0.8 %collective-permute-done.9.sib = bf16[128,256]{1,0:T(8,128)(2,1)S(1)} collective-permute-done((bf16[128,256]{1,0:T(8,128)(2,1)S(1)}, bf16[128,256]{1,0:T(8,128)(2,1)S(1)}, u32[]{:S(2)}, u32[]{:S(2)}) %collective-permute-start.9) | collective-permute-done | bytes 65568 | tf_op jit(solution)/shard_map/ppermute | solution.py:17
  36.3 1.7 %collective-permute-start.15 = (bf16[128,1024]{1,0:T(8,128)(2,1)S(1)}, bf16[128,1024]{1,0:T(8,128)(2,1)S(1)}, u32[]{:S(2)}, u32[]{:S(2)}) collective-permute-start(bf16[128,1024]{1,0:T(8,128)(2,1)S(1)} %shard_map.91.late), channel_id=1, source_target_pairs={{0,4},{4,0},{8,12},{12,8},{1,5},{5,1},{9,13},{13,9},{2,6},{6,2},{1... | collective-permute-start | bytes 786440 | tf_op jit(solution)/shard_map/ppermute | solution.py:17
  38.0 1.3 %shard_map.89 = (f32[640,256]{1,0:T(8,128)S(1)}, bf16[640,512]{1,0:T(8,128)(2,1)S(1)}, bf16[256,256]{1,0:T(8,128)(2,1)S(1)}) custom-call(f32[640,256]{1,0:T(8,128)S(1)} %get-tuple-element.41.x1, bf16[128,256]{1,0:T(8,128)(2,1)S(1)} %get-tuple-element.53.own, bf16[128,256]{1,0:T(8,128)(2,1)S(1)} %collective-permute-done.9.sib, ...), custom_call_target="tpu_custom_call" | custom-call | flops 1000000000 | tf_op jit(solution)/shard_map/pallas_call | solution.py:88
  39.3 1.0 %shard_map.90.back = bf16[128,512]{1,0:T(8,128)(2,1)S(1)} custom-call(bf16[128,384]{1,0:T(8,128)(2,1)S(1)} %get-tuple-element.58.a, bf16[128,384]{1,0:T(8,128)(2,1)S(1)} %collective-permute-done.10.b, bf16[128,384]{1,0:T(8,128)(2,1)S(1)} %collective-permute-done.11.c, bf16[128,384]{1,0:T(8,128)(2,1)S(1)} %collective-permute-done.12.d, ...), custom_call_target="tpu_custom_call" | custom-call | flops 1000000000 | tf_op jit(solution)/shard_map/pallas_call | solution.py:88
  40.7 6.6 %collective-permute-done.14.back_sib = bf16[128,512]{1,0:T(8,128)(2,1)S(1)} collective-permute-done((bf16[128,512]{1,0:T(8,128)(2,1)S(1)}, bf16[128,512]{1,0:T(8,128)(2,1)S(1)}, u32[]{:S(2)}, u32[]{:S(2)}) %collective-permute-start.14) | collective-permute-done | bytes 131104 | tf_op jit(solution)/shard_map/ppermute | solution.py:17
  47.3 1.6 %shard_map.92 = f32[1,640,256]{2,1,0:T(8,128)} custom-call(f32[640,256]{1,0:T(8,128)S(1)} %get-tuple-element.55.seen.out2, bf16[640,512]{1,0:T(8,128)(2,1)S(1)} %get-tuple-element.56.under, bf16[256,256]{1,0:T(8,128)(2,1)S(1)} %get-tuple-element.57.stack2, bf16[128,512]{1,0:T(8,128)(2,1)S(1)} %shard_map.90.back, ...), custom_call_target="tpu_custom_call" | custom-call | flops 1000000000 | tf_op jit(solution)/shard_map/pallas_call | solution.py:88
  (21 shorter events, 1.3 us)
Async XLA Ops:
  0.0 2.4 %copy-start = (bf16[128,512]{1,0:T(8,128)(2,1)S(1)}, bf16[128,512]{1,0:T(8,128)(2,1)}, u32[]{:S(2)}) copy-start(bf16[128,512]{1,0:T(8,128)(2,1)} %a.1) | copy-start | bytes 393220
  2.4 4.7 %collective-permute-start.2 = (bf16[128,512]{1,0:T(8,128)(2,1)S(1)}, bf16[128,512]{1,0:T(8,128)(2,1)S(1)}, u32[]{:S(2)}, u32[]{:S(2)}) collective-permute-start(bf16[128,512]{1,0:T(8,128)(2,1)S(1)} %copy-done), channel_id=1, source_target_pairs={{0,1},{1,0},{2,3},{3,2},{4,5},{5,4},{6,7},{7,6},{8,9},{9,8},{10,11... | collective-permute-start | bytes 393224 | tf_op jit(solution)/shard_map/ppermute | solution.py:17
  2.9 8.2 %collective-permute-start = (bf16[128,256]{1,0:T(8,128)(2,1)S(1)}, bf16[128,256]{1,0:T(8,128)(2,1)S(1)}, u32[]{:S(2)}, u32[]{:S(2)}) collective-permute-start(bf16[128,256]{1,0:T(8,128)(2,1)S(1)} %get-tuple-element.35.p), channel_id=1, source_target_pairs={{0,4},{4,0},{8,12},{12,8},{1,5},{5,1},{9,13},{13,9},{2,6},{6,2},{1... | collective-permute-start | bytes 196616 | tf_op jit(solution)/shard_map/ppermute | solution.py:17
  5.6 5.6 %collective-permute-start.4 = (bf16[128,512]{1,0:T(8,128)(2,1)S(1)}, bf16[128,512]{1,0:T(8,128)(2,1)S(1)}, u32[]{:S(2)}, u32[]{:S(2)}) collective-permute-start(bf16[128,512]{1,0:T(8,128)(2,1)S(1)} %copy-done), channel_id=1, source_target_pairs={{0,2},{1,3},{2,0},{3,1},{4,6},{5,7},{6,4},{7,5},{8,10},{9,11},{10,... | collective-permute-start | bytes 393224 | tf_op jit(solution)/shard_map/ppermute | solution.py:17
  8.0 12.1 %collective-permute-start.3 = (bf16[128,1152]{1,0:T(8,128)(2,1)S(1)}, bf16[128,1152]{1,0:T(8,128)(2,1)S(1)}, u32[]{:S(2)}, u32[]{:S(2)}) collective-permute-start(bf16[128,1152]{1,0:T(8,128)(2,1)S(1)} %get-tuple-element.45.own), channel_id=1, source_target_pairs={{0,4},{4,0},{8,12},{12,8},{1,5},{5,1},{9,13},{13,9},{2,6},{6,2},{1... | collective-permute-start | bytes 884744 | tf_op jit(solution)/shard_map/ppermute | solution.py:17
  11.2 4.1 %collective-permute-start.5 = (bf16[128,512]{1,0:T(8,128)(2,1)S(1)}, bf16[128,512]{1,0:T(8,128)(2,1)S(1)}, u32[]{:S(2)}, u32[]{:S(2)}) collective-permute-start(bf16[128,512]{1,0:T(8,128)(2,1)S(1)} %collective-permute-done.4.c), channel_id=1, source_target_pairs={{0,1},{1,0},{2,3},{3,2},{4,5},{5,4},{6,7},{7,6},{8,9},{9,8},{10,11... | collective-permute-start | bytes 393224 | tf_op jit(solution)/shard_map/ppermute | solution.py:17
  12.1 9.6 %collective-permute-start.1 = (bf16[128,512]{1,0:T(8,128)(2,1)S(1)}, bf16[128,512]{1,0:T(8,128)(2,1)S(1)}, u32[]{:S(2)}, u32[]{:S(2)}) collective-permute-start(bf16[128,512]{1,0:T(8,128)(2,1)S(1)} %get-tuple-element.43), channel_id=1, source_target_pairs={{0,4},{4,0},{8,12},{12,8},{1,5},{5,1},{9,13},{13,9},{2,6},{6,2},{1... | collective-permute-start | bytes 393224 | tf_op jit(solution)/shard_map/ppermute | solution.py:17
  12.5 11.1 %collective-permute-start.7 = (bf16[128,384]{1,0:T(8,128)(2,1)S(1)}, bf16[128,384]{1,0:T(8,128)(2,1)S(1)}, u32[]{:S(2)}, u32[]{:S(2)}) collective-permute-start(bf16[128,384]{1,0:T(8,128)(2,1)S(1)} %get-tuple-element.50), channel_id=1, source_target_pairs={{0,8},{4,12},{8,0},{12,4},{1,9},{5,13},{9,1},{13,5},{2,10},{6,14},... | collective-permute-start | bytes 294920 | tf_op jit(solution)/shard_map/ppermute | solution.py:17
  21.9 8.1 %collective-permute-start.6 = (bf16[128,512]{1,0:T(8,128)(2,1)S(1)}, bf16[128,512]{1,0:T(8,128)(2,1)S(1)}, u32[]{:S(2)}, u32[]{:S(2)}) collective-permute-start(bf16[128,512]{1,0:T(8,128)(2,1)S(1)} %get-tuple-element.48.send.seen), channel_id=1, source_target_pairs={{0,8},{4,12},{8,0},{12,4},{1,9},{5,13},{9,1},{13,5},{2,10},{6,14},... | collective-permute-start | bytes 393224 | tf_op jit(solution)/shard_map/ppermute | solution.py:17
  23.5 6.5 %collective-permute-start.8 = (bf16[128,384]{1,0:T(8,128)(2,1)S(1)}, bf16[128,384]{1,0:T(8,128)(2,1)S(1)}, u32[]{:S(2)}, u32[]{:S(2)}) collective-permute-start(bf16[128,384]{1,0:T(8,128)(2,1)S(1)} %collective-permute-done.7.nexts_far), channel_id=1, source_target_pairs={{0,4},{4,0},{8,12},{12,8},{1,5},{5,1},{9,13},{13,9},{2,6},{6,2},{1... | collective-permute-start | bytes 294920 | tf_op jit(solution)/shard_map/ppermute | solution.py:17
  30.2 4.7 %collective-permute-start.11 = (bf16[128,384]{1,0:T(8,128)(2,1)S(1)}, bf16[128,384]{1,0:T(8,128)(2,1)S(1)}, u32[]{:S(2)}, u32[]{:S(2)}) collective-permute-start(bf16[128,384]{1,0:T(8,128)(2,1)S(1)} %get-tuple-element.58.a), channel_id=1, source_target_pairs={{0,2},{1,3},{2,0},{3,1},{4,6},{5,7},{6,4},{7,5},{8,10},{9,11},{10,... | collective-permute-start | bytes 294920 | tf_op jit(solution)/shard_map/ppermute | solution.py:17
  31.1 8.2 %collective-permute-start.13 = (bf16[128,512]{1,0:T(8,128)(2,1)S(1)}, bf16[128,512]{1,0:T(8,128)(2,1)S(1)}, u32[]{:S(2)}, u32[]{:S(2)}) collective-permute-start(bf16[128,512]{1,0:T(8,128)(2,1)S(1)} %get-tuple-element.60.gram5), channel_id=1, source_target_pairs={{0,8},{4,12},{8,0},{12,4},{1,9},{5,13},{9,1},{13,5},{2,10},{6,14},... | collective-permute-start | bytes 393224 | tf_op jit(solution)/shard_map/ppermute | solution.py:17
  31.1 8.2 %collective-permute-start.10 = (bf16[128,384]{1,0:T(8,128)(2,1)S(1)}, bf16[128,384]{1,0:T(8,128)(2,1)S(1)}, u32[]{:S(2)}, u32[]{:S(2)}) collective-permute-start(bf16[128,384]{1,0:T(8,128)(2,1)S(1)} %get-tuple-element.58.a), channel_id=1, source_target_pairs={{0,1},{1,0},{2,3},{3,2},{4,5},{5,4},{6,7},{7,6},{8,9},{9,8},{10,11... | collective-permute-start | bytes 294920 | tf_op jit(solution)/shard_map/ppermute | solution.py:17
  31.1 5.2 %collective-permute-start.9 = (bf16[128,256]{1,0:T(8,128)(2,1)S(1)}, bf16[128,256]{1,0:T(8,128)(2,1)S(1)}, u32[]{:S(2)}, u32[]{:S(2)}) collective-permute-start(bf16[128,256]{1,0:T(8,128)(2,1)S(1)} %get-tuple-element.53.own), channel_id=1, source_target_pairs={{0,4},{4,0},{8,12},{12,8},{1,5},{5,1},{9,13},{13,9},{2,6},{6,2},{1... | collective-permute-start | bytes 196616 | tf_op jit(solution)/shard_map/ppermute | solution.py:17
  34.9 4.4 %collective-permute-start.12 = (bf16[128,384]{1,0:T(8,128)(2,1)S(1)}, bf16[128,384]{1,0:T(8,128)(2,1)S(1)}, u32[]{:S(2)}, u32[]{:S(2)}) collective-permute-start(bf16[128,384]{1,0:T(8,128)(2,1)S(1)} %collective-permute-done.11.c), channel_id=1, source_target_pairs={{0,1},{1,0},{2,3},{3,2},{4,5},{5,4},{6,7},{7,6},{8,9},{9,8},{10,11... | collective-permute-start | bytes 294920 | tf_op jit(solution)/shard_map/ppermute | solution.py:17
  36.3 11.0 %collective-permute-start.15 = (bf16[128,1024]{1,0:T(8,128)(2,1)S(1)}, bf16[128,1024]{1,0:T(8,128)(2,1)S(1)}, u32[]{:S(2)}, u32[]{:S(2)}) collective-permute-start(bf16[128,1024]{1,0:T(8,128)(2,1)S(1)} %shard_map.91.late), channel_id=1, source_target_pairs={{0,4},{4,0},{8,12},{12,8},{1,5},{5,1},{9,13},{13,9},{2,6},{6,2},{1... | collective-permute-start | bytes 786440 | tf_op jit(solution)/shard_map/ppermute | solution.py:17
  40.3 7.0 %collective-permute-start.14 = (bf16[128,512]{1,0:T(8,128)(2,1)S(1)}, bf16[128,512]{1,0:T(8,128)(2,1)S(1)}, u32[]{:S(2)}, u32[]{:S(2)}) collective-permute-start(bf16[128,512]{1,0:T(8,128)(2,1)S(1)} %shard_map.90.back), channel_id=1, source_target_pairs={{0,4},{4,0},{8,12},{12,8},{1,5},{5,1},{9,13},{13,9},{2,6},{6,2},{1... | collective-permute-start | bytes 393224 | tf_op jit(solution)/shard_map/ppermute | solution.py:17

commit v5 on v4

v5 whole, which is shorter than its diff:
```python
import math

import jax
import jax.numpy as jnp
from jax import lax
from jax.experimental import pallas as pl
from jax.experimental.pallas import tpu as pltpu
from jax.sharding import PartitionSpec as P

BF = jnp.bfloat16
VMEM_LIMIT = 8 * 2**20
FLOPS_PER_MICRO = 1e9


def swap(value, axis, mask):
    pairs = [(source, source ^ mask) for source in range(lax.axis_size(axis))]
    return lax.ppermute(value, axis, pairs)


def dot(a, b):
    return jnp.dot(a, b, preferred_element_type=jnp.float32)


def dot_t(a, b):
    return lax.dot_general(a, b, (((0,), (0,)), ((), ())), preferred_element_type=jnp.float32)


def ordered(upper_side, own, other):
    return jnp.where(
        upper_side, jnp.concatenate([other, own], 0), jnp.concatenate([own, other], 0)
    )


def level_step(current, project_basis, update_basis, caps_rows, level_num):
    leaf_rows = current.shape[0]
    shift_bits = level_num - 1
    partial_value = dot_t(project_basis, current.astype(BF)) * (
        1.0 / math.sqrt(leaf_rows * 2**shift_bits)
    )
    for bit_index in range(shift_bits):
        partial_value = partial_value + swap(partial_value, "leaf", 2**bit_index)
    own = partial_value.astype(BF)
    other = swap(own, "leaf", 2**shift_bits)
    upper_side = (lax.axis_index("leaf") >> shift_bits) & 1 == 1
    stacked = ordered(upper_side, own, other)
    weights = dot(caps_rows, stacked).astype(BF)
    return current - dot(update_basis, weights)


def top_step(current, project_basis, update_basis, caps_rows):
    leaf_count = lax.axis_size("leaf")
    partial_value = dot_t(project_basis, current.astype(BF)) * (
        1.0 / math.sqrt(leaf_count * current.shape[0])
    )
    column_total = lax.psum(partial_value, "leaf")
    stacked = lax.all_gather(column_total.astype(BF), "top", axis=0, tiled=True)
    weights = dot(caps_rows, stacked).astype(BF)
    return current - dot(update_basis, weights)


def step_by_step(
    right_side, leaf_inverse, left_basis, right_basis, level_caps, top_left, top_right, top_caps
):
    levels = left_basis.shape[0]
    lefts = [left_basis[k, 0] for k in range(levels)]
    rights = [right_basis[k, 0] for k in range(levels)]
    current = dot(leaf_inverse[0], right_side[0].astype(BF))
    for k in range(levels):
        current = level_step(current, rights[k], lefts[k], level_caps[k, 0], k + 1)
    current = top_step(current, top_right[0], top_left[0], top_caps)
    current = top_step(current, top_left[0], top_right[0], top_caps)
    for k in reversed(range(levels)):
        current = level_step(current, lefts[k], rights[k], level_caps[k, 0], k + 1)
    return dot_t(leaf_inverse[0], current.astype(BF))[None]


def in_hbm(value):
    return pltpu.with_memory_space_constraint(value, pltpu.HBM)


def in_vmem(value):
    return pltpu.with_memory_space_constraint(value, pltpu.VMEM)


def call(body, outs, *args, scratch=(), hbm=(), hbm_out=False, micros=1):
    vmem = pl.BlockSpec(memory_space=pltpu.VMEM)
    anywhere = pl.BlockSpec(memory_space=pl.ANY)
    return pl.pallas_call(
        body,
        out_shape=[
            jax.ShapeDtypeStruct(shape, dtype) if hbm_out else pltpu.VMEM(shape, dtype)
            for shape, dtype in outs
        ],
        in_specs=[anywhere if i in hbm else vmem for i in range(len(args))],
        out_specs=[anywhere if hbm_out else vmem] * len(outs),
        scratch_shapes=list(scratch),
        compiler_params=pltpu.CompilerParams(vmem_limit_bytes=VMEM_LIMIT),
        cost_estimate=pl.CostEstimate(
            flops=int(micros * FLOPS_PER_MICRO), bytes_accessed=0, transcendentals=0
        ),
    )(*[in_hbm(a) if i in hbm else in_vmem(a) for i, a in enumerate(args)])


def after(value, *others):
    return lax.optimization_barrier((value, *others))[0]


def tree_side(bit):
    return (lax.axis_index("leaf") >> bit) & 1


def column_side():
    leaf = lax.axis_index("leaf")
    return (leaf ^ (leaf >> 1)) & 1


def block(index, width):
    return pl.ds(pl.multiple_of(index * width, width), width)


def put_rows(scratch, upper, own, other):
    rows = own.shape[0]
    scratch[block(upper, rows), :] = own
    scratch[block(1 - upper, rows), :] = other


def put_columns(out, upper, own, other):
    width = own.shape[1]
    out[:, block(upper, width)] = own
    out[:, block(1 - upper, width)] = other


def two_levels(
    right_side, leaf_inverse, left_basis, right_basis, level_caps, top_left, top_right, top_caps
):
    rows, cols = right_side.shape[1:]
    rank = top_left.shape[2]
    half = cols // 2
    f32 = jnp.float32
    s1 = 1.0 / math.sqrt(rows)
    s2 = 1.0 / math.sqrt(rows * 2)
    st = 1.0 / math.sqrt(rows * 4)
    blocks = rows // rank
    square, wide, tall = (rank, rank), (rank, cols), (rows, cols)

    def span(i, n=1):
        return slice(i * rank, (i + n) * rank)

    def part(i, n=1):
        return slice(i * half, (i + n) * half)

    caps_far = swap(top_caps, "top", 2)

    def start_body(
        rhs_hbm, inv_hbm, lb_hbm, rb_hbm, caps_hbm, tl_hbm, tr_hbm,
        x_ref, send, keep, inv_ref, lb, rb, caps, tl, tr, rhs_v, nexts, sems,
    ):
        def load(source, target, *at):
            copy = pltpu.make_async_copy(source, target, sems.at[at])
            copy.start()
            return copy

        first = [
            load(lb_hbm.at[0], lb.at[0], 2, 0),
            load(rb_hbm.at[1], rb.at[1], 2, 1),
            load(caps_hbm, caps, 2, 2),
        ]
        copies = []
        for i in range(blocks):
            copies.append(load(rhs_hbm.at[0, span(i), :], rhs_v.at[span(i), :], 0, i))
            copies.append(
                load(
                    inv_hbm.at[0, span(i), span(0, i + 1)],
                    inv_ref.at[span(i), span(0, i + 1)],
                    1,
                    i,
                )
            )
        basis1 = load(rb_hbm.at[0], rb.at[0], 2, 3)
        rest = [
            load(lb_hbm.at[1], lb.at[1], 2, 4),
            load(tl_hbm, tl, 2, 5),
            load(tr_hbm, tr, 2, 6),
        ]
        odd = tree_side(0)
        for copy in first:
            copy.wait()
        gram = (dot_t(rb[1, 0], lb[0, 0]) * s2).astype(BF)
        nexts[...] = dot(gram, caps[0, 0]).astype(BF)
        send[:, 2 * cols :] = nexts[:, block(1 - odd, rank)]
        for i in range(blocks):
            copies[2 * i].wait()
            copies[2 * i + 1].wait()
            x_ref[span(i), :] = dot(
                inv_ref[span(i), span(0, i + 1)], rhs_v[span(0, i + 1), :].astype(BF)
            )
        basis1.wait()
        state = x_ref[...].astype(BF)
        send[:, :cols] = (dot_t(rb[0, 0], state) * s1).astype(BF)
        keep[...] = dot_t(rb[1, 0], state) * s2 - dot(nexts[:, block(odd, rank)], send[:, :cols])
        send[:, cols : 2 * cols] = keep[...].astype(BF)
        for copy in rest:
            copy.wait()

    state0, pair_send, pair_keep, inverse, lb, rb, caps, tl, tr = call(
        start_body,
        [(tall, f32), ((rank, 2 * cols + rank), BF), (wide, f32), ((rows, rows), BF)]
        + [(a.shape, a.dtype) for a in (left_basis, right_basis, level_caps, top_left, top_right)],
        right_side,
        leaf_inverse,
        left_basis,
        right_basis,
        level_caps,
        top_left,
        top_right,
        hbm=range(7),
        scratch=[
            pltpu.VMEM(tall, f32),
            pltpu.VMEM((rank, 2 * rank), BF),
            pltpu.SemaphoreType.DMA((3, max(blocks, 7))),
        ],
    )
    pair_in = swap(pair_send, "leaf", 1)
    caps_near = swap(after(top_caps, pair_send), "top", 1)
    caps_far_near = swap(after(caps_far, pair_send), "top", 1)

    def grams_body(lb, rb, caps, tl, tr, seen, out, late):
        out[:, span(0)] = (dot_t(tl[0], tl[0]) * st).astype(BF)
        for i, basis in enumerate((tl[0], tr[0])):
            out[:, span(1 + i)] = (dot_t(lb[1, 0], basis) * s2).astype(BF)
        for i, basis in enumerate((tl[0], tr[0], rb[1, 0])):
            late[:, span(i)] = (dot_t(lb[0, 0], basis) * s1).astype(BF)
        late[:, span(3, 2)] = caps[1, 0]

    grams, late = call(
        grams_body,
        [((rank, 3 * rank), BF), ((rank, 5 * rank), BF)],
        lb,
        rb,
        caps,
        tl,
        tr,
        caps_near,
        micros=10,
    )
    grams_sib = swap(grams, "leaf", 1)

    def half_body(keep, own, sib, out):
        out[...] = (
            keep[...]
            + sib[:, cols : 2 * cols]
            - dot(own[:, 2 * cols :], sib[:, :cols])
            - dot(sib[:, 2 * cols :], own[:, :cols])
        ).astype(BF)

    (half2,) = call(half_body, [(wide, BF)], pair_keep, pair_send, pair_in, micros=3)
    half2_far = swap(half2, "leaf", 3)

    def order_body(a, b, c, d, seen, out):
        here = lax.axis_index("top")
        for i, piece in enumerate((a, b, c, d)):
            for k in range(4):
                out[span(i), span(k)] = piece[:, block(here ^ k, rank)]

    (caps_all,) = call(
        order_body,
        [((4 * rank, 4 * rank), BF)],
        top_caps,
        caps_near,
        caps_far,
        caps_far_near,
        half2,
    )

    def sum_body(own, sib, seen, out):
        out[...] = (own[...].astype(f32) + sib[...]).astype(BF)

    (gram_pair,) = call(sum_body, [((rank, 3 * rank), BF)], grams, grams_sib, half2)
    gram_far = swap(gram_pair, "leaf", 3)

    def one_body(x0, own, sib, lb, caps, seen, x1, stack):
        put_rows(stack, tree_side(0), own[:, :cols], sib[:, :cols])
        coef = dot(caps[0, 0], stack[...]).astype(BF)
        x1[...] = x0[...] - dot(lb[0, 0], coef)

    (state1,) = call(
        one_body,
        [(tall, f32)],
        state0,
        pair_send,
        pair_in,
        lb,
        caps,
        half2,
        scratch=[pltpu.VMEM((2 * rank, cols), BF)],
    )

    def two_body(x1, own, far, lb, caps, tl, tr, seen, x2, send, keep, stack, scratch):
        side = column_side()
        put_rows(stack, tree_side(1), own[...], far[...])
        coef = dot(caps[1, 0], stack[...]).astype(BF)
        x2[...] = (x1[...] - dot(lb[1, 0], coef)).astype(BF)
        for i, basis in enumerate((tr[0], tl[0])):
            scratch[...] = dot_t(basis, x2[...]) * st
            send[:, part(i)] = scratch[:, block(1 - side, half)].astype(BF)
            keep[:, part(i)] = scratch[:, block(side, half)]

    state2, top_pair_send, top_keep = call(
        two_body,
        [(tall, BF), (wide, BF), (wide, f32)],
        state1,
        half2,
        half2_far,
        lb,
        caps,
        tl,
        tr,
        caps_all,
        scratch=[pltpu.VMEM((2 * rank, cols), BF), pltpu.VMEM(wide, f32)],
    )
    top_pair_in = swap(top_pair_send, "leaf", 1)

    def down_body(lb, x2, z5, z):
        z5[...] = dot_t(lb[1, 0], x2[...]) * s2
        z[:, :cols] = z5[...].astype(BF)
        z[:, cols:] = (dot_t(lb[0, 0], x2[...]) * s1).astype(BF)

    down5, down_send = call(down_body, [(wide, f32), ((rank, 2 * cols), BF)], lb, state2)
    down_in = swap(down_send, "leaf", 1)

    def add_body(own, other, out, out_b):
        out[...] = own[...] + other[:, :cols]
        out_b[...] = out[...].astype(BF)

    top_half, top_half_send = call(add_body, [(wide, f32), (wide, BF)], top_keep, top_pair_in)
    top_half_far = swap(top_half_send, "leaf", 3)
    down5, down5_send = call(add_body, [(wide, f32), (wide, BF)], down5, down_in)
    down5_far = swap(down5_send, "leaf", 3)

    def column_body(own, far, gram, gram_far, out):
        out[:, : 2 * half] = (own[...] + far[...]).astype(BF)
        out[:, 2 * half :] = (gram[:, span(0)].astype(f32) + gram_far[:, span(0)]).astype(BF)

    (top_send,) = call(
        column_body,
        [((rank, 2 * half + rank), BF)],
        top_half,
        top_half_far,
        gram_pair,
        gram_far,
    )
    top_far = swap(top_send, "top", 2)
    top_parts = top_send, swap(top_send, "top", 1), top_far, swap(top_far, "top", 1)
    late_sib = swap(after(late, top_send), "leaf", 1)

    def under_body(x2, rb, tl, tr, inv, seen, out2, under):
        for c in range(blocks):
            column = inv[c * rank :, span(c)]
            out2[span(c), :] = dot_t(column, x2[c * rank :, :])
            for i, basis in enumerate((tl[0], tr[0], rb[1, 0], rb[0, 0])):
                under[span(c), span(i)] = dot_t(column, basis[c * rank :, :]).astype(BF)

    out2, under = call(
        under_body,
        [(tall, f32), ((rows, 4 * rank), BF)],
        state2,
        rb,
        tl,
        tr,
        inverse,
        top_send,
    )

    def top_body(a, b, c, d, caps, seen, out, up, down):
        pieces = (a, b, c, d)
        for i, piece in enumerate(pieces):
            up[span(i), :] = piece[:, part(0)]
        coef = dot(caps[...], up[...]).astype(BF)
        for i, piece in enumerate(pieces):
            down[span(i), :] = (
                piece[:, part(1)] - dot(piece[:, 2 * half :], coef[span(i), :])
            ).astype(BF)
        out[:, part(0)] = coef[:rank, :]
        out[:, part(1)] = dot(caps[:rank, :], down[...]).astype(BF)

    (back_send,) = call(
        top_body,
        [(wide, BF)],
        *top_parts,
        caps_all,
        out2,
        scratch=[pltpu.VMEM((4 * rank, half), BF)] * 2,
    )
    back_in = swap(back_send, "leaf", 1)

    def last_body(
        out2, under, back, back_sib, down5, down5_far, gram, gram_far, late, late_sib,
        z, z_sib, caps, out, coefs, stack, out_v, sems,
    ):
        side = column_side()
        for i in range(2):
            put_columns(coefs.at[span(i), :], side, back[:, part(i)], back_sib[:, part(i)])
        both = coefs[span(0, 2), :]
        put_rows(
            stack,
            tree_side(1),
            (down5[...] - dot(gram[:, span(1, 2)], both)).astype(BF),
            (down5_far[...] - dot(gram_far[:, span(1, 2)], both)).astype(BF),
        )
        coef5 = dot(caps[1, 0], stack[...]).astype(BF)
        coef5_sib = dot(late_sib[:, span(3, 2)], stack[...]).astype(BF)
        coefs[span(2), :] = coef5

        def proj(zs, grams, coef):
            return (
                zs[:, cols:] - dot(grams[:, span(0, 2)], both) - dot(grams[:, span(2)], coef)
            ).astype(BF)

        put_rows(stack, tree_side(0), proj(z, late, coef5), proj(z_sib, late_sib, coef5_sib))
        coefs[span(3), :] = dot(caps[0, 0], stack[...]).astype(BF)
        copies = []
        for c in range(blocks):
            out_v[span(c), :] = out2[span(c), :] - dot(under[span(c), :], coefs[...])
            copy = pltpu.make_async_copy(out_v.at[span(c), :], out.at[0, span(c), :], sems.at[c])
            copy.start()
            copies.append(copy)
        for copy in copies:
            copy.wait()

    (out,) = call(
        last_body,
        [((1, rows, cols), f32)],
        out2,
        under,
        back_send,
        back_in,
        down5,
        down5_far,
        gram_pair,
        gram_far,
        late,
        late_sib,
        down_send,
        down_in,
        caps,
        hbm_out=True,
        scratch=[
            pltpu.VMEM((4 * rank, cols), BF),
            pltpu.VMEM((2 * rank, cols), BF),
            pltpu.VMEM(tall, f32),
            pltpu.SemaphoreType.DMA((blocks,)),
        ],
    )
    return out


def on_device(*args):
    levels = args[2].shape[0]
    sizes = lax.axis_size("leaf"), lax.axis_size("top")
    if levels == 2 and sizes == (4, 4):
        return two_levels(*args)
    return step_by_step(*args)


def solution(mesh):
    rows = P(("parts", "top"), "leaf", None)
    level_rows = P(None, ("parts", "top"), "leaf", None)
    return jax.shard_map(
        on_device,
        mesh=mesh,
        in_specs=(
            rows,
            rows,
            level_rows,
            level_rows,
            level_rows,
            rows,
            rows,
            P(("parts", "top"), None),
        ),
        out_specs=rows,
        check_vma=False,
    )
```

time: 49.1 us -> 49.7 us (1.012)
  starting transfers between devices: 16.6 us -> 22.3 us
  waiting for transfers between devices: 22.9 us -> 18.3 us
    ppermute x16, starting transfers between devices: 16.6 us -> 22.3 us  [swap(): return lax.ppermute(value, axis, pairs)]
    ppermute x16, waiting for transfers between devices: 22.9 us -> 18.3 us  [swap(): return lax.ppermute(value, axis, pairs)]
    pallas_call x11 -> x14, Pallas kernels: 9.27 us -> 8.81 us  [call(): pl.pallas_call(body, out_shape=[jax.ShapeDtypeStruct(shape, dtype) if hbm...]
  transfers between devices with their start and end apart: 16 -> 16, of which waited for: 7 -> 7; matrix products, arithmetic and copies ran while one was open for 0% -> 0% of each run, Pallas kernels for 10% -> 14%
where the time goes in v5:
time: 49.7 us; the launch traced here: 49.6 us
  starting transfers between devices  22.3 us (45%)
  waiting for transfers between devices  18.3 us (37%)
  Pallas kernels  8.81 us (18%)
    ppermute x16, starting transfers between devices, swap(): return lax.ppermute(value, axis, pairs)  22.3 us
    ppermute x16, waiting for transfers between devices, swap(): return lax.ppermute(value, axis, pairs)  18.3 us
    pallas_call x14, Pallas kernels, call(): pl.pallas_call(body, out_shape=[jax.ShapeDtypeStruct(shape, dtype) if hbm...  8.81 us
  transfers between devices with their start and end apart: 16, of which 7 were waited for; matrix products, arithmetic and copies ran while one was open for 0% of the time, Pallas kernels for 14%

profile of v5, /device:TPU:0, one launch (start us, length us, event | category | flops | bytes accessed | tf_op | source)
XLA Modules:
  0.0 49.6 jit_solution(8925902144659721100)
XLA Ops:
  0.0 2.9 %collective-permute-start.3 = (bf16[128,512]{1,0:T(8,128)(2,1)}, bf16[128,512]{1,0:T(8,128)(2,1)S(1)}, u32[]{:S(2)}, u32[]{:S(2)}) collective-permute-start(bf16[128,512]{1,0:T(8,128)(2,1)} %a.1), channel_id=1, source_target_pairs={{0,2},{1,3},{2,0},{3,1},{4,6},{5,7},{6,4},{7,5},{8,10},{9,11},{10,... | collective-permute-start | bytes 393224 | tf_op jit(solution)/shard_map/ppermute | solution.py:17
  2.9 3.1 %shard_map.82 = (f32[640,256]{1,0:T(8,128)S(1)}, bf16[128,640]{1,0:T(8,128)(2,1)S(1)}, f32[128,256]{1,0:T(8,128)S(1)}, bf16[640,640]{1,0:T(8,128)(2,1)S(1)}, bf1...) custom-call(f32[1,640,256]{2,1,0:T(8,128)} %rhs_hbm.1, ...), custom_call_target="tpu_custom_call" | custom-call | flops 1000000000 | tf_op jit(solution)/shard_map/pallas_call | solution.py:88
  6.2 1.6 %collective-permute-start = (bf16[128,640]{1,0:T(8,128)(2,1)S(1)}, bf16[128,640]{1,0:T(8,128)(2,1)S(1)}, u32[]{:S(2)}, u32[]{:S(2)}) collective-permute-start(bf16[128,640]{1,0:T(8,128)(2,1)S(1)} %get-tuple-element.31.own), channel_id=1, source_target_pairs={{0,4},{4,0},{8,12},{12,8},{1,5},{5,1},{9,13},{13,9},{2,6},{6,2},{1... | collective-permute-start | bytes 491528 | tf_op jit(solution)/shard_map/ppermute | solution.py:17
  8.0 0.5 shard_map.88
  8.4 1.2 %collective-permute-start.7 = (bf16[128,384]{1,0:T(8,128)(2,1)S(1)}, bf16[128,384]{1,0:T(8,128)(2,1)S(1)}, u32[]{:S(2)}, u32[]{:S(2)}) collective-permute-start(bf16[128,384]{1,0:T(8,128)(2,1)S(1)} %get-tuple-element.46.own), channel_id=1, source_target_pairs={{0,4},{4,0},{8,12},{12,8},{1,5},{5,1},{9,13},{13,9},{2,6},{6,2},{1... | collective-permute-start | bytes 294920 | tf_op jit(solution)/shard_map/ppermute | solution.py:17
  9.6 3.6 %collective-permute-done.sib = bf16[128,640]{1,0:T(8,128)(2,1)S(1)} collective-permute-done((bf16[128,640]{1,0:T(8,128)(2,1)S(1)}, bf16[128,640]{1,0:T(8,128)(2,1)S(1)}, u32[]{:S(2)}, u32[]{:S(2)}) %collective-permute-start) | collective-permute-done | bytes 163872 | tf_op jit(solution)/shard_map/ppermute | solution.py:17
  13.4 3.7 %collective-permute-start.1 = (bf16[128,256]{1,0:T(8,128)(2,1)S(1)}, bf16[128,256]{1,0:T(8,128)(2,1)S(1)}, u32[]{:S(2)}, u32[]{:S(2)}) collective-permute-start(bf16[128,256]{1,0:T(8,128)(2,1)S(1)} %shard_map.83.seen.own), channel_id=1, source_target_pairs={{0,12},{4,8},{8,4},{12,0},{1,13},{5,9},{9,5},{13,1},{2,14},{6,10},... | collective-permute-start | bytes 196616 | tf_op jit(solution)/shard_map/ppermute | solution.py:17
  17.1 0.4 shard_map.84.x1
  17.6 1.9 %collective-permute-done.1.far = bf16[128,256]{1,0:T(8,128)(2,1)S(1)} collective-permute-done((bf16[128,256]{1,0:T(8,128)(2,1)S(1)}, bf16[128,256]{1,0:T(8,128)(2,1)S(1)}, u32[]{:S(2)}, u32[]{:S(2)}) %collective-permute-start.1) | collective-permute-done | bytes 65568 | tf_op jit(solution)/shard_map/ppermute | solution.py:17
  19.5 0.8 %shard_map.86 = (bf16[640,256]{1,0:T(8,128)(2,1)S(1)}, bf16[128,256]{1,0:T(8,128)(2,1)S(1)}, f32[128,256]{1,0:T(8,128)S(1)}) custom-call(f32[640,256]{1,0:T(8,128)S(1)} %shard_map.84.x1, bf16[128,256]{1,0:T(8,128)(2,1)S(1)} %shard_map.83.seen.own, bf16[128,256]{1,0:T(8,128)(2,1)S(1)} %collective-permute-done.1.far, ...), custom_call_target="tpu_custom_call" | custom-call | flops 1000000000 | tf_op jit(solution)/shard_map/pallas_call | solution.py:88
  20.4 3.7 %collective-permute-start.8 = (bf16[128,384]{1,0:T(8,128)(2,1)S(1)}, bf16[128,384]{1,0:T(8,128)(2,1)S(1)}, u32[]{:S(2)}, u32[]{:S(2)}) collective-permute-start(bf16[128,384]{1,0:T(8,128)(2,1)S(1)} %shard_map.89.gram), channel_id=1, source_target_pairs={{0,12},{4,8},{8,4},{12,0},{1,13},{5,9},{9,5},{13,1},{2,14},{6,10},... | collective-permute-start | bytes 294920 | tf_op jit(solution)/shard_map/ppermute | solution.py:17
  24.1 1.5 %collective-permute-done.5.other = bf16[128,256]{1,0:T(8,128)(2,1)S(1)} collective-permute-done((bf16[128,256]{1,0:T(8,128)(2,1)S(1)}, bf16[128,256]{1,0:T(8,128)(2,1)S(1)}, u32[]{:S(2)}, u32[]{:S(2)}) %collective-permute-start.5) | collective-permute-done | bytes 65568 | tf_op jit(solution)/shard_map/ppermute | solution.py:17
  25.6 3.0 %collective-permute-start.6 = (bf16[128,256]{1,0:T(8,128)(2,1)S(1)}, bf16[128,256]{1,0:T(8,128)(2,1)S(1)}, u32[]{:S(2)}, u32[]{:S(2)}) collective-permute-start(bf16[128,256]{1,0:T(8,128)(2,1)S(1)} %get-tuple-element.45), channel_id=1, source_target_pairs={{0,12},{4,8},{8,4},{12,0},{1,13},{5,9},{9,5},{13,1},{2,14},{6,10},... | collective-permute-start | bytes 196616 | tf_op jit(solution)/shard_map/ppermute | solution.py:17
  28.6 0.3 shard_map.93
  29.0 2.7 %collective-permute-done.6.far = bf16[128,256]{1,0:T(8,128)(2,1)S(1)} collective-permute-done((bf16[128,256]{1,0:T(8,128)(2,1)S(1)}, bf16[128,256]{1,0:T(8,128)(2,1)S(1)}, u32[]{:S(2)}, u32[]{:S(2)}) %collective-permute-start.6) | collective-permute-done | bytes 65568 | tf_op jit(solution)/shard_map/ppermute | solution.py:17
  31.7 0.6 %collective-permute-start.10 = (bf16[128,384]{1,0:T(8,128)(2,1)S(1)}, bf16[128,384]{1,0:T(8,128)(2,1)S(1)}, u32[]{:S(2)}, u32[]{:S(2)}) collective-permute-start(bf16[128,384]{1,0:T(8,128)(2,1)S(1)} %shard_map.90.seen.a), channel_id=1, source_target_pairs={{0,2},{1,3},{2,0},{3,1},{4,6},{5,7},{6,4},{7,5},{8,10},{9,11},{10,... | collective-permute-start | bytes 294920 | tf_op jit(solution)/shard_map/ppermute | solution.py:17
  32.3 4.1 %collective-permute-done.10.c = bf16[128,384]{1,0:T(8,128)(2,1)S(1)} collective-permute-done((bf16[128,384]{1,0:T(8,128)(2,1)S(1)}, bf16[128,384]{1,0:T(8,128)(2,1)S(1)}, u32[]{:S(2)}, u32[]{:S(2)}) %collective-permute-start.10) | collective-permute-done | bytes 98336 | tf_op jit(solution)/shard_map/ppermute | solution.py:17
  36.4 3.1 %collective-permute-start.14 = (bf16[128,256]{1,0:T(8,128)(2,1)S(1)}, bf16[128,256]{1,0:T(8,128)(2,1)S(1)}, u32[]{:S(2)}, u32[]{:S(2)}) collective-permute-start(bf16[128,256]{1,0:T(8,128)(2,1)S(1)} %get-tuple-element.52), channel_id=1, source_target_pairs={{0,12},{4,8},{8,4},{12,0},{1,13},{5,9},{9,5},{13,1},{2,14},{6,10},... | collective-permute-start | bytes 196616 | tf_op jit(solution)/shard_map/ppermute | solution.py:17
  39.6 0.9 %shard_map.91 = (f32[640,256]{1,0:T(8,128)S(1)}, bf16[640,512]{1,0:T(8,128)(2,1)S(1)}) custom-call(bf16[640,256]{1,0:T(8,128)(2,1)S(1)} %get-tuple-element.39.x2, bf16[2,1,640,128]{3,2,1,0:T(8,128)(2,1)S(1)} %get-tuple-element.40.rb, bf16[1,640,128]{2,1,0:T(8,128)(2,1)S(1)} %get-tuple-element.35.tl, bf16[1,640,128]{2,1,0:T(8,128)(2,1)S(1)} %get-tuple-element.36.tr, ...), custom_call_target="tpu_custom_call" | custom-call | flops 1000000000 | tf_op jit(solution)/shard_map/pallas_call | solution.py:88
  40.5 0.7 %shard_map.92.back = bf16[128,256]{1,0:T(8,128)(2,1)S(1)} custom-call(bf16[128,384]{1,0:T(8,128)(2,1)S(1)} %shard_map.90.seen.a, bf16[128,384]{1,0:T(8,128)(2,1)S(1)} %collective-permute-done.9.b, bf16[128,384]{1,0:T(8,128)(2,1)S(1)} %collective-permute-done.10.c, bf16[128,384]{1,0:T(8,128)(2,1)S(1)} %collective-permute-done.11.d, ...), custom_call_target="tpu_custom_call" | custom-call | flops 1000000000 | tf_op jit(solution)/shard_map/pallas_call | solution.py:88
  41.1 2.1 %collective-permute-start.12 = (bf16[128,256]{1,0:T(8,128)(2,1)S(1)}, bf16[128,256]{1,0:T(8,128)(2,1)S(1)}, u32[]{:S(2)}, u32[]{:S(2)}) collective-permute-start(bf16[128,256]{1,0:T(8,128)(2,1)S(1)} %shard_map.92.back), channel_id=1, source_target_pairs={{0,4},{4,0},{8,12},{12,8},{1,5},{5,1},{9,13},{13,9},{2,6},{6,2},{1... | collective-permute-start | bytes 196616 | tf_op jit(solution)/shard_map/ppermute | solution.py:17
  43.2 3.4 %collective-permute-done.15.late_sib = bf16[128,640]{1,0:T(8,128)(2,1)S(1)} collective-permute-done((bf16[128,640]{1,0:T(8,128)(2,1)S(1)}, bf16[128,640]{1,0:T(8,128)(2,1)S(1)}, u32[]{:S(2)}, u32[]{:S(2)}) %collective-permute-start.15) | collective-permute-done | bytes 163872 | tf_op jit(solution)/shard_map/ppermute | solution.py:17
  46.6 1.1 %collective-permute-done.12.back_sib = bf16[128,256]{1,0:T(8,128)(2,1)S(1)} collective-permute-done((bf16[128,256]{1,0:T(8,128)(2,1)S(1)}, bf16[128,256]{1,0:T(8,128)(2,1)S(1)}, u32[]{:S(2)}, u32[]{:S(2)}) %collective-permute-start.12) | collective-permute-done | bytes 65568 | tf_op jit(solution)/shard_map/ppermute | solution.py:17
  47.7 1.8 %shard_map.95 = f32[1,640,256]{2,1,0:T(8,128)} custom-call(f32[640,256]{1,0:T(8,128)S(1)} %get-tuple-element.47.seen.out2, bf16[640,512]{1,0:T(8,128)(2,1)S(1)} %get-tuple-element.48.under, bf16[128,256]{1,0:T(8,128)(2,1)S(1)} %shard_map.92.back, bf16[128,256]{1,0:T(8,128)(2,1)S(1)} %collective-permute-done.12.back_sib, ...), custom_call_target="tpu_custom_call" | custom-call | flops 1000000000 | tf_op jit(solution)/shard_map/pallas_call | solution.py:88
  (24 shorter events, 0.8 us)
Async XLA Ops:
  0.0 6.1 %copy-start = (bf16[128,512]{1,0:T(8,128)(2,1)S(1)}, bf16[128,512]{1,0:T(8,128)(2,1)}, u32[]{:S(2)}) copy-start(bf16[128,512]{1,0:T(8,128)(2,1)} %a.1) | copy-start | bytes 393220
  0.0 7.8 %collective-permute-start.3 = (bf16[128,512]{1,0:T(8,128)(2,1)}, bf16[128,512]{1,0:T(8,128)(2,1)S(1)}, u32[]{:S(2)}, u32[]{:S(2)}) collective-permute-start(bf16[128,512]{1,0:T(8,128)(2,1)} %a.1), channel_id=1, source_target_pairs={{0,2},{1,3},{2,0},{3,1},{4,6},{5,7},{6,4},{7,5},{8,10},{9,11},{10,... | collective-permute-start | bytes 393224 | tf_op jit(solution)/shard_map/ppermute | solution.py:17
  6.1 1.9 %collective-permute-start.2 = (bf16[128,512]{1,0:T(8,128)(2,1)S(1)}, bf16[128,512]{1,0:T(8,128)(2,1)S(1)}, u32[]{:S(2)}, u32[]{:S(2)}) collective-permute-start(bf16[128,512]{1,0:T(8,128)(2,1)S(1)} %copy-done), channel_id=1, source_target_pairs={{0,1},{1,0},{2,3},{3,2},{4,5},{5,4},{6,7},{7,6},{8,9},{9,8},{10,11... | collective-permute-start | bytes 393224 | tf_op jit(solution)/shard_map/ppermute | solution.py:17
  6.2 7.1 %collective-permute-start = (bf16[128,640]{1,0:T(8,128)(2,1)S(1)}, bf16[128,640]{1,0:T(8,128)(2,1)S(1)}, u32[]{:S(2)}, u32[]{:S(2)}) collective-permute-start(bf16[128,640]{1,0:T(8,128)(2,1)S(1)} %get-tuple-element.31.own), channel_id=1, source_target_pairs={{0,4},{4,0},{8,12},{12,8},{1,5},{5,1},{9,13},{13,9},{2,6},{6,2},{1... | collective-permute-start | bytes 491528 | tf_op jit(solution)/shard_map/ppermute | solution.py:17
  7.8 9.7 %collective-permute-start.4 = (bf16[128,512]{1,0:T(8,128)(2,1)S(1)}, bf16[128,512]{1,0:T(8,128)(2,1)S(1)}, u32[]{:S(2)}, u32[]{:S(2)}) collective-permute-start(bf16[128,512]{1,0:T(8,128)(2,1)S(1)} %collective-permute-done.3.c), channel_id=1, source_target_pairs={{0,1},{1,0},{2,3},{3,2},{4,5},{5,4},{6,7},{7,6},{8,9},{9,8},{10,11... | collective-permute-start | bytes 393224 | tf_op jit(solution)/shard_map/ppermute | solution.py:17
  8.4 11.9 %collective-permute-start.7 = (bf16[128,384]{1,0:T(8,128)(2,1)S(1)}, bf16[128,384]{1,0:T(8,128)(2,1)S(1)}, u32[]{:S(2)}, u32[]{:S(2)}) collective-permute-start(bf16[128,384]{1,0:T(8,128)(2,1)S(1)} %get-tuple-element.46.own), channel_id=1, source_target_pairs={{0,4},{4,0},{8,12},{12,8},{1,5},{5,1},{9,13},{13,9},{2,6},{6,2},{1... | collective-permute-start | bytes 294920 | tf_op jit(solution)/shard_map/ppermute | solution.py:17
  13.4 6.1 %collective-permute-start.1 = (bf16[128,256]{1,0:T(8,128)(2,1)S(1)}, bf16[128,256]{1,0:T(8,128)(2,1)S(1)}, u32[]{:S(2)}, u32[]{:S(2)}) collective-permute-start(bf16[128,256]{1,0:T(8,128)(2,1)S(1)} %shard_map.83.seen.own), channel_id=1, source_target_pairs={{0,12},{4,8},{8,4},{12,0},{1,13},{5,9},{9,5},{13,1},{2,14},{6,10},... | collective-permute-start | bytes 196616 | tf_op jit(solution)/shard_map/ppermute | solution.py:17
  20.3 5.2 %collective-permute-start.5 = (bf16[128,256]{1,0:T(8,128)(2,1)S(1)}, bf16[128,256]{1,0:T(8,128)(2,1)S(1)}, u32[]{:S(2)}, u32[]{:S(2)}) collective-permute-start(bf16[128,256]{1,0:T(8,128)(2,1)S(1)} %get-tuple-element.43), channel_id=1, source_target_pairs={{0,4},{4,0},{8,12},{12,8},{1,5},{5,1},{9,13},{13,9},{2,6},{6,2},{1... | collective-permute-start | bytes 196616 | tf_op jit(solution)/shard_map/ppermute | solution.py:17
  20.4 8.6 %collective-permute-start.8 = (bf16[128,384]{1,0:T(8,128)(2,1)S(1)}, bf16[128,384]{1,0:T(8,128)(2,1)S(1)}, u32[]{:S(2)}, u32[]{:S(2)}) collective-permute-start(bf16[128,384]{1,0:T(8,128)(2,1)S(1)} %shard_map.89.gram), channel_id=1, source_target_pairs={{0,12},{4,8},{8,4},{12,0},{1,13},{5,9},{9,5},{13,1},{2,14},{6,10},... | collective-permute-start | bytes 294920 | tf_op jit(solution)/shard_map/ppermute | solution.py:17
  25.6 6.1 %collective-permute-start.6 = (bf16[128,256]{1,0:T(8,128)(2,1)S(1)}, bf16[128,256]{1,0:T(8,128)(2,1)S(1)}, u32[]{:S(2)}, u32[]{:S(2)}) collective-permute-start(bf16[128,256]{1,0:T(8,128)(2,1)S(1)} %get-tuple-element.45), channel_id=1, source_target_pairs={{0,12},{4,8},{8,4},{12,0},{1,13},{5,9},{9,5},{13,1},{2,14},{6,10},... | collective-permute-start | bytes 196616 | tf_op jit(solution)/shard_map/ppermute | solution.py:17
  28.9 7.5 %collective-permute-start.13 = (bf16[128,512]{1,0:T(8,128)(2,1)S(1)}, bf16[128,512]{1,0:T(8,128)(2,1)S(1)}, u32[]{:S(2)}, u32[]{:S(2)}) collective-permute-start(bf16[128,512]{1,0:T(8,128)(2,1)S(1)} %get-tuple-element.50.z), channel_id=1, source_target_pairs={{0,4},{4,0},{8,12},{12,8},{1,5},{5,1},{9,13},{13,9},{2,6},{6,2},{1... | collective-permute-start | bytes 393224 | tf_op jit(solution)/shard_map/ppermute | solution.py:17
  31.7 4.7 %collective-permute-start.10 = (bf16[128,384]{1,0:T(8,128)(2,1)S(1)}, bf16[128,384]{1,0:T(8,128)(2,1)S(1)}, u32[]{:S(2)}, u32[]{:S(2)}) collective-permute-start(bf16[128,384]{1,0:T(8,128)(2,1)S(1)} %shard_map.90.seen.a), channel_id=1, source_target_pairs={{0,2},{1,3},{2,0},{3,1},{4,6},{5,7},{6,4},{7,5},{8,10},{9,11},{10,... | collective-permute-start | bytes 294920 | tf_op jit(solution)/shard_map/ppermute | solution.py:17
  32.3 8.1 %collective-permute-start.9 = (bf16[128,384]{1,0:T(8,128)(2,1)S(1)}, bf16[128,384]{1,0:T(8,128)(2,1)S(1)}, u32[]{:S(2)}, u32[]{:S(2)}) collective-permute-start(bf16[128,384]{1,0:T(8,128)(2,1)S(1)} %shard_map.90.seen.a), channel_id=1, source_target_pairs={{0,1},{1,0},{2,3},{3,2},{4,5},{5,4},{6,7},{7,6},{8,9},{9,8},{10,11... | collective-permute-start | bytes 294920 | tf_op jit(solution)/shard_map/ppermute | solution.py:17
  36.4 4.0 %collective-permute-start.11 = (bf16[128,384]{1,0:T(8,128)(2,1)S(1)}, bf16[128,384]{1,0:T(8,128)(2,1)S(1)}, u32[]{:S(2)}, u32[]{:S(2)}) collective-permute-start(bf16[128,384]{1,0:T(8,128)(2,1)S(1)} %collective-permute-done.10.c), channel_id=1, source_target_pairs={{0,1},{1,0},{2,3},{3,2},{4,5},{5,4},{6,7},{7,6},{8,9},{9,8},{10,11... | collective-permute-start | bytes 294920 | tf_op jit(solution)/shard_map/ppermute | solution.py:17
  36.4 6.8 %collective-permute-start.14 = (bf16[128,256]{1,0:T(8,128)(2,1)S(1)}, bf16[128,256]{1,0:T(8,128)(2,1)S(1)}, u32[]{:S(2)}, u32[]{:S(2)}) collective-permute-start(bf16[128,256]{1,0:T(8,128)(2,1)S(1)} %get-tuple-element.52), channel_id=1, source_target_pairs={{0,12},{4,8},{8,4},{12,0},{1,13},{5,9},{9,5},{13,1},{2,14},{6,10},... | collective-permute-start | bytes 196616 | tf_op jit(solution)/shard_map/ppermute | solution.py:17
  39.6 7.1 %collective-permute-start.15 = (bf16[128,640]{1,0:T(8,128)(2,1)S(1)}, bf16[128,640]{1,0:T(8,128)(2,1)S(1)}, u32[]{:S(2)}, u32[]{:S(2)}) collective-permute-start(bf16[128,640]{1,0:T(8,128)(2,1)S(1)} %get-tuple-element.54.late), channel_id=1, source_target_pairs={{0,4},{4,0},{8,12},{12,8},{1,5},{5,1},{9,13},{13,9},{2,6},{6,2},{1... | collective-permute-start | bytes 491528 | tf_op jit(solution)/shard_map/ppermute | solution.py:17
  41.1 6.6 %collective-permute-start.12 = (bf16[128,256]{1,0:T(8,128)(2,1)S(1)}, bf16[128,256]{1,0:T(8,128)(2,1)S(1)}, u32[]{:S(2)}, u32[]{:S(2)}) collective-permute-start(bf16[128,256]{1,0:T(8,128)(2,1)S(1)} %shard_map.92.back), channel_id=1, source_target_pairs={{0,4},{4,0},{8,12},{12,8},{1,5},{5,1},{9,13},{13,9},{2,6},{6,2},{1... | collective-permute-start | bytes 196616 | tf_op jit(solution)/shard_map/ppermute | solution.py:17

commit v6 on v5

--- a/solution.py
+++ b/solution.py
@@ -148,8 +148,6 @@
 
     def part(i, n=1):
         return slice(i * half, (i + n) * half)
-
-    caps_far = swap(top_caps, "top", 2)
 
     def start_body(
         rhs_hbm, inv_hbm, lb_hbm, rb_hbm, caps_hbm, tl_hbm, tr_hbm,
@@ -221,8 +219,10 @@
         ],
     )
     pair_in = swap(pair_send, "leaf", 1)
-    caps_near = swap(after(top_caps, pair_send), "top", 1)
-    caps_far_near = swap(after(caps_far, pair_send), "top", 1)
+    caps_here = after(top_caps, pair_send)
+    caps_near = swap(caps_here, "top", 1)
+    caps_far = swap(caps_here, "top", 2)
+    caps_far_near = swap(caps_far, "top", 1)
 
     def grams_body(lb, rb, caps, tl, tr, seen, out, late):
         out[:, span(0)] = (dot_t(tl[0], tl[0]) * st).astype(BF)
@@ -255,6 +255,7 @@
 
     (half2,) = call(half_body, [(wide, BF)], pair_keep, pair_send, pair_in, micros=3)
     half2_far = swap(half2, "leaf", 3)
+    late_sib = swap(after(late, half2), "leaf", 1)
 
     def order_body(a, b, c, d, seen, out):
         here = lax.axis_index("top")
@@ -328,13 +329,15 @@
     down5, down_send = call(down_body, [(wide, f32), ((rank, 2 * cols), BF)], lb, state2)
     down_in = swap(down_send, "leaf", 1)
 
-    def add_body(own, other, out, out_b):
+    def add_body(own, other, seen, out, out_b):
         out[...] = own[...] + other[:, :cols]
         out_b[...] = out[...].astype(BF)
 
-    top_half, top_half_send = call(add_body, [(wide, f32), (wide, BF)], top_keep, top_pair_in)
+    top_half, top_half_send = call(add_body, [(wide, f32), (wide, BF)], top_keep, top_pair_in, late_sib)
     top_half_far = swap(top_half_send, "leaf", 3)
-    down5, down5_send = call(add_body, [(wide, f32), (wide, BF)], down5, down_in)
+    down5, down5_send = call(
+        add_body, [(wide, f32), (wide, BF)], down5, down_in, gram_pair
+    )
     down5_far = swap(down5_send, "leaf", 3)
 
     def column_body(own, far, gram, gram_far, out):
@@ -350,8 +353,8 @@
         gram_far,
     )
     top_far = swap(top_send, "top", 2)
-    top_parts = top_send, swap(top_send, "top", 1), top_far, swap(top_far, "top", 1)
-    late_sib = swap(after(late, top_send), "leaf", 1)
+    top_near = swap(after(top_send, down5_send), "top", 1)
+    top_parts = top_send, top_near, top_far, swap(top_far, "top", 1)
 
     def under_body(x2, rb, tl, tr, inv, seen, out2, under):
         for c in range(blocks):
@@ -368,10 +371,10 @@
         tl,
         tr,
         inverse,
-        top_send,
-    )
-
-    def top_body(a, b, c, d, caps, seen, out, up, down):
+        down5_far,
+    )
+
+    def top_body(a, b, c, d, caps, out, up, down):
         pieces = (a, b, c, d)
         for i, piece in enumerate(pieces):
             up[span(i), :] = piece[:, part(0)]
@@ -388,7 +391,6 @@
         [(wide, BF)],
         *top_parts,
         caps_all,
-        out2,
         scratch=[pltpu.VMEM((4 * rank, half), BF)] * 2,
     )
     back_in = swap(back_send, "leaf", 1)

time: 49.7 us -> 46.1 us (0.928)
  starting transfers between devices: 22.3 us -> 20.5 us
  waiting for transfers between devices: 18.3 us -> 16.5 us
    ppermute x16, starting transfers between devices: 22.3 us -> 20.5 us  [swap(): return lax.ppermute(value, axis, pairs)]
    ppermute x16, waiting for transfers between devices: 18.3 us -> 16.5 us  [swap(): return lax.ppermute(value, axis, pairs)]
  transfers between devices with their start and end apart: 16 -> 16, of which waited for: 7 -> 8; matrix products, arithmetic and copies ran while one was open for 0% -> 0% of each run, Pallas kernels for 14% -> 8%
where the time goes in v6:
time: 46.1 us; the launch traced here: 46 us
  starting transfers between devices  20.5 us (44%)
  waiting for transfers between devices  16.5 us (36%)
  Pallas kernels  8.83 us (19%)
    ppermute x16, starting transfers between devices, swap(): return lax.ppermute(value, axis, pairs)  20.5 us
    ppermute x16, waiting for transfers between devices, swap(): return lax.ppermute(value, axis, pairs)  16.5 us
    pallas_call x14, Pallas kernels, call(): pl.pallas_call(body, out_shape=[jax.ShapeDtypeStruct(shape, dtype) if hbm...  8.83 us
  transfers between devices with their start and end apart: 16, of which 8 were waited for; matrix products, arithmetic and copies ran while one was open for 0% of the time, Pallas kernels for 8%

profile of v6, /device:TPU:0, one launch (start us, length us, event | category | flops | bytes accessed | tf_op | source)
XLA Modules:
  0.0 46.0 jit_solution(4665786430990228368)
XLA Ops:
  0.0 3.2 %shard_map.82 = (f32[640,256]{1,0:T(8,128)S(1)}, bf16[128,640]{1,0:T(8,128)(2,1)S(1)}, f32[128,256]{1,0:T(8,128)S(1)}, bf16[640,640]{1,0:T(8,128)(2,1)S(1)}, bf1...) custom-call(f32[1,640,256]{2,1,0:T(8,128)} %rhs_hbm.1, ...), custom_call_target="tpu_custom_call" | custom-call | flops 1000000000 | tf_op jit(solution)/shard_map/pallas_call | solution.py:88
  3.2 0.5 %collective-permute-start.2 = (bf16[128,512]{1,0:T(8,128)(2,1)S(1)}, bf16[128,512]{1,0:T(8,128)(2,1)S(1)}, u32[]{:S(2)}, u32[]{:S(2)}) collective-permute-start(bf16[128,512]{1,0:T(8,128)(2,1)S(1)} %copy-done), channel_id=1, source_target_pairs={{0,1},{1,0},{2,3},{3,2},{4,5},{5,4},{6,7},{7,6},{8,9},{9,8},{10,11... | collective-permute-start | bytes 393224 | tf_op jit(solution)/shard_map/ppermute | solution.py:17
  3.7 2.7 %collective-permute-start = (bf16[128,640]{1,0:T(8,128)(2,1)S(1)}, bf16[128,640]{1,0:T(8,128)(2,1)S(1)}, u32[]{:S(2)}, u32[]{:S(2)}) collective-permute-start(bf16[128,640]{1,0:T(8,128)(2,1)S(1)} %get-tuple-element.31.own), channel_id=1, source_target_pairs={{0,4},{4,0},{8,12},{12,8},{1,5},{5,1},{9,13},{13,9},{2,6},{6,2},{1... | collective-permute-start | bytes 491528 | tf_op jit(solution)/shard_map/ppermute | solution.py:17
  6.3 1.5 %collective-permute-start.3 = (bf16[128,512]{1,0:T(8,128)(2,1)S(1)}, bf16[128,512]{1,0:T(8,128)(2,1)S(1)}, u32[]{:S(2)}, u32[]{:S(2)}) collective-permute-start(bf16[128,512]{1,0:T(8,128)(2,1)S(1)} %copy-done), channel_id=1, source_target_pairs={{0,2},{1,3},{2,0},{3,1},{4,6},{5,7},{6,4},{7,5},{8,10},{9,11},{10,... | collective-permute-start | bytes 393224 | tf_op jit(solution)/shard_map/ppermute | solution.py:17
  7.8 0.5 shard_map.88
  8.3 0.5 %collective-permute-start.6 = (bf16[128,384]{1,0:T(8,128)(2,1)S(1)}, bf16[128,384]{1,0:T(8,128)(2,1)S(1)}, u32[]{:S(2)}, u32[]{:S(2)}) collective-permute-start(bf16[128,384]{1,0:T(8,128)(2,1)S(1)} %get-tuple-element.43.own), channel_id=1, source_target_pairs={{0,4},{4,0},{8,12},{12,8},{1,5},{5,1},{9,13},{13,9},{2,6},{6,2},{1... | collective-permute-start | bytes 294920 | tf_op jit(solution)/shard_map/ppermute | solution.py:17
  8.8 3.1 %collective-permute-done.3.c = bf16[128,512]{1,0:T(8,128)(2,1)S(1)} collective-permute-done((bf16[128,512]{1,0:T(8,128)(2,1)S(1)}, bf16[128,512]{1,0:T(8,128)(2,1)S(1)}, u32[]{:S(2)}, u32[]{:S(2)}) %collective-permute-start.3) | collective-permute-done | bytes 131104 | tf_op jit(solution)/shard_map/ppermute | solution.py:17
  12.1 3.5 %collective-permute-start.1 = (bf16[128,256]{1,0:T(8,128)(2,1)S(1)}, bf16[128,256]{1,0:T(8,128)(2,1)S(1)}, u32[]{:S(2)}, u32[]{:S(2)}) collective-permute-start(bf16[128,256]{1,0:T(8,128)(2,1)S(1)} %shard_map.83.seen.own), channel_id=1, source_target_pairs={{0,12},{4,8},{8,4},{12,0},{1,13},{5,9},{9,5},{13,1},{2,14},{6,10},... | collective-permute-start | bytes 196616 | tf_op jit(solution)/shard_map/ppermute | solution.py:17
  16.2 2.7 %collective-permute-done.1.far = bf16[128,256]{1,0:T(8,128)(2,1)S(1)} collective-permute-done((bf16[128,256]{1,0:T(8,128)(2,1)S(1)}, bf16[128,256]{1,0:T(8,128)(2,1)S(1)}, u32[]{:S(2)}, u32[]{:S(2)}) %collective-permute-start.1) | collective-permute-done | bytes 65568 | tf_op jit(solution)/shard_map/ppermute | solution.py:17
  18.9 0.8 %shard_map.86 = (bf16[640,256]{1,0:T(8,128)(2,1)S(1)}, bf16[128,256]{1,0:T(8,128)(2,1)S(1)}, f32[128,256]{1,0:T(8,128)S(1)}) custom-call(f32[640,256]{1,0:T(8,128)S(1)} %shard_map.84.x1, bf16[128,256]{1,0:T(8,128)(2,1)S(1)} %shard_map.83.seen.own, bf16[128,256]{1,0:T(8,128)(2,1)S(1)} %collective-permute-done.1.far, ...), custom_call_target="tpu_custom_call" | custom-call | flops 1000000000 | tf_op jit(solution)/shard_map/pallas_call | solution.py:88
  19.7 0.6 %collective-permute-start.8 = (bf16[128,256]{1,0:T(8,128)(2,1)S(1)}, bf16[128,256]{1,0:T(8,128)(2,1)S(1)}, u32[]{:S(2)}, u32[]{:S(2)}) collective-permute-start(bf16[128,256]{1,0:T(8,128)(2,1)S(1)} %get-tuple-element.48), channel_id=1, source_target_pairs={{0,4},{4,0},{8,12},{12,8},{1,5},{5,1},{9,13},{13,9},{2,6},{6,2},{1... | collective-permute-start | bytes 196616 | tf_op jit(solution)/shard_map/ppermute | solution.py:17
  20.4 3.0 %collective-permute-start.11 = (bf16[128,384]{1,0:T(8,128)(2,1)S(1)}, bf16[128,384]{1,0:T(8,128)(2,1)S(1)}, u32[]{:S(2)}, u32[]{:S(2)}) collective-permute-start(bf16[128,384]{1,0:T(8,128)(2,1)S(1)} %shard_map.89.seen.gram), channel_id=1, source_target_pairs={{0,12},{4,8},{8,4},{12,0},{1,13},{5,9},{9,5},{13,1},{2,14},{6,10},... | collective-permute-start | bytes 294920 | tf_op jit(solution)/shard_map/ppermute | solution.py:17
  23.4 1.7 %collective-permute-done.8.other = bf16[128,256]{1,0:T(8,128)(2,1)S(1)} collective-permute-done((bf16[128,256]{1,0:T(8,128)(2,1)S(1)}, bf16[128,256]{1,0:T(8,128)(2,1)S(1)}, u32[]{:S(2)}, u32[]{:S(2)}) %collective-permute-start.8) | collective-permute-done | bytes 65568 | tf_op jit(solution)/shard_map/ppermute | solution.py:17
  25.1 3.1 %collective-permute-start.10 = (bf16[128,256]{1,0:T(8,128)(2,1)S(1)}, bf16[128,256]{1,0:T(8,128)(2,1)S(1)}, u32[]{:S(2)}, u32[]{:S(2)}) collective-permute-start(bf16[128,256]{1,0:T(8,128)(2,1)S(1)} %get-tuple-element.52), channel_id=1, source_target_pairs={{0,12},{4,8},{8,4},{12,0},{1,13},{5,9},{9,5},{13,1},{2,14},{6,10},... | collective-permute-start | bytes 196616 | tf_op jit(solution)/shard_map/ppermute | solution.py:17
  28.6 2.6 %collective-permute-done.10.far = bf16[128,256]{1,0:T(8,128)(2,1)S(1)} collective-permute-done((bf16[128,256]{1,0:T(8,128)(2,1)S(1)}, bf16[128,256]{1,0:T(8,128)(2,1)S(1)}, u32[]{:S(2)}, u32[]{:S(2)}) %collective-permute-start.10) | collective-permute-done | bytes 65568 | tf_op jit(solution)/shard_map/ppermute | solution.py:17
  31.2 1.6 %collective-permute-start.13 = (bf16[128,384]{1,0:T(8,128)(2,1)S(1)}, bf16[128,384]{1,0:T(8,128)(2,1)S(1)}, u32[]{:S(2)}, u32[]{:S(2)}) collective-permute-start(bf16[128,384]{1,0:T(8,128)(2,1)S(1)} %shard_map.93.a), channel_id=1, source_target_pairs={{0,2},{1,3},{2,0},{3,1},{4,6},{5,7},{6,4},{7,5},{8,10},{9,11},{10,... | collective-permute-start | bytes 294920 | tf_op jit(solution)/shard_map/ppermute | solution.py:17
  32.8 0.8 %collective-permute-done.5.other.z_sib = bf16[128,512]{1,0:T(8,128)(2,1)S(1)} collective-permute-done((bf16[128,512]{1,0:T(8,128)(2,1)S(1)}, bf16[128,512]{1,0:T(8,128)(2,1)S(1)}, u32[]{:S(2)}, u32[]{:S(2)}) %collective-permute-start.5) | collective-permute-done | bytes 131104 | tf_op jit(solution)/shard_map/ppermute | solution.py:17
  33.7 2.2 %collective-permute-done.13.c = bf16[128,384]{1,0:T(8,128)(2,1)S(1)} collective-permute-done((bf16[128,384]{1,0:T(8,128)(2,1)S(1)}, bf16[128,384]{1,0:T(8,128)(2,1)S(1)}, u32[]{:S(2)}, u32[]{:S(2)}) %collective-permute-start.13) | collective-permute-done | bytes 98336 | tf_op jit(solution)/shard_map/ppermute | solution.py:17
  35.9 3.2 %collective-permute-start.7 = (bf16[128,256]{1,0:T(8,128)(2,1)S(1)}, bf16[128,256]{1,0:T(8,128)(2,1)S(1)}, u32[]{:S(2)}, u32[]{:S(2)}) collective-permute-start(bf16[128,256]{1,0:T(8,128)(2,1)S(1)} %get-tuple-element.44), channel_id=1, source_target_pairs={{0,12},{4,8},{8,4},{12,0},{1,13},{5,9},{9,5},{13,1},{2,14},{6,10},... | collective-permute-start | bytes 196616 | tf_op jit(solution)/shard_map/ppermute | solution.py:17
  39.1 0.7 %shard_map.94.back = bf16[128,256]{1,0:T(8,128)(2,1)S(1)} custom-call(bf16[128,384]{1,0:T(8,128)(2,1)S(1)} %shard_map.93.a, bf16[128,384]{1,0:T(8,128)(2,1)S(1)} %collective-permute-done.12.b, bf16[128,384]{1,0:T(8,128)(2,1)S(1)} %collective-permute-done.13.c, bf16[128,384]{1,0:T(8,128)(2,1)S(1)} %collective-permute-done.14.d, ...), custom_call_target="tpu_custom_call" | custom-call | flops 1000000000 | tf_op jit(solution)/shard_map/pallas_call | solution.py:88
  39.9 2.4 %collective-permute-done.7.seen.down5_far = bf16[128,256]{1,0:T(8,128)(2,1)S(1)} collective-permute-done((bf16[128,256]{1,0:T(8,128)(2,1)S(1)}, bf16[128,256]{1,0:T(8,128)(2,1)S(1)}, u32[]{:S(2)}, u32[]{:S(2)}) %collective-permute-start.7) | collective-permute-done | bytes 65568 | tf_op jit(solution)/shard_map/ppermute | solution.py:17
  42.3 0.9 %shard_map.91 = (f32[640,256]{1,0:T(8,128)S(1)}, bf16[640,512]{1,0:T(8,128)(2,1)S(1)}) custom-call(bf16[640,256]{1,0:T(8,128)(2,1)S(1)} %get-tuple-element.38.x2, bf16[2,1,640,128]{3,2,1,0:T(8,128)(2,1)S(1)} %get-tuple-element.39.rb, bf16[1,640,128]{2,1,0:T(8,128)(2,1)S(1)} %get-tuple-element.35.tl, bf16[1,640,128]{2,1,0:T(8,128)(2,1)S(1)} %get-tuple-element.36.tr, ...), custom_call_target="tpu_custom_call" | custom-call | flops 1000000000 | tf_op jit(solution)/shard_map/pallas_call | solution.py:88
  43.2 1.0 %collective-permute-done.15.back_sib = bf16[128,256]{1,0:T(8,128)(2,1)S(1)} collective-permute-done((bf16[128,256]{1,0:T(8,128)(2,1)S(1)}, bf16[128,256]{1,0:T(8,128)(2,1)S(1)}, u32[]{:S(2)}, u32[]{:S(2)}) %collective-permute-start.15) | collective-permute-done | bytes 65568 | tf_op jit(solution)/shard_map/ppermute | solution.py:17
  44.1 1.8 %shard_map.95 = f32[1,640,256]{2,1,0:T(8,128)} custom-call(f32[640,256]{1,0:T(8,128)S(1)} %get-tuple-element.45.out2, bf16[640,512]{1,0:T(8,128)(2,1)S(1)} %get-tuple-element.46.under, bf16[128,256]{1,0:T(8,128)(2,1)S(1)} %shard_map.94.back, bf16[128,256]{1,0:T(8,128)(2,1)S(1)} %collective-permute-done.15.back_sib, f32[128,256]{1,0:T(8,128)S(1)} %get-tuple-element.54.down5, ...), custom_call_target="tpu_custom_call" | custom-call | flops 1000000000 | tf_op jit(solution)/shard_map/pallas_call | solution.py:88
  (24 shorter events, 1.3 us)
Async XLA Ops:
  0.0 3.2 %copy-start = (bf16[128,512]{1,0:T(8,128)(2,1)S(1)}, bf16[128,512]{1,0:T(8,128)(2,1)}, u32[]{:S(2)}) copy-start(bf16[128,512]{1,0:T(8,128)(2,1)} %a.1) | copy-start | bytes 393220
  3.2 4.7 %collective-permute-start.2 = (bf16[128,512]{1,0:T(8,128)(2,1)S(1)}, bf16[128,512]{1,0:T(8,128)(2,1)S(1)}, u32[]{:S(2)}, u32[]{:S(2)}) collective-permute-start(bf16[128,512]{1,0:T(8,128)(2,1)S(1)} %copy-done), channel_id=1, source_target_pairs={{0,1},{1,0},{2,3},{3,2},{4,5},{5,4},{6,7},{7,6},{8,9},{9,8},{10,11... | collective-permute-start | bytes 393224 | tf_op jit(solution)/shard_map/ppermute | solution.py:17
  3.7 8.2 %collective-permute-start = (bf16[128,640]{1,0:T(8,128)(2,1)S(1)}, bf16[128,640]{1,0:T(8,128)(2,1)S(1)}, u32[]{:S(2)}, u32[]{:S(2)}) collective-permute-start(bf16[128,640]{1,0:T(8,128)(2,1)S(1)} %get-tuple-element.31.own), channel_id=1, source_target_pairs={{0,4},{4,0},{8,12},{12,8},{1,5},{5,1},{9,13},{13,9},{2,6},{6,2},{1... | collective-permute-start | bytes 491528 | tf_op jit(solution)/shard_map/ppermute | solution.py:17
  6.3 5.6 %collective-permute-start.3 = (bf16[128,512]{1,0:T(8,128)(2,1)S(1)}, bf16[128,512]{1,0:T(8,128)(2,1)S(1)}, u32[]{:S(2)}, u32[]{:S(2)}) collective-permute-start(bf16[128,512]{1,0:T(8,128)(2,1)S(1)} %copy-done), channel_id=1, source_target_pairs={{0,2},{1,3},{2,0},{3,1},{4,6},{5,7},{6,4},{7,5},{8,10},{9,11},{10,... | collective-permute-start | bytes 393224 | tf_op jit(solution)/shard_map/ppermute | solution.py:17
  8.3 12.0 %collective-permute-start.6 = (bf16[128,384]{1,0:T(8,128)(2,1)S(1)}, bf16[128,384]{1,0:T(8,128)(2,1)S(1)}, u32[]{:S(2)}, u32[]{:S(2)}) collective-permute-start(bf16[128,384]{1,0:T(8,128)(2,1)S(1)} %get-tuple-element.43.own), channel_id=1, source_target_pairs={{0,4},{4,0},{8,12},{12,8},{1,5},{5,1},{9,13},{13,9},{2,6},{6,2},{1... | collective-permute-start | bytes 294920 | tf_op jit(solution)/shard_map/ppermute | solution.py:17
  11.9 4.1 %collective-permute-start.4 = (bf16[128,512]{1,0:T(8,128)(2,1)S(1)}, bf16[128,512]{1,0:T(8,128)(2,1)S(1)}, u32[]{:S(2)}, u32[]{:S(2)}) collective-permute-start(bf16[128,512]{1,0:T(8,128)(2,1)S(1)} %collective-permute-done.3.c), channel_id=1, source_target_pairs={{0,1},{1,0},{2,3},{3,2},{4,5},{5,4},{6,7},{7,6},{8,9},{9,8},{10,11... | collective-permute-start | bytes 393224 | tf_op jit(solution)/shard_map/ppermute | solution.py:17
  12.1 6.8 %collective-permute-start.1 = (bf16[128,256]{1,0:T(8,128)(2,1)S(1)}, bf16[128,256]{1,0:T(8,128)(2,1)S(1)}, u32[]{:S(2)}, u32[]{:S(2)}) collective-permute-start(bf16[128,256]{1,0:T(8,128)(2,1)S(1)} %shard_map.83.seen.own), channel_id=1, source_target_pairs={{0,12},{4,8},{8,4},{12,0},{1,13},{5,9},{9,5},{13,1},{2,14},{6,10},... | collective-permute-start | bytes 196616 | tf_op jit(solution)/shard_map/ppermute | solution.py:17
  15.6 7.8 %collective-permute-start.9 = (bf16[128,640]{1,0:T(8,128)(2,1)S(1)}, bf16[128,640]{1,0:T(8,128)(2,1)S(1)}, u32[]{:S(2)}, u32[]{:S(2)}) collective-permute-start(bf16[128,640]{1,0:T(8,128)(2,1)S(1)} %get-tuple-element.50.late), channel_id=1, source_target_pairs={{0,4},{4,0},{8,12},{12,8},{1,5},{5,1},{9,13},{13,9},{2,6},{6,2},{1... | collective-permute-start | bytes 491528 | tf_op jit(solution)/shard_map/ppermute | solution.py:17
  19.7 5.4 %collective-permute-start.8 = (bf16[128,256]{1,0:T(8,128)(2,1)S(1)}, bf16[128,256]{1,0:T(8,128)(2,1)S(1)}, u32[]{:S(2)}, u32[]{:S(2)}) collective-permute-start(bf16[128,256]{1,0:T(8,128)(2,1)S(1)} %get-tuple-element.48), channel_id=1, source_target_pairs={{0,4},{4,0},{8,12},{12,8},{1,5},{5,1},{9,13},{13,9},{2,6},{6,2},{1... | collective-permute-start | bytes 196616 | tf_op jit(solution)/shard_map/ppermute | solution.py:17
  20.4 8.3 %collective-permute-start.11 = (bf16[128,384]{1,0:T(8,128)(2,1)S(1)}, bf16[128,384]{1,0:T(8,128)(2,1)S(1)}, u32[]{:S(2)}, u32[]{:S(2)}) collective-permute-start(bf16[128,384]{1,0:T(8,128)(2,1)S(1)} %shard_map.89.seen.gram), channel_id=1, source_target_pairs={{0,12},{4,8},{8,4},{12,0},{1,13},{5,9},{9,5},{13,1},{2,14},{6,10},... | collective-permute-start | bytes 294920 | tf_op jit(solution)/shard_map/ppermute | solution.py:17
  25.1 6.1 %collective-permute-start.10 = (bf16[128,256]{1,0:T(8,128)(2,1)S(1)}, bf16[128,256]{1,0:T(8,128)(2,1)S(1)}, u32[]{:S(2)}, u32[]{:S(2)}) collective-permute-start(bf16[128,256]{1,0:T(8,128)(2,1)S(1)} %get-tuple-element.52), channel_id=1, source_target_pairs={{0,12},{4,8},{8,4},{12,0},{1,13},{5,9},{9,5},{13,1},{2,14},{6,10},... | collective-permute-start | bytes 196616 | tf_op jit(solution)/shard_map/ppermute | solution.py:17
  28.5 5.0 %collective-permute-start.5 = (bf16[128,512]{1,0:T(8,128)(2,1)S(1)}, bf16[128,512]{1,0:T(8,128)(2,1)S(1)}, u32[]{:S(2)}, u32[]{:S(2)}) collective-permute-start(bf16[128,512]{1,0:T(8,128)(2,1)S(1)} %get-tuple-element.42.z), channel_id=1, source_target_pairs={{0,4},{4,0},{8,12},{12,8},{1,5},{5,1},{9,13},{13,9},{2,6},{6,2},{1... | collective-permute-start | bytes 393224 | tf_op jit(solution)/shard_map/ppermute | solution.py:17
  31.2 4.7 %collective-permute-start.13 = (bf16[128,384]{1,0:T(8,128)(2,1)S(1)}, bf16[128,384]{1,0:T(8,128)(2,1)S(1)}, u32[]{:S(2)}, u32[]{:S(2)}) collective-permute-start(bf16[128,384]{1,0:T(8,128)(2,1)S(1)} %shard_map.93.a), channel_id=1, source_target_pairs={{0,2},{1,3},{2,0},{3,1},{4,6},{5,7},{6,4},{7,5},{8,10},{9,11},{10,... | collective-permute-start | bytes 294920 | tf_op jit(solution)/shard_map/ppermute | solution.py:17
  33.6 5.5 %collective-permute-start.12 = (bf16[128,384]{1,0:T(8,128)(2,1)S(1)}, bf16[128,384]{1,0:T(8,128)(2,1)S(1)}, u32[]{:S(2)}, u32[]{:S(2)}) collective-permute-start(bf16[128,384]{1,0:T(8,128)(2,1)S(1)} %shard_map.93.a), channel_id=1, source_target_pairs={{0,1},{1,0},{2,3},{3,2},{4,5},{5,4},{6,7},{7,6},{8,9},{9,8},{10,11... | collective-permute-start | bytes 294920 | tf_op jit(solution)/shard_map/ppermute | solution.py:17
  35.9 3.2 %collective-permute-start.14 = (bf16[128,384]{1,0:T(8,128)(2,1)S(1)}, bf16[128,384]{1,0:T(8,128)(2,1)S(1)}, u32[]{:S(2)}, u32[]{:S(2)}) collective-permute-start(bf16[128,384]{1,0:T(8,128)(2,1)S(1)} %collective-permute-done.13.c), channel_id=1, source_target_pairs={{0,1},{1,0},{2,3},{3,2},{4,5},{5,4},{6,7},{7,6},{8,9},{9,8},{10,11... | collective-permute-start | bytes 294920 | tf_op jit(solution)/shard_map/ppermute | solution.py:17
  35.9 6.4 %collective-permute-start.7 = (bf16[128,256]{1,0:T(8,128)(2,1)S(1)}, bf16[128,256]{1,0:T(8,128)(2,1)S(1)}, u32[]{:S(2)}, u32[]{:S(2)}) collective-permute-start(bf16[128,256]{1,0:T(8,128)(2,1)S(1)} %get-tuple-element.44), channel_id=1, source_target_pairs={{0,12},{4,8},{8,4},{12,0},{1,13},{5,9},{9,5},{13,1},{2,14},{6,10},... | collective-permute-start | bytes 196616 | tf_op jit(solution)/shard_map/ppermute | solution.py:17
  39.8 4.3 %collective-permute-start.15 = (bf16[128,256]{1,0:T(8,128)(2,1)S(1)}, bf16[128,256]{1,0:T(8,128)(2,1)S(1)}, u32[]{:S(2)}, u32[]{:S(2)}) collective-permute-start(bf16[128,256]{1,0:T(8,128)(2,1)S(1)} %shard_map.94.back), channel_id=1, source_target_pairs={{0,4},{4,0},{8,12},{12,8},{1,5},{5,1},{9,13},{13,9},{2,6},{6,2},{1... | collective-permute-start | bytes 196616 | tf_op jit(solution)/shard_map/ppermute | solution.py:17

commit v7 on v6

--- a/solution.py
+++ b/solution.py
@@ -222,30 +222,26 @@
     caps_here = after(top_caps, pair_send)
     caps_near = swap(caps_here, "top", 1)
     caps_far = swap(caps_here, "top", 2)
-    caps_far_near = swap(caps_far, "top", 1)
-
-    def grams_body(lb, rb, caps, tl, tr, seen, out, late):
+
+    def grams_body(lb, rb, caps, tl, tr, out):
         out[:, span(0)] = (dot_t(tl[0], tl[0]) * st).astype(BF)
         for i, basis in enumerate((tl[0], tr[0])):
             out[:, span(1 + i)] = (dot_t(lb[1, 0], basis) * s2).astype(BF)
         for i, basis in enumerate((tl[0], tr[0], rb[1, 0])):
-            late[:, span(i)] = (dot_t(lb[0, 0], basis) * s1).astype(BF)
-        late[:, span(3, 2)] = caps[1, 0]
-
-    grams, late = call(
+            out[:, span(3 + i)] = (dot_t(lb[0, 0], basis) * s1).astype(BF)
+        out[:, span(6, 2)] = caps[1, 0]
+
+    (grams,) = call(
         grams_body,
-        [((rank, 3 * rank), BF), ((rank, 5 * rank), BF)],
+        [((rank, 8 * rank), BF)],
         lb,
         rb,
         caps,
         tl,
         tr,
-        caps_near,
-        micros=10,
-    )
-    grams_sib = swap(grams, "leaf", 1)
-
-    def half_body(keep, own, sib, out):
+        micros=0.5,
+    )
+    def half_body(keep, own, sib, seen, out):
         out[...] = (
             keep[...]
             + sib[:, cols : 2 * cols]
@@ -253,31 +249,9 @@
             - dot(sib[:, 2 * cols :], own[:, :cols])
         ).astype(BF)
 
-    (half2,) = call(half_body, [(wide, BF)], pair_keep, pair_send, pair_in, micros=3)
+    (half2,) = call(half_body, [(wide, BF)], pair_keep, pair_send, pair_in, grams, micros=0.2)
     half2_far = swap(half2, "leaf", 3)
-    late_sib = swap(after(late, half2), "leaf", 1)
-
-    def order_body(a, b, c, d, seen, out):
-        here = lax.axis_index("top")
-        for i, piece in enumerate((a, b, c, d)):
-            for k in range(4):
-                out[span(i), span(k)] = piece[:, block(here ^ k, rank)]
-
-    (caps_all,) = call(
-        order_body,
-        [((4 * rank, 4 * rank), BF)],
-        top_caps,
-        caps_near,
-        caps_far,
-        caps_far_near,
-        half2,
-    )
-
-    def sum_body(own, sib, seen, out):
-        out[...] = (own[...].astype(f32) + sib[...]).astype(BF)
-
-    (gram_pair,) = call(sum_body, [((rank, 3 * rank), BF)], grams, grams_sib, half2)
-    gram_far = swap(gram_pair, "leaf", 3)
+    grams_sib = swap(after(grams, half2), "leaf", 1)
 
     def one_body(x0, own, sib, lb, caps, seen, x1, stack):
         put_rows(stack, tree_side(0), own[:, :cols], sib[:, :cols])
@@ -294,9 +268,16 @@
         caps,
         half2,
         scratch=[pltpu.VMEM((2 * rank, cols), BF)],
-    )
-
-    def two_body(x1, own, far, lb, caps, tl, tr, seen, x2, send, keep, stack, scratch):
+        micros=0.4,
+    )
+
+    def sum_body(own, sib, out):
+        out[...] = (own[:, span(0, 3)].astype(f32) + sib[:, span(0, 3)]).astype(BF)
+
+    (gram_pair,) = call(sum_body, [((rank, 3 * rank), BF)], grams, grams_sib, micros=0.1)
+    gram_far = swap(gram_pair, "leaf", 3)
+
+    def two_body(x1, own, far, lb, caps, tl, tr, x2, send, keep, stack, scratch):
         side = column_side()
         put_rows(stack, tree_side(1), own[...], far[...])
         coef = dot(caps[1, 0], stack[...]).astype(BF)
@@ -316,29 +297,49 @@
         caps,
         tl,
         tr,
-        caps_all,
         scratch=[pltpu.VMEM((2 * rank, cols), BF), pltpu.VMEM(wide, f32)],
+        micros=5,
     )
     top_pair_in = swap(top_pair_send, "leaf", 1)
+
+    caps_far_near = swap(after(caps_far, state2), "top", 1)
+
+    def order_body(a, b, c, d, out):
+        here = lax.axis_index("top")
+        for i, piece in enumerate((a, b, c, d)):
+            for k in range(4):
+                out[span(i), span(k)] = piece[:, block(here ^ k, rank)]
+
+    (caps_all,) = call(
+        order_body,
+        [((4 * rank, 4 * rank), BF)],
+        top_caps,
+        caps_near,
+        caps_far,
+        caps_far_near,
+        micros=0.1,
+    )
+
 
     def down_body(lb, x2, z5, z):
         z5[...] = dot_t(lb[1, 0], x2[...]) * s2
         z[:, :cols] = z5[...].astype(BF)
         z[:, cols:] = (dot_t(lb[0, 0], x2[...]) * s1).astype(BF)
 
-    down5, down_send = call(down_body, [(wide, f32), ((rank, 2 * cols), BF)], lb, state2)
+    down5, down_send = call(
+        down_body, [(wide, f32), ((rank, 2 * cols), BF)], lb, state2, micros=0.3
+    )
     down_in = swap(down_send, "leaf", 1)
 
-    def add_body(own, other, seen, out, out_b):
+    def add_body(own, other, seen, seen2, out, out_b):
         out[...] = own[...] + other[:, :cols]
         out_b[...] = out[...].astype(BF)
 
-    top_half, top_half_send = call(add_body, [(wide, f32), (wide, BF)], top_keep, top_pair_in, late_sib)
+    top_half, top_half_send = call(add_body, [(wide, f32), (wide, BF)], top_keep, top_pair_in, gram_pair, caps_all, micros=0.1)
     top_half_far = swap(top_half_send, "leaf", 3)
     down5, down5_send = call(
-        add_body, [(wide, f32), (wide, BF)], down5, down_in, gram_pair
-    )
-    down5_far = swap(down5_send, "leaf", 3)
+        add_body, [(wide, f32), (wide, BF)], down5, down_in, gram_pair, caps_all, micros=0.1
+    )
 
     def column_body(own, far, gram, gram_far, out):
         out[:, : 2 * half] = (own[...] + far[...]).astype(BF)
@@ -353,7 +354,7 @@
         gram_far,
     )
     top_far = swap(top_send, "top", 2)
-    top_near = swap(after(top_send, down5_send), "top", 1)
+    top_near = swap(top_send, "top", 1)
     top_parts = top_send, top_near, top_far, swap(top_far, "top", 1)
 
     def under_body(x2, rb, tl, tr, inv, seen, out2, under):
@@ -371,10 +372,10 @@
         tl,
         tr,
         inverse,
-        down5_far,
-    )
-
-    def top_body(a, b, c, d, caps, out, up, down):
+        top_send,
+    )
+
+    def top_body(a, b, c, d, caps, seen, out, up, down):
         pieces = (a, b, c, d)
         for i, piece in enumerate(pieces):
             up[span(i), :] = piece[:, part(0)]
@@ -391,12 +392,14 @@
         [(wide, BF)],
         *top_parts,
         caps_all,
+        out2,
         scratch=[pltpu.VMEM((4 * rank, half), BF)] * 2,
     )
+    down5_far = swap(after(down5_send, back_send), "leaf", 3)
     back_in = swap(back_send, "leaf", 1)
 
     def last_body(
-        out2, under, back, back_sib, down5, down5_far, gram, gram_far, late, late_sib,
+        out2, under, back, back_sib, down5, down5_far, gram, gram_far, grams, grams_sib,
         z, z_sib, caps, out, coefs, stack, out_v, sems,
     ):
         side = column_side()
@@ -410,15 +413,15 @@
             (down5_far[...] - dot(gram_far[:, span(1, 2)], both)).astype(BF),
         )
         coef5 = dot(caps[1, 0], stack[...]).astype(BF)
-        coef5_sib = dot(late_sib[:, span(3, 2)], stack[...]).astype(BF)
+        coef5_sib = dot(grams_sib[:, span(6, 2)], stack[...]).astype(BF)
         coefs[span(2), :] = coef5
 
-        def proj(zs, grams, coef):
+        def proj(zs, gram1, coef):
             return (
-                zs[:, cols:] - dot(grams[:, span(0, 2)], both) - dot(grams[:, span(2)], coef)
+                zs[:, cols:] - dot(gram1[:, span(3, 2)], both) - dot(gram1[:, span(5)], coef)
             ).astype(BF)
 
-        put_rows(stack, tree_side(0), proj(z, late, coef5), proj(z_sib, late_sib, coef5_sib))
+        put_rows(stack, tree_side(0), proj(z, grams, coef5), proj(z_sib, grams_sib, coef5_sib))
         coefs[span(3), :] = dot(caps[0, 0], stack[...]).astype(BF)
         copies = []
         for c in range(blocks):
@@ -440,8 +443,8 @@
         down5_far,
         gram_pair,
         gram_far,
-        late,
-        late_sib,
+        grams,
+        grams_sib,
         down_send,
         down_in,
         caps,

time: 46.1 us -> 49.3 us (1.069)
  waiting for transfers between devices: 16.5 us -> 25.6 us
  starting transfers between devices: 20.5 us -> 14.7 us
    ppermute x16 -> x15, waiting for transfers between devices: 16.5 us -> 25.6 us  [swap(): return lax.ppermute(value, axis, pairs)]
    ppermute x16 -> x15, starting transfers between devices: 20.5 us -> 14.7 us  [swap(): return lax.ppermute(value, axis, pairs)]
  transfers between devices with their start and end apart: 16 -> 15, of which waited for: 8 -> 9; matrix products, arithmetic and copies ran while one was open for 0% -> 0% of each run, Pallas kernels for 8% -> 6%
where the time goes in v7:
time: 49.3 us; the launch traced here: 49.1 us
  waiting for transfers between devices  25.6 us (52%)
  starting transfers between devices  14.7 us (30%)
  Pallas kernels  8.79 us (18%)
    ppermute x15, waiting for transfers between devices, swap(): return lax.ppermute(value, axis, pairs)  25.6 us
    ppermute x15, starting transfers between devices, swap(): return lax.ppermute(value, axis, pairs)  14.7 us
    pallas_call x14, Pallas kernels, call(): pl.pallas_call(body, out_shape=[jax.ShapeDtypeStruct(shape, dtype) if hbm...  8.79 us
  transfers between devices with their start and end apart: 15, of which 9 were waited for; matrix products, arithmetic and copies ran while one was open for 0% of the time, Pallas kernels for 6%

profile of v7, /device:TPU:0, one launch (start us, length us, event | category | flops | bytes accessed | tf_op | source)
XLA Modules:
  0.0 49.1 jit_solution(7198539356681222344)
XLA Ops:
  0.0 3.1 %shard_map.82 = (f32[640,256]{1,0:T(8,128)S(1)}, bf16[128,640]{1,0:T(8,128)(2,1)S(1)}, f32[128,256]{1,0:T(8,128)S(1)}, bf16[640,640]{1,0:T(8,128)(2,1)S(1)}, bf1...) custom-call(f32[1,640,256]{2,1,0:T(8,128)} %rhs_hbm.1, ...), custom_call_target="tpu_custom_call" | custom-call | flops 1000000000 | tf_op jit(solution)/shard_map/pallas_call | solution.py:88
  3.1 3.1 %collective-permute-start = (bf16[128,640]{1,0:T(8,128)(2,1)S(1)}, bf16[128,640]{1,0:T(8,128)(2,1)S(1)}, u32[]{:S(2)}, u32[]{:S(2)}) collective-permute-start(bf16[128,640]{1,0:T(8,128)(2,1)S(1)} %get-tuple-element.30.own), channel_id=1, source_target_pairs={{0,4},{4,0},{8,12},{12,8},{1,5},{5,1},{9,13},{13,9},{2,6},{6,2},{1... | collective-permute-start | bytes 491528 | tf_op jit(solution)/shard_map/ppermute | solution.py:17
  6.2 0.5 shard_map.83.seen.own.grams
  6.7 3.7 %collective-permute-done.sib = bf16[128,640]{1,0:T(8,128)(2,1)S(1)} collective-permute-done((bf16[128,640]{1,0:T(8,128)(2,1)S(1)}, bf16[128,640]{1,0:T(8,128)(2,1)S(1)}, u32[]{:S(2)}, u32[]{:S(2)}) %collective-permute-start) | collective-permute-done | bytes 163872 | tf_op jit(solution)/shard_map/ppermute | solution.py:17
  10.6 3.8 %collective-permute-start.1 = (bf16[128,256]{1,0:T(8,128)(2,1)S(1)}, bf16[128,256]{1,0:T(8,128)(2,1)S(1)}, u32[]{:S(2)}, u32[]{:S(2)}) collective-permute-start(bf16[128,256]{1,0:T(8,128)(2,1)S(1)} %shard_map.84.seen.own), channel_id=1, source_target_pairs={{0,12},{4,8},{8,4},{12,0},{1,13},{5,9},{9,5},{13,1},{2,14},{6,10},... | collective-permute-start | bytes 196616 | tf_op jit(solution)/shard_map/ppermute | solution.py:17
  14.4 1.5 %collective-permute-start.5 = (bf16[128,512]{1,0:T(8,128)(2,1)S(1)}, bf16[128,512]{1,0:T(8,128)(2,1)S(1)}, u32[]{:S(2)}, u32[]{:S(2)}) collective-permute-start(bf16[128,512]{1,0:T(8,128)(2,1)S(1)} %copy-done), channel_id=1, source_target_pairs={{0,2},{1,3},{2,0},{3,1},{4,6},{5,7},{6,4},{7,5},{8,10},{9,11},{10,... | collective-permute-start | bytes 393224 | tf_op jit(solution)/shard_map/ppermute | solution.py:17
  15.9 0.4 shard_map.85.x1
  16.4 0.4 collective-permute-done.1.far
  16.8 0.8 %shard_map.86 = (bf16[640,256]{1,0:T(8,128)(2,1)S(1)}, bf16[128,256]{1,0:T(8,128)(2,1)S(1)}, f32[128,256]{1,0:T(8,128)S(1)}) custom-call(f32[640,256]{1,0:T(8,128)S(1)} %shard_map.85.x1, bf16[128,256]{1,0:T(8,128)(2,1)S(1)} %shard_map.84.seen.own, bf16[128,256]{1,0:T(8,128)(2,1)S(1)} %collective-permute-done.1.far, ...), custom_call_target="tpu_custom_call" | custom-call | flops 5000000000 | tf_op jit(solution)/shard_map/pallas_call | solution.py:88
  17.6 2.8 %collective-permute-done.5.c = bf16[128,512]{1,0:T(8,128)(2,1)S(1)} collective-permute-done((bf16[128,512]{1,0:T(8,128)(2,1)S(1)}, bf16[128,512]{1,0:T(8,128)(2,1)S(1)}, u32[]{:S(2)}, u32[]{:S(2)}) %collective-permute-start.5) | collective-permute-done | bytes 131104 | tf_op jit(solution)/shard_map/ppermute | solution.py:17
  20.4 4.7 %collective-permute-done.3.sib.grams_sib = bf16[128,1024]{1,0:T(8,128)(2,1)S(1)} collective-permute-done((bf16[128,1024]{1,0:T(8,128)(2,1)S(1)}, bf16[128,1024]{1,0:T(8,128)(2,1)S(1)}, u32[]{:S(2)}, u32[]{:S(2)}) %collective-permute-start.3) | collective-permute-done | bytes 262176 | tf_op jit(solution)/shard_map/ppermute | solution.py:17
  25.1 1.2 %collective-permute-start.8 = (bf16[128,384]{1,0:T(8,128)(2,1)S(1)}, bf16[128,384]{1,0:T(8,128)(2,1)S(1)}, u32[]{:S(2)}, u32[]{:S(2)}) collective-permute-start(bf16[128,384]{1,0:T(8,128)(2,1)S(1)} %shard_map.87.seen.gram), channel_id=1, source_target_pairs={{0,12},{4,8},{8,4},{12,0},{1,13},{5,9},{9,5},{13,1},{2,14},{6,10},... | collective-permute-start | bytes 294920 | tf_op jit(solution)/shard_map/ppermute | solution.py:17
  26.4 2.8 %collective-permute-start.7 = (bf16[128,256]{1,0:T(8,128)(2,1)S(1)}, bf16[128,256]{1,0:T(8,128)(2,1)S(1)}, u32[]{:S(2)}, u32[]{:S(2)}) collective-permute-start(bf16[128,256]{1,0:T(8,128)(2,1)S(1)} %get-tuple-element.45), channel_id=1, source_target_pairs={{0,12},{4,8},{8,4},{12,0},{1,13},{5,9},{9,5},{13,1},{2,14},{6,10},... | collective-permute-start | bytes 196616 | tf_op jit(solution)/shard_map/ppermute | solution.py:17
  29.2 0.3 shard_map.93
  29.6 4.1 %collective-permute-done.7.far = bf16[128,256]{1,0:T(8,128)(2,1)S(1)} collective-permute-done((bf16[128,256]{1,0:T(8,128)(2,1)S(1)}, bf16[128,256]{1,0:T(8,128)(2,1)S(1)}, u32[]{:S(2)}, u32[]{:S(2)}) %collective-permute-start.7) | collective-permute-done | bytes 65568 | tf_op jit(solution)/shard_map/ppermute | solution.py:17
  33.9 4.5 %collective-permute-done.10.c = bf16[128,384]{1,0:T(8,128)(2,1)S(1)} collective-permute-done((bf16[128,384]{1,0:T(8,128)(2,1)S(1)}, bf16[128,384]{1,0:T(8,128)(2,1)S(1)}, u32[]{:S(2)}, u32[]{:S(2)}) %collective-permute-start.10) | collective-permute-done | bytes 98336 | tf_op jit(solution)/shard_map/ppermute | solution.py:17
  38.4 0.9 %shard_map.91 = (f32[640,256]{1,0:T(8,128)S(1)}, bf16[640,512]{1,0:T(8,128)(2,1)S(1)}) custom-call(bf16[640,256]{1,0:T(8,128)(2,1)S(1)} %get-tuple-element.37.x2, bf16[2,1,640,128]{3,2,1,0:T(8,128)(2,1)S(1)} %get-tuple-element.34.rb, bf16[1,640,128]{2,1,0:T(8,128)(2,1)S(1)} %get-tuple-element.35.tl, bf16[1,640,128]{2,1,0:T(8,128)(2,1)S(1)} %get-tuple-element.36.tr, ...), custom_call_target="tpu_custom_call" | custom-call | flops 1000000000 | tf_op jit(solution)/shard_map/pallas_call | solution.py:88
  39.3 0.4 collective-permute-done.11.d
  39.7 0.7 %shard_map.92.back = bf16[128,256]{1,0:T(8,128)(2,1)S(1)} custom-call(bf16[128,384]{1,0:T(8,128)(2,1)S(1)} %shard_map.90.seen.a, bf16[128,384]{1,0:T(8,128)(2,1)S(1)} %collective-permute-done.9.b, bf16[128,384]{1,0:T(8,128)(2,1)S(1)} %collective-permute-done.10.c, bf16[128,384]{1,0:T(8,128)(2,1)S(1)} %collective-permute-done.11.d, ...), custom_call_target="tpu_custom_call" | custom-call | flops 1000000000 | tf_op jit(solution)/shard_map/pallas_call | solution.py:88
  40.4 0.8 %collective-permute-start.12 = (bf16[128,256]{1,0:T(8,128)(2,1)S(1)}, bf16[128,256]{1,0:T(8,128)(2,1)S(1)}, u32[]{:S(2)}, u32[]{:S(2)}) collective-permute-start(bf16[128,256]{1,0:T(8,128)(2,1)S(1)} %shard_map.92.back), channel_id=1, source_target_pairs={{0,4},{4,0},{8,12},{12,8},{1,5},{5,1},{9,13},{13,9},{2,6},{6,2},{1... | collective-permute-start | bytes 196616 | tf_op jit(solution)/shard_map/ppermute | solution.py:17
  41.2 1.3 %collective-permute-start.14 = (bf16[128,256]{1,0:T(8,128)(2,1)S(1)}, bf16[128,256]{1,0:T(8,128)(2,1)S(1)}, u32[]{:S(2)}, u32[]{:S(2)}) collective-permute-start(bf16[128,256]{1,0:T(8,128)(2,1)S(1)} %get-tuple-element.52), channel_id=1, source_target_pairs={{0,12},{4,8},{8,4},{12,0},{1,13},{5,9},{9,5},{13,1},{2,14},{6,10},... | collective-permute-start | bytes 196616 | tf_op jit(solution)/shard_map/ppermute | solution.py:17
  42.5 2.3 %collective-permute-done.12.back_sib = bf16[128,256]{1,0:T(8,128)(2,1)S(1)} collective-permute-done((bf16[128,256]{1,0:T(8,128)(2,1)S(1)}, bf16[128,256]{1,0:T(8,128)(2,1)S(1)}, u32[]{:S(2)}, u32[]{:S(2)}) %collective-permute-start.12) | collective-permute-done | bytes 65568 | tf_op jit(solution)/shard_map/ppermute | solution.py:17
  44.7 2.6 %collective-permute-done.14.down5_far = bf16[128,256]{1,0:T(8,128)(2,1)S(1)} collective-permute-done((bf16[128,256]{1,0:T(8,128)(2,1)S(1)}, bf16[128,256]{1,0:T(8,128)(2,1)S(1)}, u32[]{:S(2)}, u32[]{:S(2)}) %collective-permute-start.14) | collective-permute-done | bytes 65568 | tf_op jit(solution)/shard_map/ppermute | solution.py:17
  47.3 1.8 %shard_map.95 = f32[1,640,256]{2,1,0:T(8,128)} custom-call(f32[640,256]{1,0:T(8,128)S(1)} %get-tuple-element.46.seen.out2, bf16[640,512]{1,0:T(8,128)(2,1)S(1)} %get-tuple-element.47.under, bf16[128,256]{1,0:T(8,128)(2,1)S(1)} %shard_map.92.back, bf16[128,256]{1,0:T(8,128)(2,1)S(1)} %collective-permute-done.12.back_sib, ...), custom_call_target="tpu_custom_call" | custom-call | flops 1000000000 | tf_op jit(solution)/shard_map/pallas_call | solution.py:88
  (22 shorter events, 0.6 us)
Async XLA Ops:
  3.1 7.3 %collective-permute-start = (bf16[128,640]{1,0:T(8,128)(2,1)S(1)}, bf16[128,640]{1,0:T(8,128)(2,1)S(1)}, u32[]{:S(2)}, u32[]{:S(2)}) collective-permute-start(bf16[128,640]{1,0:T(8,128)(2,1)S(1)} %get-tuple-element.30.own), channel_id=1, source_target_pairs={{0,4},{4,0},{8,12},{12,8},{1,5},{5,1},{9,13},{13,9},{2,6},{6,2},{1... | collective-permute-start | bytes 491528 | tf_op jit(solution)/shard_map/ppermute | solution.py:17
  10.4 4.0 %copy-start = (bf16[128,512]{1,0:T(8,128)(2,1)S(1)}, bf16[128,512]{1,0:T(8,128)(2,1)}, u32[]{:S(2)}) copy-start(bf16[128,512]{1,0:T(8,128)(2,1)} %a.1) | copy-start | bytes 393220
  10.6 6.2 %collective-permute-start.1 = (bf16[128,256]{1,0:T(8,128)(2,1)S(1)}, bf16[128,256]{1,0:T(8,128)(2,1)S(1)}, u32[]{:S(2)}, u32[]{:S(2)}) collective-permute-start(bf16[128,256]{1,0:T(8,128)(2,1)S(1)} %shard_map.84.seen.own), channel_id=1, source_target_pairs={{0,12},{4,8},{8,4},{12,0},{1,13},{5,9},{9,5},{13,1},{2,14},{6,10},... | collective-permute-start | bytes 196616 | tf_op jit(solution)/shard_map/ppermute | solution.py:17
  14.4 11.8 %collective-permute-start.4 = (bf16[128,512]{1,0:T(8,128)(2,1)S(1)}, bf16[128,512]{1,0:T(8,128)(2,1)S(1)}, u32[]{:S(2)}, u32[]{:S(2)}) collective-permute-start(bf16[128,512]{1,0:T(8,128)(2,1)S(1)} %copy-done), channel_id=1, source_target_pairs={{0,1},{1,0},{2,3},{3,2},{4,5},{5,4},{6,7},{7,6},{8,9},{9,8},{10,11... | collective-permute-start | bytes 393224 | tf_op jit(solution)/shard_map/ppermute | solution.py:17
  14.4 5.9 %collective-permute-start.5 = (bf16[128,512]{1,0:T(8,128)(2,1)S(1)}, bf16[128,512]{1,0:T(8,128)(2,1)S(1)}, u32[]{:S(2)}, u32[]{:S(2)}) collective-permute-start(bf16[128,512]{1,0:T(8,128)(2,1)S(1)} %copy-done), channel_id=1, source_target_pairs={{0,2},{1,3},{2,0},{3,1},{4,6},{5,7},{6,4},{7,5},{8,10},{9,11},{10,... | collective-permute-start | bytes 393224 | tf_op jit(solution)/shard_map/ppermute | solution.py:17
  15.9 9.1 %collective-permute-start.3 = (bf16[128,1024]{1,0:T(8,128)(2,1)S(1)}, bf16[128,1024]{1,0:T(8,128)(2,1)S(1)}, u32[]{:S(2)}, u32[]{:S(2)}) collective-permute-start(bf16[128,1024]{1,0:T(8,128)(2,1)S(1)} %shard_map.83.seen.own.grams), channel_id=1, source_target_pairs={{0,4},{4,0},{8,12},{12,8},{1,5},{5,1},{9,13},{13,9},{2,6},{6,2},{1... | collective-permute-start | bytes 786440 | tf_op jit(solution)/shard_map/ppermute | solution.py:17
  20.3 5.9 %collective-permute-start.6 = (bf16[128,512]{1,0:T(8,128)(2,1)S(1)}, bf16[128,512]{1,0:T(8,128)(2,1)S(1)}, u32[]{:S(2)}, u32[]{:S(2)}) collective-permute-start(bf16[128,512]{1,0:T(8,128)(2,1)S(1)} %collective-permute-done.5.c), channel_id=1, source_target_pairs={{0,1},{1,0},{2,3},{3,2},{4,5},{5,4},{6,7},{7,6},{8,9},{9,8},{10,11... | collective-permute-start | bytes 393224 | tf_op jit(solution)/shard_map/ppermute | solution.py:17
  20.3 6.0 %collective-permute-start.2 = (bf16[128,256]{1,0:T(8,128)(2,1)S(1)}, bf16[128,256]{1,0:T(8,128)(2,1)S(1)}, u32[]{:S(2)}, u32[]{:S(2)}) collective-permute-start(bf16[128,256]{1,0:T(8,128)(2,1)S(1)} %get-tuple-element.40), channel_id=1, source_target_pairs={{0,4},{4,0},{8,12},{12,8},{1,5},{5,1},{9,13},{13,9},{2,6},{6,2},{1... | collective-permute-start | bytes 196616 | tf_op jit(solution)/shard_map/ppermute | solution.py:17
  25.1 8.6 %collective-permute-start.8 = (bf16[128,384]{1,0:T(8,128)(2,1)S(1)}, bf16[128,384]{1,0:T(8,128)(2,1)S(1)}, u32[]{:S(2)}, u32[]{:S(2)}) collective-permute-start(bf16[128,384]{1,0:T(8,128)(2,1)S(1)} %shard_map.87.seen.gram), channel_id=1, source_target_pairs={{0,12},{4,8},{8,4},{12,0},{1,13},{5,9},{9,5},{13,1},{2,14},{6,10},... | collective-permute-start | bytes 294920 | tf_op jit(solution)/shard_map/ppermute | solution.py:17
  26.4 7.3 %collective-permute-start.7 = (bf16[128,256]{1,0:T(8,128)(2,1)S(1)}, bf16[128,256]{1,0:T(8,128)(2,1)S(1)}, u32[]{:S(2)}, u32[]{:S(2)}) collective-permute-start(bf16[128,256]{1,0:T(8,128)(2,1)S(1)} %get-tuple-element.45), channel_id=1, source_target_pairs={{0,12},{4,8},{8,4},{12,0},{1,13},{5,9},{9,5},{13,1},{2,14},{6,10},... | collective-permute-start | bytes 196616 | tf_op jit(solution)/shard_map/ppermute | solution.py:17
  29.5 8.9 %collective-permute-start.13 = (bf16[128,512]{1,0:T(8,128)(2,1)S(1)}, bf16[128,512]{1,0:T(8,128)(2,1)S(1)}, u32[]{:S(2)}, u32[]{:S(2)}) collective-permute-start(bf16[128,512]{1,0:T(8,128)(2,1)S(1)} %get-tuple-element.49.z), channel_id=1, source_target_pairs={{0,4},{4,0},{8,12},{12,8},{1,5},{5,1},{9,13},{13,9},{2,6},{6,2},{1... | collective-permute-start | bytes 393224 | tf_op jit(solution)/shard_map/ppermute | solution.py:17
  33.7 4.7 %collective-permute-start.10 = (bf16[128,384]{1,0:T(8,128)(2,1)S(1)}, bf16[128,384]{1,0:T(8,128)(2,1)S(1)}, u32[]{:S(2)}, u32[]{:S(2)}) collective-permute-start(bf16[128,384]{1,0:T(8,128)(2,1)S(1)} %shard_map.90.seen.a), channel_id=1, source_target_pairs={{0,2},{1,3},{2,0},{3,1},{4,6},{5,7},{6,4},{7,5},{8,10},{9,11},{10,... | collective-permute-start | bytes 294920 | tf_op jit(solution)/shard_map/ppermute | solution.py:17
  33.8 5.5 %collective-permute-start.9 = (bf16[128,384]{1,0:T(8,128)(2,1)S(1)}, bf16[128,384]{1,0:T(8,128)(2,1)S(1)}, u32[]{:S(2)}, u32[]{:S(2)}) collective-permute-start(bf16[128,384]{1,0:T(8,128)(2,1)S(1)} %shard_map.90.seen.a), channel_id=1, source_target_pairs={{0,1},{1,0},{2,3},{3,2},{4,5},{5,4},{6,7},{7,6},{8,9},{9,8},{10,11... | collective-permute-start | bytes 294920 | tf_op jit(solution)/shard_map/ppermute | solution.py:17
  38.4 1.3 %collective-permute-start.11 = (bf16[128,384]{1,0:T(8,128)(2,1)S(1)}, bf16[128,384]{1,0:T(8,128)(2,1)S(1)}, u32[]{:S(2)}, u32[]{:S(2)}) collective-permute-start(bf16[128,384]{1,0:T(8,128)(2,1)S(1)} %collective-permute-done.10.c), channel_id=1, source_target_pairs={{0,1},{1,0},{2,3},{3,2},{4,5},{5,4},{6,7},{7,6},{8,9},{9,8},{10,11... | collective-permute-start | bytes 294920 | tf_op jit(solution)/shard_map/ppermute | solution.py:17
  40.4 4.3 %collective-permute-start.12 = (bf16[128,256]{1,0:T(8,128)(2,1)S(1)}, bf16[128,256]{1,0:T(8,128)(2,1)S(1)}, u32[]{:S(2)}, u32[]{:S(2)}) collective-permute-start(bf16[128,256]{1,0:T(8,128)(2,1)S(1)} %shard_map.92.back), channel_id=1, source_target_pairs={{0,4},{4,0},{8,12},{12,8},{1,5},{5,1},{9,13},{13,9},{2,6},{6,2},{1... | collective-permute-start | bytes 196616 | tf_op jit(solution)/shard_map/ppermute | solution.py:17
  41.2 6.1 %collective-permute-start.14 = (bf16[128,256]{1,0:T(8,128)(2,1)S(1)}, bf16[128,256]{1,0:T(8,128)(2,1)S(1)}, u32[]{:S(2)}, u32[]{:S(2)}) collective-permute-start(bf16[128,256]{1,0:T(8,128)(2,1)S(1)} %get-tuple-element.52), channel_id=1, source_target_pairs={{0,12},{4,8},{8,4},{12,0},{1,13},{5,9},{9,5},{13,1},{2,14},{6,10},... | collective-permute-start | bytes 196616 | tf_op jit(solution)/shard_map/ppermute | solution.py:17

commit v8 on v6

--- a/solution.py
+++ b/solution.py
@@ -222,7 +222,6 @@
     caps_here = after(top_caps, pair_send)
     caps_near = swap(caps_here, "top", 1)
     caps_far = swap(caps_here, "top", 2)
-    caps_far_near = swap(caps_far, "top", 1)
 
     def grams_body(lb, rb, caps, tl, tr, seen, out, late):
         out[:, span(0)] = (dot_t(tl[0], tl[0]) * st).astype(BF)
@@ -257,29 +256,13 @@
     half2_far = swap(half2, "leaf", 3)
     late_sib = swap(after(late, half2), "leaf", 1)
 
-    def order_body(a, b, c, d, seen, out):
-        here = lax.axis_index("top")
-        for i, piece in enumerate((a, b, c, d)):
-            for k in range(4):
-                out[span(i), span(k)] = piece[:, block(here ^ k, rank)]
-
-    (caps_all,) = call(
-        order_body,
-        [((4 * rank, 4 * rank), BF)],
-        top_caps,
-        caps_near,
-        caps_far,
-        caps_far_near,
-        half2,
-    )
-
     def sum_body(own, sib, seen, out):
         out[...] = (own[...].astype(f32) + sib[...]).astype(BF)
 
     (gram_pair,) = call(sum_body, [((rank, 3 * rank), BF)], grams, grams_sib, half2)
     gram_far = swap(gram_pair, "leaf", 3)
 
-    def one_body(x0, own, sib, lb, caps, seen, x1, stack):
+    def one_body(x0, own, sib, lb, caps, seen, seen2, x1, stack):
         put_rows(stack, tree_side(0), own[:, :cols], sib[:, :cols])
         coef = dot(caps[0, 0], stack[...]).astype(BF)
         x1[...] = x0[...] - dot(lb[0, 0], coef)
@@ -293,10 +276,11 @@
         lb,
         caps,
         half2,
+        grams_sib,
         scratch=[pltpu.VMEM((2 * rank, cols), BF)],
     )
 
-    def two_body(x1, own, far, lb, caps, tl, tr, seen, x2, send, keep, stack, scratch):
+    def two_body(x1, own, far, lb, caps, tl, tr, x2, send, keep, stack, scratch):
         side = column_side()
         put_rows(stack, tree_side(1), own[...], far[...])
         coef = dot(caps[1, 0], stack[...]).astype(BF)
@@ -316,7 +300,6 @@
         caps,
         tl,
         tr,
-        caps_all,
         scratch=[pltpu.VMEM((2 * rank, cols), BF), pltpu.VMEM(wide, f32)],
     )
     top_pair_in = swap(top_pair_send, "leaf", 1)
@@ -338,9 +321,26 @@
     down5, down5_send = call(
         add_body, [(wide, f32), (wide, BF)], down5, down_in, gram_pair
     )
-    down5_far = swap(down5_send, "leaf", 3)
-
-    def column_body(own, far, gram, gram_far, out):
+
+    caps_far_near = swap(after(caps_far, down_send), "top", 1)
+
+    def order_body(a, b, c, d, out):
+        here = lax.axis_index("top")
+        for i, piece in enumerate((a, b, c, d)):
+            for k in range(4):
+                out[span(i), span(k)] = piece[:, block(here ^ k, rank)]
+
+    (caps_all,) = call(
+        order_body,
+        [((4 * rank, 4 * rank), BF)],
+        top_caps,
+        caps_near,
+        caps_far,
+        caps_far_near,
+        micros=0.1,
+    )
+
+    def column_body(own, far, gram, gram_far, seen, out):
         out[:, : 2 * half] = (own[...] + far[...]).astype(BF)
         out[:, 2 * half :] = (gram[:, span(0)].astype(f32) + gram_far[:, span(0)]).astype(BF)
 
@@ -351,9 +351,10 @@
         top_half_far,
         gram_pair,
         gram_far,
+        caps_all,
     )
     top_far = swap(top_send, "top", 2)
-    top_near = swap(after(top_send, down5_send), "top", 1)
+    top_near = swap(top_send, "top", 1)
     top_parts = top_send, top_near, top_far, swap(top_far, "top", 1)
 
     def under_body(x2, rb, tl, tr, inv, seen, out2, under):
@@ -371,10 +372,10 @@
         tl,
         tr,
         inverse,
-        down5_far,
-    )
-
-    def top_body(a, b, c, d, caps, out, up, down):
+        top_send,
+    )
+
+    def top_body(a, b, c, d, caps, seen, out, up, down):
         pieces = (a, b, c, d)
         for i, piece in enumerate(pieces):
             up[span(i), :] = piece[:, part(0)]
@@ -391,8 +392,10 @@
         [(wide, BF)],
         *top_parts,
         caps_all,
+        out2,
         scratch=[pltpu.VMEM((4 * rank, half), BF)] * 2,
     )
+    down5_far = swap(after(down5_send, back_send), "leaf", 3)
     back_in = swap(back_send, "leaf", 1)
 
     def last_body(

time: 46.1 us -> 46.5 us (level)
  starting transfers between devices: 20.5 us -> 21.3 us
    ppermute x16, starting transfers between devices: 20.5 us -> 21.3 us  [swap(): return lax.ppermute(value, axis, pairs)]
  transfers between devices with their start and end apart: 16 -> 16, of which waited for: 8 -> 8; matrix products, arithmetic and copies ran while one was open for 0% -> 0% of each run, Pallas kernels for 8% -> 7%
where the time goes in v8:
time: 46.5 us; the launch traced here: 46.3 us
  starting transfers between devices  21.3 us (46%)
  waiting for transfers between devices  16.1 us (35%)
  Pallas kernels  8.83 us (19%)
    ppermute x16, starting transfers between devices, swap(): return lax.ppermute(value, axis, pairs)  21.3 us
    ppermute x16, waiting for transfers between devices, swap(): return lax.ppermute(value, axis, pairs)  16.1 us
    pallas_call x14, Pallas kernels, call(): pl.pallas_call(body, out_shape=[jax.ShapeDtypeStruct(shape, dtype) if hbm...  8.83 us
  transfers between devices with their start and end apart: 16, of which 8 were waited for; matrix products, arithmetic and copies ran while one was open for 0% of the time, Pallas kernels for 7%

profile of v8, /device:TPU:0, one launch (start us, length us, event | category | flops | bytes accessed | tf_op | source)
XLA Modules:
  0.0 46.3 jit_solution(3175940634381927077)
XLA Ops:
  0.0 3.2 %shard_map.82 = (f32[640,256]{1,0:T(8,128)S(1)}, bf16[128,640]{1,0:T(8,128)(2,1)S(1)}, f32[128,256]{1,0:T(8,128)S(1)}, bf16[640,640]{1,0:T(8,128)(2,1)S(1)}, bf1...) custom-call(f32[1,640,256]{2,1,0:T(8,128)} %rhs_hbm.1, ...), custom_call_target="tpu_custom_call" | custom-call | flops 1000000000 | tf_op jit(solution)/shard_map/pallas_call | solution.py:88
  3.2 0.5 %collective-permute-start.1 = (bf16[128,512]{1,0:T(8,128)(2,1)S(1)}, bf16[128,512]{1,0:T(8,128)(2,1)S(1)}, u32[]{:S(2)}, u32[]{:S(2)}) collective-permute-start(bf16[128,512]{1,0:T(8,128)(2,1)S(1)} %copy-done), channel_id=1, source_target_pairs={{0,1},{1,0},{2,3},{3,2},{4,5},{5,4},{6,7},{7,6},{8,9},{9,8},{10,11... | collective-permute-start | bytes 393224 | tf_op jit(solution)/shard_map/ppermute | solution.py:17
  3.7 2.7 %collective-permute-start = (bf16[128,640]{1,0:T(8,128)(2,1)S(1)}, bf16[128,640]{1,0:T(8,128)(2,1)S(1)}, u32[]{:S(2)}, u32[]{:S(2)}) collective-permute-start(bf16[128,640]{1,0:T(8,128)(2,1)S(1)} %get-tuple-element.32.own), channel_id=1, source_target_pairs={{0,4},{4,0},{8,12},{12,8},{1,5},{5,1},{9,13},{13,9},{2,6},{6,2},{1... | collective-permute-start | bytes 491528 | tf_op jit(solution)/shard_map/ppermute | solution.py:17
  6.3 1.5 %collective-permute-start.8 = (bf16[128,512]{1,0:T(8,128)(2,1)S(1)}, bf16[128,512]{1,0:T(8,128)(2,1)S(1)}, u32[]{:S(2)}, u32[]{:S(2)}) collective-permute-start(bf16[128,512]{1,0:T(8,128)(2,1)S(1)} %copy-done), channel_id=1, source_target_pairs={{0,2},{1,3},{2,0},{3,1},{4,6},{5,7},{6,4},{7,5},{8,10},{9,11},{10,... | collective-permute-start | bytes 393224 | tf_op jit(solution)/shard_map/ppermute | solution.py:17
  7.8 0.5 shard_map.84
  8.3 0.5 %collective-permute-start.2 = (bf16[128,384]{1,0:T(8,128)(2,1)S(1)}, bf16[128,384]{1,0:T(8,128)(2,1)S(1)}, u32[]{:S(2)}, u32[]{:S(2)}) collective-permute-start(bf16[128,384]{1,0:T(8,128)(2,1)S(1)} %get-tuple-element.40.own), channel_id=1, source_target_pairs={{0,4},{4,0},{8,12},{12,8},{1,5},{5,1},{9,13},{13,9},{2,6},{6,2},{1... | collective-permute-start | bytes 294920 | tf_op jit(solution)/shard_map/ppermute | solution.py:17
  8.8 2.6 %collective-permute-done.sib = bf16[128,640]{1,0:T(8,128)(2,1)S(1)} collective-permute-done((bf16[128,640]{1,0:T(8,128)(2,1)S(1)}, bf16[128,640]{1,0:T(8,128)(2,1)S(1)}, u32[]{:S(2)}, u32[]{:S(2)}) %collective-permute-start) | collective-permute-done | bytes 163872 | tf_op jit(solution)/shard_map/ppermute | solution.py:17
  11.6 4.0 %collective-permute-start.3 = (bf16[128,256]{1,0:T(8,128)(2,1)S(1)}, bf16[128,256]{1,0:T(8,128)(2,1)S(1)}, u32[]{:S(2)}, u32[]{:S(2)}) collective-permute-start(bf16[128,256]{1,0:T(8,128)(2,1)S(1)} %shard_map.83.seen.own), channel_id=1, source_target_pairs={{0,12},{4,8},{8,4},{12,0},{1,13},{5,9},{9,5},{13,1},{2,14},{6,10},... | collective-permute-start | bytes 196616 | tf_op jit(solution)/shard_map/ppermute | solution.py:17
  15.6 0.4 shard_map.85.x1
  16.1 2.6 %collective-permute-done.3.far = bf16[128,256]{1,0:T(8,128)(2,1)S(1)} collective-permute-done((bf16[128,256]{1,0:T(8,128)(2,1)S(1)}, bf16[128,256]{1,0:T(8,128)(2,1)S(1)}, u32[]{:S(2)}, u32[]{:S(2)}) %collective-permute-start.3) | collective-permute-done | bytes 65568 | tf_op jit(solution)/shard_map/ppermute | solution.py:17
  18.6 0.8 %shard_map.86 = (bf16[640,256]{1,0:T(8,128)(2,1)S(1)}, bf16[128,256]{1,0:T(8,128)(2,1)S(1)}, f32[128,256]{1,0:T(8,128)S(1)}) custom-call(f32[640,256]{1,0:T(8,128)S(1)} %shard_map.85.x1, bf16[128,256]{1,0:T(8,128)(2,1)S(1)} %shard_map.83.seen.own, bf16[128,256]{1,0:T(8,128)(2,1)S(1)} %collective-permute-done.3.far, ...), custom_call_target="tpu_custom_call" | custom-call | flops 1000000000 | tf_op jit(solution)/shard_map/pallas_call | solution.py:88
  19.5 3.9 %collective-permute-start.7 = (bf16[128,384]{1,0:T(8,128)(2,1)S(1)}, bf16[128,384]{1,0:T(8,128)(2,1)S(1)}, u32[]{:S(2)}, u32[]{:S(2)}) collective-permute-start(bf16[128,384]{1,0:T(8,128)(2,1)S(1)} %shard_map.88.gram.seen), channel_id=1, source_target_pairs={{0,12},{4,8},{8,4},{12,0},{1,13},{5,9},{9,5},{13,1},{2,14},{6,10},... | collective-permute-start | bytes 294920 | tf_op jit(solution)/shard_map/ppermute | solution.py:17
  23.8 0.3 collective-permute-done.4.other
  24.2 3.5 %collective-permute-start.6 = (bf16[128,256]{1,0:T(8,128)(2,1)S(1)}, bf16[128,256]{1,0:T(8,128)(2,1)S(1)}, u32[]{:S(2)}, u32[]{:S(2)}) collective-permute-start(bf16[128,256]{1,0:T(8,128)(2,1)S(1)} %get-tuple-element.48), channel_id=1, source_target_pairs={{0,12},{4,8},{8,4},{12,0},{1,13},{5,9},{9,5},{13,1},{2,14},{6,10},... | collective-permute-start | bytes 196616 | tf_op jit(solution)/shard_map/ppermute | solution.py:17
  27.8 3.2 %collective-permute-done.6.far = bf16[128,256]{1,0:T(8,128)(2,1)S(1)} collective-permute-done((bf16[128,256]{1,0:T(8,128)(2,1)S(1)}, bf16[128,256]{1,0:T(8,128)(2,1)S(1)}, u32[]{:S(2)}, u32[]{:S(2)}) %collective-permute-start.6) | collective-permute-done | bytes 65568 | tf_op jit(solution)/shard_map/ppermute | solution.py:17
  31.0 1.6 %collective-permute-start.11 = (bf16[128,384]{1,0:T(8,128)(2,1)S(1)}, bf16[128,384]{1,0:T(8,128)(2,1)S(1)}, u32[]{:S(2)}, u32[]{:S(2)}) collective-permute-start(bf16[128,384]{1,0:T(8,128)(2,1)S(1)} %shard_map.91.seen.a), channel_id=1, source_target_pairs={{0,2},{1,3},{2,0},{3,1},{4,6},{5,7},{6,4},{7,5},{8,10},{9,11},{10,... | collective-permute-start | bytes 294920 | tf_op jit(solution)/shard_map/ppermute | solution.py:17
  32.6 3.1 %collective-permute-done.11.c = bf16[128,384]{1,0:T(8,128)(2,1)S(1)} collective-permute-done((bf16[128,384]{1,0:T(8,128)(2,1)S(1)}, bf16[128,384]{1,0:T(8,128)(2,1)S(1)}, u32[]{:S(2)}, u32[]{:S(2)}) %collective-permute-start.11) | collective-permute-done | bytes 98336 | tf_op jit(solution)/shard_map/ppermute | solution.py:17
  35.7 0.9 %shard_map.92 = (f32[640,256]{1,0:T(8,128)S(1)}, bf16[640,512]{1,0:T(8,128)(2,1)S(1)}) custom-call(bf16[640,256]{1,0:T(8,128)(2,1)S(1)} %get-tuple-element.41.x2, bf16[2,1,640,128]{3,2,1,0:T(8,128)(2,1)S(1)} %get-tuple-element.36.rb, bf16[1,640,128]{2,1,0:T(8,128)(2,1)S(1)} %get-tuple-element.37.tl, bf16[1,640,128]{2,1,0:T(8,128)(2,1)S(1)} %get-tuple-element.38.tr, ...), custom_call_target="tpu_custom_call" | custom-call | flops 1000000000 | tf_op jit(solution)/shard_map/pallas_call | solution.py:88
  36.6 0.4 collective-permute-done.12.d
  37.0 0.7 %shard_map.93.back = bf16[128,256]{1,0:T(8,128)(2,1)S(1)} custom-call(bf16[128,384]{1,0:T(8,128)(2,1)S(1)} %shard_map.91.seen.a, bf16[128,384]{1,0:T(8,128)(2,1)S(1)} %collective-permute-done.10.b, bf16[128,384]{1,0:T(8,128)(2,1)S(1)} %collective-permute-done.11.c, bf16[128,384]{1,0:T(8,128)(2,1)S(1)} %collective-permute-done.12.d, ...), custom_call_target="tpu_custom_call" | custom-call | flops 1000000000 | tf_op jit(solution)/shard_map/pallas_call | solution.py:88
  37.7 2.9 %collective-permute-start.15 = (bf16[128,256]{1,0:T(8,128)(2,1)S(1)}, bf16[128,256]{1,0:T(8,128)(2,1)S(1)}, u32[]{:S(2)}, u32[]{:S(2)}) collective-permute-start(bf16[128,256]{1,0:T(8,128)(2,1)S(1)} %get-tuple-element.56), channel_id=1, source_target_pairs={{0,12},{4,8},{8,4},{12,0},{1,13},{5,9},{9,5},{13,1},{2,14},{6,10},... | collective-permute-start | bytes 196616 | tf_op jit(solution)/shard_map/ppermute | solution.py:17
  40.6 1.3 %collective-permute-done.13.back_sib = bf16[128,256]{1,0:T(8,128)(2,1)S(1)} collective-permute-done((bf16[128,256]{1,0:T(8,128)(2,1)S(1)}, bf16[128,256]{1,0:T(8,128)(2,1)S(1)}, u32[]{:S(2)}, u32[]{:S(2)}) %collective-permute-start.13) | collective-permute-done | bytes 65568 | tf_op jit(solution)/shard_map/ppermute | solution.py:17
  42.0 2.5 %collective-permute-done.15.down5_far = bf16[128,256]{1,0:T(8,128)(2,1)S(1)} collective-permute-done((bf16[128,256]{1,0:T(8,128)(2,1)S(1)}, bf16[128,256]{1,0:T(8,128)(2,1)S(1)}, u32[]{:S(2)}, u32[]{:S(2)}) %collective-permute-start.15) | collective-permute-done | bytes 65568 | tf_op jit(solution)/shard_map/ppermute | solution.py:17
  44.5 1.8 %shard_map.95 = f32[1,640,256]{2,1,0:T(8,128)} custom-call(f32[640,256]{1,0:T(8,128)S(1)} %get-tuple-element.51.seen.out2, bf16[640,512]{1,0:T(8,128)(2,1)S(1)} %get-tuple-element.52.under, bf16[128,256]{1,0:T(8,128)(2,1)S(1)} %shard_map.93.back, bf16[128,256]{1,0:T(8,128)(2,1)S(1)} %collective-permute-done.13.back_sib, ...), custom_call_target="tpu_custom_call" | custom-call | flops 1000000000 | tf_op jit(solution)/shard_map/pallas_call | solution.py:88
  (24 shorter events, 0.9 us)
Async XLA Ops:
  0.0 3.2 %copy-start = (bf16[128,512]{1,0:T(8,128)(2,1)S(1)}, bf16[128,512]{1,0:T(8,128)(2,1)}, u32[]{:S(2)}) copy-start(bf16[128,512]{1,0:T(8,128)(2,1)} %a.1) | copy-start | bytes 393220
  3.2 4.7 %collective-permute-start.1 = (bf16[128,512]{1,0:T(8,128)(2,1)S(1)}, bf16[128,512]{1,0:T(8,128)(2,1)S(1)}, u32[]{:S(2)}, u32[]{:S(2)}) collective-permute-start(bf16[128,512]{1,0:T(8,128)(2,1)S(1)} %copy-done), channel_id=1, source_target_pairs={{0,1},{1,0},{2,3},{3,2},{4,5},{5,4},{6,7},{7,6},{8,9},{9,8},{10,11... | collective-permute-start | bytes 393224 | tf_op jit(solution)/shard_map/ppermute | solution.py:17
  3.7 7.7 %collective-permute-start = (bf16[128,640]{1,0:T(8,128)(2,1)S(1)}, bf16[128,640]{1,0:T(8,128)(2,1)S(1)}, u32[]{:S(2)}, u32[]{:S(2)}) collective-permute-start(bf16[128,640]{1,0:T(8,128)(2,1)S(1)} %get-tuple-element.32.own), channel_id=1, source_target_pairs={{0,4},{4,0},{8,12},{12,8},{1,5},{5,1},{9,13},{13,9},{2,6},{6,2},{1... | collective-permute-start | bytes 491528 | tf_op jit(solution)/shard_map/ppermute | solution.py:17
  6.3 17.4 %collective-permute-start.8 = (bf16[128,512]{1,0:T(8,128)(2,1)S(1)}, bf16[128,512]{1,0:T(8,128)(2,1)S(1)}, u32[]{:S(2)}, u32[]{:S(2)}) collective-permute-start(bf16[128,512]{1,0:T(8,128)(2,1)S(1)} %copy-done), channel_id=1, source_target_pairs={{0,2},{1,3},{2,0},{3,1},{4,6},{5,7},{6,4},{7,5},{8,10},{9,11},{10,... | collective-permute-start | bytes 393224 | tf_op jit(solution)/shard_map/ppermute | solution.py:17
  8.3 7.3 %collective-permute-start.2 = (bf16[128,384]{1,0:T(8,128)(2,1)S(1)}, bf16[128,384]{1,0:T(8,128)(2,1)S(1)}, u32[]{:S(2)}, u32[]{:S(2)}) collective-permute-start(bf16[128,384]{1,0:T(8,128)(2,1)S(1)} %get-tuple-element.40.own), channel_id=1, source_target_pairs={{0,4},{4,0},{8,12},{12,8},{1,5},{5,1},{9,13},{13,9},{2,6},{6,2},{1... | collective-permute-start | bytes 294920 | tf_op jit(solution)/shard_map/ppermute | solution.py:17
  11.6 7.1 %collective-permute-start.3 = (bf16[128,256]{1,0:T(8,128)(2,1)S(1)}, bf16[128,256]{1,0:T(8,128)(2,1)S(1)}, u32[]{:S(2)}, u32[]{:S(2)}) collective-permute-start(bf16[128,256]{1,0:T(8,128)(2,1)S(1)} %shard_map.83.seen.own), channel_id=1, source_target_pairs={{0,12},{4,8},{8,4},{12,0},{1,13},{5,9},{9,5},{13,1},{2,14},{6,10},... | collective-permute-start | bytes 196616 | tf_op jit(solution)/shard_map/ppermute | solution.py:17
  15.6 8.5 %collective-permute-start.5 = (bf16[128,640]{1,0:T(8,128)(2,1)S(1)}, bf16[128,640]{1,0:T(8,128)(2,1)S(1)}, u32[]{:S(2)}, u32[]{:S(2)}) collective-permute-start(bf16[128,640]{1,0:T(8,128)(2,1)S(1)} %get-tuple-element.46.late), channel_id=1, source_target_pairs={{0,4},{4,0},{8,12},{12,8},{1,5},{5,1},{9,13},{13,9},{2,6},{6,2},{1... | collective-permute-start | bytes 491528 | tf_op jit(solution)/shard_map/ppermute | solution.py:17
  19.4 4.7 %collective-permute-start.4 = (bf16[128,256]{1,0:T(8,128)(2,1)S(1)}, bf16[128,256]{1,0:T(8,128)(2,1)S(1)}, u32[]{:S(2)}, u32[]{:S(2)}) collective-permute-start(bf16[128,256]{1,0:T(8,128)(2,1)S(1)} %get-tuple-element.44), channel_id=1, source_target_pairs={{0,4},{4,0},{8,12},{12,8},{1,5},{5,1},{9,13},{13,9},{2,6},{6,2},{1... | collective-permute-start | bytes 196616 | tf_op jit(solution)/shard_map/ppermute | solution.py:17
  19.5 8.2 %collective-permute-start.7 = (bf16[128,384]{1,0:T(8,128)(2,1)S(1)}, bf16[128,384]{1,0:T(8,128)(2,1)S(1)}, u32[]{:S(2)}, u32[]{:S(2)}) collective-permute-start(bf16[128,384]{1,0:T(8,128)(2,1)S(1)} %shard_map.88.gram.seen), channel_id=1, source_target_pairs={{0,12},{4,8},{8,4},{12,0},{1,13},{5,9},{9,5},{13,1},{2,14},{6,10},... | collective-permute-start | bytes 294920 | tf_op jit(solution)/shard_map/ppermute | solution.py:17
  23.7 3.9 %collective-permute-start.9 = (bf16[128,512]{1,0:T(8,128)(2,1)S(1)}, bf16[128,512]{1,0:T(8,128)(2,1)S(1)}, u32[]{:S(2)}, u32[]{:S(2)}) collective-permute-start(bf16[128,512]{1,0:T(8,128)(2,1)S(1)} %collective-permute-done.8.c), channel_id=1, source_target_pairs={{0,1},{1,0},{2,3},{3,2},{4,5},{5,4},{6,7},{7,6},{8,9},{9,8},{10,11... | collective-permute-start | bytes 393224 | tf_op jit(solution)/shard_map/ppermute | solution.py:17
  24.2 6.8 %collective-permute-start.6 = (bf16[128,256]{1,0:T(8,128)(2,1)S(1)}, bf16[128,256]{1,0:T(8,128)(2,1)S(1)}, u32[]{:S(2)}, u32[]{:S(2)}) collective-permute-start(bf16[128,256]{1,0:T(8,128)(2,1)S(1)} %get-tuple-element.48), channel_id=1, source_target_pairs={{0,12},{4,8},{8,4},{12,0},{1,13},{5,9},{9,5},{13,1},{2,14},{6,10},... | collective-permute-start | bytes 196616 | tf_op jit(solution)/shard_map/ppermute | solution.py:17
  27.6 8.0 %collective-permute-start.14 = (bf16[128,512]{1,0:T(8,128)(2,1)S(1)}, bf16[128,512]{1,0:T(8,128)(2,1)S(1)}, u32[]{:S(2)}, u32[]{:S(2)}) collective-permute-start(bf16[128,512]{1,0:T(8,128)(2,1)S(1)} %get-tuple-element.49.z), channel_id=1, source_target_pairs={{0,4},{4,0},{8,12},{12,8},{1,5},{5,1},{9,13},{13,9},{2,6},{6,2},{1... | collective-permute-start | bytes 393224 | tf_op jit(solution)/shard_map/ppermute | solution.py:17
  31.0 4.7 %collective-permute-start.11 = (bf16[128,384]{1,0:T(8,128)(2,1)S(1)}, bf16[128,384]{1,0:T(8,128)(2,1)S(1)}, u32[]{:S(2)}, u32[]{:S(2)}) collective-permute-start(bf16[128,384]{1,0:T(8,128)(2,1)S(1)} %shard_map.91.seen.a), channel_id=1, source_target_pairs={{0,2},{1,3},{2,0},{3,1},{4,6},{5,7},{6,4},{7,5},{8,10},{9,11},{10,... | collective-permute-start | bytes 294920 | tf_op jit(solution)/shard_map/ppermute | solution.py:17
  32.6 4.0 %collective-permute-start.10 = (bf16[128,384]{1,0:T(8,128)(2,1)S(1)}, bf16[128,384]{1,0:T(8,128)(2,1)S(1)}, u32[]{:S(2)}, u32[]{:S(2)}) collective-permute-start(bf16[128,384]{1,0:T(8,128)(2,1)S(1)} %shard_map.91.seen.a), channel_id=1, source_target_pairs={{0,1},{1,0},{2,3},{3,2},{4,5},{5,4},{6,7},{7,6},{8,9},{9,8},{10,11... | collective-permute-start | bytes 294920 | tf_op jit(solution)/shard_map/ppermute | solution.py:17
  35.7 1.3 %collective-permute-start.12 = (bf16[128,384]{1,0:T(8,128)(2,1)S(1)}, bf16[128,384]{1,0:T(8,128)(2,1)S(1)}, u32[]{:S(2)}, u32[]{:S(2)}) collective-permute-start(bf16[128,384]{1,0:T(8,128)(2,1)S(1)} %collective-permute-done.11.c), channel_id=1, source_target_pairs={{0,1},{1,0},{2,3},{3,2},{4,5},{5,4},{6,7},{7,6},{8,9},{9,8},{10,11... | collective-permute-start | bytes 294920 | tf_op jit(solution)/shard_map/ppermute | solution.py:17
  37.7 4.3 %collective-permute-start.13 = (bf16[128,256]{1,0:T(8,128)(2,1)S(1)}, bf16[128,256]{1,0:T(8,128)(2,1)S(1)}, u32[]{:S(2)}, u32[]{:S(2)}) collective-permute-start(bf16[128,256]{1,0:T(8,128)(2,1)S(1)} %shard_map.93.back), channel_id=1, source_target_pairs={{0,4},{4,0},{8,12},{12,8},{1,5},{5,1},{9,13},{13,9},{2,6},{6,2},{1... | collective-permute-start | bytes 196616 | tf_op jit(solution)/shard_map/ppermute | solution.py:17
  37.7 6.7 %collective-permute-start.15 = (bf16[128,256]{1,0:T(8,128)(2,1)S(1)}, bf16[128,256]{1,0:T(8,128)(2,1)S(1)}, u32[]{:S(2)}, u32[]{:S(2)}) collective-permute-start(bf16[128,256]{1,0:T(8,128)(2,1)S(1)} %get-tuple-element.56), channel_id=1, source_target_pairs={{0,12},{4,8},{8,4},{12,0},{1,13},{5,9},{9,5},{13,1},{2,14},{6,10},... | collective-permute-start | bytes 196616 | tf_op jit(solution)/shard_map/ppermute | solution.py:17

commit v9 on v5

--- a/solution.py
+++ b/solution.py
@@ -149,22 +149,15 @@
     def part(i, n=1):
         return slice(i * half, (i + n) * half)
 
-    caps_far = swap(top_caps, "top", 2)
-
     def start_body(
         rhs_hbm, inv_hbm, lb_hbm, rb_hbm, caps_hbm, tl_hbm, tr_hbm,
-        x_ref, send, keep, inv_ref, lb, rb, caps, tl, tr, rhs_v, nexts, sems,
+        x_ref, send, inv_ref, lb, rb, caps, tl, tr, rhs_v, sems,
     ):
         def load(source, target, *at):
             copy = pltpu.make_async_copy(source, target, sems.at[at])
             copy.start()
             return copy
 
-        first = [
-            load(lb_hbm.at[0], lb.at[0], 2, 0),
-            load(rb_hbm.at[1], rb.at[1], 2, 1),
-            load(caps_hbm, caps, 2, 2),
-        ]
         copies = []
         for i in range(blocks):
             copies.append(load(rhs_hbm.at[0, span(i), :], rhs_v.at[span(i), :], 0, i))
@@ -176,35 +169,22 @@
                     i,
                 )
             )
-        basis1 = load(rb_hbm.at[0], rb.at[0], 2, 3)
-        rest = [
-            load(lb_hbm.at[1], lb.at[1], 2, 4),
-            load(tl_hbm, tl, 2, 5),
-            load(tr_hbm, tr, 2, 6),
-        ]
-        odd = tree_side(0)
-        for copy in first:
-            copy.wait()
-        gram = (dot_t(rb[1, 0], lb[0, 0]) * s2).astype(BF)
-        nexts[...] = dot(gram, caps[0, 0]).astype(BF)
-        send[:, 2 * cols :] = nexts[:, block(1 - odd, rank)]
+        pairs = ((rb_hbm, rb), (lb_hbm, lb), (tl_hbm, tl), (tr_hbm, tr), (caps_hbm, caps))
+        bases = [load(source, target, 2, i) for i, (source, target) in enumerate(pairs)]
         for i in range(blocks):
             copies[2 * i].wait()
             copies[2 * i + 1].wait()
             x_ref[span(i), :] = dot(
                 inv_ref[span(i), span(0, i + 1)], rhs_v[span(0, i + 1), :].astype(BF)
             )
-        basis1.wait()
-        state = x_ref[...].astype(BF)
-        send[:, :cols] = (dot_t(rb[0, 0], state) * s1).astype(BF)
-        keep[...] = dot_t(rb[1, 0], state) * s2 - dot(nexts[:, block(odd, rank)], send[:, :cols])
-        send[:, cols : 2 * cols] = keep[...].astype(BF)
-        for copy in rest:
+        bases[0].wait()
+        send[...] = (dot_t(rb[0, 0], x_ref[...].astype(BF)) * s1).astype(BF)
+        for copy in bases[1:]:
             copy.wait()
 
-    state0, pair_send, pair_keep, inverse, lb, rb, caps, tl, tr = call(
+    state0, proj1, inverse, lb, rb, caps, tl, tr = call(
         start_body,
-        [(tall, f32), ((rank, 2 * cols + rank), BF), (wide, f32), ((rows, rows), BF)]
+        [(tall, f32), (wide, BF), ((rows, rows), BF)]
         + [(a.shape, a.dtype) for a in (left_basis, right_basis, level_caps, top_left, top_right)],
         right_side,
         leaf_inverse,
@@ -214,49 +194,96 @@
         top_left,
         top_right,
         hbm=range(7),
-        scratch=[
-            pltpu.VMEM(tall, f32),
-            pltpu.VMEM((rank, 2 * rank), BF),
-            pltpu.SemaphoreType.DMA((3, max(blocks, 7))),
-        ],
-    )
-    pair_in = swap(pair_send, "leaf", 1)
-    caps_near = swap(after(top_caps, pair_send), "top", 1)
-    caps_far_near = swap(after(caps_far, pair_send), "top", 1)
-
-    def grams_body(lb, rb, caps, tl, tr, seen, out, late):
-        out[:, span(0)] = (dot_t(tl[0], tl[0]) * st).astype(BF)
-        for i, basis in enumerate((tl[0], tr[0])):
-            out[:, span(1 + i)] = (dot_t(lb[1, 0], basis) * s2).astype(BF)
-        for i, basis in enumerate((tl[0], tr[0], rb[1, 0])):
-            late[:, span(i)] = (dot_t(lb[0, 0], basis) * s1).astype(BF)
-        late[:, span(3, 2)] = caps[1, 0]
-
-    grams, late = call(
-        grams_body,
-        [((rank, 3 * rank), BF), ((rank, 5 * rank), BF)],
+        scratch=[pltpu.VMEM(tall, f32), pltpu.SemaphoreType.DMA((3, max(blocks, 5)))],
+    )
+    proj1_sib = swap(proj1, "leaf", 1)
+    caps_here = after(top_caps, proj1)
+    caps_near = swap(caps_here, "top", 1)
+    caps_far = swap(caps_here, "top", 2)
+
+    def early_body(lb, caps, tl, tr, seen, out):
+        for i, basis in enumerate((tr, tl)):
+            gram = (dot_t(basis[0], lb[1, 0]) * st).astype(BF)
+            out[:, span(2 * i, 2)] = dot(gram, caps[1, 0]).astype(BF)
+        out[:, span(4)] = (dot_t(tl[0], tl[0]) * st).astype(BF)
+
+    (early,) = call(
+        early_body, [((rank, 5 * rank), BF)], lb, caps, tl, tr, caps_near, micros=10
+    )
+    early_sib = swap(early, "leaf", 1)
+
+    def one_body(x0, p, p_sib, lb, rb, caps, tl, tr, x1, send, keep, stack, scratch):
+        side = column_side()
+        put_rows(stack, tree_side(0), p[...], p_sib[...])
+        coef = dot(caps[0, 0], stack[...]).astype(BF)
+        x1[...] = x0[...] - dot(lb[0, 0], coef)
+        state = x1[...].astype(BF)
+        keep[:, :cols] = dot_t(rb[1, 0], state) * s2
+        send[:, :cols] = keep[:, :cols].astype(BF)
+        for i, basis in enumerate((tr, tl)):
+            scratch[...] = dot_t(basis[0], state) * st
+            send[:, part(2 + i)] = scratch[:, block(1 - side, half)].astype(BF)
+            keep[:, part(2 + i)] = scratch[:, block(side, half)]
+
+    state1, pair_send, pair_keep = call(
+        one_body,
+        [(tall, f32), ((rank, 2 * cols), BF), ((rank, 2 * cols), f32)],
+        state0,
+        proj1,
+        proj1_sib,
         lb,
         rb,
         caps,
         tl,
         tr,
-        caps_near,
-        micros=10,
-    )
-    grams_sib = swap(grams, "leaf", 1)
-
-    def half_body(keep, own, sib, out):
-        out[...] = (
-            keep[...]
-            + sib[:, cols : 2 * cols]
-            - dot(own[:, 2 * cols :], sib[:, :cols])
-            - dot(sib[:, 2 * cols :], own[:, :cols])
-        ).astype(BF)
-
-    (half2,) = call(half_body, [(wide, BF)], pair_keep, pair_send, pair_in, micros=3)
-    half2_far = swap(half2, "leaf", 3)
-
-    def order_body(a, b, c, d, seen, out):
+        scratch=[pltpu.VMEM((2 * rank, cols), BF), pltpu.VMEM(wide, f32)],
+        micros=3,
+    )
+    pair_in = swap(pair_send, "leaf", 1)
+
+    def pair_body(own, sib, seen, send, keep, gram, scratch):
+        upper = tree_side(1)
+        for i in range(2):
+            scratch[...] = (own[:, span(2 * i, 2)].astype(f32) + sib[:, span(2 * i, 2)]).astype(BF)
+            send[:, span(i)] = scratch[:, block(1 - upper, rank)]
+            keep[:, span(2 * i)] = scratch[:, block(upper, rank)]
+            keep[:, span(2 * i + 1)] = send[:, span(i)]
+        gram[...] = own[:, span(4)].astype(f32) + sib[:, span(4)]
+        send[:, span(2)] = gram[...].astype(BF)
+
+    next_send, next_keep, gram_pair = call(
+        pair_body,
+        [((rank, 3 * rank), BF), ((rank, 4 * rank), BF), (square, f32)],
+        early,
+        early_sib,
+        state1,
+        scratch=[pltpu.VMEM((rank, 2 * rank), BF)],
+        micros=0.1,
+    )
+    next_far = swap(next_send, "leaf", 3)
+    def half_body(keep, pair, nexts, send, keep2):
+        side = column_side()
+        send[:, :cols] = (keep[:, :cols] + pair[:, :cols]).astype(BF)
+        own = send[:, block(side, half)]
+        for i in range(2):
+            keep2[:, part(i)] = (
+                keep[:, part(2 + i)] + pair[:, part(2 + i)] - dot(nexts[:, span(2 * i)], own)
+            )
+        send[:, cols:] = keep2[...].astype(BF)
+
+    cross_send, cross_keep = call(
+        half_body,
+        [((rank, 2 * cols), BF), (wide, f32)],
+        pair_keep,
+        pair_in,
+        next_keep,
+        micros=5,
+    )
+    cross_in = swap(cross_send, "leaf", 3)
+
+    caps_far_near = swap(after(caps_far, cross_send), "top", 1)
+
+    def order_body(a, b, c, d, out):
         here = lax.axis_index("top")
         for i, piece in enumerate((a, b, c, d)):
             for k in range(4):
@@ -269,89 +296,82 @@
         caps_near,
         caps_far,
         caps_far_near,
-        half2,
-    )
-
-    def sum_body(own, sib, seen, out):
-        out[...] = (own[...].astype(f32) + sib[...]).astype(BF)
-
-    (gram_pair,) = call(sum_body, [((rank, 3 * rank), BF)], grams, grams_sib, half2)
-    gram_far = swap(gram_pair, "leaf", 3)
-
-    def one_body(x0, own, sib, lb, caps, seen, x1, stack):
-        put_rows(stack, tree_side(0), own[:, :cols], sib[:, :cols])
-        coef = dot(caps[0, 0], stack[...]).astype(BF)
-        x1[...] = x0[...] - dot(lb[0, 0], coef)
-
-    (state1,) = call(
-        one_body,
-        [(tall, f32)],
-        state0,
-        pair_send,
-        pair_in,
+        micros=0.1,
+    )
+
+    def late_body(lb, rb, caps, tl, tr, seen, seen2, out, gram5):
+        for i, basis in enumerate((tl[0], tr[0])):
+            out[:, span(i)] = (dot_t(lb[0, 0], basis) * s1).astype(BF)
+            gram5[:, span(i)] = (dot_t(lb[1, 0], basis) * s2).astype(BF)
+        out[:, span(2)] = (dot_t(lb[0, 0], rb[1, 0]) * s1).astype(BF)
+        out[:, span(3, 2)] = caps[1, 0]
+
+    late, gram5 = call(
+        late_body,
+        [((rank, 5 * rank), BF), ((rank, 2 * rank), BF)],
         lb,
-        caps,
-        half2,
-        scratch=[pltpu.VMEM((2 * rank, cols), BF)],
-    )
-
-    def two_body(x1, own, far, lb, caps, tl, tr, seen, x2, send, keep, stack, scratch):
-        side = column_side()
-        put_rows(stack, tree_side(1), own[...], far[...])
-        coef = dot(caps[1, 0], stack[...]).astype(BF)
-        x2[...] = (x1[...] - dot(lb[1, 0], coef)).astype(BF)
-        for i, basis in enumerate((tr[0], tl[0])):
-            scratch[...] = dot_t(basis, x2[...]) * st
-            send[:, part(i)] = scratch[:, block(1 - side, half)].astype(BF)
-            keep[:, part(i)] = scratch[:, block(side, half)]
-
-    state2, top_pair_send, top_keep = call(
-        two_body,
-        [(tall, BF), (wide, BF), (wide, f32)],
-        state1,
-        half2,
-        half2_far,
-        lb,
+        rb,
         caps,
         tl,
         tr,
-        caps_all,
-        scratch=[pltpu.VMEM((2 * rank, cols), BF), pltpu.VMEM(wide, f32)],
-    )
-    top_pair_in = swap(top_pair_send, "leaf", 1)
-
-    def down_body(lb, x2, z5, z):
-        z5[...] = dot_t(lb[1, 0], x2[...]) * s2
-        z[:, :cols] = z5[...].astype(BF)
-        z[:, cols:] = (dot_t(lb[0, 0], x2[...]) * s1).astype(BF)
-
-    down5, down_send = call(down_body, [(wide, f32), ((rank, 2 * cols), BF)], lb, state2)
-    down_in = swap(down_send, "leaf", 1)
-
-    def add_body(own, other, out, out_b):
-        out[...] = own[...] + other[:, :cols]
-        out_b[...] = out[...].astype(BF)
-
-    top_half, top_half_send = call(add_body, [(wide, f32), (wide, BF)], top_keep, top_pair_in)
-    top_half_far = swap(top_half_send, "leaf", 3)
-    down5, down5_send = call(add_body, [(wide, f32), (wide, BF)], down5, down_in)
-    down5_far = swap(down5_send, "leaf", 3)
-
-    def column_body(own, far, gram, gram_far, out):
-        out[:, : 2 * half] = (own[...] + far[...]).astype(BF)
-        out[:, 2 * half :] = (gram[:, span(0)].astype(f32) + gram_far[:, span(0)]).astype(BF)
+        cross_send,
+        next_far,
+        micros=5,
+    )
+    late_sib = swap(late, "leaf", 1)
+
+    def column_body(send, keep2, far, nexts, nexts_far, gram, seen, seen2, out):
+        side = column_side()
+        own, other = send[:, block(side, half)], far[:, block(side, half)]
+        for i in range(2):
+            out[:, part(i)] = (
+                keep2[:, part(i)]
+                + far[:, part(2 + i)]
+                - dot(nexts[:, span(2 * i + 1)], other)
+                - dot(nexts_far[:, span(i)], own)
+            ).astype(BF)
+        out[:, 2 * half :] = (gram[...] + nexts_far[:, span(2)]).astype(BF)
 
     (top_send,) = call(
         column_body,
         [((rank, 2 * half + rank), BF)],
-        top_half,
-        top_half_far,
+        cross_send,
+        cross_keep,
+        cross_in,
+        next_keep,
+        next_far,
         gram_pair,
-        gram_far,
-    )
+        late,
+        caps_all,
+        micros=0.2,
+    )
+    top_near = swap(top_send, "top", 1)
     top_far = swap(top_send, "top", 2)
-    top_parts = top_send, swap(top_send, "top", 1), top_far, swap(top_far, "top", 1)
-    late_sib = swap(after(late, top_send), "leaf", 1)
+
+    def two_body(x1, send, far, lb, caps, gram5, seen, x2, z5, z, stack):
+        put_rows(stack, tree_side(1), send[:, :cols], far[:, :cols])
+        coef = dot(caps[1, 0], stack[...]).astype(BF)
+        x2[...] = (x1[...] - dot(lb[1, 0], coef)).astype(BF)
+        z5[...] = dot_t(lb[1, 0], x2[...]) * s2
+        z[:, :cols] = z5[...].astype(BF)
+        z[:, cols : 2 * cols] = (dot_t(lb[0, 0], x2[...]) * s1).astype(BF)
+        z[:, 2 * cols :] = gram5[...]
+
+    state2, down5, down_send = call(
+        two_body,
+        [(tall, BF), (wide, f32), ((rank, 2 * cols + 2 * rank), BF)],
+        state1,
+        cross_send,
+        cross_in,
+        lb,
+        caps,
+        gram5,
+        top_send,
+        scratch=[pltpu.VMEM((2 * rank, cols), BF)],
+        micros=0.1,
+    )
+    down_in = swap(down_send, "leaf", 1)
+    top_parts = top_send, top_near, top_far, swap(after(top_far, state2), "top", 1)
 
     def under_body(x2, rb, tl, tr, inv, seen, out2, under):
         for c in range(blocks):
@@ -368,7 +388,7 @@
         tl,
         tr,
         inverse,
-        top_send,
+        late_sib,
     )
 
     def top_body(a, b, c, d, caps, seen, out, up, down):
@@ -393,27 +413,40 @@
     )
     back_in = swap(back_send, "leaf", 1)
 
-    def last_body(
-        out2, under, back, back_sib, down5, down5_far, gram, gram_far, late, late_sib,
-        z, z_sib, caps, out, coefs, stack, out_v, sems,
-    ):
+    def down_body(back, back_sib, down5, z, z_sib, both, send):
         side = column_side()
         for i in range(2):
-            put_columns(coefs.at[span(i), :], side, back[:, part(i)], back_sib[:, part(i)])
-        both = coefs[span(0, 2), :]
-        put_rows(
-            stack,
-            tree_side(1),
-            (down5[...] - dot(gram[:, span(1, 2)], both)).astype(BF),
-            (down5_far[...] - dot(gram_far[:, span(1, 2)], both)).astype(BF),
-        )
+            put_columns(both.at[span(i), :], side, back[:, part(i)], back_sib[:, part(i)])
+        gram = (z[:, 2 * cols :].astype(f32) + z_sib[:, 2 * cols :]).astype(BF)
+        send[...] = (down5[...] + z_sib[:, :cols] - dot(gram, both[...])).astype(BF)
+
+    both, half5 = call(
+        down_body,
+        [((2 * rank, cols), BF), (wide, BF)],
+        back_send,
+        back_in,
+        down5,
+        down_send,
+        down_in,
+        micros=0.3,
+    )
+    half5_far = swap(half5, "leaf", 3)
+
+    def last_body(
+        out2, under, both, half5, half5_far, late, late_sib, z, z_sib, caps, out,
+        coefs, stack, out_v, sems,
+    ):
+        coefs[span(0, 2), :] = both[...]
+        put_rows(stack, tree_side(1), half5[...], half5_far[...])
         coef5 = dot(caps[1, 0], stack[...]).astype(BF)
         coef5_sib = dot(late_sib[:, span(3, 2)], stack[...]).astype(BF)
         coefs[span(2), :] = coef5
 
-        def proj(zs, grams, coef):
+        def proj(zs, gram, coef):
             return (
-                zs[:, cols:] - dot(grams[:, span(0, 2)], both) - dot(grams[:, span(2)], coef)
+                zs[:, cols : 2 * cols]
+                - dot(gram[:, span(0, 2)], both[...])
+                - dot(gram[:, span(2)], coef)
             ).astype(BF)
 
         put_rows(stack, tree_side(0), proj(z, late, coef5), proj(z_sib, late_sib, coef5_sib))
@@ -432,12 +465,9 @@
         [((1, rows, cols), f32)],
         out2,
         under,
-        back_send,
-        back_in,
-        down5,
-        down5_far,
-        gram_pair,
-        gram_far,
+        both,
+        half5,
+        half5_far,
         late,
         late_sib,
         down_send,

time: 49.7 us -> 46.4 us (0.934)
  waiting for transfers between devices: 18.3 us -> 13.9 us
  starting transfers between devices: 22.3 us -> 23.4 us
    ppermute x16 -> x15, waiting for transfers between devices: 18.3 us -> 13.9 us  [swap(): return lax.ppermute(value, axis, pairs)]
    ppermute x16 -> x15, starting transfers between devices: 22.3 us -> 23.4 us  [swap(): return lax.ppermute(value, axis, pairs)]
    pallas_call x14 -> x13, Pallas kernels: 8.81 us -> 8.82 us  [call(): pl.pallas_call(body, out_shape=[jax.ShapeDtypeStruct(shape, dtype) if hbm...]
  transfers between devices with their start and end apart: 16 -> 15, of which waited for: 7 -> 8; matrix products, arithmetic and copies ran while one was open for 0% -> 0% of each run, Pallas kernels for 14% -> 10%
where the time goes in v9:
time: 46.4 us; the launch traced here: 46.2 us
  starting transfers between devices  23.4 us (50%)
  waiting for transfers between devices  13.9 us (30%)
  Pallas kernels  8.82 us (19%)
    ppermute x15, starting transfers between devices, swap(): return lax.ppermute(value, axis, pairs)  23.4 us
    ppermute x15, waiting for transfers between devices, swap(): return lax.ppermute(value, axis, pairs)  13.9 us
    pallas_call x13, Pallas kernels, call(): pl.pallas_call(body, out_shape=[jax.ShapeDtypeStruct(shape, dtype) if hbm...  8.82 us
  transfers between devices with their start and end apart: 15, of which 8 were waited for; matrix products, arithmetic and copies ran while one was open for 0% of the time, Pallas kernels for 10%

profile of v9, /device:TPU:0, one launch (start us, length us, event | category | flops | bytes accessed | tf_op | source)
XLA Modules:
  0.0 46.2 jit_solution(8252592321585281814)
XLA Ops:
  0.0 2.4 %shard_map.82 = (f32[640,256]{1,0:T(8,128)S(1)}, bf16[128,256]{1,0:T(8,128)(2,1)S(1)}, bf16[640,640]{1,0:T(8,128)(2,1)S(1)}, bf16[2,1,640,128]{3,2,1,0:T(8,128)(...) custom-call(f32[1,640,256]{2,1,0:T(8,128)} %rhs_hbm.1, ...), custom_call_target="tpu_custom_call" | custom-call | flops 1000000000 | tf_op jit(solution)/shard_map/pallas_call | solution.py:88
  2.9 2.6 %collective-permute-start = (bf16[128,256]{1,0:T(8,128)(2,1)S(1)}, bf16[128,256]{1,0:T(8,128)(2,1)S(1)}, u32[]{:S(2)}, u32[]{:S(2)}) collective-permute-start(bf16[128,256]{1,0:T(8,128)(2,1)S(1)} %get-tuple-element.34.p), channel_id=1, source_target_pairs={{0,4},{4,0},{8,12},{12,8},{1,5},{5,1},{9,13},{13,9},{2,6},{6,2},{1... | collective-permute-start | bytes 196616 | tf_op jit(solution)/shard_map/ppermute | solution.py:17
  5.6 0.6 %shard_map.84.own = bf16[128,640]{1,0:T(8,128)(2,1)S(1)} custom-call(bf16[2,1,640,128]{3,2,1,0:T(8,128)(2,1)S(1)} %get-tuple-element.35.lb, bf16[2,1,128,256]{3,2,1,0:T(8,128)(2,1)S(1)} %get-tuple-element.37.caps, bf16[1,640,128]{2,1,0:T(8,128)(2,1)S(1)} %get-tuple-element.38.tl, bf16[1,640,128]{2,1,0:T(8,128)(2,1)S(1)} %get-tuple-element.39.tr, ...), custom_call_target="tpu_custom_call" | custom-call | flops 10000000000 | tf_op jit(solution)/shard_map/pallas_call | solution.py:88
  6.1 1.3 %collective-permute-start.3 = (bf16[128,640]{1,0:T(8,128)(2,1)S(1)}, bf16[128,640]{1,0:T(8,128)(2,1)S(1)}, u32[]{:S(2)}, u32[]{:S(2)}) collective-permute-start(bf16[128,640]{1,0:T(8,128)(2,1)S(1)} %shard_map.84.own), channel_id=1, source_target_pairs={{0,4},{4,0},{8,12},{12,8},{1,5},{5,1},{9,13},{13,9},{2,6},{6,2},{1... | collective-permute-start | bytes 491528 | tf_op jit(solution)/shard_map/ppermute | solution.py:17
  7.5 0.8 %collective-permute-done.p_sib = bf16[128,256]{1,0:T(8,128)(2,1)S(1)} collective-permute-done((bf16[128,256]{1,0:T(8,128)(2,1)S(1)}, bf16[128,256]{1,0:T(8,128)(2,1)S(1)}, u32[]{:S(2)}, u32[]{:S(2)}) %collective-permute-start) | collective-permute-done | bytes 65568 | tf_op jit(solution)/shard_map/ppermute | solution.py:17
  8.3 0.8 %shard_map.83 = (f32[640,256]{1,0:T(8,128)S(1)}, bf16[128,512]{1,0:T(8,128)(2,1)S(1)}, f32[128,512]{1,0:T(8,128)S(1)}) custom-call(f32[640,256]{1,0:T(8,128)S(1)} %get-tuple-element.33.x0, bf16[128,256]{1,0:T(8,128)(2,1)S(1)} %get-tuple-element.34.p, bf16[128,256]{1,0:T(8,128)(2,1)S(1)} %collective-permute-done.p_sib, ...), custom_call_target="tpu_custom_call" | custom-call | flops 3000000000 | tf_op jit(solution)/shard_map/pallas_call | solution.py:88
  9.1 1.8 %collective-permute-start.1 = (bf16[128,512]{1,0:T(8,128)(2,1)S(1)}, bf16[128,512]{1,0:T(8,128)(2,1)S(1)}, u32[]{:S(2)}, u32[]{:S(2)}) collective-permute-start(bf16[128,512]{1,0:T(8,128)(2,1)S(1)} %get-tuple-element.42), channel_id=1, source_target_pairs={{0,4},{4,0},{8,12},{12,8},{1,5},{5,1},{9,13},{13,9},{2,6},{6,2},{1... | collective-permute-start | bytes 393224 | tf_op jit(solution)/shard_map/ppermute | solution.py:17
  10.9 1.5 %collective-permute-start.6 = (bf16[128,512]{1,0:T(8,128)(2,1)S(1)}, bf16[128,512]{1,0:T(8,128)(2,1)S(1)}, u32[]{:S(2)}, u32[]{:S(2)}) collective-permute-start(bf16[128,512]{1,0:T(8,128)(2,1)S(1)} %copy-done), channel_id=1, source_target_pairs={{0,2},{1,3},{2,0},{3,1},{4,6},{5,7},{6,4},{7,5},{8,10},{9,11},{10,... | collective-permute-start | bytes 393224 | tf_op jit(solution)/shard_map/ppermute | solution.py:17
  12.4 0.8 %collective-permute-done.3.sib = bf16[128,640]{1,0:T(8,128)(2,1)S(1)} collective-permute-done((bf16[128,640]{1,0:T(8,128)(2,1)S(1)}, bf16[128,640]{1,0:T(8,128)(2,1)S(1)}, u32[]{:S(2)}, u32[]{:S(2)}) %collective-permute-start.3) | collective-permute-done | bytes 163872 | tf_op jit(solution)/shard_map/ppermute | solution.py:17
  13.3 3.0 %collective-permute-start.5 = (bf16[128,384]{1,0:T(8,128)(2,1)S(1)}, bf16[128,384]{1,0:T(8,128)(2,1)S(1)}, u32[]{:S(2)}, u32[]{:S(2)}) collective-permute-start(bf16[128,384]{1,0:T(8,128)(2,1)S(1)} %get-tuple-element.46), channel_id=1, source_target_pairs={{0,12},{4,8},{8,4},{12,0},{1,13},{5,9},{9,5},{13,1},{2,14},{6,10},... | collective-permute-start | bytes 294920 | tf_op jit(solution)/shard_map/ppermute | solution.py:17
  16.5 2.3 %collective-permute-start.4 = (bf16[128,512]{1,0:T(8,128)(2,1)S(1)}, bf16[128,512]{1,0:T(8,128)(2,1)S(1)}, u32[]{:S(2)}, u32[]{:S(2)}) collective-permute-start(bf16[128,512]{1,0:T(8,128)(2,1)S(1)} %get-tuple-element.45.seen.send), channel_id=1, source_target_pairs={{0,12},{4,8},{8,4},{12,0},{1,13},{5,9},{9,5},{13,1},{2,14},{6,10},... | collective-permute-start | bytes 393224 | tf_op jit(solution)/shard_map/ppermute | solution.py:17
  18.8 1.3 %collective-permute-done.5.seen2.nexts_far = bf16[128,384]{1,0:T(8,128)(2,1)S(1)} collective-permute-done((bf16[128,384]{1,0:T(8,128)(2,1)S(1)}, bf16[128,384]{1,0:T(8,128)(2,1)S(1)}, u32[]{:S(2)}, u32[]{:S(2)}) %collective-permute-start.5) | collective-permute-done | bytes 98336 | tf_op jit(solution)/shard_map/ppermute | solution.py:17
  20.6 3.5 %collective-permute-start.8 = (bf16[128,640]{1,0:T(8,128)(2,1)S(1)}, bf16[128,640]{1,0:T(8,128)(2,1)S(1)}, u32[]{:S(2)}, u32[]{:S(2)}) collective-permute-start(bf16[128,640]{1,0:T(8,128)(2,1)S(1)} %get-tuple-element.50.seen.late), channel_id=1, source_target_pairs={{0,4},{4,0},{8,12},{12,8},{1,5},{5,1},{9,13},{13,9},{2,6},{6,2},{1... | collective-permute-start | bytes 491528 | tf_op jit(solution)/shard_map/ppermute | solution.py:17
  24.6 1.6 %collective-permute-start.10 = (bf16[128,384]{1,0:T(8,128)(2,1)S(1)}, bf16[128,384]{1,0:T(8,128)(2,1)S(1)}, u32[]{:S(2)}, u32[]{:S(2)}) collective-permute-start(bf16[128,384]{1,0:T(8,128)(2,1)S(1)} %shard_map.89.seen.a), channel_id=1, source_target_pairs={{0,2},{1,3},{2,0},{3,1},{4,6},{5,7},{6,4},{7,5},{8,10},{9,11},{10,... | collective-permute-start | bytes 294920 | tf_op jit(solution)/shard_map/ppermute | solution.py:17
  26.2 0.7 %shard_map.90 = (bf16[640,256]{1,0:T(8,128)(2,1)S(1)}, f32[128,256]{1,0:T(8,128)S(1)}, bf16[128,768]{1,0:T(8,128)(2,1)S(1)}) custom-call(f32[640,256]{1,0:T(8,128)S(1)} %get-tuple-element.40.seen.x1, bf16[128,512]{1,0:T(8,128)(2,1)S(1)} %get-tuple-element.45.seen.send, bf16[128,512]{1,0:T(8,128)(2,1)S(1)} %collective-permute-done.4.far, ...), custom_call_target="tpu_custom_call" | custom-call | flops 100000000 | tf_op jit(solution)/shard_map/pallas_call | solution.py:88
  26.9 2.4 %collective-permute-done.10.c = bf16[128,384]{1,0:T(8,128)(2,1)S(1)} collective-permute-done((bf16[128,384]{1,0:T(8,128)(2,1)S(1)}, bf16[128,384]{1,0:T(8,128)(2,1)S(1)}, u32[]{:S(2)}, u32[]{:S(2)}) %collective-permute-start.10) | collective-permute-done | bytes 98336 | tf_op jit(solution)/shard_map/ppermute | solution.py:17
  29.3 1.9 %collective-permute-start.13 = (bf16[128,768]{1,0:T(8,128)(2,1)S(1)}, bf16[128,768]{1,0:T(8,128)(2,1)S(1)}, u32[]{:S(2)}, u32[]{:S(2)}) collective-permute-start(bf16[128,768]{1,0:T(8,128)(2,1)S(1)} %get-tuple-element.58.z), channel_id=1, source_target_pairs={{0,4},{4,0},{8,12},{12,8},{1,5},{5,1},{9,13},{13,9},{2,6},{6,2},{1... | collective-permute-start | bytes 589832 | tf_op jit(solution)/shard_map/ppermute | solution.py:17
  31.3 0.9 %shard_map.91 = (f32[640,256]{1,0:T(8,128)S(1)}, bf16[640,512]{1,0:T(8,128)(2,1)S(1)}) custom-call(bf16[640,256]{1,0:T(8,128)(2,1)S(1)} %get-tuple-element.52.x2, bf16[2,1,640,128]{3,2,1,0:T(8,128)(2,1)S(1)} %get-tuple-element.36.rb, bf16[1,640,128]{2,1,0:T(8,128)(2,1)S(1)} %get-tuple-element.38.tl, bf16[1,640,128]{2,1,0:T(8,128)(2,1)S(1)} %get-tuple-element.39.tr, ...), custom_call_target="tpu_custom_call" | custom-call | flops 1000000000 | tf_op jit(solution)/shard_map/pallas_call | solution.py:88
  32.1 0.7 %shard_map.92.back = bf16[128,256]{1,0:T(8,128)(2,1)S(1)} custom-call(bf16[128,384]{1,0:T(8,128)(2,1)S(1)} %shard_map.89.seen.a, bf16[128,384]{1,0:T(8,128)(2,1)S(1)} %collective-permute-done.9.b, bf16[128,384]{1,0:T(8,128)(2,1)S(1)} %collective-permute-done.10.c, bf16[128,384]{1,0:T(8,128)(2,1)S(1)} %collective-permute-done.11.d, ...), custom_call_target="tpu_custom_call" | custom-call | flops 1000000000 | tf_op jit(solution)/shard_map/pallas_call | solution.py:88
  33.3 3.8 %collective-permute-done.13.z_sib = bf16[128,768]{1,0:T(8,128)(2,1)S(1)} collective-permute-done((bf16[128,768]{1,0:T(8,128)(2,1)S(1)}, bf16[128,768]{1,0:T(8,128)(2,1)S(1)}, u32[]{:S(2)}, u32[]{:S(2)}) %collective-permute-start.13) | collective-permute-done | bytes 196640 | tf_op jit(solution)/shard_map/ppermute | solution.py:17
  37.1 1.1 %collective-permute-done.12.back_sib = bf16[128,256]{1,0:T(8,128)(2,1)S(1)} collective-permute-done((bf16[128,256]{1,0:T(8,128)(2,1)S(1)}, bf16[128,256]{1,0:T(8,128)(2,1)S(1)}, u32[]{:S(2)}, u32[]{:S(2)}) %collective-permute-start.12) | collective-permute-done | bytes 65568 | tf_op jit(solution)/shard_map/ppermute | solution.py:17
  38.4 2.9 %collective-permute-start.14 = (bf16[128,256]{1,0:T(8,128)(2,1)S(1)}, bf16[128,256]{1,0:T(8,128)(2,1)S(1)}, u32[]{:S(2)}, u32[]{:S(2)}) collective-permute-start(bf16[128,256]{1,0:T(8,128)(2,1)S(1)} %get-tuple-element.60.half5), channel_id=1, source_target_pairs={{0,12},{4,8},{8,4},{12,0},{1,13},{5,9},{9,5},{13,1},{2,14},{6,10},... | collective-permute-start | bytes 196616 | tf_op jit(solution)/shard_map/ppermute | solution.py:17
  41.3 3.3 %collective-permute-done.14.half5_far = bf16[128,256]{1,0:T(8,128)(2,1)S(1)} collective-permute-done((bf16[128,256]{1,0:T(8,128)(2,1)S(1)}, bf16[128,256]{1,0:T(8,128)(2,1)S(1)}, u32[]{:S(2)}, u32[]{:S(2)}) %collective-permute-start.14) | collective-permute-done | bytes 65568 | tf_op jit(solution)/shard_map/ppermute | solution.py:17
  44.6 1.6 %shard_map.94 = f32[1,640,256]{2,1,0:T(8,128)} custom-call(f32[640,256]{1,0:T(8,128)S(1)} %get-tuple-element.54.seen.out2, bf16[640,512]{1,0:T(8,128)(2,1)S(1)} %get-tuple-element.55.under, bf16[256,256]{1,0:T(8,128)(2,1)S(1)} %get-tuple-element.59.both, bf16[128,256]{1,0:T(8,128)(2,1)S(1)} %get-tuple-element.60.half5, ...), custom_call_target="tpu_custom_call" | custom-call | flops 1000000000 | tf_op jit(solution)/shard_map/pallas_call | solution.py:88
  (21 shorter events, 2.4 us)
Async XLA Ops:
  0.0 2.4 %copy-start = (bf16[128,512]{1,0:T(8,128)(2,1)S(1)}, bf16[128,512]{1,0:T(8,128)(2,1)}, u32[]{:S(2)}) copy-start(bf16[128,512]{1,0:T(8,128)(2,1)} %a.1) | copy-start | bytes 393220
  2.4 3.2 %collective-permute-start.2 = (bf16[128,512]{1,0:T(8,128)(2,1)S(1)}, bf16[128,512]{1,0:T(8,128)(2,1)S(1)}, u32[]{:S(2)}, u32[]{:S(2)}) collective-permute-start(bf16[128,512]{1,0:T(8,128)(2,1)S(1)} %copy-done), channel_id=1, source_target_pairs={{0,1},{1,0},{2,3},{3,2},{4,5},{5,4},{6,7},{7,6},{8,9},{9,8},{10,11... | collective-permute-start | bytes 393224 | tf_op jit(solution)/shard_map/ppermute | solution.py:17
  2.9 5.3 %collective-permute-start = (bf16[128,256]{1,0:T(8,128)(2,1)S(1)}, bf16[128,256]{1,0:T(8,128)(2,1)S(1)}, u32[]{:S(2)}, u32[]{:S(2)}) collective-permute-start(bf16[128,256]{1,0:T(8,128)(2,1)S(1)} %get-tuple-element.34.p), channel_id=1, source_target_pairs={{0,4},{4,0},{8,12},{12,8},{1,5},{5,1},{9,13},{13,9},{2,6},{6,2},{1... | collective-permute-start | bytes 196616 | tf_op jit(solution)/shard_map/ppermute | solution.py:17
  6.1 7.1 %collective-permute-start.3 = (bf16[128,640]{1,0:T(8,128)(2,1)S(1)}, bf16[128,640]{1,0:T(8,128)(2,1)S(1)}, u32[]{:S(2)}, u32[]{:S(2)}) collective-permute-start(bf16[128,640]{1,0:T(8,128)(2,1)S(1)} %shard_map.84.own), channel_id=1, source_target_pairs={{0,4},{4,0},{8,12},{12,8},{1,5},{5,1},{9,13},{13,9},{2,6},{6,2},{1... | collective-permute-start | bytes 491528 | tf_op jit(solution)/shard_map/ppermute | solution.py:17
  9.1 7.3 %collective-permute-start.1 = (bf16[128,512]{1,0:T(8,128)(2,1)S(1)}, bf16[128,512]{1,0:T(8,128)(2,1)S(1)}, u32[]{:S(2)}, u32[]{:S(2)}) collective-permute-start(bf16[128,512]{1,0:T(8,128)(2,1)S(1)} %get-tuple-element.42), channel_id=1, source_target_pairs={{0,4},{4,0},{8,12},{12,8},{1,5},{5,1},{9,13},{13,9},{2,6},{6,2},{1... | collective-permute-start | bytes 393224 | tf_op jit(solution)/shard_map/ppermute | solution.py:17
  10.9 7.9 %collective-permute-start.6 = (bf16[128,512]{1,0:T(8,128)(2,1)S(1)}, bf16[128,512]{1,0:T(8,128)(2,1)S(1)}, u32[]{:S(2)}, u32[]{:S(2)}) collective-permute-start(bf16[128,512]{1,0:T(8,128)(2,1)S(1)} %copy-done), channel_id=1, source_target_pairs={{0,2},{1,3},{2,0},{3,1},{4,6},{5,7},{6,4},{7,5},{8,10},{9,11},{10,... | collective-permute-start | bytes 393224 | tf_op jit(solution)/shard_map/ppermute | solution.py:17
  13.3 6.8 %collective-permute-start.5 = (bf16[128,384]{1,0:T(8,128)(2,1)S(1)}, bf16[128,384]{1,0:T(8,128)(2,1)S(1)}, u32[]{:S(2)}, u32[]{:S(2)}) collective-permute-start(bf16[128,384]{1,0:T(8,128)(2,1)S(1)} %get-tuple-element.46), channel_id=1, source_target_pairs={{0,12},{4,8},{8,4},{12,0},{1,13},{5,9},{9,5},{13,1},{2,14},{6,10},... | collective-permute-start | bytes 294920 | tf_op jit(solution)/shard_map/ppermute | solution.py:17
  16.5 7.9 %collective-permute-start.4 = (bf16[128,512]{1,0:T(8,128)(2,1)S(1)}, bf16[128,512]{1,0:T(8,128)(2,1)S(1)}, u32[]{:S(2)}, u32[]{:S(2)}) collective-permute-start(bf16[128,512]{1,0:T(8,128)(2,1)S(1)} %get-tuple-element.45.seen.send), channel_id=1, source_target_pairs={{0,12},{4,8},{8,4},{12,0},{1,13},{5,9},{9,5},{13,1},{2,14},{6,10},... | collective-permute-start | bytes 393224 | tf_op jit(solution)/shard_map/ppermute | solution.py:17
  18.8 5.2 %collective-permute-start.7 = (bf16[128,512]{1,0:T(8,128)(2,1)S(1)}, bf16[128,512]{1,0:T(8,128)(2,1)S(1)}, u32[]{:S(2)}, u32[]{:S(2)}) collective-permute-start(bf16[128,512]{1,0:T(8,128)(2,1)S(1)} %collective-permute-done.6.c), channel_id=1, source_target_pairs={{0,1},{1,0},{2,3},{3,2},{4,5},{5,4},{6,7},{7,6},{8,9},{9,8},{10,11... | collective-permute-start | bytes 393224 | tf_op jit(solution)/shard_map/ppermute | solution.py:17
  20.6 10.7 %collective-permute-start.8 = (bf16[128,640]{1,0:T(8,128)(2,1)S(1)}, bf16[128,640]{1,0:T(8,128)(2,1)S(1)}, u32[]{:S(2)}, u32[]{:S(2)}) collective-permute-start(bf16[128,640]{1,0:T(8,128)(2,1)S(1)} %get-tuple-element.50.seen.late), channel_id=1, source_target_pairs={{0,4},{4,0},{8,12},{12,8},{1,5},{5,1},{9,13},{13,9},{2,6},{6,2},{1... | collective-permute-start | bytes 491528 | tf_op jit(solution)/shard_map/ppermute | solution.py:17
  24.6 4.7 %collective-permute-start.10 = (bf16[128,384]{1,0:T(8,128)(2,1)S(1)}, bf16[128,384]{1,0:T(8,128)(2,1)S(1)}, u32[]{:S(2)}, u32[]{:S(2)}) collective-permute-start(bf16[128,384]{1,0:T(8,128)(2,1)S(1)} %shard_map.89.seen.a), channel_id=1, source_target_pairs={{0,2},{1,3},{2,0},{3,1},{4,6},{5,7},{6,4},{7,5},{8,10},{9,11},{10,... | collective-permute-start | bytes 294920 | tf_op jit(solution)/shard_map/ppermute | solution.py:17
  26.2 5.9 %collective-permute-start.9 = (bf16[128,384]{1,0:T(8,128)(2,1)S(1)}, bf16[128,384]{1,0:T(8,128)(2,1)S(1)}, u32[]{:S(2)}, u32[]{:S(2)}) collective-permute-start(bf16[128,384]{1,0:T(8,128)(2,1)S(1)} %shard_map.89.seen.a), channel_id=1, source_target_pairs={{0,1},{1,0},{2,3},{3,2},{4,5},{5,4},{6,7},{7,6},{8,9},{9,8},{10,11... | collective-permute-start | bytes 294920 | tf_op jit(solution)/shard_map/ppermute | solution.py:17
  29.3 2.8 %collective-permute-start.11 = (bf16[128,384]{1,0:T(8,128)(2,1)S(1)}, bf16[128,384]{1,0:T(8,128)(2,1)S(1)}, u32[]{:S(2)}, u32[]{:S(2)}) collective-permute-start(bf16[128,384]{1,0:T(8,128)(2,1)S(1)} %collective-permute-done.10.c), channel_id=1, source_target_pairs={{0,1},{1,0},{2,3},{3,2},{4,5},{5,4},{6,7},{7,6},{8,9},{9,8},{10,11... | collective-permute-start | bytes 294920 | tf_op jit(solution)/shard_map/ppermute | solution.py:17
  29.3 7.8 %collective-permute-start.13 = (bf16[128,768]{1,0:T(8,128)(2,1)S(1)}, bf16[128,768]{1,0:T(8,128)(2,1)S(1)}, u32[]{:S(2)}, u32[]{:S(2)}) collective-permute-start(bf16[128,768]{1,0:T(8,128)(2,1)S(1)} %get-tuple-element.58.z), channel_id=1, source_target_pairs={{0,4},{4,0},{8,12},{12,8},{1,5},{5,1},{9,13},{13,9},{2,6},{6,2},{1... | collective-permute-start | bytes 589832 | tf_op jit(solution)/shard_map/ppermute | solution.py:17
  32.8 5.4 %collective-permute-start.12 = (bf16[128,256]{1,0:T(8,128)(2,1)S(1)}, bf16[128,256]{1,0:T(8,128)(2,1)S(1)}, u32[]{:S(2)}, u32[]{:S(2)}) collective-permute-start(bf16[128,256]{1,0:T(8,128)(2,1)S(1)} %shard_map.92.back), channel_id=1, source_target_pairs={{0,4},{4,0},{8,12},{12,8},{1,5},{5,1},{9,13},{13,9},{2,6},{6,2},{1... | collective-permute-start | bytes 196616 | tf_op jit(solution)/shard_map/ppermute | solution.py:17
  38.4 6.2 %collective-permute-start.14 = (bf16[128,256]{1,0:T(8,128)(2,1)S(1)}, bf16[128,256]{1,0:T(8,128)(2,1)S(1)}, u32[]{:S(2)}, u32[]{:S(2)}) collective-permute-start(bf16[128,256]{1,0:T(8,128)(2,1)S(1)} %get-tuple-element.60.half5), channel_id=1, source_target_pairs={{0,12},{4,8},{8,4},{12,0},{1,13},{5,9},{9,5},{13,1},{2,14},{6,10},... | collective-permute-start | bytes 196616 | tf_op jit(solution)/shard_map/ppermute | solution.py:17

commit v10 on v9

--- a/solution.py
+++ b/solution.py
@@ -199,7 +199,6 @@
     proj1_sib = swap(proj1, "leaf", 1)
     caps_here = after(top_caps, proj1)
     caps_near = swap(caps_here, "top", 1)
-    caps_far = swap(caps_here, "top", 2)
 
     def early_body(lb, caps, tl, tr, seen, out):
         for i, basis in enumerate((tr, tl)):
@@ -281,7 +280,8 @@
     )
     cross_in = swap(cross_send, "leaf", 3)
 
-    caps_far_near = swap(after(caps_far, cross_send), "top", 1)
+    caps_far = swap(after(top_caps, cross_send), "top", 2)
+    caps_far_near = swap(caps_far, "top", 1)
 
     def order_body(a, b, c, d, out):
         here = lax.axis_index("top")
@@ -299,16 +299,16 @@
         micros=0.1,
     )
 
-    def late_body(lb, rb, caps, tl, tr, seen, seen2, out, gram5):
+    def late_body(lb, rb, caps, tl, tr, seen, seen2, out):
         for i, basis in enumerate((tl[0], tr[0])):
             out[:, span(i)] = (dot_t(lb[0, 0], basis) * s1).astype(BF)
-            gram5[:, span(i)] = (dot_t(lb[1, 0], basis) * s2).astype(BF)
+            out[:, span(5 + i)] = (dot_t(lb[1, 0], basis) * s2).astype(BF)
         out[:, span(2)] = (dot_t(lb[0, 0], rb[1, 0]) * s1).astype(BF)
         out[:, span(3, 2)] = caps[1, 0]
 
-    late, gram5 = call(
+    (late,) = call(
         late_body,
-        [((rank, 5 * rank), BF), ((rank, 2 * rank), BF)],
+        [((rank, 7 * rank), BF)],
         lb,
         rb,
         caps,
@@ -320,7 +320,7 @@
     )
     late_sib = swap(late, "leaf", 1)
 
-    def column_body(send, keep2, far, nexts, nexts_far, gram, seen, seen2, out):
+    def column_body(send, keep2, far, nexts, nexts_far, gram, seen, out):
         side = column_side()
         own, other = send[:, block(side, half)], far[:, block(side, half)]
         for i in range(2):
@@ -342,36 +342,33 @@
         next_far,
         gram_pair,
         late,
-        caps_all,
         micros=0.2,
     )
-    top_near = swap(top_send, "top", 1)
     top_far = swap(top_send, "top", 2)
 
-    def two_body(x1, send, far, lb, caps, gram5, seen, x2, z5, z, stack):
+    def two_body(x1, send, far, lb, caps, seen, x2, z5, z, stack):
         put_rows(stack, tree_side(1), send[:, :cols], far[:, :cols])
         coef = dot(caps[1, 0], stack[...]).astype(BF)
         x2[...] = (x1[...] - dot(lb[1, 0], coef)).astype(BF)
         z5[...] = dot_t(lb[1, 0], x2[...]) * s2
         z[:, :cols] = z5[...].astype(BF)
-        z[:, cols : 2 * cols] = (dot_t(lb[0, 0], x2[...]) * s1).astype(BF)
-        z[:, 2 * cols :] = gram5[...]
+        z[:, cols:] = (dot_t(lb[0, 0], x2[...]) * s1).astype(BF)
 
     state2, down5, down_send = call(
         two_body,
-        [(tall, BF), (wide, f32), ((rank, 2 * cols + 2 * rank), BF)],
+        [(tall, BF), (wide, f32), ((rank, 2 * cols), BF)],
         state1,
         cross_send,
         cross_in,
         lb,
         caps,
-        gram5,
         top_send,
         scratch=[pltpu.VMEM((2 * rank, cols), BF)],
         micros=0.1,
     )
     down_in = swap(down_send, "leaf", 1)
-    top_parts = top_send, top_near, top_far, swap(after(top_far, state2), "top", 1)
+    top_near = swap(after(top_send, state2), "top", 1)
+    top_parts = top_send, top_near, top_far, swap(top_far, "top", 1)
 
     def under_body(x2, rb, tl, tr, inv, seen, out2, under):
         for c in range(blocks):
@@ -413,11 +410,11 @@
     )
     back_in = swap(back_send, "leaf", 1)
 
-    def down_body(back, back_sib, down5, z, z_sib, both, send):
+    def down_body(back, back_sib, down5, z_sib, late, late_sib, both, send):
         side = column_side()
         for i in range(2):
             put_columns(both.at[span(i), :], side, back[:, part(i)], back_sib[:, part(i)])
-        gram = (z[:, 2 * cols :].astype(f32) + z_sib[:, 2 * cols :]).astype(BF)
+        gram = (late[:, span(5, 2)].astype(f32) + late_sib[:, span(5, 2)]).astype(BF)
         send[...] = (down5[...] + z_sib[:, :cols] - dot(gram, both[...])).astype(BF)
 
     both, half5 = call(
@@ -426,8 +423,9 @@
         back_send,
         back_in,
         down5,
-        down_send,
         down_in,
+        late,
+        late_sib,
         micros=0.3,
     )
     half5_far = swap(half5, "leaf", 3)
@@ -444,7 +442,7 @@
 
         def proj(zs, gram, coef):
             return (
-                zs[:, cols : 2 * cols]
+                zs[:, cols:]
                 - dot(gram[:, span(0, 2)], both[...])
                 - dot(gram[:, span(2)], coef)
             ).astype(BF)

time: 46.4 us -> 44 us (0.948)
  waiting for transfers between devices: 13.9 us -> 11.3 us
    ppermute x15, waiting for transfers between devices: 13.9 us -> 11.3 us  [swap(): return lax.ppermute(value, axis, pairs)]
where the time goes in v10:
time: 44 us; the launch traced here: 43.9 us
  starting transfers between devices  23.6 us (54%)
  waiting for transfers between devices  11.3 us (26%)
  Pallas kernels  8.81 us (20%)
    ppermute x15, starting transfers between devices, swap(): return lax.ppermute(value, axis, pairs)  23.6 us
    ppermute x15, waiting for transfers between devices, swap(): return lax.ppermute(value, axis, pairs)  11.3 us
    pallas_call x13, Pallas kernels, call(): pl.pallas_call(body, out_shape=[jax.ShapeDtypeStruct(shape, dtype) if hbm...  8.81 us
  transfers between devices with their start and end apart: 15, of which 8 were waited for; matrix products, arithmetic and copies ran while one was open for 0% of the time, Pallas kernels for 10%

profile of v10, /device:TPU:0, one launch (start us, length us, event | category | flops | bytes accessed | tf_op | source)
XLA Modules:
  0.0 43.9 jit_solution(12274101113070866716)
XLA Ops:
  0.0 2.4 %shard_map.82 = (f32[640,256]{1,0:T(8,128)S(1)}, bf16[128,256]{1,0:T(8,128)(2,1)S(1)}, bf16[640,640]{1,0:T(8,128)(2,1)S(1)}, bf16[2,1,640,128]{3,2,1,0:T(8,128)(...) custom-call(f32[1,640,256]{2,1,0:T(8,128)} %rhs_hbm.1, ...), custom_call_target="tpu_custom_call" | custom-call | flops 1000000000 | tf_op jit(solution)/shard_map/pallas_call | solution.py:88
  2.9 2.6 %collective-permute-start = (bf16[128,256]{1,0:T(8,128)(2,1)S(1)}, bf16[128,256]{1,0:T(8,128)(2,1)S(1)}, u32[]{:S(2)}, u32[]{:S(2)}) collective-permute-start(bf16[128,256]{1,0:T(8,128)(2,1)S(1)} %get-tuple-element.32.p), channel_id=1, source_target_pairs={{0,4},{4,0},{8,12},{12,8},{1,5},{5,1},{9,13},{13,9},{2,6},{6,2},{1... | collective-permute-start | bytes 196616 | tf_op jit(solution)/shard_map/ppermute | solution.py:17
  5.6 0.6 %shard_map.84.own = bf16[128,640]{1,0:T(8,128)(2,1)S(1)} custom-call(bf16[2,1,640,128]{3,2,1,0:T(8,128)(2,1)S(1)} %get-tuple-element.33.lb, bf16[2,1,128,256]{3,2,1,0:T(8,128)(2,1)S(1)} %get-tuple-element.35.caps, bf16[1,640,128]{2,1,0:T(8,128)(2,1)S(1)} %get-tuple-element.36.tl, bf16[1,640,128]{2,1,0:T(8,128)(2,1)S(1)} %get-tuple-element.37.tr, ...), custom_call_target="tpu_custom_call" | custom-call | flops 10000000000 | tf_op jit(solution)/shard_map/pallas_call | solution.py:88
  6.1 1.3 %collective-permute-start.3 = (bf16[128,640]{1,0:T(8,128)(2,1)S(1)}, bf16[128,640]{1,0:T(8,128)(2,1)S(1)}, u32[]{:S(2)}, u32[]{:S(2)}) collective-permute-start(bf16[128,640]{1,0:T(8,128)(2,1)S(1)} %shard_map.84.own), channel_id=1, source_target_pairs={{0,4},{4,0},{8,12},{12,8},{1,5},{5,1},{9,13},{13,9},{2,6},{6,2},{1... | collective-permute-start | bytes 491528 | tf_op jit(solution)/shard_map/ppermute | solution.py:17
  7.5 0.8 %collective-permute-done.p_sib = bf16[128,256]{1,0:T(8,128)(2,1)S(1)} collective-permute-done((bf16[128,256]{1,0:T(8,128)(2,1)S(1)}, bf16[128,256]{1,0:T(8,128)(2,1)S(1)}, u32[]{:S(2)}, u32[]{:S(2)}) %collective-permute-start) | collective-permute-done | bytes 65568 | tf_op jit(solution)/shard_map/ppermute | solution.py:17
  8.3 0.8 %shard_map.83 = (f32[640,256]{1,0:T(8,128)S(1)}, bf16[128,512]{1,0:T(8,128)(2,1)S(1)}, f32[128,512]{1,0:T(8,128)S(1)}) custom-call(f32[640,256]{1,0:T(8,128)S(1)} %get-tuple-element.31.x0, bf16[128,256]{1,0:T(8,128)(2,1)S(1)} %get-tuple-element.32.p, bf16[128,256]{1,0:T(8,128)(2,1)S(1)} %collective-permute-done.p_sib, ...), custom_call_target="tpu_custom_call" | custom-call | flops 3000000000 | tf_op jit(solution)/shard_map/pallas_call | solution.py:88
  9.1 1.8 %collective-permute-start.1 = (bf16[128,512]{1,0:T(8,128)(2,1)S(1)}, bf16[128,512]{1,0:T(8,128)(2,1)S(1)}, u32[]{:S(2)}, u32[]{:S(2)}) collective-permute-start(bf16[128,512]{1,0:T(8,128)(2,1)S(1)} %get-tuple-element.40), channel_id=1, source_target_pairs={{0,4},{4,0},{8,12},{12,8},{1,5},{5,1},{9,13},{13,9},{2,6},{6,2},{1... | collective-permute-start | bytes 393224 | tf_op jit(solution)/shard_map/ppermute | solution.py:17
  10.9 2.3 %collective-permute-done.3.sib = bf16[128,640]{1,0:T(8,128)(2,1)S(1)} collective-permute-done((bf16[128,640]{1,0:T(8,128)(2,1)S(1)}, bf16[128,640]{1,0:T(8,128)(2,1)S(1)}, u32[]{:S(2)}, u32[]{:S(2)}) %collective-permute-start.3) | collective-permute-done | bytes 163872 | tf_op jit(solution)/shard_map/ppermute | solution.py:17
  13.3 3.0 %collective-permute-start.5 = (bf16[128,384]{1,0:T(8,128)(2,1)S(1)}, bf16[128,384]{1,0:T(8,128)(2,1)S(1)}, u32[]{:S(2)}, u32[]{:S(2)}) collective-permute-start(bf16[128,384]{1,0:T(8,128)(2,1)S(1)} %get-tuple-element.45), channel_id=1, source_target_pairs={{0,12},{4,8},{8,4},{12,0},{1,13},{5,9},{9,5},{13,1},{2,14},{6,10},... | collective-permute-start | bytes 294920 | tf_op jit(solution)/shard_map/ppermute | solution.py:17
  16.5 2.3 %collective-permute-start.4 = (bf16[128,512]{1,0:T(8,128)(2,1)S(1)}, bf16[128,512]{1,0:T(8,128)(2,1)S(1)}, u32[]{:S(2)}, u32[]{:S(2)}) collective-permute-start(bf16[128,512]{1,0:T(8,128)(2,1)S(1)} %get-tuple-element.43.seen.send), channel_id=1, source_target_pairs={{0,12},{4,8},{8,4},{12,0},{1,13},{5,9},{9,5},{13,1},{2,14},{6,10},... | collective-permute-start | bytes 393224 | tf_op jit(solution)/shard_map/ppermute | solution.py:17
  18.8 1.5 %collective-permute-start.10 = (bf16[128,512]{1,0:T(8,128)(2,1)S(1)}, bf16[128,512]{1,0:T(8,128)(2,1)S(1)}, u32[]{:S(2)}, u32[]{:S(2)}) collective-permute-start(bf16[128,512]{1,0:T(8,128)(2,1)S(1)} %copy-done), channel_id=1, source_target_pairs={{0,2},{1,3},{2,0},{3,1},{4,6},{5,7},{6,4},{7,5},{8,10},{9,11},{10,... | collective-permute-start | bytes 393224 | tf_op jit(solution)/shard_map/ppermute | solution.py:17
  20.7 3.0 %collective-permute-start.6 = (bf16[128,896]{1,0:T(8,128)(2,1)S(1)}, bf16[128,896]{1,0:T(8,128)(2,1)S(1)}, u32[]{:S(2)}, u32[]{:S(2)}) collective-permute-start(bf16[128,896]{1,0:T(8,128)(2,1)S(1)} %shard_map.87.seen.late), channel_id=1, source_target_pairs={{0,4},{4,0},{8,12},{12,8},{1,5},{5,1},{9,13},{13,9},{2,6},{6,2},{1... | collective-permute-start | bytes 688136 | tf_op jit(solution)/shard_map/ppermute | solution.py:17
  23.8 1.0 %collective-permute-done.4.far = bf16[128,512]{1,0:T(8,128)(2,1)S(1)} collective-permute-done((bf16[128,512]{1,0:T(8,128)(2,1)S(1)}, bf16[128,512]{1,0:T(8,128)(2,1)S(1)}, u32[]{:S(2)}, u32[]{:S(2)}) %collective-permute-start.4) | collective-permute-done | bytes 131104 | tf_op jit(solution)/shard_map/ppermute | solution.py:17
  25.0 1.6 %collective-permute-start.8 = (bf16[128,384]{1,0:T(8,128)(2,1)S(1)}, bf16[128,384]{1,0:T(8,128)(2,1)S(1)}, u32[]{:S(2)}, u32[]{:S(2)}) collective-permute-start(bf16[128,384]{1,0:T(8,128)(2,1)S(1)} %shard_map.88.seen.a), channel_id=1, source_target_pairs={{0,2},{1,3},{2,0},{3,1},{4,6},{5,7},{6,4},{7,5},{8,10},{9,11},{10,... | collective-permute-start | bytes 294920 | tf_op jit(solution)/shard_map/ppermute | solution.py:17
  26.5 0.7 %shard_map.89 = (bf16[640,256]{1,0:T(8,128)(2,1)S(1)}, f32[128,256]{1,0:T(8,128)S(1)}, bf16[128,512]{1,0:T(8,128)(2,1)S(1)}) custom-call(f32[640,256]{1,0:T(8,128)S(1)} %get-tuple-element.38.seen.x1, bf16[128,512]{1,0:T(8,128)(2,1)S(1)} %get-tuple-element.43.seen.send, bf16[128,512]{1,0:T(8,128)(2,1)S(1)} %collective-permute-done.4.far, ...), custom_call_target="tpu_custom_call" | custom-call | flops 100000000 | tf_op jit(solution)/shard_map/pallas_call | solution.py:88
  27.4 1.7 %collective-permute-start.13 = (bf16[128,512]{1,0:T(8,128)(2,1)S(1)}, bf16[128,512]{1,0:T(8,128)(2,1)S(1)}, u32[]{:S(2)}, u32[]{:S(2)}) collective-permute-start(bf16[128,512]{1,0:T(8,128)(2,1)S(1)} %get-tuple-element.54.z), channel_id=1, source_target_pairs={{0,4},{4,0},{8,12},{12,8},{1,5},{5,1},{9,13},{13,9},{2,6},{6,2},{1... | collective-permute-start | bytes 393224 | tf_op jit(solution)/shard_map/ppermute | solution.py:17
  29.0 0.6 %collective-permute-done.8.c = bf16[128,384]{1,0:T(8,128)(2,1)S(1)} collective-permute-done((bf16[128,384]{1,0:T(8,128)(2,1)S(1)}, bf16[128,384]{1,0:T(8,128)(2,1)S(1)}, u32[]{:S(2)}, u32[]{:S(2)}) %collective-permute-start.8) | collective-permute-done | bytes 98336 | tf_op jit(solution)/shard_map/ppermute | solution.py:17
  29.8 0.9 %shard_map.90 = (f32[640,256]{1,0:T(8,128)S(1)}, bf16[640,512]{1,0:T(8,128)(2,1)S(1)}) custom-call(bf16[640,256]{1,0:T(8,128)(2,1)S(1)} %get-tuple-element.47.x2, bf16[2,1,640,128]{3,2,1,0:T(8,128)(2,1)S(1)} %get-tuple-element.34.rb, bf16[1,640,128]{2,1,0:T(8,128)(2,1)S(1)} %get-tuple-element.36.tl, bf16[1,640,128]{2,1,0:T(8,128)(2,1)S(1)} %get-tuple-element.37.tr, ...), custom_call_target="tpu_custom_call" | custom-call | flops 1000000000 | tf_op jit(solution)/shard_map/pallas_call | solution.py:88
  30.9 0.7 %shard_map.92.back = bf16[128,256]{1,0:T(8,128)(2,1)S(1)} custom-call(bf16[128,384]{1,0:T(8,128)(2,1)S(1)} %shard_map.88.seen.a, bf16[128,384]{1,0:T(8,128)(2,1)S(1)} %collective-permute-done.7.b, bf16[128,384]{1,0:T(8,128)(2,1)S(1)} %collective-permute-done.8.c, bf16[128,384]{1,0:T(8,128)(2,1)S(1)} %collective-permute-done.9.d, ...), custom_call_target="tpu_custom_call" | custom-call | flops 1000000000 | tf_op jit(solution)/shard_map/pallas_call | solution.py:88
  31.6 1.7 %collective-permute-start.12 = (bf16[128,256]{1,0:T(8,128)(2,1)S(1)}, bf16[128,256]{1,0:T(8,128)(2,1)S(1)}, u32[]{:S(2)}, u32[]{:S(2)}) collective-permute-start(bf16[128,256]{1,0:T(8,128)(2,1)S(1)} %shard_map.92.back), channel_id=1, source_target_pairs={{0,4},{4,0},{8,12},{12,8},{1,5},{5,1},{9,13},{13,9},{2,6},{6,2},{1... | collective-permute-start | bytes 196616 | tf_op jit(solution)/shard_map/ppermute | solution.py:17
  33.3 2.7 %collective-permute-done.12.back_sib = bf16[128,256]{1,0:T(8,128)(2,1)S(1)} collective-permute-done((bf16[128,256]{1,0:T(8,128)(2,1)S(1)}, bf16[128,256]{1,0:T(8,128)(2,1)S(1)}, u32[]{:S(2)}, u32[]{:S(2)}) %collective-permute-start.12) | collective-permute-done | bytes 65568 | tf_op jit(solution)/shard_map/ppermute | solution.py:17
  36.2 2.6 %collective-permute-start.14 = (bf16[128,256]{1,0:T(8,128)(2,1)S(1)}, bf16[128,256]{1,0:T(8,128)(2,1)S(1)}, u32[]{:S(2)}, u32[]{:S(2)}) collective-permute-start(bf16[128,256]{1,0:T(8,128)(2,1)S(1)} %get-tuple-element.56.half5), channel_id=1, source_target_pairs={{0,12},{4,8},{8,4},{12,0},{1,13},{5,9},{9,5},{13,1},{2,14},{6,10},... | collective-permute-start | bytes 196616 | tf_op jit(solution)/shard_map/ppermute | solution.py:17
  38.8 3.5 %collective-permute-done.14.half5_far = bf16[128,256]{1,0:T(8,128)(2,1)S(1)} collective-permute-done((bf16[128,256]{1,0:T(8,128)(2,1)S(1)}, bf16[128,256]{1,0:T(8,128)(2,1)S(1)}, u32[]{:S(2)}, u32[]{:S(2)}) %collective-permute-start.14) | collective-permute-done | bytes 65568 | tf_op jit(solution)/shard_map/ppermute | solution.py:17
  42.3 1.6 %shard_map.94 = f32[1,640,256]{2,1,0:T(8,128)} custom-call(f32[640,256]{1,0:T(8,128)S(1)} %get-tuple-element.49.seen.out2, bf16[640,512]{1,0:T(8,128)(2,1)S(1)} %get-tuple-element.50.under, bf16[256,256]{1,0:T(8,128)(2,1)S(1)} %get-tuple-element.55.both, bf16[128,256]{1,0:T(8,128)(2,1)S(1)} %get-tuple-element.56.half5, ...), custom_call_target="tpu_custom_call" | custom-call | flops 1000000000 | tf_op jit(solution)/shard_map/pallas_call | solution.py:88
  (21 shorter events, 2.1 us)
Async XLA Ops:
  0.0 2.4 %copy-start = (bf16[128,512]{1,0:T(8,128)(2,1)S(1)}, bf16[128,512]{1,0:T(8,128)(2,1)}, u32[]{:S(2)}) copy-start(bf16[128,512]{1,0:T(8,128)(2,1)} %a.1) | copy-start | bytes 393220
  2.4 3.2 %collective-permute-start.2 = (bf16[128,512]{1,0:T(8,128)(2,1)S(1)}, bf16[128,512]{1,0:T(8,128)(2,1)S(1)}, u32[]{:S(2)}, u32[]{:S(2)}) collective-permute-start(bf16[128,512]{1,0:T(8,128)(2,1)S(1)} %copy-done), channel_id=1, source_target_pairs={{0,1},{1,0},{2,3},{3,2},{4,5},{5,4},{6,7},{7,6},{8,9},{9,8},{10,11... | collective-permute-start | bytes 393224 | tf_op jit(solution)/shard_map/ppermute | solution.py:17
  2.9 5.3 %collective-permute-start = (bf16[128,256]{1,0:T(8,128)(2,1)S(1)}, bf16[128,256]{1,0:T(8,128)(2,1)S(1)}, u32[]{:S(2)}, u32[]{:S(2)}) collective-permute-start(bf16[128,256]{1,0:T(8,128)(2,1)S(1)} %get-tuple-element.32.p), channel_id=1, source_target_pairs={{0,4},{4,0},{8,12},{12,8},{1,5},{5,1},{9,13},{13,9},{2,6},{6,2},{1... | collective-permute-start | bytes 196616 | tf_op jit(solution)/shard_map/ppermute | solution.py:17
  6.1 7.1 %collective-permute-start.3 = (bf16[128,640]{1,0:T(8,128)(2,1)S(1)}, bf16[128,640]{1,0:T(8,128)(2,1)S(1)}, u32[]{:S(2)}, u32[]{:S(2)}) collective-permute-start(bf16[128,640]{1,0:T(8,128)(2,1)S(1)} %shard_map.84.own), channel_id=1, source_target_pairs={{0,4},{4,0},{8,12},{12,8},{1,5},{5,1},{9,13},{13,9},{2,6},{6,2},{1... | collective-permute-start | bytes 491528 | tf_op jit(solution)/shard_map/ppermute | solution.py:17
  9.1 7.3 %collective-permute-start.1 = (bf16[128,512]{1,0:T(8,128)(2,1)S(1)}, bf16[128,512]{1,0:T(8,128)(2,1)S(1)}, u32[]{:S(2)}, u32[]{:S(2)}) collective-permute-start(bf16[128,512]{1,0:T(8,128)(2,1)S(1)} %get-tuple-element.40), channel_id=1, source_target_pairs={{0,4},{4,0},{8,12},{12,8},{1,5},{5,1},{9,13},{13,9},{2,6},{6,2},{1... | collective-permute-start | bytes 393224 | tf_op jit(solution)/shard_map/ppermute | solution.py:17
  13.3 7.0 %collective-permute-start.5 = (bf16[128,384]{1,0:T(8,128)(2,1)S(1)}, bf16[128,384]{1,0:T(8,128)(2,1)S(1)}, u32[]{:S(2)}, u32[]{:S(2)}) collective-permute-start(bf16[128,384]{1,0:T(8,128)(2,1)S(1)} %get-tuple-element.45), channel_id=1, source_target_pairs={{0,12},{4,8},{8,4},{12,0},{1,13},{5,9},{9,5},{13,1},{2,14},{6,10},... | collective-permute-start | bytes 294920 | tf_op jit(solution)/shard_map/ppermute | solution.py:17
  16.5 8.2 %collective-permute-start.4 = (bf16[128,512]{1,0:T(8,128)(2,1)S(1)}, bf16[128,512]{1,0:T(8,128)(2,1)S(1)}, u32[]{:S(2)}, u32[]{:S(2)}) collective-permute-start(bf16[128,512]{1,0:T(8,128)(2,1)S(1)} %get-tuple-element.43.seen.send), channel_id=1, source_target_pairs={{0,12},{4,8},{8,4},{12,0},{1,13},{5,9},{9,5},{13,1},{2,14},{6,10},... | collective-permute-start | bytes 393224 | tf_op jit(solution)/shard_map/ppermute | solution.py:17
  18.8 5.0 %collective-permute-start.10 = (bf16[128,512]{1,0:T(8,128)(2,1)S(1)}, bf16[128,512]{1,0:T(8,128)(2,1)S(1)}, u32[]{:S(2)}, u32[]{:S(2)}) collective-permute-start(bf16[128,512]{1,0:T(8,128)(2,1)S(1)} %copy-done), channel_id=1, source_target_pairs={{0,2},{1,3},{2,0},{3,1},{4,6},{5,7},{6,4},{7,5},{8,10},{9,11},{10,... | collective-permute-start | bytes 393224 | tf_op jit(solution)/shard_map/ppermute | solution.py:17
  20.7 9.0 %collective-permute-start.6 = (bf16[128,896]{1,0:T(8,128)(2,1)S(1)}, bf16[128,896]{1,0:T(8,128)(2,1)S(1)}, u32[]{:S(2)}, u32[]{:S(2)}) collective-permute-start(bf16[128,896]{1,0:T(8,128)(2,1)S(1)} %shard_map.87.seen.late), channel_id=1, source_target_pairs={{0,4},{4,0},{8,12},{12,8},{1,5},{5,1},{9,13},{13,9},{2,6},{6,2},{1... | collective-permute-start | bytes 688136 | tf_op jit(solution)/shard_map/ppermute | solution.py:17
  23.8 5.9 %collective-permute-start.11 = (bf16[128,512]{1,0:T(8,128)(2,1)S(1)}, bf16[128,512]{1,0:T(8,128)(2,1)S(1)}, u32[]{:S(2)}, u32[]{:S(2)}) collective-permute-start(bf16[128,512]{1,0:T(8,128)(2,1)S(1)} %collective-permute-done.10.c), channel_id=1, source_target_pairs={{0,1},{1,0},{2,3},{3,2},{4,5},{5,4},{6,7},{7,6},{8,9},{9,8},{10,11... | collective-permute-start | bytes 393224 | tf_op jit(solution)/shard_map/ppermute | solution.py:17
  25.0 4.7 %collective-permute-start.8 = (bf16[128,384]{1,0:T(8,128)(2,1)S(1)}, bf16[128,384]{1,0:T(8,128)(2,1)S(1)}, u32[]{:S(2)}, u32[]{:S(2)}) collective-permute-start(bf16[128,384]{1,0:T(8,128)(2,1)S(1)} %shard_map.88.seen.a), channel_id=1, source_target_pairs={{0,2},{1,3},{2,0},{3,1},{4,6},{5,7},{6,4},{7,5},{8,10},{9,11},{10,... | collective-permute-start | bytes 294920 | tf_op jit(solution)/shard_map/ppermute | solution.py:17
  27.3 3.4 %collective-permute-start.7 = (bf16[128,384]{1,0:T(8,128)(2,1)S(1)}, bf16[128,384]{1,0:T(8,128)(2,1)S(1)}, u32[]{:S(2)}, u32[]{:S(2)}) collective-permute-start(bf16[128,384]{1,0:T(8,128)(2,1)S(1)} %shard_map.88.seen.a), channel_id=1, source_target_pairs={{0,1},{1,0},{2,3},{3,2},{4,5},{5,4},{6,7},{7,6},{8,9},{9,8},{10,11... | collective-permute-start | bytes 294920 | tf_op jit(solution)/shard_map/ppermute | solution.py:17
  27.4 5.9 %collective-permute-start.13 = (bf16[128,512]{1,0:T(8,128)(2,1)S(1)}, bf16[128,512]{1,0:T(8,128)(2,1)S(1)}, u32[]{:S(2)}, u32[]{:S(2)}) collective-permute-start(bf16[128,512]{1,0:T(8,128)(2,1)S(1)} %get-tuple-element.54.z), channel_id=1, source_target_pairs={{0,4},{4,0},{8,12},{12,8},{1,5},{5,1},{9,13},{13,9},{2,6},{6,2},{1... | collective-permute-start | bytes 393224 | tf_op jit(solution)/shard_map/ppermute | solution.py:17
  29.6 1.3 %collective-permute-start.9 = (bf16[128,384]{1,0:T(8,128)(2,1)S(1)}, bf16[128,384]{1,0:T(8,128)(2,1)S(1)}, u32[]{:S(2)}, u32[]{:S(2)}) collective-permute-start(bf16[128,384]{1,0:T(8,128)(2,1)S(1)} %collective-permute-done.8.c), channel_id=1, source_target_pairs={{0,1},{1,0},{2,3},{3,2},{4,5},{5,4},{6,7},{7,6},{8,9},{9,8},{10,11... | collective-permute-start | bytes 294920 | tf_op jit(solution)/shard_map/ppermute | solution.py:17
  31.6 4.3 %collective-permute-start.12 = (bf16[128,256]{1,0:T(8,128)(2,1)S(1)}, bf16[128,256]{1,0:T(8,128)(2,1)S(1)}, u32[]{:S(2)}, u32[]{:S(2)}) collective-permute-start(bf16[128,256]{1,0:T(8,128)(2,1)S(1)} %shard_map.92.back), channel_id=1, source_target_pairs={{0,4},{4,0},{8,12},{12,8},{1,5},{5,1},{9,13},{13,9},{2,6},{6,2},{1... | collective-permute-start | bytes 196616 | tf_op jit(solution)/shard_map/ppermute | solution.py:17
  36.2 6.1 %collective-permute-start.14 = (bf16[128,256]{1,0:T(8,128)(2,1)S(1)}, bf16[128,256]{1,0:T(8,128)(2,1)S(1)}, u32[]{:S(2)}, u32[]{:S(2)}) collective-permute-start(bf16[128,256]{1,0:T(8,128)(2,1)S(1)} %get-tuple-element.56.half5), channel_id=1, source_target_pairs={{0,12},{4,8},{8,4},{12,0},{1,13},{5,9},{9,5},{13,1},{2,14},{6,10},... | collective-permute-start | bytes 196616 | tf_op jit(solution)/shard_map/ppermute | solution.py:17

commit v11 on v10

--- a/solution.py
+++ b/solution.py
@@ -302,13 +302,13 @@
     def late_body(lb, rb, caps, tl, tr, seen, seen2, out):
         for i, basis in enumerate((tl[0], tr[0])):
             out[:, span(i)] = (dot_t(lb[0, 0], basis) * s1).astype(BF)
-            out[:, span(5 + i)] = (dot_t(lb[1, 0], basis) * s2).astype(BF)
-        out[:, span(2)] = (dot_t(lb[0, 0], rb[1, 0]) * s1).astype(BF)
-        out[:, span(3, 2)] = caps[1, 0]
+            out[:, span(4 + i)] = (dot_t(lb[1, 0], basis) * s2).astype(BF)
+        gram = (dot_t(lb[0, 0], rb[1, 0]) * s1).astype(BF)
+        out[:, span(2, 2)] = dot(gram, caps[1, 0]).astype(BF)
 
     (late,) = call(
         late_body,
-        [((rank, 7 * rank), BF)],
+        [((rank, 6 * rank), BF)],
         lb,
         rb,
         caps,
@@ -318,7 +318,6 @@
         next_far,
         micros=5,
     )
-    late_sib = swap(late, "leaf", 1)
 
     def column_body(send, keep2, far, nexts, nexts_far, gram, seen, out):
         side = column_side()
@@ -346,22 +345,24 @@
     )
     top_far = swap(top_send, "top", 2)
 
-    def two_body(x1, send, far, lb, caps, seen, x2, z5, z, stack):
+    def two_body(x1, send, far, lb, caps, late, seen, x2, z5, z, stack):
         put_rows(stack, tree_side(1), send[:, :cols], far[:, :cols])
         coef = dot(caps[1, 0], stack[...]).astype(BF)
         x2[...] = (x1[...] - dot(lb[1, 0], coef)).astype(BF)
         z5[...] = dot_t(lb[1, 0], x2[...]) * s2
         z[:, :cols] = z5[...].astype(BF)
-        z[:, cols:] = (dot_t(lb[0, 0], x2[...]) * s1).astype(BF)
+        z[:, cols : 2 * cols] = (dot_t(lb[0, 0], x2[...]) * s1).astype(BF)
+        z[:, 2 * cols :] = late[...]
 
     state2, down5, down_send = call(
         two_body,
-        [(tall, BF), (wide, f32), ((rank, 2 * cols), BF)],
+        [(tall, BF), (wide, f32), ((rank, 2 * cols + 6 * rank), BF)],
         state1,
         cross_send,
         cross_in,
         lb,
         caps,
+        late,
         top_send,
         scratch=[pltpu.VMEM((2 * rank, cols), BF)],
         micros=0.1,
@@ -370,7 +371,7 @@
     top_near = swap(after(top_send, state2), "top", 1)
     top_parts = top_send, top_near, top_far, swap(top_far, "top", 1)
 
-    def under_body(x2, rb, tl, tr, inv, seen, out2, under):
+    def under_body(x2, rb, tl, tr, inv, out2, under):
         for c in range(blocks):
             column = inv[c * rank :, span(c)]
             out2[span(c), :] = dot_t(column, x2[c * rank :, :])
@@ -385,7 +386,6 @@
         tl,
         tr,
         inverse,
-        late_sib,
     )
 
     def top_body(a, b, c, d, caps, seen, out, up, down):
@@ -410,11 +410,12 @@
     )
     back_in = swap(back_send, "leaf", 1)
 
-    def down_body(back, back_sib, down5, z_sib, late, late_sib, both, send):
+    def down_body(back, back_sib, down5, z, z_sib, both, send):
         side = column_side()
         for i in range(2):
             put_columns(both.at[span(i), :], side, back[:, part(i)], back_sib[:, part(i)])
-        gram = (late[:, span(5, 2)].astype(f32) + late_sib[:, span(5, 2)]).astype(BF)
+        at = slice(2 * cols + 4 * rank, 2 * cols + 6 * rank)
+        gram = (z[:, at].astype(f32) + z_sib[:, at]).astype(BF)
         send[...] = (down5[...] + z_sib[:, :cols] - dot(gram, both[...])).astype(BF)
 
     both, half5 = call(
@@ -423,35 +424,44 @@
         back_send,
         back_in,
         down5,
+        down_send,
         down_in,
-        late,
-        late_sib,
         micros=0.3,
     )
     half5_far = swap(half5, "leaf", 3)
 
+    def part_body(out2, under, both, z, z_sib, seen, proj, out3):
+        def down(zs):
+            return zs[:, cols : 2 * cols] - dot(zs[:, 2 * cols : 2 * cols + 2 * rank], both[...])
+
+        put_rows(proj, tree_side(0), down(z), down(z_sib))
+        out3[...] = out2[...] - dot(under[:, span(0, 2)], both[...])
+
+    proj6, out3 = call(
+        part_body,
+        [((2 * rank, cols), f32), (tall, f32)],
+        out2,
+        under,
+        both,
+        down_send,
+        down_in,
+        half5,
+        micros=0.3,
+    )
+
     def last_body(
-        out2, under, both, half5, half5_far, late, late_sib, z, z_sib, caps, out,
-        coefs, stack, out_v, sems,
+        out3, under, half5, half5_far, z, z_sib, proj6, caps, out,
+        coefs, stack, grams, out_v, sems,
     ):
-        coefs[span(0, 2), :] = both[...]
         put_rows(stack, tree_side(1), half5[...], half5_far[...])
-        coef5 = dot(caps[1, 0], stack[...]).astype(BF)
-        coef5_sib = dot(late_sib[:, span(3, 2)], stack[...]).astype(BF)
-        coefs[span(2), :] = coef5
-
-        def proj(zs, gram, coef):
-            return (
-                zs[:, cols:]
-                - dot(gram[:, span(0, 2)], both[...])
-                - dot(gram[:, span(2)], coef)
-            ).astype(BF)
-
-        put_rows(stack, tree_side(0), proj(z, late, coef5), proj(z_sib, late_sib, coef5_sib))
-        coefs[span(3), :] = dot(caps[0, 0], stack[...]).astype(BF)
+        at = slice(2 * cols + 2 * rank, 2 * cols + 4 * rank)
+        put_rows(grams, tree_side(0), z[:, at], z_sib[:, at])
+        proj = (proj6[...] - dot(grams[...], stack[...])).astype(BF)
+        coefs[span(0), :] = dot(caps[1, 0], stack[...]).astype(BF)
+        coefs[span(1), :] = dot(caps[0, 0], proj).astype(BF)
         copies = []
         for c in range(blocks):
-            out_v[span(c), :] = out2[span(c), :] - dot(under[span(c), :], coefs[...])
+            out_v[span(c), :] = out3[span(c), :] - dot(under[span(c), span(2, 2)], coefs[...])
             copy = pltpu.make_async_copy(out_v.at[span(c), :], out.at[0, span(c), :], sems.at[c])
             copy.start()
             copies.append(copy)
@@ -461,20 +471,19 @@
     (out,) = call(
         last_body,
         [((1, rows, cols), f32)],
-        out2,
+        out3,
         under,
-        both,
         half5,
         half5_far,
-        late,
-        late_sib,
         down_send,
         down_in,
+        proj6,
         caps,
         hbm_out=True,
         scratch=[
-            pltpu.VMEM((4 * rank, cols), BF),
             pltpu.VMEM((2 * rank, cols), BF),
+            pltpu.VMEM((2 * rank, cols), BF),
+            pltpu.VMEM((2 * rank, 2 * rank), BF),
             pltpu.VMEM(tall, f32),
             pltpu.SemaphoreType.DMA((blocks,)),
         ],

time: 44 us -> 45.3 us (1.030)
  waiting for transfers between devices: 11.3 us -> 13.5 us
  starting transfers between devices: 23.6 us -> 22.6 us
    ppermute x15 -> x14, waiting for transfers between devices: 11.3 us -> 13.5 us  [swap(): return lax.ppermute(value, axis, pairs)]
    ppermute x15 -> x14, starting transfers between devices: 23.6 us -> 22.6 us  [swap(): return lax.ppermute(value, axis, pairs)]
    pallas_call x13 -> x14, Pallas kernels: 8.81 us -> 9.03 us  [call(): pl.pallas_call(body, out_shape=[jax.ShapeDtypeStruct(shape, dtype) if hbm...]
  transfers between devices with their start and end apart: 15 -> 14, of which waited for: 8 -> 6; matrix products, arithmetic and copies ran while one was open for 0% -> 0% of each run, Pallas kernels for 10% -> 11%
where the time goes in v11:
time: 45.3 us; the launch traced here: 45.2 us
  starting transfers between devices  22.6 us (50%)
  waiting for transfers between devices  13.5 us (30%)
  Pallas kernels  9.03 us (20%)
    ppermute x14, starting transfers between devices, swap(): return lax.ppermute(value, axis, pairs)  22.6 us
    ppermute x14, waiting for transfers between devices, swap(): return lax.ppermute(value, axis, pairs)  13.5 us
    pallas_call x14, Pallas kernels, call(): pl.pallas_call(body, out_shape=[jax.ShapeDtypeStruct(shape, dtype) if hbm...  9.03 us
  transfers between devices with their start and end apart: 14, of which 6 were waited for; matrix products, arithmetic and copies ran while one was open for 0% of the time, Pallas kernels for 11%

profile of v11, /device:TPU:0, one launch (start us, length us, event | category | flops | bytes accessed | tf_op | source)
XLA Modules:
  0.0 45.2 jit_solution(7223098307614676273)
XLA Ops:
  0.0 2.4 %shard_map.82 = (f32[640,256]{1,0:T(8,128)S(1)}, bf16[128,256]{1,0:T(8,128)(2,1)S(1)}, bf16[640,640]{1,0:T(8,128)(2,1)S(1)}, bf16[2,1,640,128]{3,2,1,0:T(8,128)(...) custom-call(f32[1,640,256]{2,1,0:T(8,128)} %rhs_hbm.1, ...), custom_call_target="tpu_custom_call" | custom-call | flops 1000000000 | tf_op jit(solution)/shard_map/pallas_call | solution.py:88
  2.4 0.5 %collective-permute-start.2 = (bf16[128,512]{1,0:T(8,128)(2,1)S(1)}, bf16[128,512]{1,0:T(8,128)(2,1)S(1)}, u32[]{:S(2)}, u32[]{:S(2)}) collective-permute-start(bf16[128,512]{1,0:T(8,128)(2,1)S(1)} %copy-done), channel_id=1, source_target_pairs={{0,1},{1,0},{2,3},{3,2},{4,5},{5,4},{6,7},{7,6},{8,9},{9,8},{10,11... | collective-permute-start | bytes 393224 | tf_op jit(solution)/shard_map/ppermute | solution.py:17
  2.9 2.6 %collective-permute-start = (bf16[128,256]{1,0:T(8,128)(2,1)S(1)}, bf16[128,256]{1,0:T(8,128)(2,1)S(1)}, u32[]{:S(2)}, u32[]{:S(2)}) collective-permute-start(bf16[128,256]{1,0:T(8,128)(2,1)S(1)} %get-tuple-element.34.p), channel_id=1, source_target_pairs={{0,4},{4,0},{8,12},{12,8},{1,5},{5,1},{9,13},{13,9},{2,6},{6,2},{1... | collective-permute-start | bytes 196616 | tf_op jit(solution)/shard_map/ppermute | solution.py:17
  5.6 0.6 %shard_map.84.own = bf16[128,640]{1,0:T(8,128)(2,1)S(1)} custom-call(bf16[2,1,640,128]{3,2,1,0:T(8,128)(2,1)S(1)} %get-tuple-element.35.lb, bf16[2,1,128,256]{3,2,1,0:T(8,128)(2,1)S(1)} %get-tuple-element.37.caps, bf16[1,640,128]{2,1,0:T(8,128)(2,1)S(1)} %get-tuple-element.38.tl, bf16[1,640,128]{2,1,0:T(8,128)(2,1)S(1)} %get-tuple-element.39.tr, ...), custom_call_target="tpu_custom_call" | custom-call | flops 10000000000 | tf_op jit(solution)/shard_map/pallas_call | solution.py:88
  6.1 1.3 %collective-permute-start.3 = (bf16[128,640]{1,0:T(8,128)(2,1)S(1)}, bf16[128,640]{1,0:T(8,128)(2,1)S(1)}, u32[]{:S(2)}, u32[]{:S(2)}) collective-permute-start(bf16[128,640]{1,0:T(8,128)(2,1)S(1)} %shard_map.84.own), channel_id=1, source_target_pairs={{0,4},{4,0},{8,12},{12,8},{1,5},{5,1},{9,13},{13,9},{2,6},{6,2},{1... | collective-permute-start | bytes 491528 | tf_op jit(solution)/shard_map/ppermute | solution.py:17
  7.5 0.8 %collective-permute-done.p_sib = bf16[128,256]{1,0:T(8,128)(2,1)S(1)} collective-permute-done((bf16[128,256]{1,0:T(8,128)(2,1)S(1)}, bf16[128,256]{1,0:T(8,128)(2,1)S(1)}, u32[]{:S(2)}, u32[]{:S(2)}) %collective-permute-start) | collective-permute-done | bytes 65568 | tf_op jit(solution)/shard_map/ppermute | solution.py:17
  8.3 0.8 %shard_map.83 = (f32[640,256]{1,0:T(8,128)S(1)}, bf16[128,512]{1,0:T(8,128)(2,1)S(1)}, f32[128,512]{1,0:T(8,128)S(1)}) custom-call(f32[640,256]{1,0:T(8,128)S(1)} %get-tuple-element.33.x0, bf16[128,256]{1,0:T(8,128)(2,1)S(1)} %get-tuple-element.34.p, bf16[128,256]{1,0:T(8,128)(2,1)S(1)} %collective-permute-done.p_sib, ...), custom_call_target="tpu_custom_call" | custom-call | flops 3000000000 | tf_op jit(solution)/shard_map/pallas_call | solution.py:88
  9.1 1.8 %collective-permute-start.1 = (bf16[128,512]{1,0:T(8,128)(2,1)S(1)}, bf16[128,512]{1,0:T(8,128)(2,1)S(1)}, u32[]{:S(2)}, u32[]{:S(2)}) collective-permute-start(bf16[128,512]{1,0:T(8,128)(2,1)S(1)} %get-tuple-element.42), channel_id=1, source_target_pairs={{0,4},{4,0},{8,12},{12,8},{1,5},{5,1},{9,13},{13,9},{2,6},{6,2},{1... | collective-permute-start | bytes 393224 | tf_op jit(solution)/shard_map/ppermute | solution.py:17
  10.9 2.3 %collective-permute-done.3.sib = bf16[128,640]{1,0:T(8,128)(2,1)S(1)} collective-permute-done((bf16[128,640]{1,0:T(8,128)(2,1)S(1)}, bf16[128,640]{1,0:T(8,128)(2,1)S(1)}, u32[]{:S(2)}, u32[]{:S(2)}) %collective-permute-start.3) | collective-permute-done | bytes 163872 | tf_op jit(solution)/shard_map/ppermute | solution.py:17
  13.3 3.0 %collective-permute-start.5 = (bf16[128,384]{1,0:T(8,128)(2,1)S(1)}, bf16[128,384]{1,0:T(8,128)(2,1)S(1)}, u32[]{:S(2)}, u32[]{:S(2)}) collective-permute-start(bf16[128,384]{1,0:T(8,128)(2,1)S(1)} %get-tuple-element.46), channel_id=1, source_target_pairs={{0,12},{4,8},{8,4},{12,0},{1,13},{5,9},{9,5},{13,1},{2,14},{6,10},... | collective-permute-start | bytes 294920 | tf_op jit(solution)/shard_map/ppermute | solution.py:17
  16.5 2.3 %collective-permute-start.4 = (bf16[128,512]{1,0:T(8,128)(2,1)S(1)}, bf16[128,512]{1,0:T(8,128)(2,1)S(1)}, u32[]{:S(2)}, u32[]{:S(2)}) collective-permute-start(bf16[128,512]{1,0:T(8,128)(2,1)S(1)} %get-tuple-element.45.seen.send), channel_id=1, source_target_pairs={{0,12},{4,8},{8,4},{12,0},{1,13},{5,9},{9,5},{13,1},{2,14},{6,10},... | collective-permute-start | bytes 393224 | tf_op jit(solution)/shard_map/ppermute | solution.py:17
  18.8 1.5 %collective-permute-start.9 = (bf16[128,512]{1,0:T(8,128)(2,1)S(1)}, bf16[128,512]{1,0:T(8,128)(2,1)S(1)}, u32[]{:S(2)}, u32[]{:S(2)}) collective-permute-start(bf16[128,512]{1,0:T(8,128)(2,1)S(1)} %copy-done), channel_id=1, source_target_pairs={{0,2},{1,3},{2,0},{3,1},{4,6},{5,7},{6,4},{7,5},{8,10},{9,11},{10,... | collective-permute-start | bytes 393224 | tf_op jit(solution)/shard_map/ppermute | solution.py:17
  20.3 0.5 %shard_map.87.seen.late = bf16[128,768]{1,0:T(8,128)(2,1)S(1)} custom-call(bf16[2,1,640,128]{3,2,1,0:T(8,128)(2,1)S(1)} %get-tuple-element.35.lb, bf16[2,1,640,128]{3,2,1,0:T(8,128)(2,1)S(1)} %get-tuple-element.36.rb, bf16[2,1,128,256]{3,2,1,0:T(8,128)(2,1)S(1)} %get-tuple-element.37.caps, bf16[1,640,128]{2,1,0:T(8,128)(2,1)S(1)} %get-tuple-element.38.tl, ...), custom_call_target="tpu_custom_call" | custom-call | flops 5000000000 | tf_op jit(solution)/shard_map/pallas_call | solution.py:88
  20.8 2.6 %collective-permute-done.4.far = bf16[128,512]{1,0:T(8,128)(2,1)S(1)} collective-permute-done((bf16[128,512]{1,0:T(8,128)(2,1)S(1)}, bf16[128,512]{1,0:T(8,128)(2,1)S(1)}, u32[]{:S(2)}, u32[]{:S(2)}) %collective-permute-start.4) | collective-permute-done | bytes 131104 | tf_op jit(solution)/shard_map/ppermute | solution.py:17
  23.7 1.6 %collective-permute-start.7 = (bf16[128,384]{1,0:T(8,128)(2,1)S(1)}, bf16[128,384]{1,0:T(8,128)(2,1)S(1)}, u32[]{:S(2)}, u32[]{:S(2)}) collective-permute-start(bf16[128,384]{1,0:T(8,128)(2,1)S(1)} %shard_map.88.seen.a), channel_id=1, source_target_pairs={{0,2},{1,3},{2,0},{3,1},{4,6},{5,7},{6,4},{7,5},{8,10},{9,11},{10,... | collective-permute-start | bytes 294920 | tf_op jit(solution)/shard_map/ppermute | solution.py:17
  25.2 0.7 %shard_map.89 = (bf16[640,256]{1,0:T(8,128)(2,1)S(1)}, f32[128,256]{1,0:T(8,128)S(1)}, bf16[128,1280]{1,0:T(8,128)(2,1)S(1)}) custom-call(f32[640,256]{1,0:T(8,128)S(1)} %get-tuple-element.40.seen.x1, bf16[128,512]{1,0:T(8,128)(2,1)S(1)} %get-tuple-element.45.seen.send, bf16[128,512]{1,0:T(8,128)(2,1)S(1)} %collective-permute-done.4.far, ...), custom_call_target="tpu_custom_call" | custom-call | flops 100000000 | tf_op jit(solution)/shard_map/pallas_call | solution.py:88
  26.0 3.0 %collective-permute-start.12 = (bf16[128,1280]{1,0:T(8,128)(2,1)S(1)}, bf16[128,1280]{1,0:T(8,128)(2,1)S(1)}, u32[]{:S(2)}, u32[]{:S(2)}) collective-permute-start(bf16[128,1280]{1,0:T(8,128)(2,1)S(1)} %get-tuple-element.56.z), channel_id=1, source_target_pairs={{0,4},{4,0},{8,12},{12,8},{1,5},{5,1},{9,13},{13,9},{2,6},{6,2},{1... | collective-permute-start | bytes 983048 | tf_op jit(solution)/shard_map/ppermute | solution.py:17
  29.5 0.9 %shard_map.90 = (f32[640,256]{1,0:T(8,128)S(1)}, bf16[640,512]{1,0:T(8,128)(2,1)S(1)}) custom-call(bf16[640,256]{1,0:T(8,128)(2,1)S(1)} %get-tuple-element.49.x2, bf16[2,1,640,128]{3,2,1,0:T(8,128)(2,1)S(1)} %get-tuple-element.36.rb, bf16[1,640,128]{2,1,0:T(8,128)(2,1)S(1)} %get-tuple-element.38.tl, bf16[1,640,128]{2,1,0:T(8,128)(2,1)S(1)} %get-tuple-element.39.tr, ...), custom_call_target="tpu_custom_call" | custom-call | flops 1000000000 | tf_op jit(solution)/shard_map/pallas_call | solution.py:88
  30.8 0.7 %shard_map.92.back = bf16[128,256]{1,0:T(8,128)(2,1)S(1)} custom-call(bf16[128,384]{1,0:T(8,128)(2,1)S(1)} %shard_map.88.seen.a, bf16[128,384]{1,0:T(8,128)(2,1)S(1)} %collective-permute-done.6.b, bf16[128,384]{1,0:T(8,128)(2,1)S(1)} %collective-permute-done.7.c, bf16[128,384]{1,0:T(8,128)(2,1)S(1)} %collective-permute-done.8.d, ...), custom_call_target="tpu_custom_call" | custom-call | flops 1000000000 | tf_op jit(solution)/shard_map/pallas_call | solution.py:88
  31.4 1.9 %collective-permute-start.11 = (bf16[128,256]{1,0:T(8,128)(2,1)S(1)}, bf16[128,256]{1,0:T(8,128)(2,1)S(1)}, u32[]{:S(2)}, u32[]{:S(2)}) collective-permute-start(bf16[128,256]{1,0:T(8,128)(2,1)S(1)} %shard_map.92.back), channel_id=1, source_target_pairs={{0,4},{4,0},{8,12},{12,8},{1,5},{5,1},{9,13},{13,9},{2,6},{6,2},{1... | collective-permute-start | bytes 196616 | tf_op jit(solution)/shard_map/ppermute | solution.py:17
  33.3 4.0 %collective-permute-done.11.back_sib = bf16[128,256]{1,0:T(8,128)(2,1)S(1)} collective-permute-done((bf16[128,256]{1,0:T(8,128)(2,1)S(1)}, bf16[128,256]{1,0:T(8,128)(2,1)S(1)}, u32[]{:S(2)}, u32[]{:S(2)}) %collective-permute-start.11) | collective-permute-done | bytes 65568 | tf_op jit(solution)/shard_map/ppermute | solution.py:17
  37.5 2.6 %collective-permute-start.13 = (bf16[128,256]{1,0:T(8,128)(2,1)S(1)}, bf16[128,256]{1,0:T(8,128)(2,1)S(1)}, u32[]{:S(2)}, u32[]{:S(2)}) collective-permute-start(bf16[128,256]{1,0:T(8,128)(2,1)S(1)} %get-tuple-element.58.seen.half5), channel_id=1, source_target_pairs={{0,12},{4,8},{8,4},{12,0},{1,13},{5,9},{9,5},{13,1},{2,14},{6,10},... | collective-permute-start | bytes 196616 | tf_op jit(solution)/shard_map/ppermute | solution.py:17
  40.4 3.3 %collective-permute-done.13.half5_far = bf16[128,256]{1,0:T(8,128)(2,1)S(1)} collective-permute-done((bf16[128,256]{1,0:T(8,128)(2,1)S(1)}, bf16[128,256]{1,0:T(8,128)(2,1)S(1)}, u32[]{:S(2)}, u32[]{:S(2)}) %collective-permute-start.13) | collective-permute-done | bytes 65568 | tf_op jit(solution)/shard_map/ppermute | solution.py:17
  43.8 1.4 %shard_map.95 = f32[1,640,256]{2,1,0:T(8,128)} custom-call(f32[640,256]{1,0:T(8,128)S(1)} %get-tuple-element.59.out3, bf16[640,512]{1,0:T(8,128)(2,1)S(1)} %get-tuple-element.52.under, bf16[128,256]{1,0:T(8,128)(2,1)S(1)} %get-tuple-element.58.seen.half5, bf16[128,256]{1,0:T(8,128)(2,1)S(1)} %collective-permute-done.13.half5_far, ...), custom_call_target="tpu_custom_call" | custom-call | flops 1000000000 | tf_op jit(solution)/shard_map/pallas_call | solution.py:88
  (20 shorter events, 1.8 us)
Async XLA Ops:
  0.0 2.4 %copy-start = (bf16[128,512]{1,0:T(8,128)(2,1)S(1)}, bf16[128,512]{1,0:T(8,128)(2,1)}, u32[]{:S(2)}) copy-start(bf16[128,512]{1,0:T(8,128)(2,1)} %a.1) | copy-start | bytes 393220
  2.4 3.2 %collective-permute-start.2 = (bf16[128,512]{1,0:T(8,128)(2,1)S(1)}, bf16[128,512]{1,0:T(8,128)(2,1)S(1)}, u32[]{:S(2)}, u32[]{:S(2)}) collective-permute-start(bf16[128,512]{1,0:T(8,128)(2,1)S(1)} %copy-done), channel_id=1, source_target_pairs={{0,1},{1,0},{2,3},{3,2},{4,5},{5,4},{6,7},{7,6},{8,9},{9,8},{10,11... | collective-permute-start | bytes 393224 | tf_op jit(solution)/shard_map/ppermute | solution.py:17
  2.9 5.3 %collective-permute-start = (bf16[128,256]{1,0:T(8,128)(2,1)S(1)}, bf16[128,256]{1,0:T(8,128)(2,1)S(1)}, u32[]{:S(2)}, u32[]{:S(2)}) collective-permute-start(bf16[128,256]{1,0:T(8,128)(2,1)S(1)} %get-tuple-element.34.p), channel_id=1, source_target_pairs={{0,4},{4,0},{8,12},{12,8},{1,5},{5,1},{9,13},{13,9},{2,6},{6,2},{1... | collective-permute-start | bytes 196616 | tf_op jit(solution)/shard_map/ppermute | solution.py:17
  6.1 7.1 %collective-permute-start.3 = (bf16[128,640]{1,0:T(8,128)(2,1)S(1)}, bf16[128,640]{1,0:T(8,128)(2,1)S(1)}, u32[]{:S(2)}, u32[]{:S(2)}) collective-permute-start(bf16[128,640]{1,0:T(8,128)(2,1)S(1)} %shard_map.84.own), channel_id=1, source_target_pairs={{0,4},{4,0},{8,12},{12,8},{1,5},{5,1},{9,13},{13,9},{2,6},{6,2},{1... | collective-permute-start | bytes 491528 | tf_op jit(solution)/shard_map/ppermute | solution.py:17
  9.1 7.3 %collective-permute-start.1 = (bf16[128,512]{1,0:T(8,128)(2,1)S(1)}, bf16[128,512]{1,0:T(8,128)(2,1)S(1)}, u32[]{:S(2)}, u32[]{:S(2)}) collective-permute-start(bf16[128,512]{1,0:T(8,128)(2,1)S(1)} %get-tuple-element.42), channel_id=1, source_target_pairs={{0,4},{4,0},{8,12},{12,8},{1,5},{5,1},{9,13},{13,9},{2,6},{6,2},{1... | collective-permute-start | bytes 393224 | tf_op jit(solution)/shard_map/ppermute | solution.py:17
  13.3 7.0 %collective-permute-start.5 = (bf16[128,384]{1,0:T(8,128)(2,1)S(1)}, bf16[128,384]{1,0:T(8,128)(2,1)S(1)}, u32[]{:S(2)}, u32[]{:S(2)}) collective-permute-start(bf16[128,384]{1,0:T(8,128)(2,1)S(1)} %get-tuple-element.46), channel_id=1, source_target_pairs={{0,12},{4,8},{8,4},{12,0},{1,13},{5,9},{9,5},{13,1},{2,14},{6,10},... | collective-permute-start | bytes 294920 | tf_op jit(solution)/shard_map/ppermute | solution.py:17
  16.5 6.9 %collective-permute-start.4 = (bf16[128,512]{1,0:T(8,128)(2,1)S(1)}, bf16[128,512]{1,0:T(8,128)(2,1)S(1)}, u32[]{:S(2)}, u32[]{:S(2)}) collective-permute-start(bf16[128,512]{1,0:T(8,128)(2,1)S(1)} %get-tuple-element.45.seen.send), channel_id=1, source_target_pairs={{0,12},{4,8},{8,4},{12,0},{1,13},{5,9},{9,5},{13,1},{2,14},{6,10},... | collective-permute-start | bytes 393224 | tf_op jit(solution)/shard_map/ppermute | solution.py:17
  18.8 10.1 %collective-permute-start.9 = (bf16[128,512]{1,0:T(8,128)(2,1)S(1)}, bf16[128,512]{1,0:T(8,128)(2,1)S(1)}, u32[]{:S(2)}, u32[]{:S(2)}) collective-permute-start(bf16[128,512]{1,0:T(8,128)(2,1)S(1)} %copy-done), channel_id=1, source_target_pairs={{0,2},{1,3},{2,0},{3,1},{4,6},{5,7},{6,4},{7,5},{8,10},{9,11},{10,... | collective-permute-start | bytes 393224 | tf_op jit(solution)/shard_map/ppermute | solution.py:17
  23.7 5.8 %collective-permute-start.7 = (bf16[128,384]{1,0:T(8,128)(2,1)S(1)}, bf16[128,384]{1,0:T(8,128)(2,1)S(1)}, u32[]{:S(2)}, u32[]{:S(2)}) collective-permute-start(bf16[128,384]{1,0:T(8,128)(2,1)S(1)} %shard_map.88.seen.a), channel_id=1, source_target_pairs={{0,2},{1,3},{2,0},{3,1},{4,6},{5,7},{6,4},{7,5},{8,10},{9,11},{10,... | collective-permute-start | bytes 294920 | tf_op jit(solution)/shard_map/ppermute | solution.py:17
  26.0 11.4 %collective-permute-start.12 = (bf16[128,1280]{1,0:T(8,128)(2,1)S(1)}, bf16[128,1280]{1,0:T(8,128)(2,1)S(1)}, u32[]{:S(2)}, u32[]{:S(2)}) collective-permute-start(bf16[128,1280]{1,0:T(8,128)(2,1)S(1)} %get-tuple-element.56.z), channel_id=1, source_target_pairs={{0,4},{4,0},{8,12},{12,8},{1,5},{5,1},{9,13},{13,9},{2,6},{6,2},{1... | collective-permute-start | bytes 983048 | tf_op jit(solution)/shard_map/ppermute | solution.py:17
  28.9 1.4 %collective-permute-start.10 = (bf16[128,512]{1,0:T(8,128)(2,1)S(1)}, bf16[128,512]{1,0:T(8,128)(2,1)S(1)}, u32[]{:S(2)}, u32[]{:S(2)}) collective-permute-start(bf16[128,512]{1,0:T(8,128)(2,1)S(1)} %collective-permute-done.9.c), channel_id=1, source_target_pairs={{0,1},{1,0},{2,3},{3,2},{4,5},{5,4},{6,7},{7,6},{8,9},{9,8},{10,11... | collective-permute-start | bytes 393224 | tf_op jit(solution)/shard_map/ppermute | solution.py:17
  28.9 1.5 %collective-permute-start.6 = (bf16[128,384]{1,0:T(8,128)(2,1)S(1)}, bf16[128,384]{1,0:T(8,128)(2,1)S(1)}, u32[]{:S(2)}, u32[]{:S(2)}) collective-permute-start(bf16[128,384]{1,0:T(8,128)(2,1)S(1)} %shard_map.88.seen.a), channel_id=1, source_target_pairs={{0,1},{1,0},{2,3},{3,2},{4,5},{5,4},{6,7},{7,6},{8,9},{9,8},{10,11... | collective-permute-start | bytes 294920 | tf_op jit(solution)/shard_map/ppermute | solution.py:17
  29.4 1.3 %collective-permute-start.8 = (bf16[128,384]{1,0:T(8,128)(2,1)S(1)}, bf16[128,384]{1,0:T(8,128)(2,1)S(1)}, u32[]{:S(2)}, u32[]{:S(2)}) collective-permute-start(bf16[128,384]{1,0:T(8,128)(2,1)S(1)} %collective-permute-done.7.c), channel_id=1, source_target_pairs={{0,1},{1,0},{2,3},{3,2},{4,5},{5,4},{6,7},{7,6},{8,9},{9,8},{10,11... | collective-permute-start | bytes 294920 | tf_op jit(solution)/shard_map/ppermute | solution.py:17
  31.4 5.9 %collective-permute-start.11 = (bf16[128,256]{1,0:T(8,128)(2,1)S(1)}, bf16[128,256]{1,0:T(8,128)(2,1)S(1)}, u32[]{:S(2)}, u32[]{:S(2)}) collective-permute-start(bf16[128,256]{1,0:T(8,128)(2,1)S(1)} %shard_map.92.back), channel_id=1, source_target_pairs={{0,4},{4,0},{8,12},{12,8},{1,5},{5,1},{9,13},{13,9},{2,6},{6,2},{1... | collective-permute-start | bytes 196616 | tf_op jit(solution)/shard_map/ppermute | solution.py:17
  37.5 6.2 %collective-permute-start.13 = (bf16[128,256]{1,0:T(8,128)(2,1)S(1)}, bf16[128,256]{1,0:T(8,128)(2,1)S(1)}, u32[]{:S(2)}, u32[]{:S(2)}) collective-permute-start(bf16[128,256]{1,0:T(8,128)(2,1)S(1)} %get-tuple-element.58.seen.half5), channel_id=1, source_target_pairs={{0,12},{4,8},{8,4},{12,0},{1,13},{5,9},{9,5},{13,1},{2,14},{6,10},... | collective-permute-start | bytes 196616 | tf_op jit(solution)/shard_map/ppermute | solution.py:17

commit v12 on v11

--- a/solution.py
+++ b/solution.py
@@ -124,18 +124,11 @@
     scratch[block(1 - upper, rows), :] = other
 
 
-def put_columns(out, upper, own, other):
-    width = own.shape[1]
-    out[:, block(upper, width)] = own
-    out[:, block(1 - upper, width)] = other
-
-
 def two_levels(
     right_side, leaf_inverse, left_basis, right_basis, level_caps, top_left, top_right, top_caps
 ):
     rows, cols = right_side.shape[1:]
     rank = top_left.shape[2]
-    half = cols // 2
     f32 = jnp.float32
     s1 = 1.0 / math.sqrt(rows)
     s2 = 1.0 / math.sqrt(rows * 2)
@@ -145,9 +138,6 @@
 
     def span(i, n=1):
         return slice(i * rank, (i + n) * rank)
-
-    def part(i, n=1):
-        return slice(i * half, (i + n) * half)
 
     def start_body(
         rhs_hbm, inv_hbm, lb_hbm, rb_hbm, caps_hbm, tl_hbm, tr_hbm,
@@ -200,18 +190,29 @@
     caps_here = after(top_caps, proj1)
     caps_near = swap(caps_here, "top", 1)
 
-    def early_body(lb, caps, tl, tr, seen, out):
+    def early_body(lb, caps, tl, tr, seen, send, keep, scratch):
+        side = column_side()
         for i, basis in enumerate((tr, tl)):
             gram = (dot_t(basis[0], lb[1, 0]) * st).astype(BF)
-            out[:, span(2 * i, 2)] = dot(gram, caps[1, 0]).astype(BF)
-        out[:, span(4)] = (dot_t(tl[0], tl[0]) * st).astype(BF)
-
-    (early,) = call(
-        early_body, [((rank, 5 * rank), BF)], lb, caps, tl, tr, caps_near, micros=10
+            scratch[i] = dot(gram, caps[1, 0]).astype(BF)
+        send[:, : 2 * rank] = scratch[1 - side]
+        send[:, span(2)] = (dot_t(tl[0], tl[0]) * st).astype(BF)
+        keep[...] = scratch[side]
+
+    early, early_keep = call(
+        early_body,
+        [((rank, 3 * rank), BF), ((rank, 2 * rank), BF)],
+        lb,
+        caps,
+        tl,
+        tr,
+        caps_near,
+        scratch=[pltpu.VMEM((2, rank, 2 * rank), BF)],
+        micros=10,
     )
     early_sib = swap(early, "leaf", 1)
 
-    def one_body(x0, p, p_sib, lb, rb, caps, tl, tr, x1, send, keep, stack, scratch):
+    def one_body(x0, p, p_sib, lb, rb, caps, tl, tr, seen, x1, send, keep, stack, scratch):
         side = column_side()
         put_rows(stack, tree_side(0), p[...], p_sib[...])
         coef = dot(caps[0, 0], stack[...]).astype(BF)
@@ -220,9 +221,9 @@
         keep[:, :cols] = dot_t(rb[1, 0], state) * s2
         send[:, :cols] = keep[:, :cols].astype(BF)
         for i, basis in enumerate((tr, tl)):
-            scratch[...] = dot_t(basis[0], state) * st
-            send[:, part(2 + i)] = scratch[:, block(1 - side, half)].astype(BF)
-            keep[:, part(2 + i)] = scratch[:, block(side, half)]
+            scratch[i] = dot_t(basis[0], state) * st
+        send[:, cols:] = scratch[1 - side].astype(BF)
+        keep[:, cols:] = scratch[side]
 
     state1, pair_send, pair_keep = call(
         one_body,
@@ -235,39 +236,35 @@
         caps,
         tl,
         tr,
-        scratch=[pltpu.VMEM((2 * rank, cols), BF), pltpu.VMEM(wide, f32)],
+        early,
+        scratch=[pltpu.VMEM((2 * rank, cols), BF), pltpu.VMEM((2, rank, cols), f32)],
         micros=3,
     )
     pair_in = swap(pair_send, "leaf", 1)
 
-    def pair_body(own, sib, seen, send, keep, gram, scratch):
+    def pair_body(mine, own, sib, seen, send, keep, gram, scratch):
         upper = tree_side(1)
-        for i in range(2):
-            scratch[...] = (own[:, span(2 * i, 2)].astype(f32) + sib[:, span(2 * i, 2)]).astype(BF)
-            send[:, span(i)] = scratch[:, block(1 - upper, rank)]
-            keep[:, span(2 * i)] = scratch[:, block(upper, rank)]
-            keep[:, span(2 * i + 1)] = send[:, span(i)]
-        gram[...] = own[:, span(4)].astype(f32) + sib[:, span(4)]
-        send[:, span(2)] = gram[...].astype(BF)
+        scratch[...] = (mine[...].astype(f32) + sib[:, : 2 * rank]).astype(BF)
+        keep[:, span(0)] = scratch[:, block(upper, rank)]
+        keep[:, span(1)] = scratch[:, block(1 - upper, rank)]
+        send[:, span(0)] = keep[:, span(1)]
+        gram[...] = own[:, span(2)].astype(f32) + sib[:, span(2)]
+        send[:, span(1)] = gram[...].astype(BF)
 
     next_send, next_keep, gram_pair = call(
         pair_body,
-        [((rank, 3 * rank), BF), ((rank, 4 * rank), BF), (square, f32)],
+        [((rank, 2 * rank), BF), ((rank, 2 * rank), BF), (square, f32)],
+        early_keep,
         early,
         early_sib,
         state1,
         scratch=[pltpu.VMEM((rank, 2 * rank), BF)],
-        micros=0.1,
+        micros=1,
     )
     next_far = swap(next_send, "leaf", 3)
     def half_body(keep, pair, nexts, send, keep2):
-        side = column_side()
         send[:, :cols] = (keep[:, :cols] + pair[:, :cols]).astype(BF)
-        own = send[:, block(side, half)]
-        for i in range(2):
-            keep2[:, part(i)] = (
-                keep[:, part(2 + i)] + pair[:, part(2 + i)] - dot(nexts[:, span(2 * i)], own)
-            )
+        keep2[...] = keep[:, cols:] + pair[:, cols:] - dot(nexts[:, span(0)], send[:, :cols])
         send[:, cols:] = keep2[...].astype(BF)
 
     cross_send, cross_keep = call(
@@ -319,21 +316,20 @@
         micros=5,
     )
 
+    late_sib = swap(late, "leaf", 1)
+
     def column_body(send, keep2, far, nexts, nexts_far, gram, seen, out):
-        side = column_side()
-        own, other = send[:, block(side, half)], far[:, block(side, half)]
-        for i in range(2):
-            out[:, part(i)] = (
-                keep2[:, part(i)]
-                + far[:, part(2 + i)]
-                - dot(nexts[:, span(2 * i + 1)], other)
-                - dot(nexts_far[:, span(i)], own)
-            ).astype(BF)
-        out[:, 2 * half :] = (gram[...] + nexts_far[:, span(2)]).astype(BF)
+        out[:, :cols] = (
+            keep2[...]
+            + far[:, cols:]
+            - dot(nexts[:, span(1)], far[:, :cols])
+            - dot(nexts_far[:, span(0)], send[:, :cols])
+        ).astype(BF)
+        out[:, cols:] = (gram[...] + nexts_far[:, span(1)]).astype(BF)
 
     (top_send,) = call(
         column_body,
-        [((rank, 2 * half + rank), BF)],
+        [((rank, cols + rank), BF)],
         cross_send,
         cross_keep,
         cross_in,
@@ -345,24 +341,22 @@
     )
     top_far = swap(top_send, "top", 2)
 
-    def two_body(x1, send, far, lb, caps, late, seen, x2, z5, z, stack):
+    def two_body(x1, send, far, lb, caps, seen, x2, z5, z, stack):
         put_rows(stack, tree_side(1), send[:, :cols], far[:, :cols])
         coef = dot(caps[1, 0], stack[...]).astype(BF)
         x2[...] = (x1[...] - dot(lb[1, 0], coef)).astype(BF)
         z5[...] = dot_t(lb[1, 0], x2[...]) * s2
         z[:, :cols] = z5[...].astype(BF)
-        z[:, cols : 2 * cols] = (dot_t(lb[0, 0], x2[...]) * s1).astype(BF)
-        z[:, 2 * cols :] = late[...]
+        z[:, cols:] = (dot_t(lb[0, 0], x2[...]) * s1).astype(BF)
 
     state2, down5, down_send = call(
         two_body,
-        [(tall, BF), (wide, f32), ((rank, 2 * cols + 6 * rank), BF)],
+        [(tall, BF), (wide, f32), ((rank, 2 * cols), BF)],
         state1,
         cross_send,
         cross_in,
         lb,
         caps,
-        late,
         top_send,
         scratch=[pltpu.VMEM((2 * rank, cols), BF)],
         micros=0.1,
@@ -371,7 +365,7 @@
     top_near = swap(after(top_send, state2), "top", 1)
     top_parts = top_send, top_near, top_far, swap(top_far, "top", 1)
 
-    def under_body(x2, rb, tl, tr, inv, out2, under):
+    def under_body(x2, rb, tl, tr, inv, seen, out2, under):
         for c in range(blocks):
             column = inv[c * rank :, span(c)]
             out2[span(c), :] = dot_t(column, x2[c * rank :, :])
@@ -386,36 +380,36 @@
         tl,
         tr,
         inverse,
+        late_sib,
     )
 
     def top_body(a, b, c, d, caps, seen, out, up, down):
         pieces = (a, b, c, d)
         for i, piece in enumerate(pieces):
-            up[span(i), :] = piece[:, part(0)]
+            up[span(i), :] = piece[:, :cols]
         coef = dot(caps[...], up[...]).astype(BF)
         for i, piece in enumerate(pieces):
-            down[span(i), :] = (
-                piece[:, part(1)] - dot(piece[:, 2 * half :], coef[span(i), :])
-            ).astype(BF)
-        out[:, part(0)] = coef[:rank, :]
-        out[:, part(1)] = dot(caps[:rank, :], down[...]).astype(BF)
+            down[span(i), :] = dot(piece[:, cols:], coef[span(i), :]).astype(BF)
+        out[:, :cols] = coef[:rank, :]
+        out[:, cols:] = dot(caps[:rank, :], down[...]).astype(BF)
 
     (back_send,) = call(
         top_body,
-        [(wide, BF)],
+        [((rank, 2 * cols), BF)],
         *top_parts,
         caps_all,
         out2,
-        scratch=[pltpu.VMEM((4 * rank, half), BF)] * 2,
+        scratch=[pltpu.VMEM((4 * rank, cols), BF)] * 2,
     )
     back_in = swap(back_send, "leaf", 1)
 
-    def down_body(back, back_sib, down5, z, z_sib, both, send):
+    def down_body(back, back_sib, down5, z_sib, late, late_sib, both, send, pieces):
         side = column_side()
-        for i in range(2):
-            put_columns(both.at[span(i), :], side, back[:, part(i)], back_sib[:, part(i)])
-        at = slice(2 * cols + 4 * rank, 2 * cols + 6 * rank)
-        gram = (z[:, at].astype(f32) + z_sib[:, at]).astype(BF)
+        pieces[side] = back[...]
+        pieces[1 - side] = back_sib[...]
+        both[span(0), :] = pieces[0, :, :cols]
+        both[span(1), :] = (pieces[1, :, :cols].astype(f32) - pieces[0, :, cols:]).astype(BF)
+        gram = (late[:, span(4, 2)].astype(f32) + late_sib[:, span(4, 2)]).astype(BF)
         send[...] = (down5[...] + z_sib[:, :cols] - dot(gram, both[...])).astype(BF)
 
     both, half5 = call(
@@ -424,17 +418,19 @@
         back_send,
         back_in,
         down5,
-        down_send,
         down_in,
+        late,
+        late_sib,
+        scratch=[pltpu.VMEM((2, rank, 2 * cols), BF)],
         micros=0.3,
     )
     half5_far = swap(half5, "leaf", 3)
 
-    def part_body(out2, under, both, z, z_sib, seen, proj, out3):
-        def down(zs):
-            return zs[:, cols : 2 * cols] - dot(zs[:, 2 * cols : 2 * cols + 2 * rank], both[...])
-
-        put_rows(proj, tree_side(0), down(z), down(z_sib))
+    def part_body(out2, under, both, z, z_sib, late, late_sib, seen, proj, out3):
+        def down(zs, gram):
+            return zs[:, cols:] - dot(gram[:, span(0, 2)], both[...])
+
+        put_rows(proj, tree_side(0), down(z, late), down(z_sib, late_sib))
         out3[...] = out2[...] - dot(under[:, span(0, 2)], both[...])
 
     proj6, out3 = call(
@@ -445,17 +441,18 @@
         both,
         down_send,
         down_in,
+        late,
+        late_sib,
         half5,
         micros=0.3,
     )
 
     def last_body(
-        out3, under, half5, half5_far, z, z_sib, proj6, caps, out,
+        out3, under, half5, half5_far, late, late_sib, proj6, caps, out,
         coefs, stack, grams, out_v, sems,
     ):
         put_rows(stack, tree_side(1), half5[...], half5_far[...])
-        at = slice(2 * cols + 2 * rank, 2 * cols + 4 * rank)
-        put_rows(grams, tree_side(0), z[:, at], z_sib[:, at])
+        put_rows(grams, tree_side(0), late[:, span(2, 2)], late_sib[:, span(2, 2)])
         proj = (proj6[...] - dot(grams[...], stack[...])).astype(BF)
         coefs[span(0), :] = dot(caps[1, 0], stack[...]).astype(BF)
         coefs[span(1), :] = dot(caps[0, 0], proj).astype(BF)
@@ -475,8 +472,8 @@
         under,
         half5,
         half5_far,
-        down_send,
-        down_in,
+        late,
+        late_sib,
         proj6,
         caps,
         hbm_out=True,

time: 45.3 us -> 43.2 us (0.954)
  waiting for transfers between devices: 13.5 us -> 10.6 us
  starting transfers between devices: 22.6 us -> 23.3 us
    ppermute x14 -> x15, waiting for transfers between devices: 13.5 us -> 10.6 us  [swap(): return lax.ppermute(value, axis, pairs)]
    ppermute x14 -> x15, starting transfers between devices: 22.6 us -> 23.3 us  [swap(): return lax.ppermute(value, axis, pairs)]
  transfers between devices with their start and end apart: 14 -> 15, of which waited for: 6 -> 9; matrix products, arithmetic and copies ran while one was open for 0% -> 0% of each run, Pallas kernels for 11% -> 12%
where the time goes in v12:
time: 43.2 us; the launch traced here: 43 us
  starting transfers between devices  23.3 us (54%)
  waiting for transfers between devices  10.6 us (25%)
  Pallas kernels  8.99 us (21%)
    ppermute x15, starting transfers between devices, swap(): return lax.ppermute(value, axis, pairs)  23.3 us
    ppermute x15, waiting for transfers between devices, swap(): return lax.ppermute(value, axis, pairs)  10.6 us
    pallas_call x14, Pallas kernels, call(): pl.pallas_call(body, out_shape=[jax.ShapeDtypeStruct(shape, dtype) if hbm...  8.99 us
  transfers between devices with their start and end apart: 15, of which 9 were waited for; matrix products, arithmetic and copies ran while one was open for 0% of the time, Pallas kernels for 12%

profile of v12, /device:TPU:0, one launch (start us, length us, event | category | flops | bytes accessed | tf_op | source)
XLA Modules:
  0.0 43.0 jit_solution(2030582026379549228)
XLA Ops:
  0.0 2.4 %shard_map.82 = (f32[640,256]{1,0:T(8,128)S(1)}, bf16[128,256]{1,0:T(8,128)(2,1)S(1)}, bf16[640,640]{1,0:T(8,128)(2,1)S(1)}, bf16[2,1,640,128]{3,2,1,0:T(8,128)(...) custom-call(f32[1,640,256]{2,1,0:T(8,128)} %rhs_hbm.1, ...), custom_call_target="tpu_custom_call" | custom-call | flops 1000000000 | tf_op jit(solution)/shard_map/pallas_call | solution.py:88
  2.9 2.6 %collective-permute-start = (bf16[128,256]{1,0:T(8,128)(2,1)S(1)}, bf16[128,256]{1,0:T(8,128)(2,1)S(1)}, u32[]{:S(2)}, u32[]{:S(2)}) collective-permute-start(bf16[128,256]{1,0:T(8,128)(2,1)S(1)} %get-tuple-element.36.p), channel_id=1, source_target_pairs={{0,4},{4,0},{8,12},{12,8},{1,5},{5,1},{9,13},{13,9},{2,6},{6,2},{1... | collective-permute-start | bytes 196616 | tf_op jit(solution)/shard_map/ppermute | solution.py:17
  5.6 0.6 %shard_map.83 = (bf16[128,384]{1,0:T(8,128)(2,1)S(1)}, bf16[128,256]{1,0:T(8,128)(2,1)S(1)}) custom-call(bf16[2,1,640,128]{3,2,1,0:T(8,128)(2,1)S(1)} %get-tuple-element.37.lb, bf16[2,1,128,256]{3,2,1,0:T(8,128)(2,1)S(1)} %get-tuple-element.39.caps, bf16[1,640,128]{2,1,0:T(8,128)(2,1)S(1)} %get-tuple-element.40.tl, ...), custom_call_target="tpu_custom_call" | custom-call | flops 10000000000 | tf_op jit(solution)/shard_map/pallas_call | solution.py:88
  6.2 1.3 %collective-permute-start.3 = (bf16[128,384]{1,0:T(8,128)(2,1)S(1)}, bf16[128,384]{1,0:T(8,128)(2,1)S(1)}, u32[]{:S(2)}, u32[]{:S(2)}) collective-permute-start(bf16[128,384]{1,0:T(8,128)(2,1)S(1)} %get-tuple-element.43.seen.own), channel_id=1, source_target_pairs={{0,4},{4,0},{8,12},{12,8},{1,5},{5,1},{9,13},{13,9},{2,6},{6,2},{1... | collective-permute-start | bytes 294920 | tf_op jit(solution)/shard_map/ppermute | solution.py:17
  7.5 0.8 %collective-permute-done.p_sib = bf16[128,256]{1,0:T(8,128)(2,1)S(1)} collective-permute-done((bf16[128,256]{1,0:T(8,128)(2,1)S(1)}, bf16[128,256]{1,0:T(8,128)(2,1)S(1)}, u32[]{:S(2)}, u32[]{:S(2)}) %collective-permute-start) | collective-permute-done | bytes 65568 | tf_op jit(solution)/shard_map/ppermute | solution.py:17
  8.3 0.8 %shard_map.84 = (f32[640,256]{1,0:T(8,128)S(1)}, bf16[128,512]{1,0:T(8,128)(2,1)S(1)}, f32[128,512]{1,0:T(8,128)S(1)}) custom-call(f32[640,256]{1,0:T(8,128)S(1)} %get-tuple-element.35.x0, bf16[128,256]{1,0:T(8,128)(2,1)S(1)} %get-tuple-element.36.p, bf16[128,256]{1,0:T(8,128)(2,1)S(1)} %collective-permute-done.p_sib, ...), custom_call_target="tpu_custom_call" | custom-call | flops 3000000000 | tf_op jit(solution)/shard_map/pallas_call | solution.py:88
  9.1 1.8 %collective-permute-start.2 = (bf16[128,512]{1,0:T(8,128)(2,1)S(1)}, bf16[128,512]{1,0:T(8,128)(2,1)S(1)}, u32[]{:S(2)}, u32[]{:S(2)}) collective-permute-start(bf16[128,512]{1,0:T(8,128)(2,1)S(1)} %get-tuple-element.46), channel_id=1, source_target_pairs={{0,4},{4,0},{8,12},{12,8},{1,5},{5,1},{9,13},{13,9},{2,6},{6,2},{1... | collective-permute-start | bytes 393224 | tf_op jit(solution)/shard_map/ppermute | solution.py:17
  11.1 3.3 %collective-permute-start.5 = (bf16[128,256]{1,0:T(8,128)(2,1)S(1)}, bf16[128,256]{1,0:T(8,128)(2,1)S(1)}, u32[]{:S(2)}, u32[]{:S(2)}) collective-permute-start(bf16[128,256]{1,0:T(8,128)(2,1)S(1)} %get-tuple-element.51), channel_id=1, source_target_pairs={{0,12},{4,8},{8,4},{12,0},{1,13},{5,9},{9,5},{13,1},{2,14},{6,10},... | collective-permute-start | bytes 196616 | tf_op jit(solution)/shard_map/ppermute | solution.py:17
  14.6 3.6 %collective-permute-start.4 = (bf16[128,512]{1,0:T(8,128)(2,1)S(1)}, bf16[128,512]{1,0:T(8,128)(2,1)S(1)}, u32[]{:S(2)}, u32[]{:S(2)}) collective-permute-start(bf16[128,512]{1,0:T(8,128)(2,1)S(1)} %get-tuple-element.49.seen.send), channel_id=1, source_target_pairs={{0,12},{4,8},{8,4},{12,0},{1,13},{5,9},{9,5},{13,1},{2,14},{6,10},... | collective-permute-start | bytes 393224 | tf_op jit(solution)/shard_map/ppermute | solution.py:17
  18.2 0.5 %shard_map.87.seen.late = bf16[128,768]{1,0:T(8,128)(2,1)S(1)} custom-call(bf16[2,1,640,128]{3,2,1,0:T(8,128)(2,1)S(1)} %get-tuple-element.37.lb, bf16[2,1,640,128]{3,2,1,0:T(8,128)(2,1)S(1)} %get-tuple-element.38.rb, bf16[2,1,128,256]{3,2,1,0:T(8,128)(2,1)S(1)} %get-tuple-element.39.caps, bf16[1,640,128]{2,1,0:T(8,128)(2,1)S(1)} %get-tuple-element.40.tl, ...), custom_call_target="tpu_custom_call" | custom-call | flops 5000000000 | tf_op jit(solution)/shard_map/pallas_call | solution.py:88
  19.1 1.5 %collective-permute-start.10 = (bf16[128,512]{1,0:T(8,128)(2,1)S(1)}, bf16[128,512]{1,0:T(8,128)(2,1)S(1)}, u32[]{:S(2)}, u32[]{:S(2)}) collective-permute-start(bf16[128,512]{1,0:T(8,128)(2,1)S(1)} %copy-done), channel_id=1, source_target_pairs={{0,2},{1,3},{2,0},{3,1},{4,6},{5,7},{6,4},{7,5},{8,10},{9,11},{10,... | collective-permute-start | bytes 393224 | tf_op jit(solution)/shard_map/ppermute | solution.py:17
  20.6 2.1 %collective-permute-done.4.far = bf16[128,512]{1,0:T(8,128)(2,1)S(1)} collective-permute-done((bf16[128,512]{1,0:T(8,128)(2,1)S(1)}, bf16[128,512]{1,0:T(8,128)(2,1)S(1)}, u32[]{:S(2)}, u32[]{:S(2)}) %collective-permute-start.4) | collective-permute-done | bytes 131104 | tf_op jit(solution)/shard_map/ppermute | solution.py:17
  22.9 1.6 %collective-permute-start.8 = (bf16[128,384]{1,0:T(8,128)(2,1)S(1)}, bf16[128,384]{1,0:T(8,128)(2,1)S(1)}, u32[]{:S(2)}, u32[]{:S(2)}) collective-permute-start(bf16[128,384]{1,0:T(8,128)(2,1)S(1)} %shard_map.88.seen.a), channel_id=1, source_target_pairs={{0,2},{1,3},{2,0},{3,1},{4,6},{5,7},{6,4},{7,5},{8,10},{9,11},{10,... | collective-permute-start | bytes 294920 | tf_op jit(solution)/shard_map/ppermute | solution.py:17
  24.7 0.7 %shard_map.89 = (bf16[640,256]{1,0:T(8,128)(2,1)S(1)}, f32[128,256]{1,0:T(8,128)S(1)}, bf16[128,512]{1,0:T(8,128)(2,1)S(1)}) custom-call(f32[640,256]{1,0:T(8,128)S(1)} %get-tuple-element.44.seen.x1, bf16[128,512]{1,0:T(8,128)(2,1)S(1)} %get-tuple-element.49.seen.send, bf16[128,512]{1,0:T(8,128)(2,1)S(1)} %collective-permute-done.4.far, ...), custom_call_target="tpu_custom_call" | custom-call | flops 100000000 | tf_op jit(solution)/shard_map/pallas_call | solution.py:88
  25.5 0.6 %collective-permute-start.7 = (bf16[128,384]{1,0:T(8,128)(2,1)S(1)}, bf16[128,384]{1,0:T(8,128)(2,1)S(1)}, u32[]{:S(2)}, u32[]{:S(2)}) collective-permute-start(bf16[128,384]{1,0:T(8,128)(2,1)S(1)} %shard_map.88.seen.a), channel_id=1, source_target_pairs={{0,1},{1,0},{2,3},{3,2},{4,5},{5,4},{6,7},{7,6},{8,9},{9,8},{10,11... | collective-permute-start | bytes 294920 | tf_op jit(solution)/shard_map/ppermute | solution.py:17
  26.0 1.1 %collective-permute-start.13 = (bf16[128,512]{1,0:T(8,128)(2,1)S(1)}, bf16[128,512]{1,0:T(8,128)(2,1)S(1)}, u32[]{:S(2)}, u32[]{:S(2)}) collective-permute-start(bf16[128,512]{1,0:T(8,128)(2,1)S(1)} %get-tuple-element.60.z), channel_id=1, source_target_pairs={{0,4},{4,0},{8,12},{12,8},{1,5},{5,1},{9,13},{13,9},{2,6},{6,2},{1... | collective-permute-start | bytes 393224 | tf_op jit(solution)/shard_map/ppermute | solution.py:17
  27.6 0.9 %shard_map.90 = (f32[640,256]{1,0:T(8,128)S(1)}, bf16[640,512]{1,0:T(8,128)(2,1)S(1)}) custom-call(bf16[640,256]{1,0:T(8,128)(2,1)S(1)} %get-tuple-element.53.x2, bf16[2,1,640,128]{3,2,1,0:T(8,128)(2,1)S(1)} %get-tuple-element.38.rb, bf16[1,640,128]{2,1,0:T(8,128)(2,1)S(1)} %get-tuple-element.40.tl, bf16[1,640,128]{2,1,0:T(8,128)(2,1)S(1)} %get-tuple-element.41.tr, ...), custom_call_target="tpu_custom_call" | custom-call | flops 1000000000 | tf_op jit(solution)/shard_map/pallas_call | solution.py:88
  28.9 0.7 %shard_map.92.back = bf16[128,512]{1,0:T(8,128)(2,1)S(1)} custom-call(bf16[128,384]{1,0:T(8,128)(2,1)S(1)} %shard_map.88.seen.a, bf16[128,384]{1,0:T(8,128)(2,1)S(1)} %collective-permute-done.7.b, bf16[128,384]{1,0:T(8,128)(2,1)S(1)} %collective-permute-done.8.c, bf16[128,384]{1,0:T(8,128)(2,1)S(1)} %collective-permute-done.9.d, ...), custom_call_target="tpu_custom_call" | custom-call | flops 1000000000 | tf_op jit(solution)/shard_map/pallas_call | solution.py:88
  29.6 1.2 %collective-permute-start.12 = (bf16[128,512]{1,0:T(8,128)(2,1)S(1)}, bf16[128,512]{1,0:T(8,128)(2,1)S(1)}, u32[]{:S(2)}, u32[]{:S(2)}) collective-permute-start(bf16[128,512]{1,0:T(8,128)(2,1)S(1)} %shard_map.92.back), channel_id=1, source_target_pairs={{0,4},{4,0},{8,12},{12,8},{1,5},{5,1},{9,13},{13,9},{2,6},{6,2},{1... | collective-permute-start | bytes 393224 | tf_op jit(solution)/shard_map/ppermute | solution.py:17
  30.8 0.7 %collective-permute-done.13.z_sib = bf16[128,512]{1,0:T(8,128)(2,1)S(1)} collective-permute-done((bf16[128,512]{1,0:T(8,128)(2,1)S(1)}, bf16[128,512]{1,0:T(8,128)(2,1)S(1)}, u32[]{:S(2)}, u32[]{:S(2)}) %collective-permute-start.13) | collective-permute-done | bytes 131104 | tf_op jit(solution)/shard_map/ppermute | solution.py:17
  31.5 3.7 %collective-permute-done.12.back_sib = bf16[128,512]{1,0:T(8,128)(2,1)S(1)} collective-permute-done((bf16[128,512]{1,0:T(8,128)(2,1)S(1)}, bf16[128,512]{1,0:T(8,128)(2,1)S(1)}, u32[]{:S(2)}, u32[]{:S(2)}) %collective-permute-start.12) | collective-permute-done | bytes 131104 | tf_op jit(solution)/shard_map/ppermute | solution.py:17
  35.4 3.8 %collective-permute-start.14 = (bf16[128,256]{1,0:T(8,128)(2,1)S(1)}, bf16[128,256]{1,0:T(8,128)(2,1)S(1)}, u32[]{:S(2)}, u32[]{:S(2)}) collective-permute-start(bf16[128,256]{1,0:T(8,128)(2,1)S(1)} %get-tuple-element.62.seen.half5), channel_id=1, source_target_pairs={{0,12},{4,8},{8,4},{12,0},{1,13},{5,9},{9,5},{13,1},{2,14},{6,10},... | collective-permute-start | bytes 196616 | tf_op jit(solution)/shard_map/ppermute | solution.py:17
  39.5 2.1 %collective-permute-done.14.half5_far = bf16[128,256]{1,0:T(8,128)(2,1)S(1)} collective-permute-done((bf16[128,256]{1,0:T(8,128)(2,1)S(1)}, bf16[128,256]{1,0:T(8,128)(2,1)S(1)}, u32[]{:S(2)}, u32[]{:S(2)}) %collective-permute-start.14) | collective-permute-done | bytes 65568 | tf_op jit(solution)/shard_map/ppermute | solution.py:17
  41.6 1.4 %shard_map.95 = f32[1,640,256]{2,1,0:T(8,128)} custom-call(f32[640,256]{1,0:T(8,128)S(1)} %get-tuple-element.63.out3, bf16[640,512]{1,0:T(8,128)(2,1)S(1)} %get-tuple-element.56.under, bf16[128,256]{1,0:T(8,128)(2,1)S(1)} %get-tuple-element.62.seen.half5, bf16[128,256]{1,0:T(8,128)(2,1)S(1)} %collective-permute-done.14.half5_far, ...), custom_call_target="tpu_custom_call" | custom-call | flops 1000000000 | tf_op jit(solution)/shard_map/pallas_call | solution.py:88
  (22 shorter events, 3.0 us)
Async XLA Ops:
  0.0 2.4 %copy-start = (bf16[128,512]{1,0:T(8,128)(2,1)S(1)}, bf16[128,512]{1,0:T(8,128)(2,1)}, u32[]{:S(2)}) copy-start(bf16[128,512]{1,0:T(8,128)(2,1)} %a.1) | copy-start | bytes 393220
  2.4 3.2 %collective-permute-start.1 = (bf16[128,512]{1,0:T(8,128)(2,1)S(1)}, bf16[128,512]{1,0:T(8,128)(2,1)S(1)}, u32[]{:S(2)}, u32[]{:S(2)}) collective-permute-start(bf16[128,512]{1,0:T(8,128)(2,1)S(1)} %copy-done), channel_id=1, source_target_pairs={{0,1},{1,0},{2,3},{3,2},{4,5},{5,4},{6,7},{7,6},{8,9},{9,8},{10,11... | collective-permute-start | bytes 393224 | tf_op jit(solution)/shard_map/ppermute | solution.py:17
  2.9 5.3 %collective-permute-start = (bf16[128,256]{1,0:T(8,128)(2,1)S(1)}, bf16[128,256]{1,0:T(8,128)(2,1)S(1)}, u32[]{:S(2)}, u32[]{:S(2)}) collective-permute-start(bf16[128,256]{1,0:T(8,128)(2,1)S(1)} %get-tuple-element.36.p), channel_id=1, source_target_pairs={{0,4},{4,0},{8,12},{12,8},{1,5},{5,1},{9,13},{13,9},{2,6},{6,2},{1... | collective-permute-start | bytes 196616 | tf_op jit(solution)/shard_map/ppermute | solution.py:17
  6.2 4.9 %collective-permute-start.3 = (bf16[128,384]{1,0:T(8,128)(2,1)S(1)}, bf16[128,384]{1,0:T(8,128)(2,1)S(1)}, u32[]{:S(2)}, u32[]{:S(2)}) collective-permute-start(bf16[128,384]{1,0:T(8,128)(2,1)S(1)} %get-tuple-element.43.seen.own), channel_id=1, source_target_pairs={{0,4},{4,0},{8,12},{12,8},{1,5},{5,1},{9,13},{13,9},{2,6},{6,2},{1... | collective-permute-start | bytes 294920 | tf_op jit(solution)/shard_map/ppermute | solution.py:17
  9.1 5.4 %collective-permute-start.2 = (bf16[128,512]{1,0:T(8,128)(2,1)S(1)}, bf16[128,512]{1,0:T(8,128)(2,1)S(1)}, u32[]{:S(2)}, u32[]{:S(2)}) collective-permute-start(bf16[128,512]{1,0:T(8,128)(2,1)S(1)} %get-tuple-element.46), channel_id=1, source_target_pairs={{0,4},{4,0},{8,12},{12,8},{1,5},{5,1},{9,13},{13,9},{2,6},{6,2},{1... | collective-permute-start | bytes 393224 | tf_op jit(solution)/shard_map/ppermute | solution.py:17
  11.1 7.1 %collective-permute-start.5 = (bf16[128,256]{1,0:T(8,128)(2,1)S(1)}, bf16[128,256]{1,0:T(8,128)(2,1)S(1)}, u32[]{:S(2)}, u32[]{:S(2)}) collective-permute-start(bf16[128,256]{1,0:T(8,128)(2,1)S(1)} %get-tuple-element.51), channel_id=1, source_target_pairs={{0,12},{4,8},{8,4},{12,0},{1,13},{5,9},{9,5},{13,1},{2,14},{6,10},... | collective-permute-start | bytes 196616 | tf_op jit(solution)/shard_map/ppermute | solution.py:17
  14.6 8.1 %collective-permute-start.4 = (bf16[128,512]{1,0:T(8,128)(2,1)S(1)}, bf16[128,512]{1,0:T(8,128)(2,1)S(1)}, u32[]{:S(2)}, u32[]{:S(2)}) collective-permute-start(bf16[128,512]{1,0:T(8,128)(2,1)S(1)} %get-tuple-element.49.seen.send), channel_id=1, source_target_pairs={{0,12},{4,8},{8,4},{12,0},{1,13},{5,9},{9,5},{13,1},{2,14},{6,10},... | collective-permute-start | bytes 393224 | tf_op jit(solution)/shard_map/ppermute | solution.py:17
  18.8 8.8 %collective-permute-start.6 = (bf16[128,768]{1,0:T(8,128)(2,1)S(1)}, bf16[128,768]{1,0:T(8,128)(2,1)S(1)}, u32[]{:S(2)}, u32[]{:S(2)}) collective-permute-start(bf16[128,768]{1,0:T(8,128)(2,1)S(1)} %shard_map.87.seen.late), channel_id=1, source_target_pairs={{0,4},{4,0},{8,12},{12,8},{1,5},{5,1},{9,13},{13,9},{2,6},{6,2},{1... | collective-permute-start | bytes 589832 | tf_op jit(solution)/shard_map/ppermute | solution.py:17
  19.1 5.6 %collective-permute-start.10 = (bf16[128,512]{1,0:T(8,128)(2,1)S(1)}, bf16[128,512]{1,0:T(8,128)(2,1)S(1)}, u32[]{:S(2)}, u32[]{:S(2)}) collective-permute-start(bf16[128,512]{1,0:T(8,128)(2,1)S(1)} %copy-done), channel_id=1, source_target_pairs={{0,2},{1,3},{2,0},{3,1},{4,6},{5,7},{6,4},{7,5},{8,10},{9,11},{10,... | collective-permute-start | bytes 393224 | tf_op jit(solution)/shard_map/ppermute | solution.py:17
  22.9 4.7 %collective-permute-start.8 = (bf16[128,384]{1,0:T(8,128)(2,1)S(1)}, bf16[128,384]{1,0:T(8,128)(2,1)S(1)}, u32[]{:S(2)}, u32[]{:S(2)}) collective-permute-start(bf16[128,384]{1,0:T(8,128)(2,1)S(1)} %shard_map.88.seen.a), channel_id=1, source_target_pairs={{0,2},{1,3},{2,0},{3,1},{4,6},{5,7},{6,4},{7,5},{8,10},{9,11},{10,... | collective-permute-start | bytes 294920 | tf_op jit(solution)/shard_map/ppermute | solution.py:17
  24.7 3.7 %collective-permute-start.11 = (bf16[128,512]{1,0:T(8,128)(2,1)S(1)}, bf16[128,512]{1,0:T(8,128)(2,1)S(1)}, u32[]{:S(2)}, u32[]{:S(2)}) collective-permute-start(bf16[128,512]{1,0:T(8,128)(2,1)S(1)} %collective-permute-done.10.c), channel_id=1, source_target_pairs={{0,1},{1,0},{2,3},{3,2},{4,5},{5,4},{6,7},{7,6},{8,9},{9,8},{10,11... | collective-permute-start | bytes 393224 | tf_op jit(solution)/shard_map/ppermute | solution.py:17
  25.5 3.1 %collective-permute-start.7 = (bf16[128,384]{1,0:T(8,128)(2,1)S(1)}, bf16[128,384]{1,0:T(8,128)(2,1)S(1)}, u32[]{:S(2)}, u32[]{:S(2)}) collective-permute-start(bf16[128,384]{1,0:T(8,128)(2,1)S(1)} %shard_map.88.seen.a), channel_id=1, source_target_pairs={{0,1},{1,0},{2,3},{3,2},{4,5},{5,4},{6,7},{7,6},{8,9},{9,8},{10,11... | collective-permute-start | bytes 294920 | tf_op jit(solution)/shard_map/ppermute | solution.py:17
  26.0 5.5 %collective-permute-start.13 = (bf16[128,512]{1,0:T(8,128)(2,1)S(1)}, bf16[128,512]{1,0:T(8,128)(2,1)S(1)}, u32[]{:S(2)}, u32[]{:S(2)}) collective-permute-start(bf16[128,512]{1,0:T(8,128)(2,1)S(1)} %get-tuple-element.60.z), channel_id=1, source_target_pairs={{0,4},{4,0},{8,12},{12,8},{1,5},{5,1},{9,13},{13,9},{2,6},{6,2},{1... | collective-permute-start | bytes 393224 | tf_op jit(solution)/shard_map/ppermute | solution.py:17
  27.6 1.3 %collective-permute-start.9 = (bf16[128,384]{1,0:T(8,128)(2,1)S(1)}, bf16[128,384]{1,0:T(8,128)(2,1)S(1)}, u32[]{:S(2)}, u32[]{:S(2)}) collective-permute-start(bf16[128,384]{1,0:T(8,128)(2,1)S(1)} %collective-permute-done.8.c), channel_id=1, source_target_pairs={{0,1},{1,0},{2,3},{3,2},{4,5},{5,4},{6,7},{7,6},{8,9},{9,8},{10,11... | collective-permute-start | bytes 294920 | tf_op jit(solution)/shard_map/ppermute | solution.py:17
  29.6 5.7 %collective-permute-start.12 = (bf16[128,512]{1,0:T(8,128)(2,1)S(1)}, bf16[128,512]{1,0:T(8,128)(2,1)S(1)}, u32[]{:S(2)}, u32[]{:S(2)}) collective-permute-start(bf16[128,512]{1,0:T(8,128)(2,1)S(1)} %shard_map.92.back), channel_id=1, source_target_pairs={{0,4},{4,0},{8,12},{12,8},{1,5},{5,1},{9,13},{13,9},{2,6},{6,2},{1... | collective-permute-start | bytes 393224 | tf_op jit(solution)/shard_map/ppermute | solution.py:17
  35.4 6.2 %collective-permute-start.14 = (bf16[128,256]{1,0:T(8,128)(2,1)S(1)}, bf16[128,256]{1,0:T(8,128)(2,1)S(1)}, u32[]{:S(2)}, u32[]{:S(2)}) collective-permute-start(bf16[128,256]{1,0:T(8,128)(2,1)S(1)} %get-tuple-element.62.seen.half5), channel_id=1, source_target_pairs={{0,12},{4,8},{8,4},{12,0},{1,13},{5,9},{9,5},{13,1},{2,14},{6,10},... | collective-permute-start | bytes 196616 | tf_op jit(solution)/shard_map/ppermute | solution.py:17

commit v13 on v12

--- a/solution.py
+++ b/solution.py
@@ -187,8 +187,7 @@
         scratch=[pltpu.VMEM(tall, f32), pltpu.SemaphoreType.DMA((3, max(blocks, 5)))],
     )
     proj1_sib = swap(proj1, "leaf", 1)
-    caps_here = after(top_caps, proj1)
-    caps_near = swap(caps_here, "top", 1)
+    proj1_near = swap(proj1, "top", 1)
 
     def early_body(lb, caps, tl, tr, seen, send, keep, scratch):
         side = column_side()
@@ -206,7 +205,7 @@
         caps,
         tl,
         tr,
-        caps_near,
+        proj1_near,
         scratch=[pltpu.VMEM((2, rank, 2 * rank), BF)],
         micros=10,
     )
@@ -277,25 +276,15 @@
     )
     cross_in = swap(cross_send, "leaf", 3)
 
-    caps_far = swap(after(top_caps, cross_send), "top", 2)
-    caps_far_near = swap(caps_far, "top", 1)
-
-    def order_body(a, b, c, d, out):
-        here = lax.axis_index("top")
-        for i, piece in enumerate((a, b, c, d)):
-            for k in range(4):
-                out[span(i), span(k)] = piece[:, block(here ^ k, rank)]
-
-    (caps_all,) = call(
-        order_body,
-        [((4 * rank, 4 * rank), BF)],
-        top_caps,
-        caps_near,
-        caps_far,
-        caps_far_near,
-        micros=0.1,
-    )
-
+    def turn_body(gram, far, caps, seen, out):
+        whole = (gram[...] + far[:, span(1)]).astype(BF)
+        out[...] = dot(whole, caps[...]).astype(BF)
+
+    (turn,) = call(
+        turn_body, [(top_caps.shape, BF)], gram_pair, next_far, top_caps, cross_send, micros=0.1
+    )
+    turn_far = swap(turn, "top", 2)
+    turn_near = swap(turn, "top", 1)
     def late_body(lb, rb, caps, tl, tr, seen, seen2, out):
         for i, basis in enumerate((tl[0], tr[0])):
             out[:, span(i)] = (dot_t(lb[0, 0], basis) * s1).astype(BF)
@@ -318,24 +307,22 @@
 
     late_sib = swap(late, "leaf", 1)
 
-    def column_body(send, keep2, far, nexts, nexts_far, gram, seen, out):
-        out[:, :cols] = (
+    def column_body(send, keep2, far, nexts, nexts_far, seen, out):
+        out[...] = (
             keep2[...]
             + far[:, cols:]
             - dot(nexts[:, span(1)], far[:, :cols])
             - dot(nexts_far[:, span(0)], send[:, :cols])
         ).astype(BF)
-        out[:, cols:] = (gram[...] + nexts_far[:, span(1)]).astype(BF)
 
     (top_send,) = call(
         column_body,
-        [((rank, cols + rank), BF)],
+        [(wide, BF)],
         cross_send,
         cross_keep,
         cross_in,
         next_keep,
         next_far,
-        gram_pair,
         late,
         micros=0.2,
     )
@@ -365,6 +352,26 @@
     top_near = swap(after(top_send, state2), "top", 1)
     top_parts = top_send, top_near, top_far, swap(top_far, "top", 1)
 
+    turn_far_near = swap(after(turn_far, top_far), "top", 1)
+
+    def order_body(a, b, c, d, caps, out, row):
+        here = lax.axis_index("top")
+        for k in range(4):
+            for i, piece in enumerate((a, b, c, d)):
+                out[span(i), span(k)] = piece[:, block(here ^ k, rank)]
+            row[:, span(k)] = caps[:, block(here ^ k, rank)]
+
+    turn_all, caps_row = call(
+        order_body,
+        [((4 * rank, 4 * rank), BF), ((rank, 4 * rank), BF)],
+        turn,
+        turn_near,
+        turn_far,
+        turn_far_near,
+        top_caps,
+        micros=0.1,
+    )
+
     def under_body(x2, rb, tl, tr, inv, seen, out2, under):
         for c in range(blocks):
             column = inv[c * rank :, span(c)]
@@ -381,25 +388,25 @@
         tr,
         inverse,
         late_sib,
-    )
-
-    def top_body(a, b, c, d, caps, seen, out, up, down):
-        pieces = (a, b, c, d)
-        for i, piece in enumerate(pieces):
-            up[span(i), :] = piece[:, :cols]
-        coef = dot(caps[...], up[...]).astype(BF)
-        for i, piece in enumerate(pieces):
-            down[span(i), :] = dot(piece[:, cols:], coef[span(i), :]).astype(BF)
-        out[:, :cols] = coef[:rank, :]
-        out[:, cols:] = dot(caps[:rank, :], down[...]).astype(BF)
+        micros=3,
+    )
+
+    def top_body(a, b, c, d, turns, row, seen, out, up):
+        for i, piece in enumerate((a, b, c, d)):
+            up[span(i), :] = piece[...]
+        turned = dot(turns[...], up[...]).astype(BF)
+        out[:, :cols] = dot(row[...], up[...]).astype(BF)
+        out[:, cols:] = dot(row[...], turned).astype(BF)
 
     (back_send,) = call(
         top_body,
         [((rank, 2 * cols), BF)],
         *top_parts,
-        caps_all,
+        turn_all,
+        caps_row,
         out2,
-        scratch=[pltpu.VMEM((4 * rank, cols), BF)] * 2,
+        scratch=[pltpu.VMEM((4 * rank, cols), BF)],
+        micros=1,
     )
     back_in = swap(back_send, "leaf", 1)
 

time: 43.2 us -> 42.9 us (level)
  waiting for transfers between devices: 10.6 us -> 9.58 us
  starting transfers between devices: 23.3 us -> 24 us
    ppermute x15 -> x16, waiting for transfers between devices: 10.6 us -> 9.58 us  [swap(): return lax.ppermute(value, axis, pairs)]
    ppermute x15 -> x16, starting transfers between devices: 23.3 us -> 24 us  [swap(): return lax.ppermute(value, axis, pairs)]
    pallas_call x14 -> x15, Pallas kernels: 8.99 us -> 8.99 us  [call(): pl.pallas_call(body, out_shape=[jax.ShapeDtypeStruct(shape, dtype) if hbm...]
  transfers between devices with their start and end apart: 15 -> 16, of which waited for: 9 -> 7; matrix products, arithmetic and copies ran while one was open for 0% -> 0% of each run, Pallas kernels for 12% -> 12%
where the time goes in v13:
time: 42.9 us; the launch traced here: 42.7 us
  starting transfers between devices  24 us (56%)
  waiting for transfers between devices  9.58 us (22%)
  Pallas kernels  8.99 us (21%)
    ppermute x16, starting transfers between devices, swap(): return lax.ppermute(value, axis, pairs)  24 us
    ppermute x16, waiting for transfers between devices, swap(): return lax.ppermute(value, axis, pairs)  9.58 us
    pallas_call x15, Pallas kernels, call(): pl.pallas_call(body, out_shape=[jax.ShapeDtypeStruct(shape, dtype) if hbm...  8.99 us
  transfers between devices with their start and end apart: 16, of which 7 were waited for; matrix products, arithmetic and copies ran while one was open for 0% of the time, Pallas kernels for 12%

profile of v13, /device:TPU:0, one launch (start us, length us, event | category | flops | bytes accessed | tf_op | source)
XLA Modules:
  0.0 42.7 jit_solution(10192072508874805753)
XLA Ops:
  0.0 2.4 %shard_map.82 = (f32[640,256]{1,0:T(8,128)S(1)}, bf16[128,256]{1,0:T(8,128)(2,1)S(1)}, bf16[640,640]{1,0:T(8,128)(2,1)S(1)}, bf16[2,1,640,128]{3,2,1,0:T(8,128)(...) custom-call(f32[1,640,256]{2,1,0:T(8,128)} %rhs_hbm.1, ...), custom_call_target="tpu_custom_call" | custom-call | flops 1000000000 | tf_op jit(solution)/shard_map/pallas_call | solution.py:88
  2.9 2.7 %collective-permute-start = (bf16[128,256]{1,0:T(8,128)(2,1)S(1)}, bf16[128,256]{1,0:T(8,128)(2,1)S(1)}, u32[]{:S(2)}, u32[]{:S(2)}) collective-permute-start(bf16[128,256]{1,0:T(8,128)(2,1)S(1)} %get-tuple-element.37.p), channel_id=1, source_target_pairs={{0,4},{4,0},{8,12},{12,8},{1,5},{5,1},{9,13},{13,9},{2,6},{6,2},{1... | collective-permute-start | bytes 196616 | tf_op jit(solution)/shard_map/ppermute | solution.py:17
  5.5 0.6 %shard_map.83 = (bf16[128,384]{1,0:T(8,128)(2,1)S(1)}, bf16[128,256]{1,0:T(8,128)(2,1)S(1)}) custom-call(bf16[2,1,640,128]{3,2,1,0:T(8,128)(2,1)S(1)} %get-tuple-element.38.lb, bf16[2,1,128,256]{3,2,1,0:T(8,128)(2,1)S(1)} %get-tuple-element.40.caps, bf16[1,640,128]{2,1,0:T(8,128)(2,1)S(1)} %get-tuple-element.41.tl, ...), custom_call_target="tpu_custom_call" | custom-call | flops 10000000000 | tf_op jit(solution)/shard_map/pallas_call | solution.py:88
  6.1 1.2 %collective-permute-start.3 = (bf16[128,384]{1,0:T(8,128)(2,1)S(1)}, bf16[128,384]{1,0:T(8,128)(2,1)S(1)}, u32[]{:S(2)}, u32[]{:S(2)}) collective-permute-start(bf16[128,384]{1,0:T(8,128)(2,1)S(1)} %get-tuple-element.43.seen.own), channel_id=1, source_target_pairs={{0,4},{4,0},{8,12},{12,8},{1,5},{5,1},{9,13},{13,9},{2,6},{6,2},{1... | collective-permute-start | bytes 294920 | tf_op jit(solution)/shard_map/ppermute | solution.py:17
  7.4 0.9 %collective-permute-done.p_sib = bf16[128,256]{1,0:T(8,128)(2,1)S(1)} collective-permute-done((bf16[128,256]{1,0:T(8,128)(2,1)S(1)}, bf16[128,256]{1,0:T(8,128)(2,1)S(1)}, u32[]{:S(2)}, u32[]{:S(2)}) %collective-permute-start) | collective-permute-done | bytes 65568 | tf_op jit(solution)/shard_map/ppermute | solution.py:17
  8.2 0.8 %shard_map.84 = (f32[640,256]{1,0:T(8,128)S(1)}, bf16[128,512]{1,0:T(8,128)(2,1)S(1)}, f32[128,512]{1,0:T(8,128)S(1)}) custom-call(f32[640,256]{1,0:T(8,128)S(1)} %get-tuple-element.36.x0, bf16[128,256]{1,0:T(8,128)(2,1)S(1)} %get-tuple-element.37.p, bf16[128,256]{1,0:T(8,128)(2,1)S(1)} %collective-permute-done.p_sib, ...), custom_call_target="tpu_custom_call" | custom-call | flops 3000000000 | tf_op jit(solution)/shard_map/pallas_call | solution.py:88
  9.0 1.8 %collective-permute-start.2 = (bf16[128,512]{1,0:T(8,128)(2,1)S(1)}, bf16[128,512]{1,0:T(8,128)(2,1)S(1)}, u32[]{:S(2)}, u32[]{:S(2)}) collective-permute-start(bf16[128,512]{1,0:T(8,128)(2,1)S(1)} %get-tuple-element.46), channel_id=1, source_target_pairs={{0,4},{4,0},{8,12},{12,8},{1,5},{5,1},{9,13},{13,9},{2,6},{6,2},{1... | collective-permute-start | bytes 393224 | tf_op jit(solution)/shard_map/ppermute | solution.py:17
  11.1 3.3 %collective-permute-start.5 = (bf16[128,256]{1,0:T(8,128)(2,1)S(1)}, bf16[128,256]{1,0:T(8,128)(2,1)S(1)}, u32[]{:S(2)}, u32[]{:S(2)}) collective-permute-start(bf16[128,256]{1,0:T(8,128)(2,1)S(1)} %get-tuple-element.51), channel_id=1, source_target_pairs={{0,12},{4,8},{8,4},{12,0},{1,13},{5,9},{9,5},{13,1},{2,14},{6,10},... | collective-permute-start | bytes 196616 | tf_op jit(solution)/shard_map/ppermute | solution.py:17
  14.5 3.7 %collective-permute-start.4 = (bf16[128,512]{1,0:T(8,128)(2,1)S(1)}, bf16[128,512]{1,0:T(8,128)(2,1)S(1)}, u32[]{:S(2)}, u32[]{:S(2)}) collective-permute-start(bf16[128,512]{1,0:T(8,128)(2,1)S(1)} %get-tuple-element.49.seen.send), channel_id=1, source_target_pairs={{0,12},{4,8},{8,4},{12,0},{1,13},{5,9},{9,5},{13,1},{2,14},{6,10},... | collective-permute-start | bytes 393224 | tf_op jit(solution)/shard_map/ppermute | solution.py:17
  18.2 0.5 %shard_map.87.seen.late = bf16[128,768]{1,0:T(8,128)(2,1)S(1)} custom-call(bf16[2,1,640,128]{3,2,1,0:T(8,128)(2,1)S(1)} %get-tuple-element.38.lb, bf16[2,1,640,128]{3,2,1,0:T(8,128)(2,1)S(1)} %get-tuple-element.39.rb, bf16[2,1,128,256]{3,2,1,0:T(8,128)(2,1)S(1)} %get-tuple-element.40.caps, bf16[1,640,128]{2,1,0:T(8,128)(2,1)S(1)} %get-tuple-element.41.tl, ...), custom_call_target="tpu_custom_call" | custom-call | flops 5000000000 | tf_op jit(solution)/shard_map/pallas_call | solution.py:88
  19.2 1.6 %collective-permute-start.11 = (bf16[128,512]{1,0:T(8,128)(2,1)S(1)}, bf16[128,512]{1,0:T(8,128)(2,1)S(1)}, u32[]{:S(2)}, u32[]{:S(2)}) collective-permute-start(bf16[128,512]{1,0:T(8,128)(2,1)S(1)} %shard_map.91.a), channel_id=1, source_target_pairs={{0,2},{1,3},{2,0},{3,1},{4,6},{5,7},{6,4},{7,5},{8,10},{9,11},{10,... | collective-permute-start | bytes 393224 | tf_op jit(solution)/shard_map/ppermute | solution.py:17
  20.8 1.8 %collective-permute-done.4.far = bf16[128,512]{1,0:T(8,128)(2,1)S(1)} collective-permute-done((bf16[128,512]{1,0:T(8,128)(2,1)S(1)}, bf16[128,512]{1,0:T(8,128)(2,1)S(1)}, u32[]{:S(2)}, u32[]{:S(2)}) %collective-permute-start.4) | collective-permute-done | bytes 131104 | tf_op jit(solution)/shard_map/ppermute | solution.py:17
  22.8 1.5 %collective-permute-start.8 = (bf16[128,256]{1,0:T(8,128)(2,1)S(1)}, bf16[128,256]{1,0:T(8,128)(2,1)S(1)}, u32[]{:S(2)}, u32[]{:S(2)}) collective-permute-start(bf16[128,256]{1,0:T(8,128)(2,1)S(1)} %shard_map.88.seen.a), channel_id=1, source_target_pairs={{0,2},{1,3},{2,0},{3,1},{4,6},{5,7},{6,4},{7,5},{8,10},{9,11},{10,... | collective-permute-start | bytes 196616 | tf_op jit(solution)/shard_map/ppermute | solution.py:17
  24.3 0.7 %shard_map.89 = (bf16[640,256]{1,0:T(8,128)(2,1)S(1)}, f32[128,256]{1,0:T(8,128)S(1)}, bf16[128,512]{1,0:T(8,128)(2,1)S(1)}) custom-call(f32[640,256]{1,0:T(8,128)S(1)} %get-tuple-element.44.seen.x1, bf16[128,512]{1,0:T(8,128)(2,1)S(1)} %get-tuple-element.49.seen.send, bf16[128,512]{1,0:T(8,128)(2,1)S(1)} %collective-permute-done.4.far, ...), custom_call_target="tpu_custom_call" | custom-call | flops 100000000 | tf_op jit(solution)/shard_map/pallas_call | solution.py:88
  25.1 0.6 %collective-permute-start.7 = (bf16[128,256]{1,0:T(8,128)(2,1)S(1)}, bf16[128,256]{1,0:T(8,128)(2,1)S(1)}, u32[]{:S(2)}, u32[]{:S(2)}) collective-permute-start(bf16[128,256]{1,0:T(8,128)(2,1)S(1)} %shard_map.88.seen.a), channel_id=1, source_target_pairs={{0,1},{1,0},{2,3},{3,2},{4,5},{5,4},{6,7},{7,6},{8,9},{9,8},{10,11... | collective-permute-start | bytes 196616 | tf_op jit(solution)/shard_map/ppermute | solution.py:17
  25.7 1.2 %collective-permute-start.14 = (bf16[128,512]{1,0:T(8,128)(2,1)S(1)}, bf16[128,512]{1,0:T(8,128)(2,1)S(1)}, u32[]{:S(2)}, u32[]{:S(2)}) collective-permute-start(bf16[128,512]{1,0:T(8,128)(2,1)S(1)} %get-tuple-element.62.z), channel_id=1, source_target_pairs={{0,4},{4,0},{8,12},{12,8},{1,5},{5,1},{9,13},{13,9},{2,6},{6,2},{1... | collective-permute-start | bytes 393224 | tf_op jit(solution)/shard_map/ppermute | solution.py:17
  27.6 0.9 %shard_map.90 = (f32[640,256]{1,0:T(8,128)S(1)}, bf16[640,512]{1,0:T(8,128)(2,1)S(1)}) custom-call(bf16[640,256]{1,0:T(8,128)(2,1)S(1)} %get-tuple-element.52.x2, bf16[2,1,640,128]{3,2,1,0:T(8,128)(2,1)S(1)} %get-tuple-element.39.rb, bf16[1,640,128]{2,1,0:T(8,128)(2,1)S(1)} %get-tuple-element.41.tl, bf16[1,640,128]{2,1,0:T(8,128)(2,1)S(1)} %get-tuple-element.42.tr, ...), custom_call_target="tpu_custom_call" | custom-call | flops 3000000000 | tf_op jit(solution)/shard_map/pallas_call | solution.py:88
  28.7 0.5 %shard_map.93.back = bf16[128,512]{1,0:T(8,128)(2,1)S(1)} custom-call(bf16[128,256]{1,0:T(8,128)(2,1)S(1)} %shard_map.88.seen.a, bf16[128,256]{1,0:T(8,128)(2,1)S(1)} %collective-permute-done.7.b, bf16[128,256]{1,0:T(8,128)(2,1)S(1)} %collective-permute-done.8.c, bf16[128,256]{1,0:T(8,128)(2,1)S(1)} %collective-permute-done.9.d, ...), custom_call_target="tpu_custom_call" | custom-call | flops 1000000000 | tf_op jit(solution)/shard_map/pallas_call | solution.py:88
  29.2 1.3 %collective-permute-start.13 = (bf16[128,512]{1,0:T(8,128)(2,1)S(1)}, bf16[128,512]{1,0:T(8,128)(2,1)S(1)}, u32[]{:S(2)}, u32[]{:S(2)}) collective-permute-start(bf16[128,512]{1,0:T(8,128)(2,1)S(1)} %shard_map.93.back), channel_id=1, source_target_pairs={{0,4},{4,0},{8,12},{12,8},{1,5},{5,1},{9,13},{13,9},{2,6},{6,2},{1... | collective-permute-start | bytes 393224 | tf_op jit(solution)/shard_map/ppermute | solution.py:17
  30.5 0.6 %collective-permute-done.14.z_sib = bf16[128,512]{1,0:T(8,128)(2,1)S(1)} collective-permute-done((bf16[128,512]{1,0:T(8,128)(2,1)S(1)}, bf16[128,512]{1,0:T(8,128)(2,1)S(1)}, u32[]{:S(2)}, u32[]{:S(2)}) %collective-permute-start.14) | collective-permute-done | bytes 131104 | tf_op jit(solution)/shard_map/ppermute | solution.py:17
  31.1 3.7 %collective-permute-done.13.back_sib = bf16[128,512]{1,0:T(8,128)(2,1)S(1)} collective-permute-done((bf16[128,512]{1,0:T(8,128)(2,1)S(1)}, bf16[128,512]{1,0:T(8,128)(2,1)S(1)}, u32[]{:S(2)}, u32[]{:S(2)}) %collective-permute-start.13) | collective-permute-done | bytes 131104 | tf_op jit(solution)/shard_map/ppermute | solution.py:17
  35.1 3.9 %collective-permute-start.15 = (bf16[128,256]{1,0:T(8,128)(2,1)S(1)}, bf16[128,256]{1,0:T(8,128)(2,1)S(1)}, u32[]{:S(2)}, u32[]{:S(2)}) collective-permute-start(bf16[128,256]{1,0:T(8,128)(2,1)S(1)} %get-tuple-element.64.seen.half5), channel_id=1, source_target_pairs={{0,12},{4,8},{8,4},{12,0},{1,13},{5,9},{9,5},{13,1},{2,14},{6,10},... | collective-permute-start | bytes 196616 | tf_op jit(solution)/shard_map/ppermute | solution.py:17
  39.2 2.1 %collective-permute-done.15.half5_far = bf16[128,256]{1,0:T(8,128)(2,1)S(1)} collective-permute-done((bf16[128,256]{1,0:T(8,128)(2,1)S(1)}, bf16[128,256]{1,0:T(8,128)(2,1)S(1)}, u32[]{:S(2)}, u32[]{:S(2)}) %collective-permute-start.15) | collective-permute-done | bytes 65568 | tf_op jit(solution)/shard_map/ppermute | solution.py:17
  41.3 1.4 %shard_map.96 = f32[1,640,256]{2,1,0:T(8,128)} custom-call(f32[640,256]{1,0:T(8,128)S(1)} %get-tuple-element.65.out3, bf16[640,512]{1,0:T(8,128)(2,1)S(1)} %get-tuple-element.55.under, bf16[128,256]{1,0:T(8,128)(2,1)S(1)} %get-tuple-element.64.seen.half5, bf16[128,256]{1,0:T(8,128)(2,1)S(1)} %collective-permute-done.15.half5_far, ...), custom_call_target="tpu_custom_call" | custom-call | flops 1000000000 | tf_op jit(solution)/shard_map/pallas_call | solution.py:88
  (25 shorter events, 2.9 us)
Async XLA Ops:
  2.4 3.2 %collective-permute-start.1 = (bf16[128,256]{1,0:T(8,128)(2,1)S(1)}, bf16[128,256]{1,0:T(8,128)(2,1)S(1)}, u32[]{:S(2)}, u32[]{:S(2)}) collective-permute-start(bf16[128,256]{1,0:T(8,128)(2,1)S(1)} %get-tuple-element.37.p), channel_id=1, source_target_pairs={{0,1},{1,0},{2,3},{3,2},{4,5},{5,4},{6,7},{7,6},{8,9},{9,8},{10,11... | collective-permute-start | bytes 196616 | tf_op jit(solution)/shard_map/ppermute | solution.py:17
  2.9 5.3 %collective-permute-start = (bf16[128,256]{1,0:T(8,128)(2,1)S(1)}, bf16[128,256]{1,0:T(8,128)(2,1)S(1)}, u32[]{:S(2)}, u32[]{:S(2)}) collective-permute-start(bf16[128,256]{1,0:T(8,128)(2,1)S(1)} %get-tuple-element.37.p), channel_id=1, source_target_pairs={{0,4},{4,0},{8,12},{12,8},{1,5},{5,1},{9,13},{13,9},{2,6},{6,2},{1... | collective-permute-start | bytes 196616 | tf_op jit(solution)/shard_map/ppermute | solution.py:17
  6.1 4.9 %collective-permute-start.3 = (bf16[128,384]{1,0:T(8,128)(2,1)S(1)}, bf16[128,384]{1,0:T(8,128)(2,1)S(1)}, u32[]{:S(2)}, u32[]{:S(2)}) collective-permute-start(bf16[128,384]{1,0:T(8,128)(2,1)S(1)} %get-tuple-element.43.seen.own), channel_id=1, source_target_pairs={{0,4},{4,0},{8,12},{12,8},{1,5},{5,1},{9,13},{13,9},{2,6},{6,2},{1... | collective-permute-start | bytes 294920 | tf_op jit(solution)/shard_map/ppermute | solution.py:17
  9.0 5.3 %collective-permute-start.2 = (bf16[128,512]{1,0:T(8,128)(2,1)S(1)}, bf16[128,512]{1,0:T(8,128)(2,1)S(1)}, u32[]{:S(2)}, u32[]{:S(2)}) collective-permute-start(bf16[128,512]{1,0:T(8,128)(2,1)S(1)} %get-tuple-element.46), channel_id=1, source_target_pairs={{0,4},{4,0},{8,12},{12,8},{1,5},{5,1},{9,13},{13,9},{2,6},{6,2},{1... | collective-permute-start | bytes 393224 | tf_op jit(solution)/shard_map/ppermute | solution.py:17
  11.1 7.1 %collective-permute-start.5 = (bf16[128,256]{1,0:T(8,128)(2,1)S(1)}, bf16[128,256]{1,0:T(8,128)(2,1)S(1)}, u32[]{:S(2)}, u32[]{:S(2)}) collective-permute-start(bf16[128,256]{1,0:T(8,128)(2,1)S(1)} %get-tuple-element.51), channel_id=1, source_target_pairs={{0,12},{4,8},{8,4},{12,0},{1,13},{5,9},{9,5},{13,1},{2,14},{6,10},... | collective-permute-start | bytes 196616 | tf_op jit(solution)/shard_map/ppermute | solution.py:17
  14.5 4.5 %copy-start = (bf16[128,512]{1,0:T(8,128)(2,1)S(1)}, bf16[128,512]{1,0:T(8,128)(2,1)}, u32[]{:S(2)}) copy-start(bf16[128,512]{1,0:T(8,128)(2,1)} %caps.3) | copy-start | bytes 393220
  14.5 8.1 %collective-permute-start.4 = (bf16[128,512]{1,0:T(8,128)(2,1)S(1)}, bf16[128,512]{1,0:T(8,128)(2,1)S(1)}, u32[]{:S(2)}, u32[]{:S(2)}) collective-permute-start(bf16[128,512]{1,0:T(8,128)(2,1)S(1)} %get-tuple-element.49.seen.send), channel_id=1, source_target_pairs={{0,12},{4,8},{8,4},{12,0},{1,13},{5,9},{9,5},{13,1},{2,14},{6,10},... | collective-permute-start | bytes 393224 | tf_op jit(solution)/shard_map/ppermute | solution.py:17
  18.7 8.4 %collective-permute-start.6 = (bf16[128,768]{1,0:T(8,128)(2,1)S(1)}, bf16[128,768]{1,0:T(8,128)(2,1)S(1)}, u32[]{:S(2)}, u32[]{:S(2)}) collective-permute-start(bf16[128,768]{1,0:T(8,128)(2,1)S(1)} %shard_map.87.seen.late), channel_id=1, source_target_pairs={{0,4},{4,0},{8,12},{12,8},{1,5},{5,1},{9,13},{13,9},{2,6},{6,2},{1... | collective-permute-start | bytes 589832 | tf_op jit(solution)/shard_map/ppermute | solution.py:17
  19.2 6.4 %collective-permute-start.11 = (bf16[128,512]{1,0:T(8,128)(2,1)S(1)}, bf16[128,512]{1,0:T(8,128)(2,1)S(1)}, u32[]{:S(2)}, u32[]{:S(2)}) collective-permute-start(bf16[128,512]{1,0:T(8,128)(2,1)S(1)} %shard_map.91.a), channel_id=1, source_target_pairs={{0,2},{1,3},{2,0},{3,1},{4,6},{5,7},{6,4},{7,5},{8,10},{9,11},{10,... | collective-permute-start | bytes 393224 | tf_op jit(solution)/shard_map/ppermute | solution.py:17
  22.8 4.3 %collective-permute-start.8 = (bf16[128,256]{1,0:T(8,128)(2,1)S(1)}, bf16[128,256]{1,0:T(8,128)(2,1)S(1)}, u32[]{:S(2)}, u32[]{:S(2)}) collective-permute-start(bf16[128,256]{1,0:T(8,128)(2,1)S(1)} %shard_map.88.seen.a), channel_id=1, source_target_pairs={{0,2},{1,3},{2,0},{3,1},{4,6},{5,7},{6,4},{7,5},{8,10},{9,11},{10,... | collective-permute-start | bytes 196616 | tf_op jit(solution)/shard_map/ppermute | solution.py:17
  24.3 4.2 %collective-permute-start.10 = (bf16[128,512]{1,0:T(8,128)(2,1)S(1)}, bf16[128,512]{1,0:T(8,128)(2,1)S(1)}, u32[]{:S(2)}, u32[]{:S(2)}) collective-permute-start(bf16[128,512]{1,0:T(8,128)(2,1)S(1)} %shard_map.91.a), channel_id=1, source_target_pairs={{0,1},{1,0},{2,3},{3,2},{4,5},{5,4},{6,7},{7,6},{8,9},{9,8},{10,11... | collective-permute-start | bytes 393224 | tf_op jit(solution)/shard_map/ppermute | solution.py:17
  25.1 3.6 %collective-permute-start.7 = (bf16[128,256]{1,0:T(8,128)(2,1)S(1)}, bf16[128,256]{1,0:T(8,128)(2,1)S(1)}, u32[]{:S(2)}, u32[]{:S(2)}) collective-permute-start(bf16[128,256]{1,0:T(8,128)(2,1)S(1)} %shard_map.88.seen.a), channel_id=1, source_target_pairs={{0,1},{1,0},{2,3},{3,2},{4,5},{5,4},{6,7},{7,6},{8,9},{9,8},{10,11... | collective-permute-start | bytes 196616 | tf_op jit(solution)/shard_map/ppermute | solution.py:17
  25.7 5.5 %collective-permute-start.14 = (bf16[128,512]{1,0:T(8,128)(2,1)S(1)}, bf16[128,512]{1,0:T(8,128)(2,1)S(1)}, u32[]{:S(2)}, u32[]{:S(2)}) collective-permute-start(bf16[128,512]{1,0:T(8,128)(2,1)S(1)} %get-tuple-element.62.z), channel_id=1, source_target_pairs={{0,4},{4,0},{8,12},{12,8},{1,5},{5,1},{9,13},{13,9},{2,6},{6,2},{1... | collective-permute-start | bytes 393224 | tf_op jit(solution)/shard_map/ppermute | solution.py:17
  27.1 1.4 %collective-permute-start.12 = (bf16[128,512]{1,0:T(8,128)(2,1)S(1)}, bf16[128,512]{1,0:T(8,128)(2,1)S(1)}, u32[]{:S(2)}, u32[]{:S(2)}) collective-permute-start(bf16[128,512]{1,0:T(8,128)(2,1)S(1)} %collective-permute-done.11.c), channel_id=1, source_target_pairs={{0,1},{1,0},{2,3},{3,2},{4,5},{5,4},{6,7},{7,6},{8,9},{9,8},{10,11... | collective-permute-start | bytes 393224 | tf_op jit(solution)/shard_map/ppermute | solution.py:17
  27.1 1.5 %collective-permute-start.9 = (bf16[128,256]{1,0:T(8,128)(2,1)S(1)}, bf16[128,256]{1,0:T(8,128)(2,1)S(1)}, u32[]{:S(2)}, u32[]{:S(2)}) collective-permute-start(bf16[128,256]{1,0:T(8,128)(2,1)S(1)} %collective-permute-done.8.c), channel_id=1, source_target_pairs={{0,1},{1,0},{2,3},{3,2},{4,5},{5,4},{6,7},{7,6},{8,9},{9,8},{10,11... | collective-permute-start | bytes 196616 | tf_op jit(solution)/shard_map/ppermute | solution.py:17
  29.2 5.7 %collective-permute-start.13 = (bf16[128,512]{1,0:T(8,128)(2,1)S(1)}, bf16[128,512]{1,0:T(8,128)(2,1)S(1)}, u32[]{:S(2)}, u32[]{:S(2)}) collective-permute-start(bf16[128,512]{1,0:T(8,128)(2,1)S(1)} %shard_map.93.back), channel_id=1, source_target_pairs={{0,4},{4,0},{8,12},{12,8},{1,5},{5,1},{9,13},{13,9},{2,6},{6,2},{1... | collective-permute-start | bytes 393224 | tf_op jit(solution)/shard_map/ppermute | solution.py:17
  35.1 6.2 %collective-permute-start.15 = (bf16[128,256]{1,0:T(8,128)(2,1)S(1)}, bf16[128,256]{1,0:T(8,128)(2,1)S(1)}, u32[]{:S(2)}, u32[]{:S(2)}) collective-permute-start(bf16[128,256]{1,0:T(8,128)(2,1)S(1)} %get-tuple-element.64.seen.half5), channel_id=1, source_target_pairs={{0,12},{4,8},{8,4},{12,0},{1,13},{5,9},{9,5},{13,1},{2,14},{6,10},... | collective-permute-start | bytes 196616 | tf_op jit(solution)/shard_map/ppermute | solution.py:17

commit v14 on v13

--- a/solution.py
+++ b/solution.py
@@ -261,31 +261,7 @@
         micros=1,
     )
     next_far = swap(next_send, "leaf", 3)
-    def half_body(keep, pair, nexts, send, keep2):
-        send[:, :cols] = (keep[:, :cols] + pair[:, :cols]).astype(BF)
-        keep2[...] = keep[:, cols:] + pair[:, cols:] - dot(nexts[:, span(0)], send[:, :cols])
-        send[:, cols:] = keep2[...].astype(BF)
-
-    cross_send, cross_keep = call(
-        half_body,
-        [((rank, 2 * cols), BF), (wide, f32)],
-        pair_keep,
-        pair_in,
-        next_keep,
-        micros=5,
-    )
-    cross_in = swap(cross_send, "leaf", 3)
-
-    def turn_body(gram, far, caps, seen, out):
-        whole = (gram[...] + far[:, span(1)]).astype(BF)
-        out[...] = dot(whole, caps[...]).astype(BF)
-
-    (turn,) = call(
-        turn_body, [(top_caps.shape, BF)], gram_pair, next_far, top_caps, cross_send, micros=0.1
-    )
-    turn_far = swap(turn, "top", 2)
-    turn_near = swap(turn, "top", 1)
-    def late_body(lb, rb, caps, tl, tr, seen, seen2, out):
+    def late_body(lb, rb, caps, tl, tr, seen, out):
         for i, basis in enumerate((tl[0], tr[0])):
             out[:, span(i)] = (dot_t(lb[0, 0], basis) * s1).astype(BF)
             out[:, span(4 + i)] = (dot_t(lb[1, 0], basis) * s2).astype(BF)
@@ -300,12 +276,36 @@
         caps,
         tl,
         tr,
-        cross_send,
-        next_far,
+        next_send,
+        micros=0.5,
+    )
+
+    def half_body(keep, pair, nexts, seen, send, keep2):
+        send[:, :cols] = (keep[:, :cols] + pair[:, :cols]).astype(BF)
+        keep2[...] = keep[:, cols:] + pair[:, cols:] - dot(nexts[:, span(0)], send[:, :cols])
+        send[:, cols:] = keep2[...].astype(BF)
+
+    cross_send, cross_keep = call(
+        half_body,
+        [((rank, 2 * cols), BF), (wide, f32)],
+        pair_keep,
+        pair_in,
+        next_keep,
+        late,
         micros=5,
     )
-
-    late_sib = swap(late, "leaf", 1)
+    cross_in = swap(cross_send, "leaf", 3)
+
+    def turn_body(gram, far, caps, seen, out):
+        whole = (gram[...] + far[:, span(1)]).astype(BF)
+        out[...] = dot(whole, caps[...]).astype(BF)
+
+    (turn,) = call(
+        turn_body, [(top_caps.shape, BF)], gram_pair, next_far, top_caps, cross_send, micros=5
+    )
+    turn_far = swap(turn, "top", 2)
+    turn_near = swap(turn, "top", 1)
+    late_sib = swap(after(late, cross_send), "leaf", 1)
 
     def column_body(send, keep2, far, nexts, nexts_far, seen, out):
         out[...] = (
@@ -323,7 +323,7 @@
         cross_in,
         next_keep,
         next_far,
-        late,
+        turn,
         micros=0.2,
     )
     top_far = swap(top_send, "top", 2)

time: 42.9 us -> 43.5 us (1.014)
  waiting for transfers between devices: 9.58 us -> 13.1 us
  starting transfers between devices: 24 us -> 21.1 us
    ppermute x16, waiting for transfers between devices: 9.58 us -> 13.1 us  [swap(): return lax.ppermute(value, axis, pairs)]
    ppermute x16, starting transfers between devices: 24 us -> 21.1 us  [swap(): return lax.ppermute(value, axis, pairs)]
where the time goes in v14:
time: 43.5 us; the launch traced here: 43.4 us
  starting transfers between devices  21.1 us (49%)
  waiting for transfers between devices  13.1 us (30%)
  Pallas kernels  8.98 us (21%)
    ppermute x16, starting transfers between devices, swap(): return lax.ppermute(value, axis, pairs)  21.1 us
    ppermute x16, waiting for transfers between devices, swap(): return lax.ppermute(value, axis, pairs)  13.1 us
    pallas_call x15, Pallas kernels, call(): pl.pallas_call(body, out_shape=[jax.ShapeDtypeStruct(shape, dtype) if hbm...  8.98 us
  transfers between devices with their start and end apart: 16, of which 7 were waited for; matrix products, arithmetic and copies ran while one was open for 0% of the time, Pallas kernels for 12%

profile of v14, /device:TPU:0, one launch (start us, length us, event | category | flops | bytes accessed | tf_op | source)
XLA Modules:
  0.0 43.4 jit_solution(8204287695001356381)
XLA Ops:
  0.0 2.4 %shard_map.82 = (f32[640,256]{1,0:T(8,128)S(1)}, bf16[128,256]{1,0:T(8,128)(2,1)S(1)}, bf16[640,640]{1,0:T(8,128)(2,1)S(1)}, bf16[2,1,640,128]{3,2,1,0:T(8,128)(...) custom-call(f32[1,640,256]{2,1,0:T(8,128)} %rhs_hbm.1, ...), custom_call_target="tpu_custom_call" | custom-call | flops 1000000000 | tf_op jit(solution)/shard_map/pallas_call | solution.py:88
  2.9 2.7 %collective-permute-start = (bf16[128,256]{1,0:T(8,128)(2,1)S(1)}, bf16[128,256]{1,0:T(8,128)(2,1)S(1)}, u32[]{:S(2)}, u32[]{:S(2)}) collective-permute-start(bf16[128,256]{1,0:T(8,128)(2,1)S(1)} %get-tuple-element.38.p), channel_id=1, source_target_pairs={{0,4},{4,0},{8,12},{12,8},{1,5},{5,1},{9,13},{13,9},{2,6},{6,2},{1... | collective-permute-start | bytes 196616 | tf_op jit(solution)/shard_map/ppermute | solution.py:17
  5.5 0.6 %shard_map.83 = (bf16[128,384]{1,0:T(8,128)(2,1)S(1)}, bf16[128,256]{1,0:T(8,128)(2,1)S(1)}) custom-call(bf16[2,1,640,128]{3,2,1,0:T(8,128)(2,1)S(1)} %get-tuple-element.39.lb, bf16[2,1,128,256]{3,2,1,0:T(8,128)(2,1)S(1)} %get-tuple-element.41.caps, bf16[1,640,128]{2,1,0:T(8,128)(2,1)S(1)} %get-tuple-element.42.tl, ...), custom_call_target="tpu_custom_call" | custom-call | flops 10000000000 | tf_op jit(solution)/shard_map/pallas_call | solution.py:88
  6.1 1.2 %collective-permute-start.3 = (bf16[128,384]{1,0:T(8,128)(2,1)S(1)}, bf16[128,384]{1,0:T(8,128)(2,1)S(1)}, u32[]{:S(2)}, u32[]{:S(2)}) collective-permute-start(bf16[128,384]{1,0:T(8,128)(2,1)S(1)} %get-tuple-element.44.seen.own), channel_id=1, source_target_pairs={{0,4},{4,0},{8,12},{12,8},{1,5},{5,1},{9,13},{13,9},{2,6},{6,2},{1... | collective-permute-start | bytes 294920 | tf_op jit(solution)/shard_map/ppermute | solution.py:17
  7.4 0.9 %collective-permute-done.p_sib = bf16[128,256]{1,0:T(8,128)(2,1)S(1)} collective-permute-done((bf16[128,256]{1,0:T(8,128)(2,1)S(1)}, bf16[128,256]{1,0:T(8,128)(2,1)S(1)}, u32[]{:S(2)}, u32[]{:S(2)}) %collective-permute-start) | collective-permute-done | bytes 65568 | tf_op jit(solution)/shard_map/ppermute | solution.py:17
  8.2 0.8 %shard_map.84 = (f32[640,256]{1,0:T(8,128)S(1)}, bf16[128,512]{1,0:T(8,128)(2,1)S(1)}, f32[128,512]{1,0:T(8,128)S(1)}) custom-call(f32[640,256]{1,0:T(8,128)S(1)} %get-tuple-element.37.x0, bf16[128,256]{1,0:T(8,128)(2,1)S(1)} %get-tuple-element.38.p, bf16[128,256]{1,0:T(8,128)(2,1)S(1)} %collective-permute-done.p_sib, ...), custom_call_target="tpu_custom_call" | custom-call | flops 3000000000 | tf_op jit(solution)/shard_map/pallas_call | solution.py:88
  9.0 1.8 %collective-permute-start.2 = (bf16[128,512]{1,0:T(8,128)(2,1)S(1)}, bf16[128,512]{1,0:T(8,128)(2,1)S(1)}, u32[]{:S(2)}, u32[]{:S(2)}) collective-permute-start(bf16[128,512]{1,0:T(8,128)(2,1)S(1)} %get-tuple-element.47), channel_id=1, source_target_pairs={{0,4},{4,0},{8,12},{12,8},{1,5},{5,1},{9,13},{13,9},{2,6},{6,2},{1... | collective-permute-start | bytes 393224 | tf_op jit(solution)/shard_map/ppermute | solution.py:17
  11.1 3.3 %collective-permute-start.5 = (bf16[128,256]{1,0:T(8,128)(2,1)S(1)}, bf16[128,256]{1,0:T(8,128)(2,1)S(1)}, u32[]{:S(2)}, u32[]{:S(2)}) collective-permute-start(bf16[128,256]{1,0:T(8,128)(2,1)S(1)} %get-tuple-element.50.seen), channel_id=1, source_target_pairs={{0,12},{4,8},{8,4},{12,0},{1,13},{5,9},{9,5},{13,1},{2,14},{6,10},... | collective-permute-start | bytes 196616 | tf_op jit(solution)/shard_map/ppermute | solution.py:17
  14.4 0.5 %shard_map.86.seen.late = bf16[128,768]{1,0:T(8,128)(2,1)S(1)} custom-call(bf16[2,1,640,128]{3,2,1,0:T(8,128)(2,1)S(1)} %get-tuple-element.39.lb, bf16[2,1,640,128]{3,2,1,0:T(8,128)(2,1)S(1)} %get-tuple-element.40.rb, bf16[2,1,128,256]{3,2,1,0:T(8,128)(2,1)S(1)} %get-tuple-element.41.caps, bf16[1,640,128]{2,1,0:T(8,128)(2,1)S(1)} %get-tuple-element.42.tl, ...), custom_call_target="tpu_custom_call" | custom-call | flops 500000000 | tf_op jit(solution)/shard_map/pallas_call | solution.py:88
  15.1 3.1 %collective-permute-start.4 = (bf16[128,512]{1,0:T(8,128)(2,1)S(1)}, bf16[128,512]{1,0:T(8,128)(2,1)S(1)}, u32[]{:S(2)}, u32[]{:S(2)}) collective-permute-start(bf16[128,512]{1,0:T(8,128)(2,1)S(1)} %get-tuple-element.51.seen.send), channel_id=1, source_target_pairs={{0,12},{4,8},{8,4},{12,0},{1,13},{5,9},{9,5},{13,1},{2,14},{6,10},... | collective-permute-start | bytes 393224 | tf_op jit(solution)/shard_map/ppermute | solution.py:17
  18.6 1.6 %collective-permute-start.11 = (bf16[128,512]{1,0:T(8,128)(2,1)S(1)}, bf16[128,512]{1,0:T(8,128)(2,1)S(1)}, u32[]{:S(2)}, u32[]{:S(2)}) collective-permute-start(bf16[128,512]{1,0:T(8,128)(2,1)S(1)} %shard_map.88.seen.a), channel_id=1, source_target_pairs={{0,2},{1,3},{2,0},{3,1},{4,6},{5,7},{6,4},{7,5},{8,10},{9,11},{10,... | collective-permute-start | bytes 393224 | tf_op jit(solution)/shard_map/ppermute | solution.py:17
  20.2 3.2 %collective-permute-done.4.far = bf16[128,512]{1,0:T(8,128)(2,1)S(1)} collective-permute-done((bf16[128,512]{1,0:T(8,128)(2,1)S(1)}, bf16[128,512]{1,0:T(8,128)(2,1)S(1)}, u32[]{:S(2)}, u32[]{:S(2)}) %collective-permute-start.4) | collective-permute-done | bytes 131104 | tf_op jit(solution)/shard_map/ppermute | solution.py:17
  23.5 1.6 %collective-permute-start.8 = (bf16[128,256]{1,0:T(8,128)(2,1)S(1)}, bf16[128,256]{1,0:T(8,128)(2,1)S(1)}, u32[]{:S(2)}, u32[]{:S(2)}) collective-permute-start(bf16[128,256]{1,0:T(8,128)(2,1)S(1)} %shard_map.89.seen.a), channel_id=1, source_target_pairs={{0,2},{1,3},{2,0},{3,1},{4,6},{5,7},{6,4},{7,5},{8,10},{9,11},{10,... | collective-permute-start | bytes 196616 | tf_op jit(solution)/shard_map/ppermute | solution.py:17
  25.1 0.7 %shard_map.90 = (bf16[640,256]{1,0:T(8,128)(2,1)S(1)}, f32[128,256]{1,0:T(8,128)S(1)}, bf16[128,512]{1,0:T(8,128)(2,1)S(1)}) custom-call(f32[640,256]{1,0:T(8,128)S(1)} %get-tuple-element.45.seen.x1, bf16[128,512]{1,0:T(8,128)(2,1)S(1)} %get-tuple-element.51.seen.send, bf16[128,512]{1,0:T(8,128)(2,1)S(1)} %collective-permute-done.4.far, ...), custom_call_target="tpu_custom_call" | custom-call | flops 100000000 | tf_op jit(solution)/shard_map/pallas_call | solution.py:88
  25.9 0.6 %collective-permute-start.7 = (bf16[128,256]{1,0:T(8,128)(2,1)S(1)}, bf16[128,256]{1,0:T(8,128)(2,1)S(1)}, u32[]{:S(2)}, u32[]{:S(2)}) collective-permute-start(bf16[128,256]{1,0:T(8,128)(2,1)S(1)} %shard_map.89.seen.a), channel_id=1, source_target_pairs={{0,1},{1,0},{2,3},{3,2},{4,5},{5,4},{6,7},{7,6},{8,9},{9,8},{10,11... | collective-permute-start | bytes 196616 | tf_op jit(solution)/shard_map/ppermute | solution.py:17
  26.8 1.1 %collective-permute-done.8.c = bf16[128,256]{1,0:T(8,128)(2,1)S(1)} collective-permute-done((bf16[128,256]{1,0:T(8,128)(2,1)S(1)}, bf16[128,256]{1,0:T(8,128)(2,1)S(1)}, u32[]{:S(2)}, u32[]{:S(2)}) %collective-permute-start.8) | collective-permute-done | bytes 65568 | tf_op jit(solution)/shard_map/ppermute | solution.py:17
  28.4 0.9 %shard_map.91 = (f32[640,256]{1,0:T(8,128)S(1)}, bf16[640,512]{1,0:T(8,128)(2,1)S(1)}) custom-call(bf16[640,256]{1,0:T(8,128)(2,1)S(1)} %get-tuple-element.54.x2, bf16[2,1,640,128]{3,2,1,0:T(8,128)(2,1)S(1)} %get-tuple-element.40.rb, bf16[1,640,128]{2,1,0:T(8,128)(2,1)S(1)} %get-tuple-element.42.tl, bf16[1,640,128]{2,1,0:T(8,128)(2,1)S(1)} %get-tuple-element.43.tr, ...), custom_call_target="tpu_custom_call" | custom-call | flops 3000000000 | tf_op jit(solution)/shard_map/pallas_call | solution.py:88
  29.4 0.5 %shard_map.93.back = bf16[128,512]{1,0:T(8,128)(2,1)S(1)} custom-call(bf16[128,256]{1,0:T(8,128)(2,1)S(1)} %shard_map.89.seen.a, bf16[128,256]{1,0:T(8,128)(2,1)S(1)} %collective-permute-done.7.b, bf16[128,256]{1,0:T(8,128)(2,1)S(1)} %collective-permute-done.8.c, bf16[128,256]{1,0:T(8,128)(2,1)S(1)} %collective-permute-done.9.d, ...), custom_call_target="tpu_custom_call" | custom-call | flops 1000000000 | tf_op jit(solution)/shard_map/pallas_call | solution.py:88
  30.0 0.6 %collective-permute-start.13 = (bf16[128,512]{1,0:T(8,128)(2,1)S(1)}, bf16[128,512]{1,0:T(8,128)(2,1)S(1)}, u32[]{:S(2)}, u32[]{:S(2)}) collective-permute-start(bf16[128,512]{1,0:T(8,128)(2,1)S(1)} %shard_map.93.back), channel_id=1, source_target_pairs={{0,4},{4,0},{8,12},{12,8},{1,5},{5,1},{9,13},{13,9},{2,6},{6,2},{1... | collective-permute-start | bytes 393224 | tf_op jit(solution)/shard_map/ppermute | solution.py:17
  30.6 1.3 %collective-permute-done.14.z_sib = bf16[128,512]{1,0:T(8,128)(2,1)S(1)} collective-permute-done((bf16[128,512]{1,0:T(8,128)(2,1)S(1)}, bf16[128,512]{1,0:T(8,128)(2,1)S(1)}, u32[]{:S(2)}, u32[]{:S(2)}) %collective-permute-start.14) | collective-permute-done | bytes 131104 | tf_op jit(solution)/shard_map/ppermute | solution.py:17
  31.9 3.7 %collective-permute-done.13.back_sib = bf16[128,512]{1,0:T(8,128)(2,1)S(1)} collective-permute-done((bf16[128,512]{1,0:T(8,128)(2,1)S(1)}, bf16[128,512]{1,0:T(8,128)(2,1)S(1)}, u32[]{:S(2)}, u32[]{:S(2)}) %collective-permute-start.13) | collective-permute-done | bytes 131104 | tf_op jit(solution)/shard_map/ppermute | solution.py:17
  35.8 3.1 %collective-permute-start.15 = (bf16[128,256]{1,0:T(8,128)(2,1)S(1)}, bf16[128,256]{1,0:T(8,128)(2,1)S(1)}, u32[]{:S(2)}, u32[]{:S(2)}) collective-permute-start(bf16[128,256]{1,0:T(8,128)(2,1)S(1)} %get-tuple-element.66.seen.half5), channel_id=1, source_target_pairs={{0,12},{4,8},{8,4},{12,0},{1,13},{5,9},{9,5},{13,1},{2,14},{6,10},... | collective-permute-start | bytes 196616 | tf_op jit(solution)/shard_map/ppermute | solution.py:17
  39.2 2.7 %collective-permute-done.15.half5_far = bf16[128,256]{1,0:T(8,128)(2,1)S(1)} collective-permute-done((bf16[128,256]{1,0:T(8,128)(2,1)S(1)}, bf16[128,256]{1,0:T(8,128)(2,1)S(1)}, u32[]{:S(2)}, u32[]{:S(2)}) %collective-permute-start.15) | collective-permute-done | bytes 65568 | tf_op jit(solution)/shard_map/ppermute | solution.py:17
  42.0 1.4 %shard_map.96 = f32[1,640,256]{2,1,0:T(8,128)} custom-call(f32[640,256]{1,0:T(8,128)S(1)} %get-tuple-element.67.out3, bf16[640,512]{1,0:T(8,128)(2,1)S(1)} %get-tuple-element.58.under, bf16[128,256]{1,0:T(8,128)(2,1)S(1)} %get-tuple-element.66.seen.half5, bf16[128,256]{1,0:T(8,128)(2,1)S(1)} %collective-permute-done.15.half5_far, ...), custom_call_target="tpu_custom_call" | custom-call | flops 1000000000 | tf_op jit(solution)/shard_map/pallas_call | solution.py:88
  (25 shorter events, 3.0 us)
Async XLA Ops:
  2.4 3.2 %collective-permute-start.1 = (bf16[128,256]{1,0:T(8,128)(2,1)S(1)}, bf16[128,256]{1,0:T(8,128)(2,1)S(1)}, u32[]{:S(2)}, u32[]{:S(2)}) collective-permute-start(bf16[128,256]{1,0:T(8,128)(2,1)S(1)} %get-tuple-element.38.p), channel_id=1, source_target_pairs={{0,1},{1,0},{2,3},{3,2},{4,5},{5,4},{6,7},{7,6},{8,9},{9,8},{10,11... | collective-permute-start | bytes 196616 | tf_op jit(solution)/shard_map/ppermute | solution.py:17
  2.9 5.3 %collective-permute-start = (bf16[128,256]{1,0:T(8,128)(2,1)S(1)}, bf16[128,256]{1,0:T(8,128)(2,1)S(1)}, u32[]{:S(2)}, u32[]{:S(2)}) collective-permute-start(bf16[128,256]{1,0:T(8,128)(2,1)S(1)} %get-tuple-element.38.p), channel_id=1, source_target_pairs={{0,4},{4,0},{8,12},{12,8},{1,5},{5,1},{9,13},{13,9},{2,6},{6,2},{1... | collective-permute-start | bytes 196616 | tf_op jit(solution)/shard_map/ppermute | solution.py:17
  6.1 4.9 %collective-permute-start.3 = (bf16[128,384]{1,0:T(8,128)(2,1)S(1)}, bf16[128,384]{1,0:T(8,128)(2,1)S(1)}, u32[]{:S(2)}, u32[]{:S(2)}) collective-permute-start(bf16[128,384]{1,0:T(8,128)(2,1)S(1)} %get-tuple-element.44.seen.own), channel_id=1, source_target_pairs={{0,4},{4,0},{8,12},{12,8},{1,5},{5,1},{9,13},{13,9},{2,6},{6,2},{1... | collective-permute-start | bytes 294920 | tf_op jit(solution)/shard_map/ppermute | solution.py:17
  9.0 5.8 %collective-permute-start.2 = (bf16[128,512]{1,0:T(8,128)(2,1)S(1)}, bf16[128,512]{1,0:T(8,128)(2,1)S(1)}, u32[]{:S(2)}, u32[]{:S(2)}) collective-permute-start(bf16[128,512]{1,0:T(8,128)(2,1)S(1)} %get-tuple-element.47), channel_id=1, source_target_pairs={{0,4},{4,0},{8,12},{12,8},{1,5},{5,1},{9,13},{13,9},{2,6},{6,2},{1... | collective-permute-start | bytes 393224 | tf_op jit(solution)/shard_map/ppermute | solution.py:17
  11.1 7.3 %collective-permute-start.5 = (bf16[128,256]{1,0:T(8,128)(2,1)S(1)}, bf16[128,256]{1,0:T(8,128)(2,1)S(1)}, u32[]{:S(2)}, u32[]{:S(2)}) collective-permute-start(bf16[128,256]{1,0:T(8,128)(2,1)S(1)} %get-tuple-element.50.seen), channel_id=1, source_target_pairs={{0,12},{4,8},{8,4},{12,0},{1,13},{5,9},{9,5},{13,1},{2,14},{6,10},... | collective-permute-start | bytes 196616 | tf_op jit(solution)/shard_map/ppermute | solution.py:17
  14.9 3.5 %copy-start = (bf16[128,512]{1,0:T(8,128)(2,1)S(1)}, bf16[128,512]{1,0:T(8,128)(2,1)}, u32[]{:S(2)}) copy-start(bf16[128,512]{1,0:T(8,128)(2,1)} %caps.3) | copy-start | bytes 393220
  15.1 8.3 %collective-permute-start.4 = (bf16[128,512]{1,0:T(8,128)(2,1)S(1)}, bf16[128,512]{1,0:T(8,128)(2,1)S(1)}, u32[]{:S(2)}, u32[]{:S(2)}) collective-permute-start(bf16[128,512]{1,0:T(8,128)(2,1)S(1)} %get-tuple-element.51.seen.send), channel_id=1, source_target_pairs={{0,12},{4,8},{8,4},{12,0},{1,13},{5,9},{9,5},{13,1},{2,14},{6,10},... | collective-permute-start | bytes 393224 | tf_op jit(solution)/shard_map/ppermute | solution.py:17
  18.2 9.7 %collective-permute-start.6 = (bf16[128,768]{1,0:T(8,128)(2,1)S(1)}, bf16[128,768]{1,0:T(8,128)(2,1)S(1)}, u32[]{:S(2)}, u32[]{:S(2)}) collective-permute-start(bf16[128,768]{1,0:T(8,128)(2,1)S(1)} %shard_map.86.seen.late), channel_id=1, source_target_pairs={{0,4},{4,0},{8,12},{12,8},{1,5},{5,1},{9,13},{13,9},{2,6},{6,2},{1... | collective-permute-start | bytes 589832 | tf_op jit(solution)/shard_map/ppermute | solution.py:17
  18.6 7.8 %collective-permute-start.11 = (bf16[128,512]{1,0:T(8,128)(2,1)S(1)}, bf16[128,512]{1,0:T(8,128)(2,1)S(1)}, u32[]{:S(2)}, u32[]{:S(2)}) collective-permute-start(bf16[128,512]{1,0:T(8,128)(2,1)S(1)} %shard_map.88.seen.a), channel_id=1, source_target_pairs={{0,2},{1,3},{2,0},{3,1},{4,6},{5,7},{6,4},{7,5},{8,10},{9,11},{10,... | collective-permute-start | bytes 393224 | tf_op jit(solution)/shard_map/ppermute | solution.py:17
  23.5 4.3 %collective-permute-start.8 = (bf16[128,256]{1,0:T(8,128)(2,1)S(1)}, bf16[128,256]{1,0:T(8,128)(2,1)S(1)}, u32[]{:S(2)}, u32[]{:S(2)}) collective-permute-start(bf16[128,256]{1,0:T(8,128)(2,1)S(1)} %shard_map.89.seen.a), channel_id=1, source_target_pairs={{0,2},{1,3},{2,0},{3,1},{4,6},{5,7},{6,4},{7,5},{8,10},{9,11},{10,... | collective-permute-start | bytes 196616 | tf_op jit(solution)/shard_map/ppermute | solution.py:17
  25.1 4.2 %collective-permute-start.10 = (bf16[128,512]{1,0:T(8,128)(2,1)S(1)}, bf16[128,512]{1,0:T(8,128)(2,1)S(1)}, u32[]{:S(2)}, u32[]{:S(2)}) collective-permute-start(bf16[128,512]{1,0:T(8,128)(2,1)S(1)} %shard_map.88.seen.a), channel_id=1, source_target_pairs={{0,1},{1,0},{2,3},{3,2},{4,5},{5,4},{6,7},{7,6},{8,9},{9,8},{10,11... | collective-permute-start | bytes 393224 | tf_op jit(solution)/shard_map/ppermute | solution.py:17
  25.9 3.6 %collective-permute-start.7 = (bf16[128,256]{1,0:T(8,128)(2,1)S(1)}, bf16[128,256]{1,0:T(8,128)(2,1)S(1)}, u32[]{:S(2)}, u32[]{:S(2)}) collective-permute-start(bf16[128,256]{1,0:T(8,128)(2,1)S(1)} %shard_map.89.seen.a), channel_id=1, source_target_pairs={{0,1},{1,0},{2,3},{3,2},{4,5},{5,4},{6,7},{7,6},{8,9},{9,8},{10,11... | collective-permute-start | bytes 196616 | tf_op jit(solution)/shard_map/ppermute | solution.py:17
  26.4 5.5 %collective-permute-start.14 = (bf16[128,512]{1,0:T(8,128)(2,1)S(1)}, bf16[128,512]{1,0:T(8,128)(2,1)S(1)}, u32[]{:S(2)}, u32[]{:S(2)}) collective-permute-start(bf16[128,512]{1,0:T(8,128)(2,1)S(1)} %get-tuple-element.64.z), channel_id=1, source_target_pairs={{0,4},{4,0},{8,12},{12,8},{1,5},{5,1},{9,13},{13,9},{2,6},{6,2},{1... | collective-permute-start | bytes 393224 | tf_op jit(solution)/shard_map/ppermute | solution.py:17
  27.9 1.4 %collective-permute-start.12 = (bf16[128,512]{1,0:T(8,128)(2,1)S(1)}, bf16[128,512]{1,0:T(8,128)(2,1)S(1)}, u32[]{:S(2)}, u32[]{:S(2)}) collective-permute-start(bf16[128,512]{1,0:T(8,128)(2,1)S(1)} %collective-permute-done.11.c), channel_id=1, source_target_pairs={{0,1},{1,0},{2,3},{3,2},{4,5},{5,4},{6,7},{7,6},{8,9},{9,8},{10,11... | collective-permute-start | bytes 393224 | tf_op jit(solution)/shard_map/ppermute | solution.py:17
  27.9 1.5 %collective-permute-start.9 = (bf16[128,256]{1,0:T(8,128)(2,1)S(1)}, bf16[128,256]{1,0:T(8,128)(2,1)S(1)}, u32[]{:S(2)}, u32[]{:S(2)}) collective-permute-start(bf16[128,256]{1,0:T(8,128)(2,1)S(1)} %collective-permute-done.8.c), channel_id=1, source_target_pairs={{0,1},{1,0},{2,3},{3,2},{4,5},{5,4},{6,7},{7,6},{8,9},{9,8},{10,11... | collective-permute-start | bytes 196616 | tf_op jit(solution)/shard_map/ppermute | solution.py:17
  30.0 5.7 %collective-permute-start.13 = (bf16[128,512]{1,0:T(8,128)(2,1)S(1)}, bf16[128,512]{1,0:T(8,128)(2,1)S(1)}, u32[]{:S(2)}, u32[]{:S(2)}) collective-permute-start(bf16[128,512]{1,0:T(8,128)(2,1)S(1)} %shard_map.93.back), channel_id=1, source_target_pairs={{0,4},{4,0},{8,12},{12,8},{1,5},{5,1},{9,13},{13,9},{2,6},{6,2},{1... | collective-permute-start | bytes 393224 | tf_op jit(solution)/shard_map/ppermute | solution.py:17
  35.8 6.1 %collective-permute-start.15 = (bf16[128,256]{1,0:T(8,128)(2,1)S(1)}, bf16[128,256]{1,0:T(8,128)(2,1)S(1)}, u32[]{:S(2)}, u32[]{:S(2)}) collective-permute-start(bf16[128,256]{1,0:T(8,128)(2,1)S(1)} %get-tuple-element.66.seen.half5), channel_id=1, source_target_pairs={{0,12},{4,8},{8,4},{12,0},{1,13},{5,9},{9,5},{13,1},{2,14},{6,10},... | collective-permute-start | bytes 196616 | tf_op jit(solution)/shard_map/ppermute | solution.py:17

commit v15 on v13

--- a/solution.py
+++ b/solution.py
@@ -328,17 +328,17 @@
     )
     top_far = swap(top_send, "top", 2)
 
-    def two_body(x1, send, far, lb, caps, seen, x2, z5, z, stack):
+    def two_body(x1, send, far, lb, caps, seen, x2, z5, z5_b, z6, stack):
         put_rows(stack, tree_side(1), send[:, :cols], far[:, :cols])
         coef = dot(caps[1, 0], stack[...]).astype(BF)
         x2[...] = (x1[...] - dot(lb[1, 0], coef)).astype(BF)
         z5[...] = dot_t(lb[1, 0], x2[...]) * s2
-        z[:, :cols] = z5[...].astype(BF)
-        z[:, cols:] = (dot_t(lb[0, 0], x2[...]) * s1).astype(BF)
-
-    state2, down5, down_send = call(
+        z5_b[...] = z5[...].astype(BF)
+        z6[...] = (dot_t(lb[0, 0], x2[...]) * s1).astype(BF)
+
+    state2, down5, down5_send, down6 = call(
         two_body,
-        [(tall, BF), (wide, f32), ((rank, 2 * cols), BF)],
+        [(tall, BF), (wide, f32), (wide, BF), (wide, BF)],
         state1,
         cross_send,
         cross_in,
@@ -348,7 +348,7 @@
         scratch=[pltpu.VMEM((2 * rank, cols), BF)],
         micros=0.1,
     )
-    down_in = swap(down_send, "leaf", 1)
+    down_in = swap(down5_send, "leaf", 1)
     top_near = swap(after(top_send, state2), "top", 1)
     top_parts = top_send, top_near, top_far, swap(top_far, "top", 1)
 
@@ -391,7 +391,7 @@
         micros=3,
     )
 
-    def top_body(a, b, c, d, turns, row, seen, out, up):
+    def top_body(a, b, c, d, turns, row, seen, seen2, out, up):
         for i, piece in enumerate((a, b, c, d)):
             up[span(i), :] = piece[...]
         turned = dot(turns[...], up[...]).astype(BF)
@@ -405,6 +405,7 @@
         turn_all,
         caps_row,
         out2,
+        down_in,
         scratch=[pltpu.VMEM((4 * rank, cols), BF)],
         micros=1,
     )
@@ -417,7 +418,7 @@
         both[span(0), :] = pieces[0, :, :cols]
         both[span(1), :] = (pieces[1, :, :cols].astype(f32) - pieces[0, :, cols:]).astype(BF)
         gram = (late[:, span(4, 2)].astype(f32) + late_sib[:, span(4, 2)]).astype(BF)
-        send[...] = (down5[...] + z_sib[:, :cols] - dot(gram, both[...])).astype(BF)
+        send[...] = (down5[...] + z_sib[...] - dot(gram, both[...])).astype(BF)
 
     both, half5 = call(
         down_body,
@@ -431,13 +432,14 @@
         scratch=[pltpu.VMEM((2, rank, 2 * cols), BF)],
         micros=0.3,
     )
+    down6_sib = swap(after(down6, half5), "leaf", 1)
     half5_far = swap(half5, "leaf", 3)
 
-    def part_body(out2, under, both, z, z_sib, late, late_sib, seen, proj, out3):
-        def down(zs, gram):
-            return zs[:, cols:] - dot(gram[:, span(0, 2)], both[...])
-
-        put_rows(proj, tree_side(0), down(z, late), down(z_sib, late_sib))
+    def part_body(out2, under, both, late, late_sib, seen, proj, out3):
+        def down(gram):
+            return dot(gram[:, span(0, 2)], both[...])
+
+        put_rows(proj, tree_side(0), down(late), down(late_sib))
         out3[...] = out2[...] - dot(under[:, span(0, 2)], both[...])
 
     proj6, out3 = call(
@@ -446,8 +448,6 @@
         out2,
         under,
         both,
-        down_send,
-        down_in,
         late,
         late_sib,
         half5,
@@ -455,12 +455,13 @@
     )
 
     def last_body(
-        out3, under, half5, half5_far, late, late_sib, proj6, caps, out,
-        coefs, stack, grams, out_v, sems,
+        out3, under, half5, half5_far, late, late_sib, proj6, z, z_sib, caps, out,
+        coefs, stack, grams, zs, out_v, sems,
     ):
         put_rows(stack, tree_side(1), half5[...], half5_far[...])
         put_rows(grams, tree_side(0), late[:, span(2, 2)], late_sib[:, span(2, 2)])
-        proj = (proj6[...] - dot(grams[...], stack[...])).astype(BF)
+        put_rows(zs, tree_side(0), z[...], z_sib[...])
+        proj = (zs[...] - proj6[...] - dot(grams[...], stack[...])).astype(BF)
         coefs[span(0), :] = dot(caps[1, 0], stack[...]).astype(BF)
         coefs[span(1), :] = dot(caps[0, 0], proj).astype(BF)
         copies = []
@@ -482,12 +483,15 @@
         late,
         late_sib,
         proj6,
+        down6,
+        down6_sib,
         caps,
         hbm_out=True,
         scratch=[
             pltpu.VMEM((2 * rank, cols), BF),
             pltpu.VMEM((2 * rank, cols), BF),
             pltpu.VMEM((2 * rank, 2 * rank), BF),
+            pltpu.VMEM((2 * rank, cols), BF),
             pltpu.VMEM(tall, f32),
             pltpu.SemaphoreType.DMA((blocks,)),
         ],

time: 42.9 us -> 45.4 us (1.058)
  waiting for transfers between devices: 9.58 us -> 12.1 us
    ppermute x16 -> x17, waiting for transfers between devices: 9.58 us -> 12.1 us  [swap(): return lax.ppermute(value, axis, pairs)]
    ppermute x16 -> x17, starting transfers between devices: 24 us -> 24.1 us  [swap(): return lax.ppermute(value, axis, pairs)]
  transfers between devices with their start and end apart: 16 -> 17, of which waited for: 7 -> 8; matrix products, arithmetic and copies ran while one was open for 0% -> 0% of each run, Pallas kernels for 12% -> 10%
where the time goes in v15:
time: 45.4 us; the launch traced here: 45.3 us
  starting transfers between devices  24.1 us (53%)
  waiting for transfers between devices  12.1 us (27%)
  Pallas kernels  8.99 us (20%)
    ppermute x17, starting transfers between devices, swap(): return lax.ppermute(value, axis, pairs)  24.1 us
    ppermute x17, waiting for transfers between devices, swap(): return lax.ppermute(value, axis, pairs)  12.1 us
    pallas_call x15, Pallas kernels, call(): pl.pallas_call(body, out_shape=[jax.ShapeDtypeStruct(shape, dtype) if hbm...  8.99 us
  transfers between devices with their start and end apart: 17, of which 8 were waited for; matrix products, arithmetic and copies ran while one was open for 0% of the time, Pallas kernels for 10%

profile of v15, /device:TPU:0, one launch (start us, length us, event | category | flops | bytes accessed | tf_op | source)
XLA Modules:
  0.0 45.3 jit_solution(2989312712874929105)
XLA Ops:
  0.0 2.4 %shard_map.82 = (f32[640,256]{1,0:T(8,128)S(1)}, bf16[128,256]{1,0:T(8,128)(2,1)S(1)}, bf16[640,640]{1,0:T(8,128)(2,1)S(1)}, bf16[2,1,640,128]{3,2,1,0:T(8,128)(...) custom-call(f32[1,640,256]{2,1,0:T(8,128)} %rhs_hbm.1, ...), custom_call_target="tpu_custom_call" | custom-call | flops 1000000000 | tf_op jit(solution)/shard_map/pallas_call | solution.py:88
  2.9 2.7 %collective-permute-start = (bf16[128,256]{1,0:T(8,128)(2,1)S(1)}, bf16[128,256]{1,0:T(8,128)(2,1)S(1)}, u32[]{:S(2)}, u32[]{:S(2)}) collective-permute-start(bf16[128,256]{1,0:T(8,128)(2,1)S(1)} %get-tuple-element.39.p), channel_id=1, source_target_pairs={{0,4},{4,0},{8,12},{12,8},{1,5},{5,1},{9,13},{13,9},{2,6},{6,2},{1... | collective-permute-start | bytes 196616 | tf_op jit(solution)/shard_map/ppermute | solution.py:17
  5.5 0.6 %shard_map.83 = (bf16[128,384]{1,0:T(8,128)(2,1)S(1)}, bf16[128,256]{1,0:T(8,128)(2,1)S(1)}) custom-call(bf16[2,1,640,128]{3,2,1,0:T(8,128)(2,1)S(1)} %get-tuple-element.40.lb, bf16[2,1,128,256]{3,2,1,0:T(8,128)(2,1)S(1)} %get-tuple-element.42.caps, bf16[1,640,128]{2,1,0:T(8,128)(2,1)S(1)} %get-tuple-element.43.tl, ...), custom_call_target="tpu_custom_call" | custom-call | flops 10000000000 | tf_op jit(solution)/shard_map/pallas_call | solution.py:88
  6.1 1.2 %collective-permute-start.3 = (bf16[128,384]{1,0:T(8,128)(2,1)S(1)}, bf16[128,384]{1,0:T(8,128)(2,1)S(1)}, u32[]{:S(2)}, u32[]{:S(2)}) collective-permute-start(bf16[128,384]{1,0:T(8,128)(2,1)S(1)} %get-tuple-element.45.seen.own), channel_id=1, source_target_pairs={{0,4},{4,0},{8,12},{12,8},{1,5},{5,1},{9,13},{13,9},{2,6},{6,2},{1... | collective-permute-start | bytes 294920 | tf_op jit(solution)/shard_map/ppermute | solution.py:17
  7.4 0.9 %collective-permute-done.p_sib = bf16[128,256]{1,0:T(8,128)(2,1)S(1)} collective-permute-done((bf16[128,256]{1,0:T(8,128)(2,1)S(1)}, bf16[128,256]{1,0:T(8,128)(2,1)S(1)}, u32[]{:S(2)}, u32[]{:S(2)}) %collective-permute-start) | collective-permute-done | bytes 65568 | tf_op jit(solution)/shard_map/ppermute | solution.py:17
  8.2 0.8 %shard_map.84 = (f32[640,256]{1,0:T(8,128)S(1)}, bf16[128,512]{1,0:T(8,128)(2,1)S(1)}, f32[128,512]{1,0:T(8,128)S(1)}) custom-call(f32[640,256]{1,0:T(8,128)S(1)} %get-tuple-element.38.x0, bf16[128,256]{1,0:T(8,128)(2,1)S(1)} %get-tuple-element.39.p, bf16[128,256]{1,0:T(8,128)(2,1)S(1)} %collective-permute-done.p_sib, ...), custom_call_target="tpu_custom_call" | custom-call | flops 3000000000 | tf_op jit(solution)/shard_map/pallas_call | solution.py:88
  9.0 1.8 %collective-permute-start.2 = (bf16[128,512]{1,0:T(8,128)(2,1)S(1)}, bf16[128,512]{1,0:T(8,128)(2,1)S(1)}, u32[]{:S(2)}, u32[]{:S(2)}) collective-permute-start(bf16[128,512]{1,0:T(8,128)(2,1)S(1)} %get-tuple-element.48), channel_id=1, source_target_pairs={{0,4},{4,0},{8,12},{12,8},{1,5},{5,1},{9,13},{13,9},{2,6},{6,2},{1... | collective-permute-start | bytes 393224 | tf_op jit(solution)/shard_map/ppermute | solution.py:17
  11.1 3.3 %collective-permute-start.5 = (bf16[128,256]{1,0:T(8,128)(2,1)S(1)}, bf16[128,256]{1,0:T(8,128)(2,1)S(1)}, u32[]{:S(2)}, u32[]{:S(2)}) collective-permute-start(bf16[128,256]{1,0:T(8,128)(2,1)S(1)} %get-tuple-element.53), channel_id=1, source_target_pairs={{0,12},{4,8},{8,4},{12,0},{1,13},{5,9},{9,5},{13,1},{2,14},{6,10},... | collective-permute-start | bytes 196616 | tf_op jit(solution)/shard_map/ppermute | solution.py:17
  14.5 3.7 %collective-permute-start.4 = (bf16[128,512]{1,0:T(8,128)(2,1)S(1)}, bf16[128,512]{1,0:T(8,128)(2,1)S(1)}, u32[]{:S(2)}, u32[]{:S(2)}) collective-permute-start(bf16[128,512]{1,0:T(8,128)(2,1)S(1)} %get-tuple-element.51.seen.send), channel_id=1, source_target_pairs={{0,12},{4,8},{8,4},{12,0},{1,13},{5,9},{9,5},{13,1},{2,14},{6,10},... | collective-permute-start | bytes 393224 | tf_op jit(solution)/shard_map/ppermute | solution.py:17
  18.2 0.5 %shard_map.87.seen.late = bf16[128,768]{1,0:T(8,128)(2,1)S(1)} custom-call(bf16[2,1,640,128]{3,2,1,0:T(8,128)(2,1)S(1)} %get-tuple-element.40.lb, bf16[2,1,640,128]{3,2,1,0:T(8,128)(2,1)S(1)} %get-tuple-element.41.rb, bf16[2,1,128,256]{3,2,1,0:T(8,128)(2,1)S(1)} %get-tuple-element.42.caps, bf16[1,640,128]{2,1,0:T(8,128)(2,1)S(1)} %get-tuple-element.43.tl, ...), custom_call_target="tpu_custom_call" | custom-call | flops 5000000000 | tf_op jit(solution)/shard_map/pallas_call | solution.py:88
  19.2 1.6 %collective-permute-start.11 = (bf16[128,512]{1,0:T(8,128)(2,1)S(1)}, bf16[128,512]{1,0:T(8,128)(2,1)S(1)}, u32[]{:S(2)}, u32[]{:S(2)}) collective-permute-start(bf16[128,512]{1,0:T(8,128)(2,1)S(1)} %shard_map.91.a), channel_id=1, source_target_pairs={{0,2},{1,3},{2,0},{3,1},{4,6},{5,7},{6,4},{7,5},{8,10},{9,11},{10,... | collective-permute-start | bytes 393224 | tf_op jit(solution)/shard_map/ppermute | solution.py:17
  20.8 1.8 %collective-permute-done.4.far = bf16[128,512]{1,0:T(8,128)(2,1)S(1)} collective-permute-done((bf16[128,512]{1,0:T(8,128)(2,1)S(1)}, bf16[128,512]{1,0:T(8,128)(2,1)S(1)}, u32[]{:S(2)}, u32[]{:S(2)}) %collective-permute-start.4) | collective-permute-done | bytes 131104 | tf_op jit(solution)/shard_map/ppermute | solution.py:17
  22.8 1.5 %collective-permute-start.8 = (bf16[128,256]{1,0:T(8,128)(2,1)S(1)}, bf16[128,256]{1,0:T(8,128)(2,1)S(1)}, u32[]{:S(2)}, u32[]{:S(2)}) collective-permute-start(bf16[128,256]{1,0:T(8,128)(2,1)S(1)} %shard_map.88.seen.a), channel_id=1, source_target_pairs={{0,2},{1,3},{2,0},{3,1},{4,6},{5,7},{6,4},{7,5},{8,10},{9,11},{10,... | collective-permute-start | bytes 196616 | tf_op jit(solution)/shard_map/ppermute | solution.py:17
  24.3 0.7 %shard_map.89 = (bf16[640,256]{1,0:T(8,128)(2,1)S(1)}, f32[128,256]{1,0:T(8,128)S(1)}, bf16[128,256]{1,0:T(8,128)(2,1)S(1)}, bf16[128,256]{1,0:T(8,128)(2,1)S(1)}) custom-call(f32[640,256]{1,0:T(8,128)S(1)} %get-tuple-element.46.seen.x1, bf16[128,512]{1,0:T(8,128)(2,1)S(1)} %get-tuple-element.51.seen.send, bf16[128,512]{1,0:T(8,128)(2,1)S(1)} %collective-permute-done.4.far, ...), custom_call_target="tpu_custom_call" | custom-call | flops 100000000 | tf_op jit(solution)/shard_map/pallas_call | solution.py:88
  25.1 0.6 %collective-permute-start.7 = (bf16[128,256]{1,0:T(8,128)(2,1)S(1)}, bf16[128,256]{1,0:T(8,128)(2,1)S(1)}, u32[]{:S(2)}, u32[]{:S(2)}) collective-permute-start(bf16[128,256]{1,0:T(8,128)(2,1)S(1)} %shard_map.88.seen.a), channel_id=1, source_target_pairs={{0,1},{1,0},{2,3},{3,2},{4,5},{5,4},{6,7},{7,6},{8,9},{9,8},{10,11... | collective-permute-start | bytes 196616 | tf_op jit(solution)/shard_map/ppermute | solution.py:17
  25.7 1.2 %collective-permute-start.13 = (bf16[128,256]{1,0:T(8,128)(2,1)S(1)}, bf16[128,256]{1,0:T(8,128)(2,1)S(1)}, u32[]{:S(2)}, u32[]{:S(2)}) collective-permute-start(bf16[128,256]{1,0:T(8,128)(2,1)S(1)} %get-tuple-element.63), channel_id=1, source_target_pairs={{0,4},{4,0},{8,12},{12,8},{1,5},{5,1},{9,13},{13,9},{2,6},{6,2},{1... | collective-permute-start | bytes 196616 | tf_op jit(solution)/shard_map/ppermute | solution.py:17
  27.6 0.9 %shard_map.90 = (f32[640,256]{1,0:T(8,128)S(1)}, bf16[640,512]{1,0:T(8,128)(2,1)S(1)}) custom-call(bf16[640,256]{1,0:T(8,128)(2,1)S(1)} %get-tuple-element.54.x2, bf16[2,1,640,128]{3,2,1,0:T(8,128)(2,1)S(1)} %get-tuple-element.41.rb, bf16[1,640,128]{2,1,0:T(8,128)(2,1)S(1)} %get-tuple-element.43.tl, bf16[1,640,128]{2,1,0:T(8,128)(2,1)S(1)} %get-tuple-element.44.tr, ...), custom_call_target="tpu_custom_call" | custom-call | flops 3000000000 | tf_op jit(solution)/shard_map/pallas_call | solution.py:88
  28.7 1.3 %collective-permute-done.13.seen2.z_sib = bf16[128,256]{1,0:T(8,128)(2,1)S(1)} collective-permute-done((bf16[128,256]{1,0:T(8,128)(2,1)S(1)}, bf16[128,256]{1,0:T(8,128)(2,1)S(1)}, u32[]{:S(2)}, u32[]{:S(2)}) %collective-permute-start.13) | collective-permute-done | bytes 65568 | tf_op jit(solution)/shard_map/ppermute | solution.py:17
  30.5 1.3 %collective-permute-start.14 = (bf16[128,512]{1,0:T(8,128)(2,1)S(1)}, bf16[128,512]{1,0:T(8,128)(2,1)S(1)}, u32[]{:S(2)}, u32[]{:S(2)}) collective-permute-start(bf16[128,512]{1,0:T(8,128)(2,1)S(1)} %shard_map.93.back), channel_id=1, source_target_pairs={{0,4},{4,0},{8,12},{12,8},{1,5},{5,1},{9,13},{13,9},{2,6},{6,2},{1... | collective-permute-start | bytes 393224 | tf_op jit(solution)/shard_map/ppermute | solution.py:17
  31.8 3.7 %collective-permute-done.14.back_sib = bf16[128,512]{1,0:T(8,128)(2,1)S(1)} collective-permute-done((bf16[128,512]{1,0:T(8,128)(2,1)S(1)}, bf16[128,512]{1,0:T(8,128)(2,1)S(1)}, u32[]{:S(2)}, u32[]{:S(2)}) %collective-permute-start.14) | collective-permute-done | bytes 131104 | tf_op jit(solution)/shard_map/ppermute | solution.py:17
  35.7 3.9 %collective-permute-start.15 = (bf16[128,256]{1,0:T(8,128)(2,1)S(1)}, bf16[128,256]{1,0:T(8,128)(2,1)S(1)}, u32[]{:S(2)}, u32[]{:S(2)}) collective-permute-start(bf16[128,256]{1,0:T(8,128)(2,1)S(1)} %get-tuple-element.66.seen.half5), channel_id=1, source_target_pairs={{0,12},{4,8},{8,4},{12,0},{1,13},{5,9},{9,5},{13,1},{2,14},{6,10},... | collective-permute-start | bytes 196616 | tf_op jit(solution)/shard_map/ppermute | solution.py:17
  39.9 2.0 %collective-permute-done.15.half5_far = bf16[128,256]{1,0:T(8,128)(2,1)S(1)} collective-permute-done((bf16[128,256]{1,0:T(8,128)(2,1)S(1)}, bf16[128,256]{1,0:T(8,128)(2,1)S(1)}, u32[]{:S(2)}, u32[]{:S(2)}) %collective-permute-start.15) | collective-permute-done | bytes 65568 | tf_op jit(solution)/shard_map/ppermute | solution.py:17
  41.8 2.0 %collective-permute-done.16.z_sib = bf16[128,256]{1,0:T(8,128)(2,1)S(1)} collective-permute-done((bf16[128,256]{1,0:T(8,128)(2,1)S(1)}, bf16[128,256]{1,0:T(8,128)(2,1)S(1)}, u32[]{:S(2)}, u32[]{:S(2)}) %collective-permute-start.16) | collective-permute-done | bytes 65568 | tf_op jit(solution)/shard_map/ppermute | solution.py:17
  43.8 1.4 %shard_map.96 = f32[1,640,256]{2,1,0:T(8,128)} custom-call(f32[640,256]{1,0:T(8,128)S(1)} %get-tuple-element.67.out3, bf16[640,512]{1,0:T(8,128)(2,1)S(1)} %get-tuple-element.57.under, bf16[128,256]{1,0:T(8,128)(2,1)S(1)} %get-tuple-element.66.seen.half5, bf16[128,256]{1,0:T(8,128)(2,1)S(1)} %collective-permute-done.15.half5_far, ...), custom_call_target="tpu_custom_call" | custom-call | flops 1000000000 | tf_op jit(solution)/shard_map/pallas_call | solution.py:88
  (27 shorter events, 3.5 us)
Async XLA Ops:
  2.4 3.2 %collective-permute-start.1 = (bf16[128,256]{1,0:T(8,128)(2,1)S(1)}, bf16[128,256]{1,0:T(8,128)(2,1)S(1)}, u32[]{:S(2)}, u32[]{:S(2)}) collective-permute-start(bf16[128,256]{1,0:T(8,128)(2,1)S(1)} %get-tuple-element.39.p), channel_id=1, source_target_pairs={{0,1},{1,0},{2,3},{3,2},{4,5},{5,4},{6,7},{7,6},{8,9},{9,8},{10,11... | collective-permute-start | bytes 196616 | tf_op jit(solution)/shard_map/ppermute | solution.py:17
  2.9 5.3 %collective-permute-start = (bf16[128,256]{1,0:T(8,128)(2,1)S(1)}, bf16[128,256]{1,0:T(8,128)(2,1)S(1)}, u32[]{:S(2)}, u32[]{:S(2)}) collective-permute-start(bf16[128,256]{1,0:T(8,128)(2,1)S(1)} %get-tuple-element.39.p), channel_id=1, source_target_pairs={{0,4},{4,0},{8,12},{12,8},{1,5},{5,1},{9,13},{13,9},{2,6},{6,2},{1... | collective-permute-start | bytes 196616 | tf_op jit(solution)/shard_map/ppermute | solution.py:17
  6.1 4.9 %collective-permute-start.3 = (bf16[128,384]{1,0:T(8,128)(2,1)S(1)}, bf16[128,384]{1,0:T(8,128)(2,1)S(1)}, u32[]{:S(2)}, u32[]{:S(2)}) collective-permute-start(bf16[128,384]{1,0:T(8,128)(2,1)S(1)} %get-tuple-element.45.seen.own), channel_id=1, source_target_pairs={{0,4},{4,0},{8,12},{12,8},{1,5},{5,1},{9,13},{13,9},{2,6},{6,2},{1... | collective-permute-start | bytes 294920 | tf_op jit(solution)/shard_map/ppermute | solution.py:17
  9.0 5.3 %collective-permute-start.2 = (bf16[128,512]{1,0:T(8,128)(2,1)S(1)}, bf16[128,512]{1,0:T(8,128)(2,1)S(1)}, u32[]{:S(2)}, u32[]{:S(2)}) collective-permute-start(bf16[128,512]{1,0:T(8,128)(2,1)S(1)} %get-tuple-element.48), channel_id=1, source_target_pairs={{0,4},{4,0},{8,12},{12,8},{1,5},{5,1},{9,13},{13,9},{2,6},{6,2},{1... | collective-permute-start | bytes 393224 | tf_op jit(solution)/shard_map/ppermute | solution.py:17
  11.1 7.1 %collective-permute-start.5 = (bf16[128,256]{1,0:T(8,128)(2,1)S(1)}, bf16[128,256]{1,0:T(8,128)(2,1)S(1)}, u32[]{:S(2)}, u32[]{:S(2)}) collective-permute-start(bf16[128,256]{1,0:T(8,128)(2,1)S(1)} %get-tuple-element.53), channel_id=1, source_target_pairs={{0,12},{4,8},{8,4},{12,0},{1,13},{5,9},{9,5},{13,1},{2,14},{6,10},... | collective-permute-start | bytes 196616 | tf_op jit(solution)/shard_map/ppermute | solution.py:17
  14.5 4.5 %copy-start = (bf16[128,512]{1,0:T(8,128)(2,1)S(1)}, bf16[128,512]{1,0:T(8,128)(2,1)}, u32[]{:S(2)}) copy-start(bf16[128,512]{1,0:T(8,128)(2,1)} %caps.3) | copy-start | bytes 393220
  14.5 8.1 %collective-permute-start.4 = (bf16[128,512]{1,0:T(8,128)(2,1)S(1)}, bf16[128,512]{1,0:T(8,128)(2,1)S(1)}, u32[]{:S(2)}, u32[]{:S(2)}) collective-permute-start(bf16[128,512]{1,0:T(8,128)(2,1)S(1)} %get-tuple-element.51.seen.send), channel_id=1, source_target_pairs={{0,12},{4,8},{8,4},{12,0},{1,13},{5,9},{9,5},{13,1},{2,14},{6,10},... | collective-permute-start | bytes 393224 | tf_op jit(solution)/shard_map/ppermute | solution.py:17
  18.7 8.4 %collective-permute-start.6 = (bf16[128,768]{1,0:T(8,128)(2,1)S(1)}, bf16[128,768]{1,0:T(8,128)(2,1)S(1)}, u32[]{:S(2)}, u32[]{:S(2)}) collective-permute-start(bf16[128,768]{1,0:T(8,128)(2,1)S(1)} %shard_map.87.seen.late), channel_id=1, source_target_pairs={{0,4},{4,0},{8,12},{12,8},{1,5},{5,1},{9,13},{13,9},{2,6},{6,2},{1... | collective-permute-start | bytes 589832 | tf_op jit(solution)/shard_map/ppermute | solution.py:17
  19.2 6.4 %collective-permute-start.11 = (bf16[128,512]{1,0:T(8,128)(2,1)S(1)}, bf16[128,512]{1,0:T(8,128)(2,1)S(1)}, u32[]{:S(2)}, u32[]{:S(2)}) collective-permute-start(bf16[128,512]{1,0:T(8,128)(2,1)S(1)} %shard_map.91.a), channel_id=1, source_target_pairs={{0,2},{1,3},{2,0},{3,1},{4,6},{5,7},{6,4},{7,5},{8,10},{9,11},{10,... | collective-permute-start | bytes 393224 | tf_op jit(solution)/shard_map/ppermute | solution.py:17
  22.8 4.3 %collective-permute-start.8 = (bf16[128,256]{1,0:T(8,128)(2,1)S(1)}, bf16[128,256]{1,0:T(8,128)(2,1)S(1)}, u32[]{:S(2)}, u32[]{:S(2)}) collective-permute-start(bf16[128,256]{1,0:T(8,128)(2,1)S(1)} %shard_map.88.seen.a), channel_id=1, source_target_pairs={{0,2},{1,3},{2,0},{3,1},{4,6},{5,7},{6,4},{7,5},{8,10},{9,11},{10,... | collective-permute-start | bytes 196616 | tf_op jit(solution)/shard_map/ppermute | solution.py:17
  24.3 4.2 %collective-permute-start.10 = (bf16[128,512]{1,0:T(8,128)(2,1)S(1)}, bf16[128,512]{1,0:T(8,128)(2,1)S(1)}, u32[]{:S(2)}, u32[]{:S(2)}) collective-permute-start(bf16[128,512]{1,0:T(8,128)(2,1)S(1)} %shard_map.91.a), channel_id=1, source_target_pairs={{0,1},{1,0},{2,3},{3,2},{4,5},{5,4},{6,7},{7,6},{8,9},{9,8},{10,11... | collective-permute-start | bytes 393224 | tf_op jit(solution)/shard_map/ppermute | solution.py:17
  25.1 3.6 %collective-permute-start.7 = (bf16[128,256]{1,0:T(8,128)(2,1)S(1)}, bf16[128,256]{1,0:T(8,128)(2,1)S(1)}, u32[]{:S(2)}, u32[]{:S(2)}) collective-permute-start(bf16[128,256]{1,0:T(8,128)(2,1)S(1)} %shard_map.88.seen.a), channel_id=1, source_target_pairs={{0,1},{1,0},{2,3},{3,2},{4,5},{5,4},{6,7},{7,6},{8,9},{9,8},{10,11... | collective-permute-start | bytes 196616 | tf_op jit(solution)/shard_map/ppermute | solution.py:17
  25.7 4.3 %collective-permute-start.13 = (bf16[128,256]{1,0:T(8,128)(2,1)S(1)}, bf16[128,256]{1,0:T(8,128)(2,1)S(1)}, u32[]{:S(2)}, u32[]{:S(2)}) collective-permute-start(bf16[128,256]{1,0:T(8,128)(2,1)S(1)} %get-tuple-element.63), channel_id=1, source_target_pairs={{0,4},{4,0},{8,12},{12,8},{1,5},{5,1},{9,13},{13,9},{2,6},{6,2},{1... | collective-permute-start | bytes 196616 | tf_op jit(solution)/shard_map/ppermute | solution.py:17
  27.1 1.4 %collective-permute-start.12 = (bf16[128,512]{1,0:T(8,128)(2,1)S(1)}, bf16[128,512]{1,0:T(8,128)(2,1)S(1)}, u32[]{:S(2)}, u32[]{:S(2)}) collective-permute-start(bf16[128,512]{1,0:T(8,128)(2,1)S(1)} %collective-permute-done.11.c), channel_id=1, source_target_pairs={{0,1},{1,0},{2,3},{3,2},{4,5},{5,4},{6,7},{7,6},{8,9},{9,8},{10,11... | collective-permute-start | bytes 393224 | tf_op jit(solution)/shard_map/ppermute | solution.py:17
  27.1 2.8 %collective-permute-start.9 = (bf16[128,256]{1,0:T(8,128)(2,1)S(1)}, bf16[128,256]{1,0:T(8,128)(2,1)S(1)}, u32[]{:S(2)}, u32[]{:S(2)}) collective-permute-start(bf16[128,256]{1,0:T(8,128)(2,1)S(1)} %collective-permute-done.8.c), channel_id=1, source_target_pairs={{0,1},{1,0},{2,3},{3,2},{4,5},{5,4},{6,7},{7,6},{8,9},{9,8},{10,11... | collective-permute-start | bytes 196616 | tf_op jit(solution)/shard_map/ppermute | solution.py:17
  30.5 5.0 %collective-permute-start.14 = (bf16[128,512]{1,0:T(8,128)(2,1)S(1)}, bf16[128,512]{1,0:T(8,128)(2,1)S(1)}, u32[]{:S(2)}, u32[]{:S(2)}) collective-permute-start(bf16[128,512]{1,0:T(8,128)(2,1)S(1)} %shard_map.93.back), channel_id=1, source_target_pairs={{0,4},{4,0},{8,12},{12,8},{1,5},{5,1},{9,13},{13,9},{2,6},{6,2},{1... | collective-permute-start | bytes 393224 | tf_op jit(solution)/shard_map/ppermute | solution.py:17
  35.7 6.1 %collective-permute-start.15 = (bf16[128,256]{1,0:T(8,128)(2,1)S(1)}, bf16[128,256]{1,0:T(8,128)(2,1)S(1)}, u32[]{:S(2)}, u32[]{:S(2)}) collective-permute-start(bf16[128,256]{1,0:T(8,128)(2,1)S(1)} %get-tuple-element.66.seen.half5), channel_id=1, source_target_pairs={{0,12},{4,8},{8,4},{12,0},{1,13},{5,9},{9,5},{13,1},{2,14},{6,10},... | collective-permute-start | bytes 196616 | tf_op jit(solution)/shard_map/ppermute | solution.py:17
  39.6 4.3 %collective-permute-start.16 = (bf16[128,256]{1,0:T(8,128)(2,1)S(1)}, bf16[128,256]{1,0:T(8,128)(2,1)S(1)}, u32[]{:S(2)}, u32[]{:S(2)}) collective-permute-start(bf16[128,256]{1,0:T(8,128)(2,1)S(1)} %get-tuple-element.70.z), channel_id=1, source_target_pairs={{0,4},{4,0},{8,12},{12,8},{1,5},{5,1},{9,13},{13,9},{2,6},{6,2},{1... | collective-permute-start | bytes 196616 | tf_op jit(solution)/shard_map/ppermute | solution.py:17

commit v16 on v13

--- a/solution.py
+++ b/solution.py
@@ -141,13 +141,14 @@
 
     def start_body(
         rhs_hbm, inv_hbm, lb_hbm, rb_hbm, caps_hbm, tl_hbm, tr_hbm,
-        x_ref, send, inv_ref, lb, rb, caps, tl, tr, rhs_v, sems,
+        x_ref, send, inv_ref, lb, rb, caps, tl, tr, rhs_v, basis_t, sems,
     ):
         def load(source, target, *at):
             copy = pltpu.make_async_copy(source, target, sems.at[at])
             copy.start()
             return copy
 
+        first = load(rb_hbm.at[0], rb.at[0], 2, 0)
         copies = []
         for i in range(blocks):
             copies.append(load(rhs_hbm.at[0, span(i), :], rhs_v.at[span(i), :], 0, i))
@@ -159,17 +160,18 @@
                     i,
                 )
             )
-        pairs = ((rb_hbm, rb), (lb_hbm, lb), (tl_hbm, tl), (tr_hbm, tr), (caps_hbm, caps))
-        bases = [load(source, target, 2, i) for i, (source, target) in enumerate(pairs)]
+        pairs = (rb_hbm.at[1], rb.at[1]), (lb_hbm, lb), (tl_hbm, tl), (tr_hbm, tr), (caps_hbm, caps)
+        bases = [load(source, target, 2, 1 + i) for i, (source, target) in enumerate(pairs)]
+        first.wait()
+        basis_t[...] = rb[0, 0].T
         for i in range(blocks):
             copies[2 * i].wait()
             copies[2 * i + 1].wait()
             x_ref[span(i), :] = dot(
                 inv_ref[span(i), span(0, i + 1)], rhs_v[span(0, i + 1), :].astype(BF)
             )
-        bases[0].wait()
-        send[...] = (dot_t(rb[0, 0], x_ref[...].astype(BF)) * s1).astype(BF)
-        for copy in bases[1:]:
+        send[...] = (dot(basis_t[...], x_ref[...].astype(BF)) * s1).astype(BF)
+        for copy in bases:
             copy.wait()
 
     state0, proj1, inverse, lb, rb, caps, tl, tr = call(
@@ -184,7 +186,11 @@
         top_left,
         top_right,
         hbm=range(7),
-        scratch=[pltpu.VMEM(tall, f32), pltpu.SemaphoreType.DMA((3, max(blocks, 5)))],
+        scratch=[
+            pltpu.VMEM(tall, f32),
+            pltpu.VMEM((rank, rows), BF),
+            pltpu.SemaphoreType.DMA((3, max(blocks, 6))),
+        ],
     )
     proj1_sib = swap(proj1, "leaf", 1)
     proj1_near = swap(proj1, "top", 1)
@@ -211,18 +217,22 @@
     )
     early_sib = swap(early, "leaf", 1)
 
-    def one_body(x0, p, p_sib, lb, rb, caps, tl, tr, seen, x1, send, keep, stack, scratch):
+    def flip_body(rb, tl, tr, seen, out):
+        for i, basis in enumerate((rb[1, 0], tr[0], tl[0])):
+            out[span(i), :] = basis.T
+
+    (bases_t,) = call(flip_body, [((3 * rank, rows), BF)], rb, tl, tr, early, micros=0.2)
+
+    def one_body(x0, p, p_sib, lb, caps, bases_t, x1, send, keep, stack, seen):
         side = column_side()
         put_rows(stack, tree_side(0), p[...], p_sib[...])
         coef = dot(caps[0, 0], stack[...]).astype(BF)
         x1[...] = x0[...] - dot(lb[0, 0], coef)
-        state = x1[...].astype(BF)
-        keep[:, :cols] = dot_t(rb[1, 0], state) * s2
+        seen[...] = dot(bases_t[...], x1[...].astype(BF))
+        keep[:, :cols] = seen[span(0), :] * s2
         send[:, :cols] = keep[:, :cols].astype(BF)
-        for i, basis in enumerate((tr, tl)):
-            scratch[i] = dot_t(basis[0], state) * st
-        send[:, cols:] = scratch[1 - side].astype(BF)
-        keep[:, cols:] = scratch[side]
+        send[:, cols:] = (seen[block(2 - side, rank), :] * st).astype(BF)
+        keep[:, cols:] = seen[block(1 + side, rank), :] * st
 
     state1, pair_send, pair_keep = call(
         one_body,
@@ -231,12 +241,9 @@
         proj1,
         proj1_sib,
         lb,
-        rb,
         caps,
-        tl,
-        tr,
-        early,
-        scratch=[pltpu.VMEM((2 * rank, cols), BF), pltpu.VMEM((2, rank, cols), f32)],
+        bases_t,
+        scratch=[pltpu.VMEM((2 * rank, cols), BF), pltpu.VMEM((3 * rank, cols), f32)],
         micros=3,
     )
     pair_in = swap(pair_send, "leaf", 1)

time: 42.9 us -> 42.8 us (level)
    pallas_call x15 -> x16, Pallas kernels: 8.99 us -> 9.13 us  [call(): pl.pallas_call(body, out_shape=[jax.ShapeDtypeStruct(shape, dtype) if hbm...]
where the time goes in v16:
time: 42.8 us; the launch traced here: 42.7 us
  starting transfers between devices  23.8 us (56%)
  waiting for transfers between devices  9.61 us (22%)
  Pallas kernels  9.13 us (21%)
    ppermute x16, starting transfers between devices, swap(): return lax.ppermute(value, axis, pairs)  23.8 us
    ppermute x16, waiting for transfers between devices, swap(): return lax.ppermute(value, axis, pairs)  9.61 us
    pallas_call x16, Pallas kernels, call(): pl.pallas_call(body, out_shape=[jax.ShapeDtypeStruct(shape, dtype) if hbm...  9.13 us
  transfers between devices with their start and end apart: 16, of which 7 were waited for; matrix products, arithmetic and copies ran while one was open for 0% of the time, Pallas kernels for 12%

profile of v16, /device:TPU:0, one launch (start us, length us, event | category | flops | bytes accessed | tf_op | source)
XLA Modules:
  0.0 42.7 jit_solution(11551651869776898869)
XLA Ops:
  0.0 2.4 %shard_map.82 = (f32[640,256]{1,0:T(8,128)S(1)}, bf16[128,256]{1,0:T(8,128)(2,1)S(1)}, bf16[640,640]{1,0:T(8,128)(2,1)S(1)}, bf16[2,1,640,128]{3,2,1,0:T(8,128)(...) custom-call(f32[1,640,256]{2,1,0:T(8,128)} %rhs_hbm.1, ...), custom_call_target="tpu_custom_call" | custom-call | flops 1000000000 | tf_op jit(solution)/shard_map/pallas_call | solution.py:88
  2.9 2.7 %collective-permute-start = (bf16[128,256]{1,0:T(8,128)(2,1)S(1)}, bf16[128,256]{1,0:T(8,128)(2,1)S(1)}, u32[]{:S(2)}, u32[]{:S(2)}) collective-permute-start(bf16[128,256]{1,0:T(8,128)(2,1)S(1)} %get-tuple-element.37.p), channel_id=1, source_target_pairs={{0,4},{4,0},{8,12},{12,8},{1,5},{5,1},{9,13},{13,9},{2,6},{6,2},{1... | collective-permute-start | bytes 196616 | tf_op jit(solution)/shard_map/ppermute | solution.py:17
  5.6 0.6 %shard_map.83 = (bf16[128,384]{1,0:T(8,128)(2,1)S(1)}, bf16[128,256]{1,0:T(8,128)(2,1)S(1)}) custom-call(bf16[2,1,640,128]{3,2,1,0:T(8,128)(2,1)S(1)} %get-tuple-element.38.lb, bf16[2,1,128,256]{3,2,1,0:T(8,128)(2,1)S(1)} %get-tuple-element.39.caps, bf16[1,640,128]{2,1,0:T(8,128)(2,1)S(1)} %get-tuple-element.41.tl, ...), custom_call_target="tpu_custom_call" | custom-call | flops 10000000000 | tf_op jit(solution)/shard_map/pallas_call | solution.py:88
  6.1 1.2 %collective-permute-start.3 = (bf16[128,384]{1,0:T(8,128)(2,1)S(1)}, bf16[128,384]{1,0:T(8,128)(2,1)S(1)}, u32[]{:S(2)}, u32[]{:S(2)}) collective-permute-start(bf16[128,384]{1,0:T(8,128)(2,1)S(1)} %get-tuple-element.43.seen.own), channel_id=1, source_target_pairs={{0,4},{4,0},{8,12},{12,8},{1,5},{5,1},{9,13},{13,9},{2,6},{6,2},{1... | collective-permute-start | bytes 294920 | tf_op jit(solution)/shard_map/ppermute | solution.py:17
  7.6 0.7 %collective-permute-done.p_sib = bf16[128,256]{1,0:T(8,128)(2,1)S(1)} collective-permute-done((bf16[128,256]{1,0:T(8,128)(2,1)S(1)}, bf16[128,256]{1,0:T(8,128)(2,1)S(1)}, u32[]{:S(2)}, u32[]{:S(2)}) %collective-permute-start) | collective-permute-done | bytes 65568 | tf_op jit(solution)/shard_map/ppermute | solution.py:17
  8.3 0.8 %shard_map.85 = (f32[640,256]{1,0:T(8,128)S(1)}, bf16[128,512]{1,0:T(8,128)(2,1)S(1)}, f32[128,512]{1,0:T(8,128)S(1)}) custom-call(f32[640,256]{1,0:T(8,128)S(1)} %get-tuple-element.36.x0, bf16[128,256]{1,0:T(8,128)(2,1)S(1)} %get-tuple-element.37.p, bf16[128,256]{1,0:T(8,128)(2,1)S(1)} %collective-permute-done.p_sib, ...), custom_call_target="tpu_custom_call" | custom-call | flops 3000000000 | tf_op jit(solution)/shard_map/pallas_call | solution.py:88
  9.0 1.8 %collective-permute-start.2 = (bf16[128,512]{1,0:T(8,128)(2,1)S(1)}, bf16[128,512]{1,0:T(8,128)(2,1)S(1)}, u32[]{:S(2)}, u32[]{:S(2)}) collective-permute-start(bf16[128,512]{1,0:T(8,128)(2,1)S(1)} %get-tuple-element.46), channel_id=1, source_target_pairs={{0,4},{4,0},{8,12},{12,8},{1,5},{5,1},{9,13},{13,9},{2,6},{6,2},{1... | collective-permute-start | bytes 393224 | tf_op jit(solution)/shard_map/ppermute | solution.py:17
  11.1 3.3 %collective-permute-start.5 = (bf16[128,256]{1,0:T(8,128)(2,1)S(1)}, bf16[128,256]{1,0:T(8,128)(2,1)S(1)}, u32[]{:S(2)}, u32[]{:S(2)}) collective-permute-start(bf16[128,256]{1,0:T(8,128)(2,1)S(1)} %get-tuple-element.51), channel_id=1, source_target_pairs={{0,12},{4,8},{8,4},{12,0},{1,13},{5,9},{9,5},{13,1},{2,14},{6,10},... | collective-permute-start | bytes 196616 | tf_op jit(solution)/shard_map/ppermute | solution.py:17
  14.6 3.6 %collective-permute-start.4 = (bf16[128,512]{1,0:T(8,128)(2,1)S(1)}, bf16[128,512]{1,0:T(8,128)(2,1)S(1)}, u32[]{:S(2)}, u32[]{:S(2)}) collective-permute-start(bf16[128,512]{1,0:T(8,128)(2,1)S(1)} %get-tuple-element.49.seen.send), channel_id=1, source_target_pairs={{0,12},{4,8},{8,4},{12,0},{1,13},{5,9},{9,5},{13,1},{2,14},{6,10},... | collective-permute-start | bytes 393224 | tf_op jit(solution)/shard_map/ppermute | solution.py:17
  18.2 0.5 %shard_map.88.seen.late = bf16[128,768]{1,0:T(8,128)(2,1)S(1)} custom-call(bf16[2,1,640,128]{3,2,1,0:T(8,128)(2,1)S(1)} %get-tuple-element.38.lb, bf16[2,1,640,128]{3,2,1,0:T(8,128)(2,1)S(1)} %get-tuple-element.40.rb, bf16[2,1,128,256]{3,2,1,0:T(8,128)(2,1)S(1)} %get-tuple-element.39.caps, bf16[1,640,128]{2,1,0:T(8,128)(2,1)S(1)} %get-tuple-element.41.tl, ...), custom_call_target="tpu_custom_call" | custom-call | flops 5000000000 | tf_op jit(solution)/shard_map/pallas_call | solution.py:88
  19.2 1.6 %collective-permute-start.11 = (bf16[128,512]{1,0:T(8,128)(2,1)S(1)}, bf16[128,512]{1,0:T(8,128)(2,1)S(1)}, u32[]{:S(2)}, u32[]{:S(2)}) collective-permute-start(bf16[128,512]{1,0:T(8,128)(2,1)S(1)} %shard_map.92.a), channel_id=1, source_target_pairs={{0,2},{1,3},{2,0},{3,1},{4,6},{5,7},{6,4},{7,5},{8,10},{9,11},{10,... | collective-permute-start | bytes 393224 | tf_op jit(solution)/shard_map/ppermute | solution.py:17
  20.8 1.9 %collective-permute-done.4.far = bf16[128,512]{1,0:T(8,128)(2,1)S(1)} collective-permute-done((bf16[128,512]{1,0:T(8,128)(2,1)S(1)}, bf16[128,512]{1,0:T(8,128)(2,1)S(1)}, u32[]{:S(2)}, u32[]{:S(2)}) %collective-permute-start.4) | collective-permute-done | bytes 131104 | tf_op jit(solution)/shard_map/ppermute | solution.py:17
  22.8 1.6 %collective-permute-start.8 = (bf16[128,256]{1,0:T(8,128)(2,1)S(1)}, bf16[128,256]{1,0:T(8,128)(2,1)S(1)}, u32[]{:S(2)}, u32[]{:S(2)}) collective-permute-start(bf16[128,256]{1,0:T(8,128)(2,1)S(1)} %shard_map.89.seen.a), channel_id=1, source_target_pairs={{0,2},{1,3},{2,0},{3,1},{4,6},{5,7},{6,4},{7,5},{8,10},{9,11},{10,... | collective-permute-start | bytes 196616 | tf_op jit(solution)/shard_map/ppermute | solution.py:17
  24.4 0.7 %shard_map.90 = (bf16[640,256]{1,0:T(8,128)(2,1)S(1)}, f32[128,256]{1,0:T(8,128)S(1)}, bf16[128,512]{1,0:T(8,128)(2,1)S(1)}) custom-call(f32[640,256]{1,0:T(8,128)S(1)} %get-tuple-element.44.seen.x1, bf16[128,512]{1,0:T(8,128)(2,1)S(1)} %get-tuple-element.49.seen.send, bf16[128,512]{1,0:T(8,128)(2,1)S(1)} %collective-permute-done.4.far, ...), custom_call_target="tpu_custom_call" | custom-call | flops 100000000 | tf_op jit(solution)/shard_map/pallas_call | solution.py:88
  25.1 0.6 %collective-permute-start.7 = (bf16[128,256]{1,0:T(8,128)(2,1)S(1)}, bf16[128,256]{1,0:T(8,128)(2,1)S(1)}, u32[]{:S(2)}, u32[]{:S(2)}) collective-permute-start(bf16[128,256]{1,0:T(8,128)(2,1)S(1)} %shard_map.89.seen.a), channel_id=1, source_target_pairs={{0,1},{1,0},{2,3},{3,2},{4,5},{5,4},{6,7},{7,6},{8,9},{9,8},{10,11... | collective-permute-start | bytes 196616 | tf_op jit(solution)/shard_map/ppermute | solution.py:17
  25.7 1.2 %collective-permute-start.14 = (bf16[128,512]{1,0:T(8,128)(2,1)S(1)}, bf16[128,512]{1,0:T(8,128)(2,1)S(1)}, u32[]{:S(2)}, u32[]{:S(2)}) collective-permute-start(bf16[128,512]{1,0:T(8,128)(2,1)S(1)} %get-tuple-element.62.z), channel_id=1, source_target_pairs={{0,4},{4,0},{8,12},{12,8},{1,5},{5,1},{9,13},{13,9},{2,6},{6,2},{1... | collective-permute-start | bytes 393224 | tf_op jit(solution)/shard_map/ppermute | solution.py:17
  27.7 0.9 %shard_map.91 = (f32[640,256]{1,0:T(8,128)S(1)}, bf16[640,512]{1,0:T(8,128)(2,1)S(1)}) custom-call(bf16[640,256]{1,0:T(8,128)(2,1)S(1)} %get-tuple-element.52.x2, bf16[2,1,640,128]{3,2,1,0:T(8,128)(2,1)S(1)} %get-tuple-element.40.rb, bf16[1,640,128]{2,1,0:T(8,128)(2,1)S(1)} %get-tuple-element.41.tl, bf16[1,640,128]{2,1,0:T(8,128)(2,1)S(1)} %get-tuple-element.42.tr, ...), custom_call_target="tpu_custom_call" | custom-call | flops 3000000000 | tf_op jit(solution)/shard_map/pallas_call | solution.py:88
  28.7 0.5 %shard_map.94.back = bf16[128,512]{1,0:T(8,128)(2,1)S(1)} custom-call(bf16[128,256]{1,0:T(8,128)(2,1)S(1)} %shard_map.89.seen.a, bf16[128,256]{1,0:T(8,128)(2,1)S(1)} %collective-permute-done.7.b, bf16[128,256]{1,0:T(8,128)(2,1)S(1)} %collective-permute-done.8.c, bf16[128,256]{1,0:T(8,128)(2,1)S(1)} %collective-permute-done.9.d, ...), custom_call_target="tpu_custom_call" | custom-call | flops 1000000000 | tf_op jit(solution)/shard_map/pallas_call | solution.py:88
  29.2 1.2 %collective-permute-start.13 = (bf16[128,512]{1,0:T(8,128)(2,1)S(1)}, bf16[128,512]{1,0:T(8,128)(2,1)S(1)}, u32[]{:S(2)}, u32[]{:S(2)}) collective-permute-start(bf16[128,512]{1,0:T(8,128)(2,1)S(1)} %shard_map.94.back), channel_id=1, source_target_pairs={{0,4},{4,0},{8,12},{12,8},{1,5},{5,1},{9,13},{13,9},{2,6},{6,2},{1... | collective-permute-start | bytes 393224 | tf_op jit(solution)/shard_map/ppermute | solution.py:17
  30.5 0.7 %collective-permute-done.14.z_sib = bf16[128,512]{1,0:T(8,128)(2,1)S(1)} collective-permute-done((bf16[128,512]{1,0:T(8,128)(2,1)S(1)}, bf16[128,512]{1,0:T(8,128)(2,1)S(1)}, u32[]{:S(2)}, u32[]{:S(2)}) %collective-permute-start.14) | collective-permute-done | bytes 131104 | tf_op jit(solution)/shard_map/ppermute | solution.py:17
  31.2 3.7 %collective-permute-done.13.back_sib = bf16[128,512]{1,0:T(8,128)(2,1)S(1)} collective-permute-done((bf16[128,512]{1,0:T(8,128)(2,1)S(1)}, bf16[128,512]{1,0:T(8,128)(2,1)S(1)}, u32[]{:S(2)}, u32[]{:S(2)}) %collective-permute-start.13) | collective-permute-done | bytes 131104 | tf_op jit(solution)/shard_map/ppermute | solution.py:17
  35.1 3.8 %collective-permute-start.15 = (bf16[128,256]{1,0:T(8,128)(2,1)S(1)}, bf16[128,256]{1,0:T(8,128)(2,1)S(1)}, u32[]{:S(2)}, u32[]{:S(2)}) collective-permute-start(bf16[128,256]{1,0:T(8,128)(2,1)S(1)} %get-tuple-element.64.seen.half5), channel_id=1, source_target_pairs={{0,12},{4,8},{8,4},{12,0},{1,13},{5,9},{9,5},{13,1},{2,14},{6,10},... | collective-permute-start | bytes 196616 | tf_op jit(solution)/shard_map/ppermute | solution.py:17
  39.2 2.1 %collective-permute-done.15.half5_far = bf16[128,256]{1,0:T(8,128)(2,1)S(1)} collective-permute-done((bf16[128,256]{1,0:T(8,128)(2,1)S(1)}, bf16[128,256]{1,0:T(8,128)(2,1)S(1)}, u32[]{:S(2)}, u32[]{:S(2)}) %collective-permute-start.15) | collective-permute-done | bytes 65568 | tf_op jit(solution)/shard_map/ppermute | solution.py:17
  41.3 1.4 %shard_map.97 = f32[1,640,256]{2,1,0:T(8,128)} custom-call(f32[640,256]{1,0:T(8,128)S(1)} %get-tuple-element.65.out3, bf16[640,512]{1,0:T(8,128)(2,1)S(1)} %get-tuple-element.55.under, bf16[128,256]{1,0:T(8,128)(2,1)S(1)} %get-tuple-element.64.seen.half5, bf16[128,256]{1,0:T(8,128)(2,1)S(1)} %collective-permute-done.15.half5_far, ...), custom_call_target="tpu_custom_call" | custom-call | flops 1000000000 | tf_op jit(solution)/shard_map/pallas_call | solution.py:88
  (26 shorter events, 3.2 us)
Async XLA Ops:
  2.4 3.2 %collective-permute-start.1 = (bf16[128,256]{1,0:T(8,128)(2,1)S(1)}, bf16[128,256]{1,0:T(8,128)(2,1)S(1)}, u32[]{:S(2)}, u32[]{:S(2)}) collective-permute-start(bf16[128,256]{1,0:T(8,128)(2,1)S(1)} %get-tuple-element.37.p), channel_id=1, source_target_pairs={{0,1},{1,0},{2,3},{3,2},{4,5},{5,4},{6,7},{7,6},{8,9},{9,8},{10,11... | collective-permute-start | bytes 196616 | tf_op jit(solution)/shard_map/ppermute | solution.py:17
  2.9 5.3 %collective-permute-start = (bf16[128,256]{1,0:T(8,128)(2,1)S(1)}, bf16[128,256]{1,0:T(8,128)(2,1)S(1)}, u32[]{:S(2)}, u32[]{:S(2)}) collective-permute-start(bf16[128,256]{1,0:T(8,128)(2,1)S(1)} %get-tuple-element.37.p), channel_id=1, source_target_pairs={{0,4},{4,0},{8,12},{12,8},{1,5},{5,1},{9,13},{13,9},{2,6},{6,2},{1... | collective-permute-start | bytes 196616 | tf_op jit(solution)/shard_map/ppermute | solution.py:17
  6.1 4.9 %collective-permute-start.3 = (bf16[128,384]{1,0:T(8,128)(2,1)S(1)}, bf16[128,384]{1,0:T(8,128)(2,1)S(1)}, u32[]{:S(2)}, u32[]{:S(2)}) collective-permute-start(bf16[128,384]{1,0:T(8,128)(2,1)S(1)} %get-tuple-element.43.seen.own), channel_id=1, source_target_pairs={{0,4},{4,0},{8,12},{12,8},{1,5},{5,1},{9,13},{13,9},{2,6},{6,2},{1... | collective-permute-start | bytes 294920 | tf_op jit(solution)/shard_map/ppermute | solution.py:17
  9.0 5.4 %collective-permute-start.2 = (bf16[128,512]{1,0:T(8,128)(2,1)S(1)}, bf16[128,512]{1,0:T(8,128)(2,1)S(1)}, u32[]{:S(2)}, u32[]{:S(2)}) collective-permute-start(bf16[128,512]{1,0:T(8,128)(2,1)S(1)} %get-tuple-element.46), channel_id=1, source_target_pairs={{0,4},{4,0},{8,12},{12,8},{1,5},{5,1},{9,13},{13,9},{2,6},{6,2},{1... | collective-permute-start | bytes 393224 | tf_op jit(solution)/shard_map/ppermute | solution.py:17
  11.1 7.0 %collective-permute-start.5 = (bf16[128,256]{1,0:T(8,128)(2,1)S(1)}, bf16[128,256]{1,0:T(8,128)(2,1)S(1)}, u32[]{:S(2)}, u32[]{:S(2)}) collective-permute-start(bf16[128,256]{1,0:T(8,128)(2,1)S(1)} %get-tuple-element.51), channel_id=1, source_target_pairs={{0,12},{4,8},{8,4},{12,0},{1,13},{5,9},{9,5},{13,1},{2,14},{6,10},... | collective-permute-start | bytes 196616 | tf_op jit(solution)/shard_map/ppermute | solution.py:17
  14.5 4.5 %copy-start = (bf16[128,512]{1,0:T(8,128)(2,1)S(1)}, bf16[128,512]{1,0:T(8,128)(2,1)}, u32[]{:S(2)}) copy-start(bf16[128,512]{1,0:T(8,128)(2,1)} %caps.3) | copy-start | bytes 393220
  14.6 8.1 %collective-permute-start.4 = (bf16[128,512]{1,0:T(8,128)(2,1)S(1)}, bf16[128,512]{1,0:T(8,128)(2,1)S(1)}, u32[]{:S(2)}, u32[]{:S(2)}) collective-permute-start(bf16[128,512]{1,0:T(8,128)(2,1)S(1)} %get-tuple-element.49.seen.send), channel_id=1, source_target_pairs={{0,12},{4,8},{8,4},{12,0},{1,13},{5,9},{9,5},{13,1},{2,14},{6,10},... | collective-permute-start | bytes 393224 | tf_op jit(solution)/shard_map/ppermute | solution.py:17
  18.7 8.4 %collective-permute-start.6 = (bf16[128,768]{1,0:T(8,128)(2,1)S(1)}, bf16[128,768]{1,0:T(8,128)(2,1)S(1)}, u32[]{:S(2)}, u32[]{:S(2)}) collective-permute-start(bf16[128,768]{1,0:T(8,128)(2,1)S(1)} %shard_map.88.seen.late), channel_id=1, source_target_pairs={{0,4},{4,0},{8,12},{12,8},{1,5},{5,1},{9,13},{13,9},{2,6},{6,2},{1... | collective-permute-start | bytes 589832 | tf_op jit(solution)/shard_map/ppermute | solution.py:17
  19.2 6.5 %collective-permute-start.11 = (bf16[128,512]{1,0:T(8,128)(2,1)S(1)}, bf16[128,512]{1,0:T(8,128)(2,1)S(1)}, u32[]{:S(2)}, u32[]{:S(2)}) collective-permute-start(bf16[128,512]{1,0:T(8,128)(2,1)S(1)} %shard_map.92.a), channel_id=1, source_target_pairs={{0,2},{1,3},{2,0},{3,1},{4,6},{5,7},{6,4},{7,5},{8,10},{9,11},{10,... | collective-permute-start | bytes 393224 | tf_op jit(solution)/shard_map/ppermute | solution.py:17
  22.8 4.3 %collective-permute-start.8 = (bf16[128,256]{1,0:T(8,128)(2,1)S(1)}, bf16[128,256]{1,0:T(8,128)(2,1)S(1)}, u32[]{:S(2)}, u32[]{:S(2)}) collective-permute-start(bf16[128,256]{1,0:T(8,128)(2,1)S(1)} %shard_map.89.seen.a), channel_id=1, source_target_pairs={{0,2},{1,3},{2,0},{3,1},{4,6},{5,7},{6,4},{7,5},{8,10},{9,11},{10,... | collective-permute-start | bytes 196616 | tf_op jit(solution)/shard_map/ppermute | solution.py:17
  24.4 4.2 %collective-permute-start.10 = (bf16[128,512]{1,0:T(8,128)(2,1)S(1)}, bf16[128,512]{1,0:T(8,128)(2,1)S(1)}, u32[]{:S(2)}, u32[]{:S(2)}) collective-permute-start(bf16[128,512]{1,0:T(8,128)(2,1)S(1)} %shard_map.92.a), channel_id=1, source_target_pairs={{0,1},{1,0},{2,3},{3,2},{4,5},{5,4},{6,7},{7,6},{8,9},{9,8},{10,11... | collective-permute-start | bytes 393224 | tf_op jit(solution)/shard_map/ppermute | solution.py:17
  25.1 3.6 %collective-permute-start.7 = (bf16[128,256]{1,0:T(8,128)(2,1)S(1)}, bf16[128,256]{1,0:T(8,128)(2,1)S(1)}, u32[]{:S(2)}, u32[]{:S(2)}) collective-permute-start(bf16[128,256]{1,0:T(8,128)(2,1)S(1)} %shard_map.89.seen.a), channel_id=1, source_target_pairs={{0,1},{1,0},{2,3},{3,2},{4,5},{5,4},{6,7},{7,6},{8,9},{9,8},{10,11... | collective-permute-start | bytes 196616 | tf_op jit(solution)/shard_map/ppermute | solution.py:17
  25.7 5.5 %collective-permute-start.14 = (bf16[128,512]{1,0:T(8,128)(2,1)S(1)}, bf16[128,512]{1,0:T(8,128)(2,1)S(1)}, u32[]{:S(2)}, u32[]{:S(2)}) collective-permute-start(bf16[128,512]{1,0:T(8,128)(2,1)S(1)} %get-tuple-element.62.z), channel_id=1, source_target_pairs={{0,4},{4,0},{8,12},{12,8},{1,5},{5,1},{9,13},{13,9},{2,6},{6,2},{1... | collective-permute-start | bytes 393224 | tf_op jit(solution)/shard_map/ppermute | solution.py:17
  27.1 1.4 %collective-permute-start.12 = (bf16[128,512]{1,0:T(8,128)(2,1)S(1)}, bf16[128,512]{1,0:T(8,128)(2,1)S(1)}, u32[]{:S(2)}, u32[]{:S(2)}) collective-permute-start(bf16[128,512]{1,0:T(8,128)(2,1)S(1)} %collective-permute-done.11.c), channel_id=1, source_target_pairs={{0,1},{1,0},{2,3},{3,2},{4,5},{5,4},{6,7},{7,6},{8,9},{9,8},{10,11... | collective-permute-start | bytes 393224 | tf_op jit(solution)/shard_map/ppermute | solution.py:17
  27.2 1.5 %collective-permute-start.9 = (bf16[128,256]{1,0:T(8,128)(2,1)S(1)}, bf16[128,256]{1,0:T(8,128)(2,1)S(1)}, u32[]{:S(2)}, u32[]{:S(2)}) collective-permute-start(bf16[128,256]{1,0:T(8,128)(2,1)S(1)} %collective-permute-done.8.c), channel_id=1, source_target_pairs={{0,1},{1,0},{2,3},{3,2},{4,5},{5,4},{6,7},{7,6},{8,9},{9,8},{10,11... | collective-permute-start | bytes 196616 | tf_op jit(solution)/shard_map/ppermute | solution.py:17
  29.2 5.7 %collective-permute-start.13 = (bf16[128,512]{1,0:T(8,128)(2,1)S(1)}, bf16[128,512]{1,0:T(8,128)(2,1)S(1)}, u32[]{:S(2)}, u32[]{:S(2)}) collective-permute-start(bf16[128,512]{1,0:T(8,128)(2,1)S(1)} %shard_map.94.back), channel_id=1, source_target_pairs={{0,4},{4,0},{8,12},{12,8},{1,5},{5,1},{9,13},{13,9},{2,6},{6,2},{1... | collective-permute-start | bytes 393224 | tf_op jit(solution)/shard_map/ppermute | solution.py:17
  35.1 6.2 %collective-permute-start.15 = (bf16[128,256]{1,0:T(8,128)(2,1)S(1)}, bf16[128,256]{1,0:T(8,128)(2,1)S(1)}, u32[]{:S(2)}, u32[]{:S(2)}) collective-permute-start(bf16[128,256]{1,0:T(8,128)(2,1)S(1)} %get-tuple-element.64.seen.half5), channel_id=1, source_target_pairs={{0,12},{4,8},{8,4},{12,0},{1,13},{5,9},{9,5},{13,1},{2,14},{6,10},... | collective-permute-start | bytes 196616 | tf_op jit(solution)/shard_map/ppermute | solution.py:17

commit v17 on v16

--- a/solution.py
+++ b/solution.py
@@ -149,13 +149,14 @@
             return copy
 
         first = load(rb_hbm.at[0], rb.at[0], 2, 0)
+        groups = [(i, min(2, blocks - i)) for i in range(0, blocks, 2)]
         copies = []
-        for i in range(blocks):
-            copies.append(load(rhs_hbm.at[0, span(i), :], rhs_v.at[span(i), :], 0, i))
+        for i, n in groups:
+            copies.append(load(rhs_hbm.at[0, span(i, n), :], rhs_v.at[span(i, n), :], 0, i))
             copies.append(
                 load(
-                    inv_hbm.at[0, span(i), span(0, i + 1)],
-                    inv_ref.at[span(i), span(0, i + 1)],
+                    inv_hbm.at[0, span(i, n), span(0, i + n)],
+                    inv_ref.at[span(i, n), span(0, i + n)],
                     1,
                     i,
                 )
@@ -164,11 +165,11 @@
         bases = [load(source, target, 2, 1 + i) for i, (source, target) in enumerate(pairs)]
         first.wait()
         basis_t[...] = rb[0, 0].T
-        for i in range(blocks):
-            copies[2 * i].wait()
-            copies[2 * i + 1].wait()
-            x_ref[span(i), :] = dot(
-                inv_ref[span(i), span(0, i + 1)], rhs_v[span(0, i + 1), :].astype(BF)
+        for i, n in groups:
+            copies[i].wait()
+            copies[i + 1].wait()
+            x_ref[span(i, n), :] = dot(
+                inv_ref[span(i, n), span(0, i + n)], rhs_v[span(0, i + n), :].astype(BF)
             )
         send[...] = (dot(basis_t[...], x_ref[...].astype(BF)) * s1).astype(BF)
         for copy in bases:
@@ -217,11 +218,22 @@
     )
     early_sib = swap(early, "leaf", 1)
 
-    def flip_body(rb, tl, tr, seen, out):
+    def flip_body(lb, rb, tl, tr, seen, out, out2):
         for i, basis in enumerate((rb[1, 0], tr[0], tl[0])):
             out[span(i), :] = basis.T
-
-    (bases_t,) = call(flip_body, [((3 * rank, rows), BF)], rb, tl, tr, early, micros=0.2)
+        for i, basis in enumerate((lb[1, 0], lb[0, 0])):
+            out2[span(i), :] = basis.T
+
+    bases_t, lefts_t = call(
+        flip_body,
+        [((3 * rank, rows), BF), ((2 * rank, rows), BF)],
+        lb,
+        rb,
+        tl,
+        tr,
+        early,
+        micros=0.2,
+    )
 
     def one_body(x0, p, p_sib, lb, caps, bases_t, x1, send, keep, stack, seen):
         side = column_side()
@@ -335,13 +347,14 @@
     )
     top_far = swap(top_send, "top", 2)
 
-    def two_body(x1, send, far, lb, caps, seen, x2, z5, z, stack):
+    def two_body(x1, send, far, lb, caps, lefts_t, seen, x2, z5, z, stack, both):
         put_rows(stack, tree_side(1), send[:, :cols], far[:, :cols])
         coef = dot(caps[1, 0], stack[...]).astype(BF)
         x2[...] = (x1[...] - dot(lb[1, 0], coef)).astype(BF)
-        z5[...] = dot_t(lb[1, 0], x2[...]) * s2
+        both[...] = dot(lefts_t[...], x2[...])
+        z5[...] = both[span(0), :] * s2
         z[:, :cols] = z5[...].astype(BF)
-        z[:, cols:] = (dot_t(lb[0, 0], x2[...]) * s1).astype(BF)
+        z[:, cols:] = (both[span(1), :] * s1).astype(BF)
 
     state2, down5, down_send = call(
         two_body,
@@ -351,8 +364,9 @@
         cross_in,
         lb,
         caps,
+        lefts_t,
         top_send,
-        scratch=[pltpu.VMEM((2 * rank, cols), BF)],
+        scratch=[pltpu.VMEM((2 * rank, cols), BF), pltpu.VMEM((2 * rank, cols), f32)],
         micros=0.1,
     )
     down_in = swap(down_send, "leaf", 1)

time: 42.8 us -> 42.6 us (level)
  no operation moved by 1% of the time
where the time goes in v17:
time: 42.6 us; the launch traced here: 42.4 us
  starting transfers between devices  23.8 us (56%)
  waiting for transfers between devices  9.59 us (23%)
  Pallas kernels  8.88 us (21%)
    ppermute x16, starting transfers between devices, swap(): return lax.ppermute(value, axis, pairs)  23.8 us
    ppermute x16, waiting for transfers between devices, swap(): return lax.ppermute(value, axis, pairs)  9.59 us
    pallas_call x16, Pallas kernels, call(): pl.pallas_call(body, out_shape=[jax.ShapeDtypeStruct(shape, dtype) if hbm...  8.88 us
  transfers between devices with their start and end apart: 16, of which 7 were waited for; matrix products, arithmetic and copies ran while one was open for 0% of the time, Pallas kernels for 12%

profile of v17, /device:TPU:0, one launch (start us, length us, event | category | flops | bytes accessed | tf_op | source)
XLA Modules:
  0.0 42.4 jit_solution(7034872393147548060)
XLA Ops:
  0.0 2.1 %shard_map.82 = (f32[640,256]{1,0:T(8,128)S(1)}, bf16[128,256]{1,0:T(8,128)(2,1)S(1)}, bf16[640,640]{1,0:T(8,128)(2,1)S(1)}, bf16[2,1,640,128]{3,2,1,0:T(8,128)(...) custom-call(f32[1,640,256]{2,1,0:T(8,128)} %rhs_hbm.1, ...), custom_call_target="tpu_custom_call" | custom-call | flops 1000000000 | tf_op jit(solution)/shard_map/pallas_call | solution.py:88
  2.6 2.6 %collective-permute-start = (bf16[128,256]{1,0:T(8,128)(2,1)S(1)}, bf16[128,256]{1,0:T(8,128)(2,1)S(1)}, u32[]{:S(2)}, u32[]{:S(2)}) collective-permute-start(bf16[128,256]{1,0:T(8,128)(2,1)S(1)} %get-tuple-element.39.p), channel_id=1, source_target_pairs={{0,4},{4,0},{8,12},{12,8},{1,5},{5,1},{9,13},{13,9},{2,6},{6,2},{1... | collective-permute-start | bytes 196616 | tf_op jit(solution)/shard_map/ppermute | solution.py:17
  5.3 0.6 %shard_map.83 = (bf16[128,384]{1,0:T(8,128)(2,1)S(1)}, bf16[128,256]{1,0:T(8,128)(2,1)S(1)}) custom-call(bf16[2,1,640,128]{3,2,1,0:T(8,128)(2,1)S(1)} %get-tuple-element.40.lb, bf16[2,1,128,256]{3,2,1,0:T(8,128)(2,1)S(1)} %get-tuple-element.41.caps, bf16[1,640,128]{2,1,0:T(8,128)(2,1)S(1)} %get-tuple-element.43.tl, ...), custom_call_target="tpu_custom_call" | custom-call | flops 10000000000 | tf_op jit(solution)/shard_map/pallas_call | solution.py:88
  5.9 1.2 %collective-permute-start.3 = (bf16[128,384]{1,0:T(8,128)(2,1)S(1)}, bf16[128,384]{1,0:T(8,128)(2,1)S(1)}, u32[]{:S(2)}, u32[]{:S(2)}) collective-permute-start(bf16[128,384]{1,0:T(8,128)(2,1)S(1)} %get-tuple-element.45.seen.own), channel_id=1, source_target_pairs={{0,4},{4,0},{8,12},{12,8},{1,5},{5,1},{9,13},{13,9},{2,6},{6,2},{1... | collective-permute-start | bytes 294920 | tf_op jit(solution)/shard_map/ppermute | solution.py:17
  7.4 0.6 %collective-permute-done.p_sib = bf16[128,256]{1,0:T(8,128)(2,1)S(1)} collective-permute-done((bf16[128,256]{1,0:T(8,128)(2,1)S(1)}, bf16[128,256]{1,0:T(8,128)(2,1)S(1)}, u32[]{:S(2)}, u32[]{:S(2)}) %collective-permute-start) | collective-permute-done | bytes 65568 | tf_op jit(solution)/shard_map/ppermute | solution.py:17
  8.0 0.8 %shard_map.85 = (f32[640,256]{1,0:T(8,128)S(1)}, bf16[128,512]{1,0:T(8,128)(2,1)S(1)}, f32[128,512]{1,0:T(8,128)S(1)}) custom-call(f32[640,256]{1,0:T(8,128)S(1)} %get-tuple-element.38.x0, bf16[128,256]{1,0:T(8,128)(2,1)S(1)} %get-tuple-element.39.p, bf16[128,256]{1,0:T(8,128)(2,1)S(1)} %collective-permute-done.p_sib, ...), custom_call_target="tpu_custom_call" | custom-call | flops 3000000000 | tf_op jit(solution)/shard_map/pallas_call | solution.py:88
  8.7 1.8 %collective-permute-start.2 = (bf16[128,512]{1,0:T(8,128)(2,1)S(1)}, bf16[128,512]{1,0:T(8,128)(2,1)S(1)}, u32[]{:S(2)}, u32[]{:S(2)}) collective-permute-start(bf16[128,512]{1,0:T(8,128)(2,1)S(1)} %get-tuple-element.49), channel_id=1, source_target_pairs={{0,4},{4,0},{8,12},{12,8},{1,5},{5,1},{9,13},{13,9},{2,6},{6,2},{1... | collective-permute-start | bytes 393224 | tf_op jit(solution)/shard_map/ppermute | solution.py:17
  10.9 3.3 %collective-permute-start.5 = (bf16[128,256]{1,0:T(8,128)(2,1)S(1)}, bf16[128,256]{1,0:T(8,128)(2,1)S(1)}, u32[]{:S(2)}, u32[]{:S(2)}) collective-permute-start(bf16[128,256]{1,0:T(8,128)(2,1)S(1)} %get-tuple-element.55), channel_id=1, source_target_pairs={{0,12},{4,8},{8,4},{12,0},{1,13},{5,9},{9,5},{13,1},{2,14},{6,10},... | collective-permute-start | bytes 196616 | tf_op jit(solution)/shard_map/ppermute | solution.py:17
  14.3 3.6 %collective-permute-start.4 = (bf16[128,512]{1,0:T(8,128)(2,1)S(1)}, bf16[128,512]{1,0:T(8,128)(2,1)S(1)}, u32[]{:S(2)}, u32[]{:S(2)}) collective-permute-start(bf16[128,512]{1,0:T(8,128)(2,1)S(1)} %get-tuple-element.52.seen.send), channel_id=1, source_target_pairs={{0,12},{4,8},{8,4},{12,0},{1,13},{5,9},{9,5},{13,1},{2,14},{6,10},... | collective-permute-start | bytes 393224 | tf_op jit(solution)/shard_map/ppermute | solution.py:17
  17.9 0.5 %shard_map.88.seen.late = bf16[128,768]{1,0:T(8,128)(2,1)S(1)} custom-call(bf16[2,1,640,128]{3,2,1,0:T(8,128)(2,1)S(1)} %get-tuple-element.40.lb, bf16[2,1,640,128]{3,2,1,0:T(8,128)(2,1)S(1)} %get-tuple-element.42.rb, bf16[2,1,128,256]{3,2,1,0:T(8,128)(2,1)S(1)} %get-tuple-element.41.caps, bf16[1,640,128]{2,1,0:T(8,128)(2,1)S(1)} %get-tuple-element.43.tl, ...), custom_call_target="tpu_custom_call" | custom-call | flops 5000000000 | tf_op jit(solution)/shard_map/pallas_call | solution.py:88
  18.9 1.6 %collective-permute-start.11 = (bf16[128,512]{1,0:T(8,128)(2,1)S(1)}, bf16[128,512]{1,0:T(8,128)(2,1)S(1)}, u32[]{:S(2)}, u32[]{:S(2)}) collective-permute-start(bf16[128,512]{1,0:T(8,128)(2,1)S(1)} %shard_map.92.a), channel_id=1, source_target_pairs={{0,2},{1,3},{2,0},{3,1},{4,6},{5,7},{6,4},{7,5},{8,10},{9,11},{10,... | collective-permute-start | bytes 393224 | tf_op jit(solution)/shard_map/ppermute | solution.py:17
  20.5 1.9 %collective-permute-done.4.far = bf16[128,512]{1,0:T(8,128)(2,1)S(1)} collective-permute-done((bf16[128,512]{1,0:T(8,128)(2,1)S(1)}, bf16[128,512]{1,0:T(8,128)(2,1)S(1)}, u32[]{:S(2)}, u32[]{:S(2)}) %collective-permute-start.4) | collective-permute-done | bytes 131104 | tf_op jit(solution)/shard_map/ppermute | solution.py:17
  22.5 1.6 %collective-permute-start.8 = (bf16[128,256]{1,0:T(8,128)(2,1)S(1)}, bf16[128,256]{1,0:T(8,128)(2,1)S(1)}, u32[]{:S(2)}, u32[]{:S(2)}) collective-permute-start(bf16[128,256]{1,0:T(8,128)(2,1)S(1)} %shard_map.89.seen.a), channel_id=1, source_target_pairs={{0,2},{1,3},{2,0},{3,1},{4,6},{5,7},{6,4},{7,5},{8,10},{9,11},{10,... | collective-permute-start | bytes 196616 | tf_op jit(solution)/shard_map/ppermute | solution.py:17
  24.1 0.7 %shard_map.90 = (bf16[640,256]{1,0:T(8,128)(2,1)S(1)}, f32[128,256]{1,0:T(8,128)S(1)}, bf16[128,512]{1,0:T(8,128)(2,1)S(1)}) custom-call(f32[640,256]{1,0:T(8,128)S(1)} %get-tuple-element.47.seen.x1, bf16[128,512]{1,0:T(8,128)(2,1)S(1)} %get-tuple-element.52.seen.send, bf16[128,512]{1,0:T(8,128)(2,1)S(1)} %collective-permute-done.4.far, ...), custom_call_target="tpu_custom_call" | custom-call | flops 100000000 | tf_op jit(solution)/shard_map/pallas_call | solution.py:88
  24.8 0.6 %collective-permute-start.7 = (bf16[128,256]{1,0:T(8,128)(2,1)S(1)}, bf16[128,256]{1,0:T(8,128)(2,1)S(1)}, u32[]{:S(2)}, u32[]{:S(2)}) collective-permute-start(bf16[128,256]{1,0:T(8,128)(2,1)S(1)} %shard_map.89.seen.a), channel_id=1, source_target_pairs={{0,1},{1,0},{2,3},{3,2},{4,5},{5,4},{6,7},{7,6},{8,9},{9,8},{10,11... | collective-permute-start | bytes 196616 | tf_op jit(solution)/shard_map/ppermute | solution.py:17
  25.4 1.2 %collective-permute-start.14 = (bf16[128,512]{1,0:T(8,128)(2,1)S(1)}, bf16[128,512]{1,0:T(8,128)(2,1)S(1)}, u32[]{:S(2)}, u32[]{:S(2)}) collective-permute-start(bf16[128,512]{1,0:T(8,128)(2,1)S(1)} %get-tuple-element.66.z), channel_id=1, source_target_pairs={{0,4},{4,0},{8,12},{12,8},{1,5},{5,1},{9,13},{13,9},{2,6},{6,2},{1... | collective-permute-start | bytes 393224 | tf_op jit(solution)/shard_map/ppermute | solution.py:17
  27.4 0.9 %shard_map.91 = (f32[640,256]{1,0:T(8,128)S(1)}, bf16[640,512]{1,0:T(8,128)(2,1)S(1)}) custom-call(bf16[640,256]{1,0:T(8,128)(2,1)S(1)} %get-tuple-element.56.x2, bf16[2,1,640,128]{3,2,1,0:T(8,128)(2,1)S(1)} %get-tuple-element.42.rb, bf16[1,640,128]{2,1,0:T(8,128)(2,1)S(1)} %get-tuple-element.43.tl, bf16[1,640,128]{2,1,0:T(8,128)(2,1)S(1)} %get-tuple-element.44.tr, ...), custom_call_target="tpu_custom_call" | custom-call | flops 3000000000 | tf_op jit(solution)/shard_map/pallas_call | solution.py:88
  28.4 0.5 %shard_map.94.back = bf16[128,512]{1,0:T(8,128)(2,1)S(1)} custom-call(bf16[128,256]{1,0:T(8,128)(2,1)S(1)} %shard_map.89.seen.a, bf16[128,256]{1,0:T(8,128)(2,1)S(1)} %collective-permute-done.7.b, bf16[128,256]{1,0:T(8,128)(2,1)S(1)} %collective-permute-done.8.c, bf16[128,256]{1,0:T(8,128)(2,1)S(1)} %collective-permute-done.9.d, ...), custom_call_target="tpu_custom_call" | custom-call | flops 1000000000 | tf_op jit(solution)/shard_map/pallas_call | solution.py:88
  29.0 1.2 %collective-permute-start.13 = (bf16[128,512]{1,0:T(8,128)(2,1)S(1)}, bf16[128,512]{1,0:T(8,128)(2,1)S(1)}, u32[]{:S(2)}, u32[]{:S(2)}) collective-permute-start(bf16[128,512]{1,0:T(8,128)(2,1)S(1)} %shard_map.94.back), channel_id=1, source_target_pairs={{0,4},{4,0},{8,12},{12,8},{1,5},{5,1},{9,13},{13,9},{2,6},{6,2},{1... | collective-permute-start | bytes 393224 | tf_op jit(solution)/shard_map/ppermute | solution.py:17
  30.2 0.6 %collective-permute-done.14.z_sib = bf16[128,512]{1,0:T(8,128)(2,1)S(1)} collective-permute-done((bf16[128,512]{1,0:T(8,128)(2,1)S(1)}, bf16[128,512]{1,0:T(8,128)(2,1)S(1)}, u32[]{:S(2)}, u32[]{:S(2)}) %collective-permute-start.14) | collective-permute-done | bytes 131104 | tf_op jit(solution)/shard_map/ppermute | solution.py:17
  30.8 3.8 %collective-permute-done.13.back_sib = bf16[128,512]{1,0:T(8,128)(2,1)S(1)} collective-permute-done((bf16[128,512]{1,0:T(8,128)(2,1)S(1)}, bf16[128,512]{1,0:T(8,128)(2,1)S(1)}, u32[]{:S(2)}, u32[]{:S(2)}) %collective-permute-start.13) | collective-permute-done | bytes 131104 | tf_op jit(solution)/shard_map/ppermute | solution.py:17
  34.8 3.8 %collective-permute-start.15 = (bf16[128,256]{1,0:T(8,128)(2,1)S(1)}, bf16[128,256]{1,0:T(8,128)(2,1)S(1)}, u32[]{:S(2)}, u32[]{:S(2)}) collective-permute-start(bf16[128,256]{1,0:T(8,128)(2,1)S(1)} %get-tuple-element.68.seen.half5), channel_id=1, source_target_pairs={{0,12},{4,8},{8,4},{12,0},{1,13},{5,9},{9,5},{13,1},{2,14},{6,10},... | collective-permute-start | bytes 196616 | tf_op jit(solution)/shard_map/ppermute | solution.py:17
  38.9 2.1 %collective-permute-done.15.half5_far = bf16[128,256]{1,0:T(8,128)(2,1)S(1)} collective-permute-done((bf16[128,256]{1,0:T(8,128)(2,1)S(1)}, bf16[128,256]{1,0:T(8,128)(2,1)S(1)}, u32[]{:S(2)}, u32[]{:S(2)}) %collective-permute-start.15) | collective-permute-done | bytes 65568 | tf_op jit(solution)/shard_map/ppermute | solution.py:17
  41.0 1.4 %shard_map.97 = f32[1,640,256]{2,1,0:T(8,128)} custom-call(f32[640,256]{1,0:T(8,128)S(1)} %get-tuple-element.69.out3, bf16[640,512]{1,0:T(8,128)(2,1)S(1)} %get-tuple-element.59.under, bf16[128,256]{1,0:T(8,128)(2,1)S(1)} %get-tuple-element.68.seen.half5, bf16[128,256]{1,0:T(8,128)(2,1)S(1)} %collective-permute-done.15.half5_far, ...), custom_call_target="tpu_custom_call" | custom-call | flops 1000000000 | tf_op jit(solution)/shard_map/pallas_call | solution.py:88
  (26 shorter events, 3.4 us)
Async XLA Ops:
  2.1 3.2 %collective-permute-start.1 = (bf16[128,256]{1,0:T(8,128)(2,1)S(1)}, bf16[128,256]{1,0:T(8,128)(2,1)S(1)}, u32[]{:S(2)}, u32[]{:S(2)}) collective-permute-start(bf16[128,256]{1,0:T(8,128)(2,1)S(1)} %get-tuple-element.39.p), channel_id=1, source_target_pairs={{0,1},{1,0},{2,3},{3,2},{4,5},{5,4},{6,7},{7,6},{8,9},{9,8},{10,11... | collective-permute-start | bytes 196616 | tf_op jit(solution)/shard_map/ppermute | solution.py:17
  2.6 5.3 %collective-permute-start = (bf16[128,256]{1,0:T(8,128)(2,1)S(1)}, bf16[128,256]{1,0:T(8,128)(2,1)S(1)}, u32[]{:S(2)}, u32[]{:S(2)}) collective-permute-start(bf16[128,256]{1,0:T(8,128)(2,1)S(1)} %get-tuple-element.39.p), channel_id=1, source_target_pairs={{0,4},{4,0},{8,12},{12,8},{1,5},{5,1},{9,13},{13,9},{2,6},{6,2},{1... | collective-permute-start | bytes 196616 | tf_op jit(solution)/shard_map/ppermute | solution.py:17
  5.9 4.9 %collective-permute-start.3 = (bf16[128,384]{1,0:T(8,128)(2,1)S(1)}, bf16[128,384]{1,0:T(8,128)(2,1)S(1)}, u32[]{:S(2)}, u32[]{:S(2)}) collective-permute-start(bf16[128,384]{1,0:T(8,128)(2,1)S(1)} %get-tuple-element.45.seen.own), channel_id=1, source_target_pairs={{0,4},{4,0},{8,12},{12,8},{1,5},{5,1},{9,13},{13,9},{2,6},{6,2},{1... | collective-permute-start | bytes 294920 | tf_op jit(solution)/shard_map/ppermute | solution.py:17
  8.7 5.4 %collective-permute-start.2 = (bf16[128,512]{1,0:T(8,128)(2,1)S(1)}, bf16[128,512]{1,0:T(8,128)(2,1)S(1)}, u32[]{:S(2)}, u32[]{:S(2)}) collective-permute-start(bf16[128,512]{1,0:T(8,128)(2,1)S(1)} %get-tuple-element.49), channel_id=1, source_target_pairs={{0,4},{4,0},{8,12},{12,8},{1,5},{5,1},{9,13},{13,9},{2,6},{6,2},{1... | collective-permute-start | bytes 393224 | tf_op jit(solution)/shard_map/ppermute | solution.py:17
  10.9 7.0 %collective-permute-start.5 = (bf16[128,256]{1,0:T(8,128)(2,1)S(1)}, bf16[128,256]{1,0:T(8,128)(2,1)S(1)}, u32[]{:S(2)}, u32[]{:S(2)}) collective-permute-start(bf16[128,256]{1,0:T(8,128)(2,1)S(1)} %get-tuple-element.55), channel_id=1, source_target_pairs={{0,12},{4,8},{8,4},{12,0},{1,13},{5,9},{9,5},{13,1},{2,14},{6,10},... | collective-permute-start | bytes 196616 | tf_op jit(solution)/shard_map/ppermute | solution.py:17
  14.3 4.5 %copy-start = (bf16[128,512]{1,0:T(8,128)(2,1)S(1)}, bf16[128,512]{1,0:T(8,128)(2,1)}, u32[]{:S(2)}) copy-start(bf16[128,512]{1,0:T(8,128)(2,1)} %caps.3) | copy-start | bytes 393220
  14.3 8.1 %collective-permute-start.4 = (bf16[128,512]{1,0:T(8,128)(2,1)S(1)}, bf16[128,512]{1,0:T(8,128)(2,1)S(1)}, u32[]{:S(2)}, u32[]{:S(2)}) collective-permute-start(bf16[128,512]{1,0:T(8,128)(2,1)S(1)} %get-tuple-element.52.seen.send), channel_id=1, source_target_pairs={{0,12},{4,8},{8,4},{12,0},{1,13},{5,9},{9,5},{13,1},{2,14},{6,10},... | collective-permute-start | bytes 393224 | tf_op jit(solution)/shard_map/ppermute | solution.py:17
  18.4 8.4 %collective-permute-start.6 = (bf16[128,768]{1,0:T(8,128)(2,1)S(1)}, bf16[128,768]{1,0:T(8,128)(2,1)S(1)}, u32[]{:S(2)}, u32[]{:S(2)}) collective-permute-start(bf16[128,768]{1,0:T(8,128)(2,1)S(1)} %shard_map.88.seen.late), channel_id=1, source_target_pairs={{0,4},{4,0},{8,12},{12,8},{1,5},{5,1},{9,13},{13,9},{2,6},{6,2},{1... | collective-permute-start | bytes 589832 | tf_op jit(solution)/shard_map/ppermute | solution.py:17
  18.9 6.4 %collective-permute-start.11 = (bf16[128,512]{1,0:T(8,128)(2,1)S(1)}, bf16[128,512]{1,0:T(8,128)(2,1)S(1)}, u32[]{:S(2)}, u32[]{:S(2)}) collective-permute-start(bf16[128,512]{1,0:T(8,128)(2,1)S(1)} %shard_map.92.a), channel_id=1, source_target_pairs={{0,2},{1,3},{2,0},{3,1},{4,6},{5,7},{6,4},{7,5},{8,10},{9,11},{10,... | collective-permute-start | bytes 393224 | tf_op jit(solution)/shard_map/ppermute | solution.py:17
  22.5 4.3 %collective-permute-start.8 = (bf16[128,256]{1,0:T(8,128)(2,1)S(1)}, bf16[128,256]{1,0:T(8,128)(2,1)S(1)}, u32[]{:S(2)}, u32[]{:S(2)}) collective-permute-start(bf16[128,256]{1,0:T(8,128)(2,1)S(1)} %shard_map.89.seen.a), channel_id=1, source_target_pairs={{0,2},{1,3},{2,0},{3,1},{4,6},{5,7},{6,4},{7,5},{8,10},{9,11},{10,... | collective-permute-start | bytes 196616 | tf_op jit(solution)/shard_map/ppermute | solution.py:17
  24.1 4.2 %collective-permute-start.10 = (bf16[128,512]{1,0:T(8,128)(2,1)S(1)}, bf16[128,512]{1,0:T(8,128)(2,1)S(1)}, u32[]{:S(2)}, u32[]{:S(2)}) collective-permute-start(bf16[128,512]{1,0:T(8,128)(2,1)S(1)} %shard_map.92.a), channel_id=1, source_target_pairs={{0,1},{1,0},{2,3},{3,2},{4,5},{5,4},{6,7},{7,6},{8,9},{9,8},{10,11... | collective-permute-start | bytes 393224 | tf_op jit(solution)/shard_map/ppermute | solution.py:17
  24.8 3.6 %collective-permute-start.7 = (bf16[128,256]{1,0:T(8,128)(2,1)S(1)}, bf16[128,256]{1,0:T(8,128)(2,1)S(1)}, u32[]{:S(2)}, u32[]{:S(2)}) collective-permute-start(bf16[128,256]{1,0:T(8,128)(2,1)S(1)} %shard_map.89.seen.a), channel_id=1, source_target_pairs={{0,1},{1,0},{2,3},{3,2},{4,5},{5,4},{6,7},{7,6},{8,9},{9,8},{10,11... | collective-permute-start | bytes 196616 | tf_op jit(solution)/shard_map/ppermute | solution.py:17
  25.4 5.5 %collective-permute-start.14 = (bf16[128,512]{1,0:T(8,128)(2,1)S(1)}, bf16[128,512]{1,0:T(8,128)(2,1)S(1)}, u32[]{:S(2)}, u32[]{:S(2)}) collective-permute-start(bf16[128,512]{1,0:T(8,128)(2,1)S(1)} %get-tuple-element.66.z), channel_id=1, source_target_pairs={{0,4},{4,0},{8,12},{12,8},{1,5},{5,1},{9,13},{13,9},{2,6},{6,2},{1... | collective-permute-start | bytes 393224 | tf_op jit(solution)/shard_map/ppermute | solution.py:17
  26.9 1.4 %collective-permute-start.12 = (bf16[128,512]{1,0:T(8,128)(2,1)S(1)}, bf16[128,512]{1,0:T(8,128)(2,1)S(1)}, u32[]{:S(2)}, u32[]{:S(2)}) collective-permute-start(bf16[128,512]{1,0:T(8,128)(2,1)S(1)} %collective-permute-done.11.c), channel_id=1, source_target_pairs={{0,1},{1,0},{2,3},{3,2},{4,5},{5,4},{6,7},{7,6},{8,9},{9,8},{10,11... | collective-permute-start | bytes 393224 | tf_op jit(solution)/shard_map/ppermute | solution.py:17
  26.9 1.5 %collective-permute-start.9 = (bf16[128,256]{1,0:T(8,128)(2,1)S(1)}, bf16[128,256]{1,0:T(8,128)(2,1)S(1)}, u32[]{:S(2)}, u32[]{:S(2)}) collective-permute-start(bf16[128,256]{1,0:T(8,128)(2,1)S(1)} %collective-permute-done.8.c), channel_id=1, source_target_pairs={{0,1},{1,0},{2,3},{3,2},{4,5},{5,4},{6,7},{7,6},{8,9},{9,8},{10,11... | collective-permute-start | bytes 196616 | tf_op jit(solution)/shard_map/ppermute | solution.py:17
  29.0 5.7 %collective-permute-start.13 = (bf16[128,512]{1,0:T(8,128)(2,1)S(1)}, bf16[128,512]{1,0:T(8,128)(2,1)S(1)}, u32[]{:S(2)}, u32[]{:S(2)}) collective-permute-start(bf16[128,512]{1,0:T(8,128)(2,1)S(1)} %shard_map.94.back), channel_id=1, source_target_pairs={{0,4},{4,0},{8,12},{12,8},{1,5},{5,1},{9,13},{13,9},{2,6},{6,2},{1... | collective-permute-start | bytes 393224 | tf_op jit(solution)/shard_map/ppermute | solution.py:17
  34.8 6.2 %collective-permute-start.15 = (bf16[128,256]{1,0:T(8,128)(2,1)S(1)}, bf16[128,256]{1,0:T(8,128)(2,1)S(1)}, u32[]{:S(2)}, u32[]{:S(2)}) collective-permute-start(bf16[128,256]{1,0:T(8,128)(2,1)S(1)} %get-tuple-element.68.seen.half5), channel_id=1, source_target_pairs={{0,12},{4,8},{8,4},{12,0},{1,13},{5,9},{9,5},{13,1},{2,14},{6,10},... | collective-permute-start | bytes 196616 | tf_op jit(solution)/shard_map/ppermute | solution.py:17

commit v18 on v17

--- a/solution.py
+++ b/solution.py
@@ -134,6 +134,8 @@
     s2 = 1.0 / math.sqrt(rows * 2)
     st = 1.0 / math.sqrt(rows * 4)
     blocks = rows // rank
+    upper = (blocks + 1) // 2
+    groups = [(i, n) for i, n in ((0, upper), (upper, blocks - upper)) if n]
     square, wide, tall = (rank, rank), (rank, cols), (rows, cols)
 
     def span(i, n=1):
@@ -149,7 +151,6 @@
             return copy
 
         first = load(rb_hbm.at[0], rb.at[0], 2, 0)
-        groups = [(i, min(2, blocks - i)) for i in range(0, blocks, 2)]
         copies = []
         for i, n in groups:
             copies.append(load(rhs_hbm.at[0, span(i, n), :], rhs_v.at[span(i, n), :], 0, i))
@@ -165,9 +166,9 @@
         bases = [load(source, target, 2, 1 + i) for i, (source, target) in enumerate(pairs)]
         first.wait()
         basis_t[...] = rb[0, 0].T
-        for i, n in groups:
-            copies[i].wait()
-            copies[i + 1].wait()
+        for (i, n), k in zip(groups, range(0, len(copies), 2)):
+            copies[k].wait()
+            copies[k + 1].wait()
             x_ref[span(i, n), :] = dot(
                 inv_ref[span(i, n), span(0, i + n)], rhs_v[span(0, i + n), :].astype(BF)
             )
@@ -218,15 +219,17 @@
     )
     early_sib = swap(early, "leaf", 1)
 
-    def flip_body(lb, rb, tl, tr, seen, out, out2):
+    def flip_body(lb, rb, tl, tr, seen, out, out2, out3):
         for i, basis in enumerate((rb[1, 0], tr[0], tl[0])):
             out[span(i), :] = basis.T
         for i, basis in enumerate((lb[1, 0], lb[0, 0])):
             out2[span(i), :] = basis.T
-
-    bases_t, lefts_t = call(
+        for i, basis in enumerate((tl[0], tr[0], rb[1, 0], rb[0, 0])):
+            out3[:, span(i)] = basis
+
+    bases_t, lefts_t, updates = call(
         flip_body,
-        [((3 * rank, rows), BF), ((2 * rank, rows), BF)],
+        [((3 * rank, rows), BF), ((2 * rank, rows), BF), ((rows, 4 * rank), BF)],
         lb,
         rb,
         tl,
@@ -393,20 +396,17 @@
         micros=0.1,
     )
 
-    def under_body(x2, rb, tl, tr, inv, seen, out2, under):
-        for c in range(blocks):
-            column = inv[c * rank :, span(c)]
-            out2[span(c), :] = dot_t(column, x2[c * rank :, :])
-            for i, basis in enumerate((tl[0], tr[0], rb[1, 0], rb[0, 0])):
-                under[span(c), span(i)] = dot_t(column, basis[c * rank :, :]).astype(BF)
+    def under_body(x2, updates, inv, seen, out2, under):
+        for i, n in groups:
+            column = inv[i * rank :, span(i, n)]
+            out2[span(i, n), :] = dot_t(column, x2[i * rank :, :])
+            under[span(i, n), :] = dot_t(column, updates[i * rank :, :]).astype(BF)
 
     out2, under = call(
         under_body,
         [(tall, f32), ((rows, 4 * rank), BF)],
         state2,
-        rb,
-        tl,
-        tr,
+        updates,
         inverse,
         late_sib,
         micros=3,

time: 42.6 us -> 42.7 us (level)
  no operation moved by 1% of the time
where the time goes in v18:
time: 42.7 us; the launch traced here: 42.5 us
  starting transfers between devices  23.8 us (56%)
  waiting for transfers between devices  9.75 us (23%)
  Pallas kernels  8.83 us (21%)
    ppermute x16, starting transfers between devices, swap(): return lax.ppermute(value, axis, pairs)  23.8 us
    ppermute x16, waiting for transfers between devices, swap(): return lax.ppermute(value, axis, pairs)  9.75 us
    pallas_call x16, Pallas kernels, call(): pl.pallas_call(body, out_shape=[jax.ShapeDtypeStruct(shape, dtype) if hbm...  8.83 us
  transfers between devices with their start and end apart: 16, of which 7 were waited for; matrix products, arithmetic and copies ran while one was open for 0% of the time, Pallas kernels for 12%

profile of v18, /device:TPU:0, one launch (start us, length us, event | category | flops | bytes accessed | tf_op | source)
XLA Modules:
  0.0 42.5 jit_solution(2314417170310273857)
XLA Ops:
  0.0 2.1 %shard_map.82 = (f32[640,256]{1,0:T(8,128)S(1)}, bf16[128,256]{1,0:T(8,128)(2,1)S(1)}, bf16[640,640]{1,0:T(8,128)(2,1)S(1)}, bf16[2,1,640,128]{3,2,1,0:T(8,128)(...) custom-call(f32[1,640,256]{2,1,0:T(8,128)} %rhs_hbm.1, ...), custom_call_target="tpu_custom_call" | custom-call | flops 1000000000 | tf_op jit(solution)/shard_map/pallas_call | solution.py:88
  2.7 2.6 %collective-permute-start = (bf16[128,256]{1,0:T(8,128)(2,1)S(1)}, bf16[128,256]{1,0:T(8,128)(2,1)S(1)}, u32[]{:S(2)}, u32[]{:S(2)}) collective-permute-start(bf16[128,256]{1,0:T(8,128)(2,1)S(1)} %get-tuple-element.40.p), channel_id=1, source_target_pairs={{0,4},{4,0},{8,12},{12,8},{1,5},{5,1},{9,13},{13,9},{2,6},{6,2},{1... | collective-permute-start | bytes 196616 | tf_op jit(solution)/shard_map/ppermute | solution.py:17
  5.3 0.6 %shard_map.83 = (bf16[128,384]{1,0:T(8,128)(2,1)S(1)}, bf16[128,256]{1,0:T(8,128)(2,1)S(1)}) custom-call(bf16[2,1,640,128]{3,2,1,0:T(8,128)(2,1)S(1)} %get-tuple-element.41.lb, bf16[2,1,128,256]{3,2,1,0:T(8,128)(2,1)S(1)} %get-tuple-element.42.caps, bf16[1,640,128]{2,1,0:T(8,128)(2,1)S(1)} %get-tuple-element.44.tl, ...), custom_call_target="tpu_custom_call" | custom-call | flops 10000000000 | tf_op jit(solution)/shard_map/pallas_call | solution.py:88
  5.9 1.2 %collective-permute-start.3 = (bf16[128,384]{1,0:T(8,128)(2,1)S(1)}, bf16[128,384]{1,0:T(8,128)(2,1)S(1)}, u32[]{:S(2)}, u32[]{:S(2)}) collective-permute-start(bf16[128,384]{1,0:T(8,128)(2,1)S(1)} %get-tuple-element.46.seen.own), channel_id=1, source_target_pairs={{0,4},{4,0},{8,12},{12,8},{1,5},{5,1},{9,13},{13,9},{2,6},{6,2},{1... | collective-permute-start | bytes 294920 | tf_op jit(solution)/shard_map/ppermute | solution.py:17
  7.5 0.6 %collective-permute-done.p_sib = bf16[128,256]{1,0:T(8,128)(2,1)S(1)} collective-permute-done((bf16[128,256]{1,0:T(8,128)(2,1)S(1)}, bf16[128,256]{1,0:T(8,128)(2,1)S(1)}, u32[]{:S(2)}, u32[]{:S(2)}) %collective-permute-start) | collective-permute-done | bytes 65568 | tf_op jit(solution)/shard_map/ppermute | solution.py:17
  8.0 0.8 %shard_map.85 = (f32[640,256]{1,0:T(8,128)S(1)}, bf16[128,512]{1,0:T(8,128)(2,1)S(1)}, f32[128,512]{1,0:T(8,128)S(1)}) custom-call(f32[640,256]{1,0:T(8,128)S(1)} %get-tuple-element.39.x0, bf16[128,256]{1,0:T(8,128)(2,1)S(1)} %get-tuple-element.40.p, bf16[128,256]{1,0:T(8,128)(2,1)S(1)} %collective-permute-done.p_sib, ...), custom_call_target="tpu_custom_call" | custom-call | flops 3000000000 | tf_op jit(solution)/shard_map/pallas_call | solution.py:88
  8.8 1.8 %collective-permute-start.2 = (bf16[128,512]{1,0:T(8,128)(2,1)S(1)}, bf16[128,512]{1,0:T(8,128)(2,1)S(1)}, u32[]{:S(2)}, u32[]{:S(2)}) collective-permute-start(bf16[128,512]{1,0:T(8,128)(2,1)S(1)} %get-tuple-element.50), channel_id=1, source_target_pairs={{0,4},{4,0},{8,12},{12,8},{1,5},{5,1},{9,13},{13,9},{2,6},{6,2},{1... | collective-permute-start | bytes 393224 | tf_op jit(solution)/shard_map/ppermute | solution.py:17
  10.9 3.3 %collective-permute-start.5 = (bf16[128,256]{1,0:T(8,128)(2,1)S(1)}, bf16[128,256]{1,0:T(8,128)(2,1)S(1)}, u32[]{:S(2)}, u32[]{:S(2)}) collective-permute-start(bf16[128,256]{1,0:T(8,128)(2,1)S(1)} %get-tuple-element.56), channel_id=1, source_target_pairs={{0,12},{4,8},{8,4},{12,0},{1,13},{5,9},{9,5},{13,1},{2,14},{6,10},... | collective-permute-start | bytes 196616 | tf_op jit(solution)/shard_map/ppermute | solution.py:17
  14.3 3.6 %collective-permute-start.4 = (bf16[128,512]{1,0:T(8,128)(2,1)S(1)}, bf16[128,512]{1,0:T(8,128)(2,1)S(1)}, u32[]{:S(2)}, u32[]{:S(2)}) collective-permute-start(bf16[128,512]{1,0:T(8,128)(2,1)S(1)} %get-tuple-element.53.seen.send), channel_id=1, source_target_pairs={{0,12},{4,8},{8,4},{12,0},{1,13},{5,9},{9,5},{13,1},{2,14},{6,10},... | collective-permute-start | bytes 393224 | tf_op jit(solution)/shard_map/ppermute | solution.py:17
  17.9 0.5 %shard_map.88.seen.late = bf16[128,768]{1,0:T(8,128)(2,1)S(1)} custom-call(bf16[2,1,640,128]{3,2,1,0:T(8,128)(2,1)S(1)} %get-tuple-element.41.lb, bf16[2,1,640,128]{3,2,1,0:T(8,128)(2,1)S(1)} %get-tuple-element.43.rb, bf16[2,1,128,256]{3,2,1,0:T(8,128)(2,1)S(1)} %get-tuple-element.42.caps, bf16[1,640,128]{2,1,0:T(8,128)(2,1)S(1)} %get-tuple-element.44.tl, ...), custom_call_target="tpu_custom_call" | custom-call | flops 5000000000 | tf_op jit(solution)/shard_map/pallas_call | solution.py:88
  18.9 1.6 %collective-permute-start.11 = (bf16[128,512]{1,0:T(8,128)(2,1)S(1)}, bf16[128,512]{1,0:T(8,128)(2,1)S(1)}, u32[]{:S(2)}, u32[]{:S(2)}) collective-permute-start(bf16[128,512]{1,0:T(8,128)(2,1)S(1)} %shard_map.92.a), channel_id=1, source_target_pairs={{0,2},{1,3},{2,0},{3,1},{4,6},{5,7},{6,4},{7,5},{8,10},{9,11},{10,... | collective-permute-start | bytes 393224 | tf_op jit(solution)/shard_map/ppermute | solution.py:17
  20.5 1.9 %collective-permute-done.4.far = bf16[128,512]{1,0:T(8,128)(2,1)S(1)} collective-permute-done((bf16[128,512]{1,0:T(8,128)(2,1)S(1)}, bf16[128,512]{1,0:T(8,128)(2,1)S(1)}, u32[]{:S(2)}, u32[]{:S(2)}) %collective-permute-start.4) | collective-permute-done | bytes 131104 | tf_op jit(solution)/shard_map/ppermute | solution.py:17
  22.6 1.6 %collective-permute-start.8 = (bf16[128,256]{1,0:T(8,128)(2,1)S(1)}, bf16[128,256]{1,0:T(8,128)(2,1)S(1)}, u32[]{:S(2)}, u32[]{:S(2)}) collective-permute-start(bf16[128,256]{1,0:T(8,128)(2,1)S(1)} %shard_map.89.seen.a), channel_id=1, source_target_pairs={{0,2},{1,3},{2,0},{3,1},{4,6},{5,7},{6,4},{7,5},{8,10},{9,11},{10,... | collective-permute-start | bytes 196616 | tf_op jit(solution)/shard_map/ppermute | solution.py:17
  24.1 0.7 %shard_map.90 = (bf16[640,256]{1,0:T(8,128)(2,1)S(1)}, f32[128,256]{1,0:T(8,128)S(1)}, bf16[128,512]{1,0:T(8,128)(2,1)S(1)}) custom-call(f32[640,256]{1,0:T(8,128)S(1)} %get-tuple-element.48.seen.x1, bf16[128,512]{1,0:T(8,128)(2,1)S(1)} %get-tuple-element.53.seen.send, bf16[128,512]{1,0:T(8,128)(2,1)S(1)} %collective-permute-done.4.far, ...), custom_call_target="tpu_custom_call" | custom-call | flops 100000000 | tf_op jit(solution)/shard_map/pallas_call | solution.py:88
  24.8 0.6 %collective-permute-start.7 = (bf16[128,256]{1,0:T(8,128)(2,1)S(1)}, bf16[128,256]{1,0:T(8,128)(2,1)S(1)}, u32[]{:S(2)}, u32[]{:S(2)}) collective-permute-start(bf16[128,256]{1,0:T(8,128)(2,1)S(1)} %shard_map.89.seen.a), channel_id=1, source_target_pairs={{0,1},{1,0},{2,3},{3,2},{4,5},{5,4},{6,7},{7,6},{8,9},{9,8},{10,11... | collective-permute-start | bytes 196616 | tf_op jit(solution)/shard_map/ppermute | solution.py:17
  25.4 1.2 %collective-permute-start.14 = (bf16[128,512]{1,0:T(8,128)(2,1)S(1)}, bf16[128,512]{1,0:T(8,128)(2,1)S(1)}, u32[]{:S(2)}, u32[]{:S(2)}) collective-permute-start(bf16[128,512]{1,0:T(8,128)(2,1)S(1)} %get-tuple-element.68.z), channel_id=1, source_target_pairs={{0,4},{4,0},{8,12},{12,8},{1,5},{5,1},{9,13},{13,9},{2,6},{6,2},{1... | collective-permute-start | bytes 393224 | tf_op jit(solution)/shard_map/ppermute | solution.py:17
  27.4 0.8 %shard_map.91 = (f32[640,256]{1,0:T(8,128)S(1)}, bf16[640,512]{1,0:T(8,128)(2,1)S(1)}) custom-call(bf16[640,256]{1,0:T(8,128)(2,1)S(1)} %get-tuple-element.57.x2, bf16[640,512]{1,0:T(8,128)(2,1)S(1)} %get-tuple-element.58.updates, bf16[640,640]{1,0:T(8,128)(2,1)S(1)} %get-tuple-element.59.inv, bf16[128,768]{1,0:T(8,128)(2,1)S(1)} %collective-permute-done.6.seen.late_sib), custom_call_target="tpu_custom_call" | custom-call | flops 3000000000 | tf_op jit(solution)/shard_map/pallas_call | solution.py:88
  28.4 0.5 %shard_map.94.back = bf16[128,512]{1,0:T(8,128)(2,1)S(1)} custom-call(bf16[128,256]{1,0:T(8,128)(2,1)S(1)} %shard_map.89.seen.a, bf16[128,256]{1,0:T(8,128)(2,1)S(1)} %collective-permute-done.7.b, bf16[128,256]{1,0:T(8,128)(2,1)S(1)} %collective-permute-done.8.c, bf16[128,256]{1,0:T(8,128)(2,1)S(1)} %collective-permute-done.9.d, ...), custom_call_target="tpu_custom_call" | custom-call | flops 1000000000 | tf_op jit(solution)/shard_map/pallas_call | solution.py:88
  28.9 1.2 %collective-permute-start.13 = (bf16[128,512]{1,0:T(8,128)(2,1)S(1)}, bf16[128,512]{1,0:T(8,128)(2,1)S(1)}, u32[]{:S(2)}, u32[]{:S(2)}) collective-permute-start(bf16[128,512]{1,0:T(8,128)(2,1)S(1)} %shard_map.94.back), channel_id=1, source_target_pairs={{0,4},{4,0},{8,12},{12,8},{1,5},{5,1},{9,13},{13,9},{2,6},{6,2},{1... | collective-permute-start | bytes 393224 | tf_op jit(solution)/shard_map/ppermute | solution.py:17
  30.2 0.7 %collective-permute-done.14.z_sib = bf16[128,512]{1,0:T(8,128)(2,1)S(1)} collective-permute-done((bf16[128,512]{1,0:T(8,128)(2,1)S(1)}, bf16[128,512]{1,0:T(8,128)(2,1)S(1)}, u32[]{:S(2)}, u32[]{:S(2)}) %collective-permute-start.14) | collective-permute-done | bytes 131104 | tf_op jit(solution)/shard_map/ppermute | solution.py:17
  30.9 3.8 %collective-permute-done.13.back_sib = bf16[128,512]{1,0:T(8,128)(2,1)S(1)} collective-permute-done((bf16[128,512]{1,0:T(8,128)(2,1)S(1)}, bf16[128,512]{1,0:T(8,128)(2,1)S(1)}, u32[]{:S(2)}, u32[]{:S(2)}) %collective-permute-start.13) | collective-permute-done | bytes 131104 | tf_op jit(solution)/shard_map/ppermute | solution.py:17
  34.9 3.8 %collective-permute-start.15 = (bf16[128,256]{1,0:T(8,128)(2,1)S(1)}, bf16[128,256]{1,0:T(8,128)(2,1)S(1)}, u32[]{:S(2)}, u32[]{:S(2)}) collective-permute-start(bf16[128,256]{1,0:T(8,128)(2,1)S(1)} %get-tuple-element.70.seen.half5), channel_id=1, source_target_pairs={{0,12},{4,8},{8,4},{12,0},{1,13},{5,9},{9,5},{13,1},{2,14},{6,10},... | collective-permute-start | bytes 196616 | tf_op jit(solution)/shard_map/ppermute | solution.py:17
  39.0 2.1 %collective-permute-done.15.half5_far = bf16[128,256]{1,0:T(8,128)(2,1)S(1)} collective-permute-done((bf16[128,256]{1,0:T(8,128)(2,1)S(1)}, bf16[128,256]{1,0:T(8,128)(2,1)S(1)}, u32[]{:S(2)}, u32[]{:S(2)}) %collective-permute-start.15) | collective-permute-done | bytes 65568 | tf_op jit(solution)/shard_map/ppermute | solution.py:17
  41.1 1.4 %shard_map.97 = f32[1,640,256]{2,1,0:T(8,128)} custom-call(f32[640,256]{1,0:T(8,128)S(1)} %get-tuple-element.71.out3, bf16[640,512]{1,0:T(8,128)(2,1)S(1)} %get-tuple-element.61.under, bf16[128,256]{1,0:T(8,128)(2,1)S(1)} %get-tuple-element.70.seen.half5, bf16[128,256]{1,0:T(8,128)(2,1)S(1)} %collective-permute-done.15.half5_far, ...), custom_call_target="tpu_custom_call" | custom-call | flops 1000000000 | tf_op jit(solution)/shard_map/pallas_call | solution.py:88
  (26 shorter events, 3.5 us)
Async XLA Ops:
  2.2 3.2 %collective-permute-start.1 = (bf16[128,256]{1,0:T(8,128)(2,1)S(1)}, bf16[128,256]{1,0:T(8,128)(2,1)S(1)}, u32[]{:S(2)}, u32[]{:S(2)}) collective-permute-start(bf16[128,256]{1,0:T(8,128)(2,1)S(1)} %get-tuple-element.40.p), channel_id=1, source_target_pairs={{0,1},{1,0},{2,3},{3,2},{4,5},{5,4},{6,7},{7,6},{8,9},{9,8},{10,11... | collective-permute-start | bytes 196616 | tf_op jit(solution)/shard_map/ppermute | solution.py:17
  2.7 5.3 %collective-permute-start = (bf16[128,256]{1,0:T(8,128)(2,1)S(1)}, bf16[128,256]{1,0:T(8,128)(2,1)S(1)}, u32[]{:S(2)}, u32[]{:S(2)}) collective-permute-start(bf16[128,256]{1,0:T(8,128)(2,1)S(1)} %get-tuple-element.40.p), channel_id=1, source_target_pairs={{0,4},{4,0},{8,12},{12,8},{1,5},{5,1},{9,13},{13,9},{2,6},{6,2},{1... | collective-permute-start | bytes 196616 | tf_op jit(solution)/shard_map/ppermute | solution.py:17
  5.9 4.9 %collective-permute-start.3 = (bf16[128,384]{1,0:T(8,128)(2,1)S(1)}, bf16[128,384]{1,0:T(8,128)(2,1)S(1)}, u32[]{:S(2)}, u32[]{:S(2)}) collective-permute-start(bf16[128,384]{1,0:T(8,128)(2,1)S(1)} %get-tuple-element.46.seen.own), channel_id=1, source_target_pairs={{0,4},{4,0},{8,12},{12,8},{1,5},{5,1},{9,13},{13,9},{2,6},{6,2},{1... | collective-permute-start | bytes 294920 | tf_op jit(solution)/shard_map/ppermute | solution.py:17
  8.8 5.4 %collective-permute-start.2 = (bf16[128,512]{1,0:T(8,128)(2,1)S(1)}, bf16[128,512]{1,0:T(8,128)(2,1)S(1)}, u32[]{:S(2)}, u32[]{:S(2)}) collective-permute-start(bf16[128,512]{1,0:T(8,128)(2,1)S(1)} %get-tuple-element.50), channel_id=1, source_target_pairs={{0,4},{4,0},{8,12},{12,8},{1,5},{5,1},{9,13},{13,9},{2,6},{6,2},{1... | collective-permute-start | bytes 393224 | tf_op jit(solution)/shard_map/ppermute | solution.py:17
  10.9 7.0 %collective-permute-start.5 = (bf16[128,256]{1,0:T(8,128)(2,1)S(1)}, bf16[128,256]{1,0:T(8,128)(2,1)S(1)}, u32[]{:S(2)}, u32[]{:S(2)}) collective-permute-start(bf16[128,256]{1,0:T(8,128)(2,1)S(1)} %get-tuple-element.56), channel_id=1, source_target_pairs={{0,12},{4,8},{8,4},{12,0},{1,13},{5,9},{9,5},{13,1},{2,14},{6,10},... | collective-permute-start | bytes 196616 | tf_op jit(solution)/shard_map/ppermute | solution.py:17
  14.3 4.5 %copy-start = (bf16[128,512]{1,0:T(8,128)(2,1)S(1)}, bf16[128,512]{1,0:T(8,128)(2,1)}, u32[]{:S(2)}) copy-start(bf16[128,512]{1,0:T(8,128)(2,1)} %caps.3) | copy-start | bytes 393220
  14.3 8.1 %collective-permute-start.4 = (bf16[128,512]{1,0:T(8,128)(2,1)S(1)}, bf16[128,512]{1,0:T(8,128)(2,1)S(1)}, u32[]{:S(2)}, u32[]{:S(2)}) collective-permute-start(bf16[128,512]{1,0:T(8,128)(2,1)S(1)} %get-tuple-element.53.seen.send), channel_id=1, source_target_pairs={{0,12},{4,8},{8,4},{12,0},{1,13},{5,9},{9,5},{13,1},{2,14},{6,10},... | collective-permute-start | bytes 393224 | tf_op jit(solution)/shard_map/ppermute | solution.py:17
  18.5 8.5 %collective-permute-start.6 = (bf16[128,768]{1,0:T(8,128)(2,1)S(1)}, bf16[128,768]{1,0:T(8,128)(2,1)S(1)}, u32[]{:S(2)}, u32[]{:S(2)}) collective-permute-start(bf16[128,768]{1,0:T(8,128)(2,1)S(1)} %shard_map.88.seen.late), channel_id=1, source_target_pairs={{0,4},{4,0},{8,12},{12,8},{1,5},{5,1},{9,13},{13,9},{2,6},{6,2},{1... | collective-permute-start | bytes 589832 | tf_op jit(solution)/shard_map/ppermute | solution.py:17
  18.9 6.4 %collective-permute-start.11 = (bf16[128,512]{1,0:T(8,128)(2,1)S(1)}, bf16[128,512]{1,0:T(8,128)(2,1)S(1)}, u32[]{:S(2)}, u32[]{:S(2)}) collective-permute-start(bf16[128,512]{1,0:T(8,128)(2,1)S(1)} %shard_map.92.a), channel_id=1, source_target_pairs={{0,2},{1,3},{2,0},{3,1},{4,6},{5,7},{6,4},{7,5},{8,10},{9,11},{10,... | collective-permute-start | bytes 393224 | tf_op jit(solution)/shard_map/ppermute | solution.py:17
  22.6 4.3 %collective-permute-start.8 = (bf16[128,256]{1,0:T(8,128)(2,1)S(1)}, bf16[128,256]{1,0:T(8,128)(2,1)S(1)}, u32[]{:S(2)}, u32[]{:S(2)}) collective-permute-start(bf16[128,256]{1,0:T(8,128)(2,1)S(1)} %shard_map.89.seen.a), channel_id=1, source_target_pairs={{0,2},{1,3},{2,0},{3,1},{4,6},{5,7},{6,4},{7,5},{8,10},{9,11},{10,... | collective-permute-start | bytes 196616 | tf_op jit(solution)/shard_map/ppermute | solution.py:17
  24.1 4.1 %collective-permute-start.10 = (bf16[128,512]{1,0:T(8,128)(2,1)S(1)}, bf16[128,512]{1,0:T(8,128)(2,1)S(1)}, u32[]{:S(2)}, u32[]{:S(2)}) collective-permute-start(bf16[128,512]{1,0:T(8,128)(2,1)S(1)} %shard_map.92.a), channel_id=1, source_target_pairs={{0,1},{1,0},{2,3},{3,2},{4,5},{5,4},{6,7},{7,6},{8,9},{9,8},{10,11... | collective-permute-start | bytes 393224 | tf_op jit(solution)/shard_map/ppermute | solution.py:17
  24.8 3.6 %collective-permute-start.7 = (bf16[128,256]{1,0:T(8,128)(2,1)S(1)}, bf16[128,256]{1,0:T(8,128)(2,1)S(1)}, u32[]{:S(2)}, u32[]{:S(2)}) collective-permute-start(bf16[128,256]{1,0:T(8,128)(2,1)S(1)} %shard_map.89.seen.a), channel_id=1, source_target_pairs={{0,1},{1,0},{2,3},{3,2},{4,5},{5,4},{6,7},{7,6},{8,9},{9,8},{10,11... | collective-permute-start | bytes 196616 | tf_op jit(solution)/shard_map/ppermute | solution.py:17
  25.4 5.5 %collective-permute-start.14 = (bf16[128,512]{1,0:T(8,128)(2,1)S(1)}, bf16[128,512]{1,0:T(8,128)(2,1)S(1)}, u32[]{:S(2)}, u32[]{:S(2)}) collective-permute-start(bf16[128,512]{1,0:T(8,128)(2,1)S(1)} %get-tuple-element.68.z), channel_id=1, source_target_pairs={{0,4},{4,0},{8,12},{12,8},{1,5},{5,1},{9,13},{13,9},{2,6},{6,2},{1... | collective-permute-start | bytes 393224 | tf_op jit(solution)/shard_map/ppermute | solution.py:17
  26.9 1.3 %collective-permute-start.12 = (bf16[128,512]{1,0:T(8,128)(2,1)S(1)}, bf16[128,512]{1,0:T(8,128)(2,1)S(1)}, u32[]{:S(2)}, u32[]{:S(2)}) collective-permute-start(bf16[128,512]{1,0:T(8,128)(2,1)S(1)} %collective-permute-done.11.c), channel_id=1, source_target_pairs={{0,1},{1,0},{2,3},{3,2},{4,5},{5,4},{6,7},{7,6},{8,9},{9,8},{10,11... | collective-permute-start | bytes 393224 | tf_op jit(solution)/shard_map/ppermute | solution.py:17
  26.9 1.5 %collective-permute-start.9 = (bf16[128,256]{1,0:T(8,128)(2,1)S(1)}, bf16[128,256]{1,0:T(8,128)(2,1)S(1)}, u32[]{:S(2)}, u32[]{:S(2)}) collective-permute-start(bf16[128,256]{1,0:T(8,128)(2,1)S(1)} %collective-permute-done.8.c), channel_id=1, source_target_pairs={{0,1},{1,0},{2,3},{3,2},{4,5},{5,4},{6,7},{7,6},{8,9},{9,8},{10,11... | collective-permute-start | bytes 196616 | tf_op jit(solution)/shard_map/ppermute | solution.py:17
  28.9 5.7 %collective-permute-start.13 = (bf16[128,512]{1,0:T(8,128)(2,1)S(1)}, bf16[128,512]{1,0:T(8,128)(2,1)S(1)}, u32[]{:S(2)}, u32[]{:S(2)}) collective-permute-start(bf16[128,512]{1,0:T(8,128)(2,1)S(1)} %shard_map.94.back), channel_id=1, source_target_pairs={{0,4},{4,0},{8,12},{12,8},{1,5},{5,1},{9,13},{13,9},{2,6},{6,2},{1... | collective-permute-start | bytes 393224 | tf_op jit(solution)/shard_map/ppermute | solution.py:17
  34.9 6.2 %collective-permute-start.15 = (bf16[128,256]{1,0:T(8,128)(2,1)S(1)}, bf16[128,256]{1,0:T(8,128)(2,1)S(1)}, u32[]{:S(2)}, u32[]{:S(2)}) collective-permute-start(bf16[128,256]{1,0:T(8,128)(2,1)S(1)} %get-tuple-element.70.seen.half5), channel_id=1, source_target_pairs={{0,12},{4,8},{8,4},{12,0},{1,13},{5,9},{9,5},{13,1},{2,14},{6,10},... | collective-permute-start | bytes 196616 | tf_op jit(solution)/shard_map/ppermute | solution.py:17

commit v19 on v17

--- a/solution.py
+++ b/solution.py
@@ -452,7 +452,7 @@
         scratch=[pltpu.VMEM((2, rank, 2 * cols), BF)],
         micros=0.3,
     )
-    half5_far = swap(half5, "leaf", 3)
+    half5_far = swap(half5, "leaf", 2)
 
     def part_body(out2, under, both, z, z_sib, late, late_sib, seen, proj, out3):
         def down(zs, gram):

time: 42.6 us -> 42.6 us (level)
  waiting for transfers between devices: 9.59 us -> 10.5 us
  starting transfers between devices: 23.8 us -> 22.9 us
    ppermute x16, starting transfers between devices: 23.8 us -> 22.9 us  [swap(): return lax.ppermute(value, axis, pairs)]
    ppermute x16, waiting for transfers between devices: 9.59 us -> 10.5 us  [swap(): return lax.ppermute(value, axis, pairs)]
where the time goes in v19:
time: 42.6 us; the launch traced here: 42.4 us
  starting transfers between devices  22.9 us (54%)
  waiting for transfers between devices  10.5 us (25%)
  Pallas kernels  8.88 us (21%)
    ppermute x16, starting transfers between devices, swap(): return lax.ppermute(value, axis, pairs)  22.9 us
    ppermute x16, waiting for transfers between devices, swap(): return lax.ppermute(value, axis, pairs)  10.5 us
    pallas_call x16, Pallas kernels, call(): pl.pallas_call(body, out_shape=[jax.ShapeDtypeStruct(shape, dtype) if hbm...  8.88 us
  transfers between devices with their start and end apart: 16, of which 7 were waited for; matrix products, arithmetic and copies ran while one was open for 0% of the time, Pallas kernels for 12%

profile of v19, /device:TPU:0, one launch (start us, length us, event | category | flops | bytes accessed | tf_op | source)
XLA Modules:
  0.0 42.4 jit_solution(9170055032829135951)
XLA Ops:
  0.0 2.1 %shard_map.82 = (f32[640,256]{1,0:T(8,128)S(1)}, bf16[128,256]{1,0:T(8,128)(2,1)S(1)}, bf16[640,640]{1,0:T(8,128)(2,1)S(1)}, bf16[2,1,640,128]{3,2,1,0:T(8,128)(...) custom-call(f32[1,640,256]{2,1,0:T(8,128)} %rhs_hbm.1, ...), custom_call_target="tpu_custom_call" | custom-call | flops 1000000000 | tf_op jit(solution)/shard_map/pallas_call | solution.py:88
  2.6 2.6 %collective-permute-start = (bf16[128,256]{1,0:T(8,128)(2,1)S(1)}, bf16[128,256]{1,0:T(8,128)(2,1)S(1)}, u32[]{:S(2)}, u32[]{:S(2)}) collective-permute-start(bf16[128,256]{1,0:T(8,128)(2,1)S(1)} %get-tuple-element.39.p), channel_id=1, source_target_pairs={{0,4},{4,0},{8,12},{12,8},{1,5},{5,1},{9,13},{13,9},{2,6},{6,2},{1... | collective-permute-start | bytes 196616 | tf_op jit(solution)/shard_map/ppermute | solution.py:17
  5.3 0.6 %shard_map.83 = (bf16[128,384]{1,0:T(8,128)(2,1)S(1)}, bf16[128,256]{1,0:T(8,128)(2,1)S(1)}) custom-call(bf16[2,1,640,128]{3,2,1,0:T(8,128)(2,1)S(1)} %get-tuple-element.40.lb, bf16[2,1,128,256]{3,2,1,0:T(8,128)(2,1)S(1)} %get-tuple-element.41.caps, bf16[1,640,128]{2,1,0:T(8,128)(2,1)S(1)} %get-tuple-element.43.tl, ...), custom_call_target="tpu_custom_call" | custom-call | flops 10000000000 | tf_op jit(solution)/shard_map/pallas_call | solution.py:88
  5.9 1.2 %collective-permute-start.3 = (bf16[128,384]{1,0:T(8,128)(2,1)S(1)}, bf16[128,384]{1,0:T(8,128)(2,1)S(1)}, u32[]{:S(2)}, u32[]{:S(2)}) collective-permute-start(bf16[128,384]{1,0:T(8,128)(2,1)S(1)} %get-tuple-element.45.seen.own), channel_id=1, source_target_pairs={{0,4},{4,0},{8,12},{12,8},{1,5},{5,1},{9,13},{13,9},{2,6},{6,2},{1... | collective-permute-start | bytes 294920 | tf_op jit(solution)/shard_map/ppermute | solution.py:17
  7.4 0.6 %collective-permute-done.p_sib = bf16[128,256]{1,0:T(8,128)(2,1)S(1)} collective-permute-done((bf16[128,256]{1,0:T(8,128)(2,1)S(1)}, bf16[128,256]{1,0:T(8,128)(2,1)S(1)}, u32[]{:S(2)}, u32[]{:S(2)}) %collective-permute-start) | collective-permute-done | bytes 65568 | tf_op jit(solution)/shard_map/ppermute | solution.py:17
  8.0 0.8 %shard_map.85 = (f32[640,256]{1,0:T(8,128)S(1)}, bf16[128,512]{1,0:T(8,128)(2,1)S(1)}, f32[128,512]{1,0:T(8,128)S(1)}) custom-call(f32[640,256]{1,0:T(8,128)S(1)} %get-tuple-element.38.x0, bf16[128,256]{1,0:T(8,128)(2,1)S(1)} %get-tuple-element.39.p, bf16[128,256]{1,0:T(8,128)(2,1)S(1)} %collective-permute-done.p_sib, ...), custom_call_target="tpu_custom_call" | custom-call | flops 3000000000 | tf_op jit(solution)/shard_map/pallas_call | solution.py:88
  8.7 1.8 %collective-permute-start.2 = (bf16[128,512]{1,0:T(8,128)(2,1)S(1)}, bf16[128,512]{1,0:T(8,128)(2,1)S(1)}, u32[]{:S(2)}, u32[]{:S(2)}) collective-permute-start(bf16[128,512]{1,0:T(8,128)(2,1)S(1)} %get-tuple-element.49), channel_id=1, source_target_pairs={{0,4},{4,0},{8,12},{12,8},{1,5},{5,1},{9,13},{13,9},{2,6},{6,2},{1... | collective-permute-start | bytes 393224 | tf_op jit(solution)/shard_map/ppermute | solution.py:17
  10.9 3.3 %collective-permute-start.5 = (bf16[128,256]{1,0:T(8,128)(2,1)S(1)}, bf16[128,256]{1,0:T(8,128)(2,1)S(1)}, u32[]{:S(2)}, u32[]{:S(2)}) collective-permute-start(bf16[128,256]{1,0:T(8,128)(2,1)S(1)} %get-tuple-element.55), channel_id=1, source_target_pairs={{0,12},{4,8},{8,4},{12,0},{1,13},{5,9},{9,5},{13,1},{2,14},{6,10},... | collective-permute-start | bytes 196616 | tf_op jit(solution)/shard_map/ppermute | solution.py:17
  14.3 3.6 %collective-permute-start.4 = (bf16[128,512]{1,0:T(8,128)(2,1)S(1)}, bf16[128,512]{1,0:T(8,128)(2,1)S(1)}, u32[]{:S(2)}, u32[]{:S(2)}) collective-permute-start(bf16[128,512]{1,0:T(8,128)(2,1)S(1)} %get-tuple-element.52.seen.send), channel_id=1, source_target_pairs={{0,12},{4,8},{8,4},{12,0},{1,13},{5,9},{9,5},{13,1},{2,14},{6,10},... | collective-permute-start | bytes 393224 | tf_op jit(solution)/shard_map/ppermute | solution.py:17
  17.9 0.5 %shard_map.88.seen.late = bf16[128,768]{1,0:T(8,128)(2,1)S(1)} custom-call(bf16[2,1,640,128]{3,2,1,0:T(8,128)(2,1)S(1)} %get-tuple-element.40.lb, bf16[2,1,640,128]{3,2,1,0:T(8,128)(2,1)S(1)} %get-tuple-element.42.rb, bf16[2,1,128,256]{3,2,1,0:T(8,128)(2,1)S(1)} %get-tuple-element.41.caps, bf16[1,640,128]{2,1,0:T(8,128)(2,1)S(1)} %get-tuple-element.43.tl, ...), custom_call_target="tpu_custom_call" | custom-call | flops 5000000000 | tf_op jit(solution)/shard_map/pallas_call | solution.py:88
  18.9 1.6 %collective-permute-start.11 = (bf16[128,512]{1,0:T(8,128)(2,1)S(1)}, bf16[128,512]{1,0:T(8,128)(2,1)S(1)}, u32[]{:S(2)}, u32[]{:S(2)}) collective-permute-start(bf16[128,512]{1,0:T(8,128)(2,1)S(1)} %shard_map.92.a), channel_id=1, source_target_pairs={{0,2},{1,3},{2,0},{3,1},{4,6},{5,7},{6,4},{7,5},{8,10},{9,11},{10,... | collective-permute-start | bytes 393224 | tf_op jit(solution)/shard_map/ppermute | solution.py:17
  20.5 1.9 %collective-permute-done.4.far = bf16[128,512]{1,0:T(8,128)(2,1)S(1)} collective-permute-done((bf16[128,512]{1,0:T(8,128)(2,1)S(1)}, bf16[128,512]{1,0:T(8,128)(2,1)S(1)}, u32[]{:S(2)}, u32[]{:S(2)}) %collective-permute-start.4) | collective-permute-done | bytes 131104 | tf_op jit(solution)/shard_map/ppermute | solution.py:17
  22.5 1.6 %collective-permute-start.8 = (bf16[128,256]{1,0:T(8,128)(2,1)S(1)}, bf16[128,256]{1,0:T(8,128)(2,1)S(1)}, u32[]{:S(2)}, u32[]{:S(2)}) collective-permute-start(bf16[128,256]{1,0:T(8,128)(2,1)S(1)} %shard_map.89.seen.a), channel_id=1, source_target_pairs={{0,2},{1,3},{2,0},{3,1},{4,6},{5,7},{6,4},{7,5},{8,10},{9,11},{10,... | collective-permute-start | bytes 196616 | tf_op jit(solution)/shard_map/ppermute | solution.py:17
  24.1 0.7 %shard_map.90 = (bf16[640,256]{1,0:T(8,128)(2,1)S(1)}, f32[128,256]{1,0:T(8,128)S(1)}, bf16[128,512]{1,0:T(8,128)(2,1)S(1)}) custom-call(f32[640,256]{1,0:T(8,128)S(1)} %get-tuple-element.47.seen.x1, bf16[128,512]{1,0:T(8,128)(2,1)S(1)} %get-tuple-element.52.seen.send, bf16[128,512]{1,0:T(8,128)(2,1)S(1)} %collective-permute-done.4.far, ...), custom_call_target="tpu_custom_call" | custom-call | flops 100000000 | tf_op jit(solution)/shard_map/pallas_call | solution.py:88
  24.8 0.6 %collective-permute-start.7 = (bf16[128,256]{1,0:T(8,128)(2,1)S(1)}, bf16[128,256]{1,0:T(8,128)(2,1)S(1)}, u32[]{:S(2)}, u32[]{:S(2)}) collective-permute-start(bf16[128,256]{1,0:T(8,128)(2,1)S(1)} %shard_map.89.seen.a), channel_id=1, source_target_pairs={{0,1},{1,0},{2,3},{3,2},{4,5},{5,4},{6,7},{7,6},{8,9},{9,8},{10,11... | collective-permute-start | bytes 196616 | tf_op jit(solution)/shard_map/ppermute | solution.py:17
  25.4 1.2 %collective-permute-start.14 = (bf16[128,512]{1,0:T(8,128)(2,1)S(1)}, bf16[128,512]{1,0:T(8,128)(2,1)S(1)}, u32[]{:S(2)}, u32[]{:S(2)}) collective-permute-start(bf16[128,512]{1,0:T(8,128)(2,1)S(1)} %get-tuple-element.66.z), channel_id=1, source_target_pairs={{0,4},{4,0},{8,12},{12,8},{1,5},{5,1},{9,13},{13,9},{2,6},{6,2},{1... | collective-permute-start | bytes 393224 | tf_op jit(solution)/shard_map/ppermute | solution.py:17
  27.4 0.9 %shard_map.91 = (f32[640,256]{1,0:T(8,128)S(1)}, bf16[640,512]{1,0:T(8,128)(2,1)S(1)}) custom-call(bf16[640,256]{1,0:T(8,128)(2,1)S(1)} %get-tuple-element.56.x2, bf16[2,1,640,128]{3,2,1,0:T(8,128)(2,1)S(1)} %get-tuple-element.42.rb, bf16[1,640,128]{2,1,0:T(8,128)(2,1)S(1)} %get-tuple-element.43.tl, bf16[1,640,128]{2,1,0:T(8,128)(2,1)S(1)} %get-tuple-element.44.tr, ...), custom_call_target="tpu_custom_call" | custom-call | flops 3000000000 | tf_op jit(solution)/shard_map/pallas_call | solution.py:88
  28.4 0.5 %shard_map.94.back = bf16[128,512]{1,0:T(8,128)(2,1)S(1)} custom-call(bf16[128,256]{1,0:T(8,128)(2,1)S(1)} %shard_map.89.seen.a, bf16[128,256]{1,0:T(8,128)(2,1)S(1)} %collective-permute-done.7.b, bf16[128,256]{1,0:T(8,128)(2,1)S(1)} %collective-permute-done.8.c, bf16[128,256]{1,0:T(8,128)(2,1)S(1)} %collective-permute-done.9.d, ...), custom_call_target="tpu_custom_call" | custom-call | flops 1000000000 | tf_op jit(solution)/shard_map/pallas_call | solution.py:88
  29.0 1.2 %collective-permute-start.13 = (bf16[128,512]{1,0:T(8,128)(2,1)S(1)}, bf16[128,512]{1,0:T(8,128)(2,1)S(1)}, u32[]{:S(2)}, u32[]{:S(2)}) collective-permute-start(bf16[128,512]{1,0:T(8,128)(2,1)S(1)} %shard_map.94.back), channel_id=1, source_target_pairs={{0,4},{4,0},{8,12},{12,8},{1,5},{5,1},{9,13},{13,9},{2,6},{6,2},{1... | collective-permute-start | bytes 393224 | tf_op jit(solution)/shard_map/ppermute | solution.py:17
  30.2 0.6 %collective-permute-done.14.z_sib = bf16[128,512]{1,0:T(8,128)(2,1)S(1)} collective-permute-done((bf16[128,512]{1,0:T(8,128)(2,1)S(1)}, bf16[128,512]{1,0:T(8,128)(2,1)S(1)}, u32[]{:S(2)}, u32[]{:S(2)}) %collective-permute-start.14) | collective-permute-done | bytes 131104 | tf_op jit(solution)/shard_map/ppermute | solution.py:17
  30.8 3.8 %collective-permute-done.13.back_sib = bf16[128,512]{1,0:T(8,128)(2,1)S(1)} collective-permute-done((bf16[128,512]{1,0:T(8,128)(2,1)S(1)}, bf16[128,512]{1,0:T(8,128)(2,1)S(1)}, u32[]{:S(2)}, u32[]{:S(2)}) %collective-permute-start.13) | collective-permute-done | bytes 131104 | tf_op jit(solution)/shard_map/ppermute | solution.py:17
  34.8 2.9 %collective-permute-start.15 = (bf16[128,256]{1,0:T(8,128)(2,1)S(1)}, bf16[128,256]{1,0:T(8,128)(2,1)S(1)}, u32[]{:S(2)}, u32[]{:S(2)}) collective-permute-start(bf16[128,256]{1,0:T(8,128)(2,1)S(1)} %get-tuple-element.68.seen.half5), channel_id=1, source_target_pairs={{0,8},{4,12},{8,0},{12,4},{1,9},{5,13},{9,1},{13,5},{2,10},{6,14},... | collective-permute-start | bytes 196616 | tf_op jit(solution)/shard_map/ppermute | solution.py:17
  38.0 3.0 %collective-permute-done.15.half5_far = bf16[128,256]{1,0:T(8,128)(2,1)S(1)} collective-permute-done((bf16[128,256]{1,0:T(8,128)(2,1)S(1)}, bf16[128,256]{1,0:T(8,128)(2,1)S(1)}, u32[]{:S(2)}, u32[]{:S(2)}) %collective-permute-start.15) | collective-permute-done | bytes 65568 | tf_op jit(solution)/shard_map/ppermute | solution.py:17
  41.0 1.4 %shard_map.97 = f32[1,640,256]{2,1,0:T(8,128)} custom-call(f32[640,256]{1,0:T(8,128)S(1)} %get-tuple-element.69.out3, bf16[640,512]{1,0:T(8,128)(2,1)S(1)} %get-tuple-element.59.under, bf16[128,256]{1,0:T(8,128)(2,1)S(1)} %get-tuple-element.68.seen.half5, bf16[128,256]{1,0:T(8,128)(2,1)S(1)} %collective-permute-done.15.half5_far, ...), custom_call_target="tpu_custom_call" | custom-call | flops 1000000000 | tf_op jit(solution)/shard_map/pallas_call | solution.py:88
  (26 shorter events, 3.4 us)
Async XLA Ops:
  2.1 3.2 %collective-permute-start.1 = (bf16[128,256]{1,0:T(8,128)(2,1)S(1)}, bf16[128,256]{1,0:T(8,128)(2,1)S(1)}, u32[]{:S(2)}, u32[]{:S(2)}) collective-permute-start(bf16[128,256]{1,0:T(8,128)(2,1)S(1)} %get-tuple-element.39.p), channel_id=1, source_target_pairs={{0,1},{1,0},{2,3},{3,2},{4,5},{5,4},{6,7},{7,6},{8,9},{9,8},{10,11... | collective-permute-start | bytes 196616 | tf_op jit(solution)/shard_map/ppermute | solution.py:17
  2.6 5.3 %collective-permute-start = (bf16[128,256]{1,0:T(8,128)(2,1)S(1)}, bf16[128,256]{1,0:T(8,128)(2,1)S(1)}, u32[]{:S(2)}, u32[]{:S(2)}) collective-permute-start(bf16[128,256]{1,0:T(8,128)(2,1)S(1)} %get-tuple-element.39.p), channel_id=1, source_target_pairs={{0,4},{4,0},{8,12},{12,8},{1,5},{5,1},{9,13},{13,9},{2,6},{6,2},{1... | collective-permute-start | bytes 196616 | tf_op jit(solution)/shard_map/ppermute | solution.py:17
  5.9 4.9 %collective-permute-start.3 = (bf16[128,384]{1,0:T(8,128)(2,1)S(1)}, bf16[128,384]{1,0:T(8,128)(2,1)S(1)}, u32[]{:S(2)}, u32[]{:S(2)}) collective-permute-start(bf16[128,384]{1,0:T(8,128)(2,1)S(1)} %get-tuple-element.45.seen.own), channel_id=1, source_target_pairs={{0,4},{4,0},{8,12},{12,8},{1,5},{5,1},{9,13},{13,9},{2,6},{6,2},{1... | collective-permute-start | bytes 294920 | tf_op jit(solution)/shard_map/ppermute | solution.py:17
  8.7 5.4 %collective-permute-start.2 = (bf16[128,512]{1,0:T(8,128)(2,1)S(1)}, bf16[128,512]{1,0:T(8,128)(2,1)S(1)}, u32[]{:S(2)}, u32[]{:S(2)}) collective-permute-start(bf16[128,512]{1,0:T(8,128)(2,1)S(1)} %get-tuple-element.49), channel_id=1, source_target_pairs={{0,4},{4,0},{8,12},{12,8},{1,5},{5,1},{9,13},{13,9},{2,6},{6,2},{1... | collective-permute-start | bytes 393224 | tf_op jit(solution)/shard_map/ppermute | solution.py:17
  10.9 7.0 %collective-permute-start.5 = (bf16[128,256]{1,0:T(8,128)(2,1)S(1)}, bf16[128,256]{1,0:T(8,128)(2,1)S(1)}, u32[]{:S(2)}, u32[]{:S(2)}) collective-permute-start(bf16[128,256]{1,0:T(8,128)(2,1)S(1)} %get-tuple-element.55), channel_id=1, source_target_pairs={{0,12},{4,8},{8,4},{12,0},{1,13},{5,9},{9,5},{13,1},{2,14},{6,10},... | collective-permute-start | bytes 196616 | tf_op jit(solution)/shard_map/ppermute | solution.py:17
  14.3 4.5 %copy-start = (bf16[128,512]{1,0:T(8,128)(2,1)S(1)}, bf16[128,512]{1,0:T(8,128)(2,1)}, u32[]{:S(2)}) copy-start(bf16[128,512]{1,0:T(8,128)(2,1)} %caps.3) | copy-start | bytes 393220
  14.3 8.1 %collective-permute-start.4 = (bf16[128,512]{1,0:T(8,128)(2,1)S(1)}, bf16[128,512]{1,0:T(8,128)(2,1)S(1)}, u32[]{:S(2)}, u32[]{:S(2)}) collective-permute-start(bf16[128,512]{1,0:T(8,128)(2,1)S(1)} %get-tuple-element.52.seen.send), channel_id=1, source_target_pairs={{0,12},{4,8},{8,4},{12,0},{1,13},{5,9},{9,5},{13,1},{2,14},{6,10},... | collective-permute-start | bytes 393224 | tf_op jit(solution)/shard_map/ppermute | solution.py:17
  18.4 8.4 %collective-permute-start.6 = (bf16[128,768]{1,0:T(8,128)(2,1)S(1)}, bf16[128,768]{1,0:T(8,128)(2,1)S(1)}, u32[]{:S(2)}, u32[]{:S(2)}) collective-permute-start(bf16[128,768]{1,0:T(8,128)(2,1)S(1)} %shard_map.88.seen.late), channel_id=1, source_target_pairs={{0,4},{4,0},{8,12},{12,8},{1,5},{5,1},{9,13},{13,9},{2,6},{6,2},{1... | collective-permute-start | bytes 589832 | tf_op jit(solution)/shard_map/ppermute | solution.py:17
  18.9 6.4 %collective-permute-start.11 = (bf16[128,512]{1,0:T(8,128)(2,1)S(1)}, bf16[128,512]{1,0:T(8,128)(2,1)S(1)}, u32[]{:S(2)}, u32[]{:S(2)}) collective-permute-start(bf16[128,512]{1,0:T(8,128)(2,1)S(1)} %shard_map.92.a), channel_id=1, source_target_pairs={{0,2},{1,3},{2,0},{3,1},{4,6},{5,7},{6,4},{7,5},{8,10},{9,11},{10,... | collective-permute-start | bytes 393224 | tf_op jit(solution)/shard_map/ppermute | solution.py:17
  22.5 4.3 %collective-permute-start.8 = (bf16[128,256]{1,0:T(8,128)(2,1)S(1)}, bf16[128,256]{1,0:T(8,128)(2,1)S(1)}, u32[]{:S(2)}, u32[]{:S(2)}) collective-permute-start(bf16[128,256]{1,0:T(8,128)(2,1)S(1)} %shard_map.89.seen.a), channel_id=1, source_target_pairs={{0,2},{1,3},{2,0},{3,1},{4,6},{5,7},{6,4},{7,5},{8,10},{9,11},{10,... | collective-permute-start | bytes 196616 | tf_op jit(solution)/shard_map/ppermute | solution.py:17
  24.1 4.2 %collective-permute-start.10 = (bf16[128,512]{1,0:T(8,128)(2,1)S(1)}, bf16[128,512]{1,0:T(8,128)(2,1)S(1)}, u32[]{:S(2)}, u32[]{:S(2)}) collective-permute-start(bf16[128,512]{1,0:T(8,128)(2,1)S(1)} %shard_map.92.a), channel_id=1, source_target_pairs={{0,1},{1,0},{2,3},{3,2},{4,5},{5,4},{6,7},{7,6},{8,9},{9,8},{10,11... | collective-permute-start | bytes 393224 | tf_op jit(solution)/shard_map/ppermute | solution.py:17
  24.8 3.6 %collective-permute-start.7 = (bf16[128,256]{1,0:T(8,128)(2,1)S(1)}, bf16[128,256]{1,0:T(8,128)(2,1)S(1)}, u32[]{:S(2)}, u32[]{:S(2)}) collective-permute-start(bf16[128,256]{1,0:T(8,128)(2,1)S(1)} %shard_map.89.seen.a), channel_id=1, source_target_pairs={{0,1},{1,0},{2,3},{3,2},{4,5},{5,4},{6,7},{7,6},{8,9},{9,8},{10,11... | collective-permute-start | bytes 196616 | tf_op jit(solution)/shard_map/ppermute | solution.py:17
  25.4 5.5 %collective-permute-start.14 = (bf16[128,512]{1,0:T(8,128)(2,1)S(1)}, bf16[128,512]{1,0:T(8,128)(2,1)S(1)}, u32[]{:S(2)}, u32[]{:S(2)}) collective-permute-start(bf16[128,512]{1,0:T(8,128)(2,1)S(1)} %get-tuple-element.66.z), channel_id=1, source_target_pairs={{0,4},{4,0},{8,12},{12,8},{1,5},{5,1},{9,13},{13,9},{2,6},{6,2},{1... | collective-permute-start | bytes 393224 | tf_op jit(solution)/shard_map/ppermute | solution.py:17
  26.9 1.4 %collective-permute-start.12 = (bf16[128,512]{1,0:T(8,128)(2,1)S(1)}, bf16[128,512]{1,0:T(8,128)(2,1)S(1)}, u32[]{:S(2)}, u32[]{:S(2)}) collective-permute-start(bf16[128,512]{1,0:T(8,128)(2,1)S(1)} %collective-permute-done.11.c), channel_id=1, source_target_pairs={{0,1},{1,0},{2,3},{3,2},{4,5},{5,4},{6,7},{7,6},{8,9},{9,8},{10,11... | collective-permute-start | bytes 393224 | tf_op jit(solution)/shard_map/ppermute | solution.py:17
  26.9 1.5 %collective-permute-start.9 = (bf16[128,256]{1,0:T(8,128)(2,1)S(1)}, bf16[128,256]{1,0:T(8,128)(2,1)S(1)}, u32[]{:S(2)}, u32[]{:S(2)}) collective-permute-start(bf16[128,256]{1,0:T(8,128)(2,1)S(1)} %collective-permute-done.8.c), channel_id=1, source_target_pairs={{0,1},{1,0},{2,3},{3,2},{4,5},{5,4},{6,7},{7,6},{8,9},{9,8},{10,11... | collective-permute-start | bytes 196616 | tf_op jit(solution)/shard_map/ppermute | solution.py:17
  29.0 5.7 %collective-permute-start.13 = (bf16[128,512]{1,0:T(8,128)(2,1)S(1)}, bf16[128,512]{1,0:T(8,128)(2,1)S(1)}, u32[]{:S(2)}, u32[]{:S(2)}) collective-permute-start(bf16[128,512]{1,0:T(8,128)(2,1)S(1)} %shard_map.94.back), channel_id=1, source_target_pairs={{0,4},{4,0},{8,12},{12,8},{1,5},{5,1},{9,13},{13,9},{2,6},{6,2},{1... | collective-permute-start | bytes 393224 | tf_op jit(solution)/shard_map/ppermute | solution.py:17
  34.8 6.2 %collective-permute-start.15 = (bf16[128,256]{1,0:T(8,128)(2,1)S(1)}, bf16[128,256]{1,0:T(8,128)(2,1)S(1)}, u32[]{:S(2)}, u32[]{:S(2)}) collective-permute-start(bf16[128,256]{1,0:T(8,128)(2,1)S(1)} %get-tuple-element.68.seen.half5), channel_id=1, source_target_pairs={{0,8},{4,12},{8,0},{12,4},{1,9},{5,13},{9,1},{13,5},{2,10},{6,14},... | collective-permute-start | bytes 196616 | tf_op jit(solution)/shard_map/ppermute | solution.py:17

commit v20 on v18

--- a/solution.py
+++ b/solution.py
@@ -452,7 +452,7 @@
         scratch=[pltpu.VMEM((2, rank, 2 * cols), BF)],
         micros=0.3,
     )
-    half5_far = swap(half5, "leaf", 3)
+    half5_far = swap(half5, "leaf", 2)
 
     def part_body(out2, under, both, z, z_sib, late, late_sib, seen, proj, out3):
         def down(zs, gram):

time: 42.7 us -> 42.7 us (level)
  waiting for transfers between devices: 9.75 us -> 10.7 us
  starting transfers between devices: 23.8 us -> 22.9 us
    ppermute x16, starting transfers between devices: 23.8 us -> 22.9 us  [swap(): return lax.ppermute(value, axis, pairs)]
    ppermute x16, waiting for transfers between devices: 9.75 us -> 10.7 us  [swap(): return lax.ppermute(value, axis, pairs)]
where the time goes in v20:
time: 42.7 us; the launch traced here: 42.5 us
  starting transfers between devices  22.9 us (54%)
  waiting for transfers between devices  10.7 us (25%)
  Pallas kernels  8.83 us (21%)
    ppermute x16, starting transfers between devices, swap(): return lax.ppermute(value, axis, pairs)  22.9 us
    ppermute x16, waiting for transfers between devices, swap(): return lax.ppermute(value, axis, pairs)  10.7 us
    pallas_call x16, Pallas kernels, call(): pl.pallas_call(body, out_shape=[jax.ShapeDtypeStruct(shape, dtype) if hbm...  8.83 us
  transfers between devices with their start and end apart: 16, of which 7 were waited for; matrix products, arithmetic and copies ran while one was open for 0% of the time, Pallas kernels for 12%

profile of v20, /device:TPU:0, one launch (start us, length us, event | category | flops | bytes accessed | tf_op | source)
XLA Modules:
  0.0 42.5 jit_solution(15121592278874587080)
XLA Ops:
  0.0 2.1 %shard_map.82 = (f32[640,256]{1,0:T(8,128)S(1)}, bf16[128,256]{1,0:T(8,128)(2,1)S(1)}, bf16[640,640]{1,0:T(8,128)(2,1)S(1)}, bf16[2,1,640,128]{3,2,1,0:T(8,128)(...) custom-call(f32[1,640,256]{2,1,0:T(8,128)} %rhs_hbm.1, ...), custom_call_target="tpu_custom_call" | custom-call | flops 1000000000 | tf_op jit(solution)/shard_map/pallas_call | solution.py:88
  2.7 2.6 %collective-permute-start = (bf16[128,256]{1,0:T(8,128)(2,1)S(1)}, bf16[128,256]{1,0:T(8,128)(2,1)S(1)}, u32[]{:S(2)}, u32[]{:S(2)}) collective-permute-start(bf16[128,256]{1,0:T(8,128)(2,1)S(1)} %get-tuple-element.40.p), channel_id=1, source_target_pairs={{0,4},{4,0},{8,12},{12,8},{1,5},{5,1},{9,13},{13,9},{2,6},{6,2},{1... | collective-permute-start | bytes 196616 | tf_op jit(solution)/shard_map/ppermute | solution.py:17
  5.3 0.6 %shard_map.83 = (bf16[128,384]{1,0:T(8,128)(2,1)S(1)}, bf16[128,256]{1,0:T(8,128)(2,1)S(1)}) custom-call(bf16[2,1,640,128]{3,2,1,0:T(8,128)(2,1)S(1)} %get-tuple-element.41.lb, bf16[2,1,128,256]{3,2,1,0:T(8,128)(2,1)S(1)} %get-tuple-element.42.caps, bf16[1,640,128]{2,1,0:T(8,128)(2,1)S(1)} %get-tuple-element.44.tl, ...), custom_call_target="tpu_custom_call" | custom-call | flops 10000000000 | tf_op jit(solution)/shard_map/pallas_call | solution.py:88
  5.9 1.2 %collective-permute-start.3 = (bf16[128,384]{1,0:T(8,128)(2,1)S(1)}, bf16[128,384]{1,0:T(8,128)(2,1)S(1)}, u32[]{:S(2)}, u32[]{:S(2)}) collective-permute-start(bf16[128,384]{1,0:T(8,128)(2,1)S(1)} %get-tuple-element.46.seen.own), channel_id=1, source_target_pairs={{0,4},{4,0},{8,12},{12,8},{1,5},{5,1},{9,13},{13,9},{2,6},{6,2},{1... | collective-permute-start | bytes 294920 | tf_op jit(solution)/shard_map/ppermute | solution.py:17
  7.5 0.6 %collective-permute-done.p_sib = bf16[128,256]{1,0:T(8,128)(2,1)S(1)} collective-permute-done((bf16[128,256]{1,0:T(8,128)(2,1)S(1)}, bf16[128,256]{1,0:T(8,128)(2,1)S(1)}, u32[]{:S(2)}, u32[]{:S(2)}) %collective-permute-start) | collective-permute-done | bytes 65568 | tf_op jit(solution)/shard_map/ppermute | solution.py:17
  8.0 0.8 %shard_map.85 = (f32[640,256]{1,0:T(8,128)S(1)}, bf16[128,512]{1,0:T(8,128)(2,1)S(1)}, f32[128,512]{1,0:T(8,128)S(1)}) custom-call(f32[640,256]{1,0:T(8,128)S(1)} %get-tuple-element.39.x0, bf16[128,256]{1,0:T(8,128)(2,1)S(1)} %get-tuple-element.40.p, bf16[128,256]{1,0:T(8,128)(2,1)S(1)} %collective-permute-done.p_sib, ...), custom_call_target="tpu_custom_call" | custom-call | flops 3000000000 | tf_op jit(solution)/shard_map/pallas_call | solution.py:88
  8.8 1.8 %collective-permute-start.2 = (bf16[128,512]{1,0:T(8,128)(2,1)S(1)}, bf16[128,512]{1,0:T(8,128)(2,1)S(1)}, u32[]{:S(2)}, u32[]{:S(2)}) collective-permute-start(bf16[128,512]{1,0:T(8,128)(2,1)S(1)} %get-tuple-element.50), channel_id=1, source_target_pairs={{0,4},{4,0},{8,12},{12,8},{1,5},{5,1},{9,13},{13,9},{2,6},{6,2},{1... | collective-permute-start | bytes 393224 | tf_op jit(solution)/shard_map/ppermute | solution.py:17
  10.9 3.3 %collective-permute-start.5 = (bf16[128,256]{1,0:T(8,128)(2,1)S(1)}, bf16[128,256]{1,0:T(8,128)(2,1)S(1)}, u32[]{:S(2)}, u32[]{:S(2)}) collective-permute-start(bf16[128,256]{1,0:T(8,128)(2,1)S(1)} %get-tuple-element.56), channel_id=1, source_target_pairs={{0,12},{4,8},{8,4},{12,0},{1,13},{5,9},{9,5},{13,1},{2,14},{6,10},... | collective-permute-start | bytes 196616 | tf_op jit(solution)/shard_map/ppermute | solution.py:17
  14.3 3.6 %collective-permute-start.4 = (bf16[128,512]{1,0:T(8,128)(2,1)S(1)}, bf16[128,512]{1,0:T(8,128)(2,1)S(1)}, u32[]{:S(2)}, u32[]{:S(2)}) collective-permute-start(bf16[128,512]{1,0:T(8,128)(2,1)S(1)} %get-tuple-element.53.seen.send), channel_id=1, source_target_pairs={{0,12},{4,8},{8,4},{12,0},{1,13},{5,9},{9,5},{13,1},{2,14},{6,10},... | collective-permute-start | bytes 393224 | tf_op jit(solution)/shard_map/ppermute | solution.py:17
  17.9 0.5 %shard_map.88.seen.late = bf16[128,768]{1,0:T(8,128)(2,1)S(1)} custom-call(bf16[2,1,640,128]{3,2,1,0:T(8,128)(2,1)S(1)} %get-tuple-element.41.lb, bf16[2,1,640,128]{3,2,1,0:T(8,128)(2,1)S(1)} %get-tuple-element.43.rb, bf16[2,1,128,256]{3,2,1,0:T(8,128)(2,1)S(1)} %get-tuple-element.42.caps, bf16[1,640,128]{2,1,0:T(8,128)(2,1)S(1)} %get-tuple-element.44.tl, ...), custom_call_target="tpu_custom_call" | custom-call | flops 5000000000 | tf_op jit(solution)/shard_map/pallas_call | solution.py:88
  18.9 1.6 %collective-permute-start.11 = (bf16[128,512]{1,0:T(8,128)(2,1)S(1)}, bf16[128,512]{1,0:T(8,128)(2,1)S(1)}, u32[]{:S(2)}, u32[]{:S(2)}) collective-permute-start(bf16[128,512]{1,0:T(8,128)(2,1)S(1)} %shard_map.92.a), channel_id=1, source_target_pairs={{0,2},{1,3},{2,0},{3,1},{4,6},{5,7},{6,4},{7,5},{8,10},{9,11},{10,... | collective-permute-start | bytes 393224 | tf_op jit(solution)/shard_map/ppermute | solution.py:17
  20.5 1.9 %collective-permute-done.4.far = bf16[128,512]{1,0:T(8,128)(2,1)S(1)} collective-permute-done((bf16[128,512]{1,0:T(8,128)(2,1)S(1)}, bf16[128,512]{1,0:T(8,128)(2,1)S(1)}, u32[]{:S(2)}, u32[]{:S(2)}) %collective-permute-start.4) | collective-permute-done | bytes 131104 | tf_op jit(solution)/shard_map/ppermute | solution.py:17
  22.6 1.6 %collective-permute-start.8 = (bf16[128,256]{1,0:T(8,128)(2,1)S(1)}, bf16[128,256]{1,0:T(8,128)(2,1)S(1)}, u32[]{:S(2)}, u32[]{:S(2)}) collective-permute-start(bf16[128,256]{1,0:T(8,128)(2,1)S(1)} %shard_map.89.seen.a), channel_id=1, source_target_pairs={{0,2},{1,3},{2,0},{3,1},{4,6},{5,7},{6,4},{7,5},{8,10},{9,11},{10,... | collective-permute-start | bytes 196616 | tf_op jit(solution)/shard_map/ppermute | solution.py:17
  24.1 0.7 %shard_map.90 = (bf16[640,256]{1,0:T(8,128)(2,1)S(1)}, f32[128,256]{1,0:T(8,128)S(1)}, bf16[128,512]{1,0:T(8,128)(2,1)S(1)}) custom-call(f32[640,256]{1,0:T(8,128)S(1)} %get-tuple-element.48.seen.x1, bf16[128,512]{1,0:T(8,128)(2,1)S(1)} %get-tuple-element.53.seen.send, bf16[128,512]{1,0:T(8,128)(2,1)S(1)} %collective-permute-done.4.far, ...), custom_call_target="tpu_custom_call" | custom-call | flops 100000000 | tf_op jit(solution)/shard_map/pallas_call | solution.py:88
  24.8 0.6 %collective-permute-start.7 = (bf16[128,256]{1,0:T(8,128)(2,1)S(1)}, bf16[128,256]{1,0:T(8,128)(2,1)S(1)}, u32[]{:S(2)}, u32[]{:S(2)}) collective-permute-start(bf16[128,256]{1,0:T(8,128)(2,1)S(1)} %shard_map.89.seen.a), channel_id=1, source_target_pairs={{0,1},{1,0},{2,3},{3,2},{4,5},{5,4},{6,7},{7,6},{8,9},{9,8},{10,11... | collective-permute-start | bytes 196616 | tf_op jit(solution)/shard_map/ppermute | solution.py:17
  25.4 1.2 %collective-permute-start.14 = (bf16[128,512]{1,0:T(8,128)(2,1)S(1)}, bf16[128,512]{1,0:T(8,128)(2,1)S(1)}, u32[]{:S(2)}, u32[]{:S(2)}) collective-permute-start(bf16[128,512]{1,0:T(8,128)(2,1)S(1)} %get-tuple-element.68.z), channel_id=1, source_target_pairs={{0,4},{4,0},{8,12},{12,8},{1,5},{5,1},{9,13},{13,9},{2,6},{6,2},{1... | collective-permute-start | bytes 393224 | tf_op jit(solution)/shard_map/ppermute | solution.py:17
  27.4 0.8 %shard_map.91 = (f32[640,256]{1,0:T(8,128)S(1)}, bf16[640,512]{1,0:T(8,128)(2,1)S(1)}) custom-call(bf16[640,256]{1,0:T(8,128)(2,1)S(1)} %get-tuple-element.57.x2, bf16[640,512]{1,0:T(8,128)(2,1)S(1)} %get-tuple-element.58.updates, bf16[640,640]{1,0:T(8,128)(2,1)S(1)} %get-tuple-element.59.inv, bf16[128,768]{1,0:T(8,128)(2,1)S(1)} %collective-permute-done.6.seen.late_sib), custom_call_target="tpu_custom_call" | custom-call | flops 3000000000 | tf_op jit(solution)/shard_map/pallas_call | solution.py:88
  28.4 0.5 %shard_map.94.back = bf16[128,512]{1,0:T(8,128)(2,1)S(1)} custom-call(bf16[128,256]{1,0:T(8,128)(2,1)S(1)} %shard_map.89.seen.a, bf16[128,256]{1,0:T(8,128)(2,1)S(1)} %collective-permute-done.7.b, bf16[128,256]{1,0:T(8,128)(2,1)S(1)} %collective-permute-done.8.c, bf16[128,256]{1,0:T(8,128)(2,1)S(1)} %collective-permute-done.9.d, ...), custom_call_target="tpu_custom_call" | custom-call | flops 1000000000 | tf_op jit(solution)/shard_map/pallas_call | solution.py:88
  28.9 1.2 %collective-permute-start.13 = (bf16[128,512]{1,0:T(8,128)(2,1)S(1)}, bf16[128,512]{1,0:T(8,128)(2,1)S(1)}, u32[]{:S(2)}, u32[]{:S(2)}) collective-permute-start(bf16[128,512]{1,0:T(8,128)(2,1)S(1)} %shard_map.94.back), channel_id=1, source_target_pairs={{0,4},{4,0},{8,12},{12,8},{1,5},{5,1},{9,13},{13,9},{2,6},{6,2},{1... | collective-permute-start | bytes 393224 | tf_op jit(solution)/shard_map/ppermute | solution.py:17
  30.2 0.7 %collective-permute-done.14.z_sib = bf16[128,512]{1,0:T(8,128)(2,1)S(1)} collective-permute-done((bf16[128,512]{1,0:T(8,128)(2,1)S(1)}, bf16[128,512]{1,0:T(8,128)(2,1)S(1)}, u32[]{:S(2)}, u32[]{:S(2)}) %collective-permute-start.14) | collective-permute-done | bytes 131104 | tf_op jit(solution)/shard_map/ppermute | solution.py:17
  30.9 3.8 %collective-permute-done.13.back_sib = bf16[128,512]{1,0:T(8,128)(2,1)S(1)} collective-permute-done((bf16[128,512]{1,0:T(8,128)(2,1)S(1)}, bf16[128,512]{1,0:T(8,128)(2,1)S(1)}, u32[]{:S(2)}, u32[]{:S(2)}) %collective-permute-start.13) | collective-permute-done | bytes 131104 | tf_op jit(solution)/shard_map/ppermute | solution.py:17
  34.9 2.9 %collective-permute-start.15 = (bf16[128,256]{1,0:T(8,128)(2,1)S(1)}, bf16[128,256]{1,0:T(8,128)(2,1)S(1)}, u32[]{:S(2)}, u32[]{:S(2)}) collective-permute-start(bf16[128,256]{1,0:T(8,128)(2,1)S(1)} %get-tuple-element.70.seen.half5), channel_id=1, source_target_pairs={{0,8},{4,12},{8,0},{12,4},{1,9},{5,13},{9,1},{13,5},{2,10},{6,14},... | collective-permute-start | bytes 196616 | tf_op jit(solution)/shard_map/ppermute | solution.py:17
  38.0 3.1 %collective-permute-done.15.half5_far = bf16[128,256]{1,0:T(8,128)(2,1)S(1)} collective-permute-done((bf16[128,256]{1,0:T(8,128)(2,1)S(1)}, bf16[128,256]{1,0:T(8,128)(2,1)S(1)}, u32[]{:S(2)}, u32[]{:S(2)}) %collective-permute-start.15) | collective-permute-done | bytes 65568 | tf_op jit(solution)/shard_map/ppermute | solution.py:17
  41.1 1.4 %shard_map.97 = f32[1,640,256]{2,1,0:T(8,128)} custom-call(f32[640,256]{1,0:T(8,128)S(1)} %get-tuple-element.71.out3, bf16[640,512]{1,0:T(8,128)(2,1)S(1)} %get-tuple-element.61.under, bf16[128,256]{1,0:T(8,128)(2,1)S(1)} %get-tuple-element.70.seen.half5, bf16[128,256]{1,0:T(8,128)(2,1)S(1)} %collective-permute-done.15.half5_far, ...), custom_call_target="tpu_custom_call" | custom-call | flops 1000000000 | tf_op jit(solution)/shard_map/pallas_call | solution.py:88
  (26 shorter events, 3.5 us)
Async XLA Ops:
  2.2 3.2 %collective-permute-start.1 = (bf16[128,256]{1,0:T(8,128)(2,1)S(1)}, bf16[128,256]{1,0:T(8,128)(2,1)S(1)}, u32[]{:S(2)}, u32[]{:S(2)}) collective-permute-start(bf16[128,256]{1,0:T(8,128)(2,1)S(1)} %get-tuple-element.40.p), channel_id=1, source_target_pairs={{0,1},{1,0},{2,3},{3,2},{4,5},{5,4},{6,7},{7,6},{8,9},{9,8},{10,11... | collective-permute-start | bytes 196616 | tf_op jit(solution)/shard_map/ppermute | solution.py:17
  2.7 5.3 %collective-permute-start = (bf16[128,256]{1,0:T(8,128)(2,1)S(1)}, bf16[128,256]{1,0:T(8,128)(2,1)S(1)}, u32[]{:S(2)}, u32[]{:S(2)}) collective-permute-start(bf16[128,256]{1,0:T(8,128)(2,1)S(1)} %get-tuple-element.40.p), channel_id=1, source_target_pairs={{0,4},{4,0},{8,12},{12,8},{1,5},{5,1},{9,13},{13,9},{2,6},{6,2},{1... | collective-permute-start | bytes 196616 | tf_op jit(solution)/shard_map/ppermute | solution.py:17
  5.9 4.9 %collective-permute-start.3 = (bf16[128,384]{1,0:T(8,128)(2,1)S(1)}, bf16[128,384]{1,0:T(8,128)(2,1)S(1)}, u32[]{:S(2)}, u32[]{:S(2)}) collective-permute-start(bf16[128,384]{1,0:T(8,128)(2,1)S(1)} %get-tuple-element.46.seen.own), channel_id=1, source_target_pairs={{0,4},{4,0},{8,12},{12,8},{1,5},{5,1},{9,13},{13,9},{2,6},{6,2},{1... | collective-permute-start | bytes 294920 | tf_op jit(solution)/shard_map/ppermute | solution.py:17
  8.8 5.4 %collective-permute-start.2 = (bf16[128,512]{1,0:T(8,128)(2,1)S(1)}, bf16[128,512]{1,0:T(8,128)(2,1)S(1)}, u32[]{:S(2)}, u32[]{:S(2)}) collective-permute-start(bf16[128,512]{1,0:T(8,128)(2,1)S(1)} %get-tuple-element.50), channel_id=1, source_target_pairs={{0,4},{4,0},{8,12},{12,8},{1,5},{5,1},{9,13},{13,9},{2,6},{6,2},{1... | collective-permute-start | bytes 393224 | tf_op jit(solution)/shard_map/ppermute | solution.py:17
  10.9 7.0 %collective-permute-start.5 = (bf16[128,256]{1,0:T(8,128)(2,1)S(1)}, bf16[128,256]{1,0:T(8,128)(2,1)S(1)}, u32[]{:S(2)}, u32[]{:S(2)}) collective-permute-start(bf16[128,256]{1,0:T(8,128)(2,1)S(1)} %get-tuple-element.56), channel_id=1, source_target_pairs={{0,12},{4,8},{8,4},{12,0},{1,13},{5,9},{9,5},{13,1},{2,14},{6,10},... | collective-permute-start | bytes 196616 | tf_op jit(solution)/shard_map/ppermute | solution.py:17
  14.3 4.5 %copy-start = (bf16[128,512]{1,0:T(8,128)(2,1)S(1)}, bf16[128,512]{1,0:T(8,128)(2,1)}, u32[]{:S(2)}) copy-start(bf16[128,512]{1,0:T(8,128)(2,1)} %caps.3) | copy-start | bytes 393220
  14.3 8.1 %collective-permute-start.4 = (bf16[128,512]{1,0:T(8,128)(2,1)S(1)}, bf16[128,512]{1,0:T(8,128)(2,1)S(1)}, u32[]{:S(2)}, u32[]{:S(2)}) collective-permute-start(bf16[128,512]{1,0:T(8,128)(2,1)S(1)} %get-tuple-element.53.seen.send), channel_id=1, source_target_pairs={{0,12},{4,8},{8,4},{12,0},{1,13},{5,9},{9,5},{13,1},{2,14},{6,10},... | collective-permute-start | bytes 393224 | tf_op jit(solution)/shard_map/ppermute | solution.py:17
  18.5 8.5 %collective-permute-start.6 = (bf16[128,768]{1,0:T(8,128)(2,1)S(1)}, bf16[128,768]{1,0:T(8,128)(2,1)S(1)}, u32[]{:S(2)}, u32[]{:S(2)}) collective-permute-start(bf16[128,768]{1,0:T(8,128)(2,1)S(1)} %shard_map.88.seen.late), channel_id=1, source_target_pairs={{0,4},{4,0},{8,12},{12,8},{1,5},{5,1},{9,13},{13,9},{2,6},{6,2},{1... | collective-permute-start | bytes 589832 | tf_op jit(solution)/shard_map/ppermute | solution.py:17
  18.9 6.4 %collective-permute-start.11 = (bf16[128,512]{1,0:T(8,128)(2,1)S(1)}, bf16[128,512]{1,0:T(8,128)(2,1)S(1)}, u32[]{:S(2)}, u32[]{:S(2)}) collective-permute-start(bf16[128,512]{1,0:T(8,128)(2,1)S(1)} %shard_map.92.a), channel_id=1, source_target_pairs={{0,2},{1,3},{2,0},{3,1},{4,6},{5,7},{6,4},{7,5},{8,10},{9,11},{10,... | collective-permute-start | bytes 393224 | tf_op jit(solution)/shard_map/ppermute | solution.py:17
  22.6 4.3 %collective-permute-start.8 = (bf16[128,256]{1,0:T(8,128)(2,1)S(1)}, bf16[128,256]{1,0:T(8,128)(2,1)S(1)}, u32[]{:S(2)}, u32[]{:S(2)}) collective-permute-start(bf16[128,256]{1,0:T(8,128)(2,1)S(1)} %shard_map.89.seen.a), channel_id=1, source_target_pairs={{0,2},{1,3},{2,0},{3,1},{4,6},{5,7},{6,4},{7,5},{8,10},{9,11},{10,... | collective-permute-start | bytes 196616 | tf_op jit(solution)/shard_map/ppermute | solution.py:17
  24.1 4.1 %collective-permute-start.10 = (bf16[128,512]{1,0:T(8,128)(2,1)S(1)}, bf16[128,512]{1,0:T(8,128)(2,1)S(1)}, u32[]{:S(2)}, u32[]{:S(2)}) collective-permute-start(bf16[128,512]{1,0:T(8,128)(2,1)S(1)} %shard_map.92.a), channel_id=1, source_target_pairs={{0,1},{1,0},{2,3},{3,2},{4,5},{5,4},{6,7},{7,6},{8,9},{9,8},{10,11... | collective-permute-start | bytes 393224 | tf_op jit(solution)/shard_map/ppermute | solution.py:17
  24.8 3.6 %collective-permute-start.7 = (bf16[128,256]{1,0:T(8,128)(2,1)S(1)}, bf16[128,256]{1,0:T(8,128)(2,1)S(1)}, u32[]{:S(2)}, u32[]{:S(2)}) collective-permute-start(bf16[128,256]{1,0:T(8,128)(2,1)S(1)} %shard_map.89.seen.a), channel_id=1, source_target_pairs={{0,1},{1,0},{2,3},{3,2},{4,5},{5,4},{6,7},{7,6},{8,9},{9,8},{10,11... | collective-permute-start | bytes 196616 | tf_op jit(solution)/shard_map/ppermute | solution.py:17
  25.4 5.5 %collective-permute-start.14 = (bf16[128,512]{1,0:T(8,128)(2,1)S(1)}, bf16[128,512]{1,0:T(8,128)(2,1)S(1)}, u32[]{:S(2)}, u32[]{:S(2)}) collective-permute-start(bf16[128,512]{1,0:T(8,128)(2,1)S(1)} %get-tuple-element.68.z), channel_id=1, source_target_pairs={{0,4},{4,0},{8,12},{12,8},{1,5},{5,1},{9,13},{13,9},{2,6},{6,2},{1... | collective-permute-start | bytes 393224 | tf_op jit(solution)/shard_map/ppermute | solution.py:17
  26.9 1.3 %collective-permute-start.12 = (bf16[128,512]{1,0:T(8,128)(2,1)S(1)}, bf16[128,512]{1,0:T(8,128)(2,1)S(1)}, u32[]{:S(2)}, u32[]{:S(2)}) collective-permute-start(bf16[128,512]{1,0:T(8,128)(2,1)S(1)} %collective-permute-done.11.c), channel_id=1, source_target_pairs={{0,1},{1,0},{2,3},{3,2},{4,5},{5,4},{6,7},{7,6},{8,9},{9,8},{10,11... | collective-permute-start | bytes 393224 | tf_op jit(solution)/shard_map/ppermute | solution.py:17
  26.9 1.5 %collective-permute-start.9 = (bf16[128,256]{1,0:T(8,128)(2,1)S(1)}, bf16[128,256]{1,0:T(8,128)(2,1)S(1)}, u32[]{:S(2)}, u32[]{:S(2)}) collective-permute-start(bf16[128,256]{1,0:T(8,128)(2,1)S(1)} %collective-permute-done.8.c), channel_id=1, source_target_pairs={{0,1},{1,0},{2,3},{3,2},{4,5},{5,4},{6,7},{7,6},{8,9},{9,8},{10,11... | collective-permute-start | bytes 196616 | tf_op jit(solution)/shard_map/ppermute | solution.py:17
  28.9 5.7 %collective-permute-start.13 = (bf16[128,512]{1,0:T(8,128)(2,1)S(1)}, bf16[128,512]{1,0:T(8,128)(2,1)S(1)}, u32[]{:S(2)}, u32[]{:S(2)}) collective-permute-start(bf16[128,512]{1,0:T(8,128)(2,1)S(1)} %shard_map.94.back), channel_id=1, source_target_pairs={{0,4},{4,0},{8,12},{12,8},{1,5},{5,1},{9,13},{13,9},{2,6},{6,2},{1... | collective-permute-start | bytes 393224 | tf_op jit(solution)/shard_map/ppermute | solution.py:17
  34.9 6.2 %collective-permute-start.15 = (bf16[128,256]{1,0:T(8,128)(2,1)S(1)}, bf16[128,256]{1,0:T(8,128)(2,1)S(1)}, u32[]{:S(2)}, u32[]{:S(2)}) collective-permute-start(bf16[128,256]{1,0:T(8,128)(2,1)S(1)} %get-tuple-element.70.seen.half5), channel_id=1, source_target_pairs={{0,8},{4,12},{8,0},{12,4},{1,9},{5,13},{9,1},{13,5},{2,10},{6,14},... | collective-permute-start | bytes 196616 | tf_op jit(solution)/shard_map/ppermute | solution.py:17

commit v21 on v19

--- a/solution.py
+++ b/solution.py
@@ -485,9 +485,10 @@
         coefs[span(0), :] = dot(caps[1, 0], stack[...]).astype(BF)
         coefs[span(1), :] = dot(caps[0, 0], proj).astype(BF)
         copies = []
-        for c in range(blocks):
-            out_v[span(c), :] = out3[span(c), :] - dot(under[span(c), span(2, 2)], coefs[...])
-            copy = pltpu.make_async_copy(out_v.at[span(c), :], out.at[0, span(c), :], sems.at[c])
+        for c in range(0, blocks, 2):
+            at = span(c, min(2, blocks - c))
+            out_v[at, :] = out3[at, :] - dot(under[at, span(2, 2)], coefs[...])
+            copy = pltpu.make_async_copy(out_v.at[at, :], out.at[0, at, :], sems.at[c])
             copy.start()
             copies.append(copy)
         for copy in copies:

time: 42.6 us -> 42.6 us (level)
  no operation moved by 1% of the time
where the time goes in v21:
time: 42.6 us; the launch traced here: 42.5 us
  starting transfers between devices  22.9 us (54%)
  waiting for transfers between devices  10.5 us (25%)
  Pallas kernels  8.92 us (21%)
    ppermute x16, starting transfers between devices, swap(): return lax.ppermute(value, axis, pairs)  22.9 us
    ppermute x16, waiting for transfers between devices, swap(): return lax.ppermute(value, axis, pairs)  10.5 us
    pallas_call x16, Pallas kernels, call(): pl.pallas_call(body, out_shape=[jax.ShapeDtypeStruct(shape, dtype) if hbm...  8.92 us
  transfers between devices with their start and end apart: 16, of which 7 were waited for; matrix products, arithmetic and copies ran while one was open for 0% of the time, Pallas kernels for 12%

profile of v21, /device:TPU:0, one launch (start us, length us, event | category | flops | bytes accessed | tf_op | source)
XLA Modules:
  0.0 42.5 jit_solution(12725439129504712491)
XLA Ops:
  0.0 2.1 %shard_map.82 = (f32[640,256]{1,0:T(8,128)S(1)}, bf16[128,256]{1,0:T(8,128)(2,1)S(1)}, bf16[640,640]{1,0:T(8,128)(2,1)S(1)}, bf16[2,1,640,128]{3,2,1,0:T(8,128)(...) custom-call(f32[1,640,256]{2,1,0:T(8,128)} %rhs_hbm.1, ...), custom_call_target="tpu_custom_call" | custom-call | flops 1000000000 | tf_op jit(solution)/shard_map/pallas_call | solution.py:88
  2.6 2.6 %collective-permute-start = (bf16[128,256]{1,0:T(8,128)(2,1)S(1)}, bf16[128,256]{1,0:T(8,128)(2,1)S(1)}, u32[]{:S(2)}, u32[]{:S(2)}) collective-permute-start(bf16[128,256]{1,0:T(8,128)(2,1)S(1)} %get-tuple-element.39.p), channel_id=1, source_target_pairs={{0,4},{4,0},{8,12},{12,8},{1,5},{5,1},{9,13},{13,9},{2,6},{6,2},{1... | collective-permute-start | bytes 196616 | tf_op jit(solution)/shard_map/ppermute | solution.py:17
  5.3 0.6 %shard_map.83 = (bf16[128,384]{1,0:T(8,128)(2,1)S(1)}, bf16[128,256]{1,0:T(8,128)(2,1)S(1)}) custom-call(bf16[2,1,640,128]{3,2,1,0:T(8,128)(2,1)S(1)} %get-tuple-element.40.lb, bf16[2,1,128,256]{3,2,1,0:T(8,128)(2,1)S(1)} %get-tuple-element.41.caps, bf16[1,640,128]{2,1,0:T(8,128)(2,1)S(1)} %get-tuple-element.43.tl, ...), custom_call_target="tpu_custom_call" | custom-call | flops 10000000000 | tf_op jit(solution)/shard_map/pallas_call | solution.py:88
  5.9 1.2 %collective-permute-start.3 = (bf16[128,384]{1,0:T(8,128)(2,1)S(1)}, bf16[128,384]{1,0:T(8,128)(2,1)S(1)}, u32[]{:S(2)}, u32[]{:S(2)}) collective-permute-start(bf16[128,384]{1,0:T(8,128)(2,1)S(1)} %get-tuple-element.45.seen.own), channel_id=1, source_target_pairs={{0,4},{4,0},{8,12},{12,8},{1,5},{5,1},{9,13},{13,9},{2,6},{6,2},{1... | collective-permute-start | bytes 294920 | tf_op jit(solution)/shard_map/ppermute | solution.py:17
  7.4 0.6 %collective-permute-done.p_sib = bf16[128,256]{1,0:T(8,128)(2,1)S(1)} collective-permute-done((bf16[128,256]{1,0:T(8,128)(2,1)S(1)}, bf16[128,256]{1,0:T(8,128)(2,1)S(1)}, u32[]{:S(2)}, u32[]{:S(2)}) %collective-permute-start) | collective-permute-done | bytes 65568 | tf_op jit(solution)/shard_map/ppermute | solution.py:17
  8.0 0.8 %shard_map.85 = (f32[640,256]{1,0:T(8,128)S(1)}, bf16[128,512]{1,0:T(8,128)(2,1)S(1)}, f32[128,512]{1,0:T(8,128)S(1)}) custom-call(f32[640,256]{1,0:T(8,128)S(1)} %get-tuple-element.38.x0, bf16[128,256]{1,0:T(8,128)(2,1)S(1)} %get-tuple-element.39.p, bf16[128,256]{1,0:T(8,128)(2,1)S(1)} %collective-permute-done.p_sib, ...), custom_call_target="tpu_custom_call" | custom-call | flops 3000000000 | tf_op jit(solution)/shard_map/pallas_call | solution.py:88
  8.7 1.8 %collective-permute-start.2 = (bf16[128,512]{1,0:T(8,128)(2,1)S(1)}, bf16[128,512]{1,0:T(8,128)(2,1)S(1)}, u32[]{:S(2)}, u32[]{:S(2)}) collective-permute-start(bf16[128,512]{1,0:T(8,128)(2,1)S(1)} %get-tuple-element.49), channel_id=1, source_target_pairs={{0,4},{4,0},{8,12},{12,8},{1,5},{5,1},{9,13},{13,9},{2,6},{6,2},{1... | collective-permute-start | bytes 393224 | tf_op jit(solution)/shard_map/ppermute | solution.py:17
  10.9 3.3 %collective-permute-start.5 = (bf16[128,256]{1,0:T(8,128)(2,1)S(1)}, bf16[128,256]{1,0:T(8,128)(2,1)S(1)}, u32[]{:S(2)}, u32[]{:S(2)}) collective-permute-start(bf16[128,256]{1,0:T(8,128)(2,1)S(1)} %get-tuple-element.55), channel_id=1, source_target_pairs={{0,12},{4,8},{8,4},{12,0},{1,13},{5,9},{9,5},{13,1},{2,14},{6,10},... | collective-permute-start | bytes 196616 | tf_op jit(solution)/shard_map/ppermute | solution.py:17
  14.3 3.6 %collective-permute-start.4 = (bf16[128,512]{1,0:T(8,128)(2,1)S(1)}, bf16[128,512]{1,0:T(8,128)(2,1)S(1)}, u32[]{:S(2)}, u32[]{:S(2)}) collective-permute-start(bf16[128,512]{1,0:T(8,128)(2,1)S(1)} %get-tuple-element.52.seen.send), channel_id=1, source_target_pairs={{0,12},{4,8},{8,4},{12,0},{1,13},{5,9},{9,5},{13,1},{2,14},{6,10},... | collective-permute-start | bytes 393224 | tf_op jit(solution)/shard_map/ppermute | solution.py:17
  17.9 0.5 %shard_map.88.seen.late = bf16[128,768]{1,0:T(8,128)(2,1)S(1)} custom-call(bf16[2,1,640,128]{3,2,1,0:T(8,128)(2,1)S(1)} %get-tuple-element.40.lb, bf16[2,1,640,128]{3,2,1,0:T(8,128)(2,1)S(1)} %get-tuple-element.42.rb, bf16[2,1,128,256]{3,2,1,0:T(8,128)(2,1)S(1)} %get-tuple-element.41.caps, bf16[1,640,128]{2,1,0:T(8,128)(2,1)S(1)} %get-tuple-element.43.tl, ...), custom_call_target="tpu_custom_call" | custom-call | flops 5000000000 | tf_op jit(solution)/shard_map/pallas_call | solution.py:88
  18.9 1.6 %collective-permute-start.11 = (bf16[128,512]{1,0:T(8,128)(2,1)S(1)}, bf16[128,512]{1,0:T(8,128)(2,1)S(1)}, u32[]{:S(2)}, u32[]{:S(2)}) collective-permute-start(bf16[128,512]{1,0:T(8,128)(2,1)S(1)} %shard_map.92.a), channel_id=1, source_target_pairs={{0,2},{1,3},{2,0},{3,1},{4,6},{5,7},{6,4},{7,5},{8,10},{9,11},{10,... | collective-permute-start | bytes 393224 | tf_op jit(solution)/shard_map/ppermute | solution.py:17
  20.5 1.9 %collective-permute-done.4.far = bf16[128,512]{1,0:T(8,128)(2,1)S(1)} collective-permute-done((bf16[128,512]{1,0:T(8,128)(2,1)S(1)}, bf16[128,512]{1,0:T(8,128)(2,1)S(1)}, u32[]{:S(2)}, u32[]{:S(2)}) %collective-permute-start.4) | collective-permute-done | bytes 131104 | tf_op jit(solution)/shard_map/ppermute | solution.py:17
  22.5 1.6 %collective-permute-start.8 = (bf16[128,256]{1,0:T(8,128)(2,1)S(1)}, bf16[128,256]{1,0:T(8,128)(2,1)S(1)}, u32[]{:S(2)}, u32[]{:S(2)}) collective-permute-start(bf16[128,256]{1,0:T(8,128)(2,1)S(1)} %shard_map.89.seen.a), channel_id=1, source_target_pairs={{0,2},{1,3},{2,0},{3,1},{4,6},{5,7},{6,4},{7,5},{8,10},{9,11},{10,... | collective-permute-start | bytes 196616 | tf_op jit(solution)/shard_map/ppermute | solution.py:17
  24.1 0.7 %shard_map.90 = (bf16[640,256]{1,0:T(8,128)(2,1)S(1)}, f32[128,256]{1,0:T(8,128)S(1)}, bf16[128,512]{1,0:T(8,128)(2,1)S(1)}) custom-call(f32[640,256]{1,0:T(8,128)S(1)} %get-tuple-element.47.seen.x1, bf16[128,512]{1,0:T(8,128)(2,1)S(1)} %get-tuple-element.52.seen.send, bf16[128,512]{1,0:T(8,128)(2,1)S(1)} %collective-permute-done.4.far, ...), custom_call_target="tpu_custom_call" | custom-call | flops 100000000 | tf_op jit(solution)/shard_map/pallas_call | solution.py:88
  24.8 0.6 %collective-permute-start.7 = (bf16[128,256]{1,0:T(8,128)(2,1)S(1)}, bf16[128,256]{1,0:T(8,128)(2,1)S(1)}, u32[]{:S(2)}, u32[]{:S(2)}) collective-permute-start(bf16[128,256]{1,0:T(8,128)(2,1)S(1)} %shard_map.89.seen.a), channel_id=1, source_target_pairs={{0,1},{1,0},{2,3},{3,2},{4,5},{5,4},{6,7},{7,6},{8,9},{9,8},{10,11... | collective-permute-start | bytes 196616 | tf_op jit(solution)/shard_map/ppermute | solution.py:17
  25.4 1.2 %collective-permute-start.14 = (bf16[128,512]{1,0:T(8,128)(2,1)S(1)}, bf16[128,512]{1,0:T(8,128)(2,1)S(1)}, u32[]{:S(2)}, u32[]{:S(2)}) collective-permute-start(bf16[128,512]{1,0:T(8,128)(2,1)S(1)} %get-tuple-element.66.z), channel_id=1, source_target_pairs={{0,4},{4,0},{8,12},{12,8},{1,5},{5,1},{9,13},{13,9},{2,6},{6,2},{1... | collective-permute-start | bytes 393224 | tf_op jit(solution)/shard_map/ppermute | solution.py:17
  27.4 0.9 %shard_map.91 = (f32[640,256]{1,0:T(8,128)S(1)}, bf16[640,512]{1,0:T(8,128)(2,1)S(1)}) custom-call(bf16[640,256]{1,0:T(8,128)(2,1)S(1)} %get-tuple-element.56.x2, bf16[2,1,640,128]{3,2,1,0:T(8,128)(2,1)S(1)} %get-tuple-element.42.rb, bf16[1,640,128]{2,1,0:T(8,128)(2,1)S(1)} %get-tuple-element.43.tl, bf16[1,640,128]{2,1,0:T(8,128)(2,1)S(1)} %get-tuple-element.44.tr, ...), custom_call_target="tpu_custom_call" | custom-call | flops 3000000000 | tf_op jit(solution)/shard_map/pallas_call | solution.py:88
  28.4 0.5 %shard_map.94.back = bf16[128,512]{1,0:T(8,128)(2,1)S(1)} custom-call(bf16[128,256]{1,0:T(8,128)(2,1)S(1)} %shard_map.89.seen.a, bf16[128,256]{1,0:T(8,128)(2,1)S(1)} %collective-permute-done.7.b, bf16[128,256]{1,0:T(8,128)(2,1)S(1)} %collective-permute-done.8.c, bf16[128,256]{1,0:T(8,128)(2,1)S(1)} %collective-permute-done.9.d, ...), custom_call_target="tpu_custom_call" | custom-call | flops 1000000000 | tf_op jit(solution)/shard_map/pallas_call | solution.py:88
  29.0 1.2 %collective-permute-start.13 = (bf16[128,512]{1,0:T(8,128)(2,1)S(1)}, bf16[128,512]{1,0:T(8,128)(2,1)S(1)}, u32[]{:S(2)}, u32[]{:S(2)}) collective-permute-start(bf16[128,512]{1,0:T(8,128)(2,1)S(1)} %shard_map.94.back), channel_id=1, source_target_pairs={{0,4},{4,0},{8,12},{12,8},{1,5},{5,1},{9,13},{13,9},{2,6},{6,2},{1... | collective-permute-start | bytes 393224 | tf_op jit(solution)/shard_map/ppermute | solution.py:17
  30.2 0.6 %collective-permute-done.14.z_sib = bf16[128,512]{1,0:T(8,128)(2,1)S(1)} collective-permute-done((bf16[128,512]{1,0:T(8,128)(2,1)S(1)}, bf16[128,512]{1,0:T(8,128)(2,1)S(1)}, u32[]{:S(2)}, u32[]{:S(2)}) %collective-permute-start.14) | collective-permute-done | bytes 131104 | tf_op jit(solution)/shard_map/ppermute | solution.py:17
  30.8 3.8 %collective-permute-done.13.back_sib = bf16[128,512]{1,0:T(8,128)(2,1)S(1)} collective-permute-done((bf16[128,512]{1,0:T(8,128)(2,1)S(1)}, bf16[128,512]{1,0:T(8,128)(2,1)S(1)}, u32[]{:S(2)}, u32[]{:S(2)}) %collective-permute-start.13) | collective-permute-done | bytes 131104 | tf_op jit(solution)/shard_map/ppermute | solution.py:17
  34.8 2.9 %collective-permute-start.15 = (bf16[128,256]{1,0:T(8,128)(2,1)S(1)}, bf16[128,256]{1,0:T(8,128)(2,1)S(1)}, u32[]{:S(2)}, u32[]{:S(2)}) collective-permute-start(bf16[128,256]{1,0:T(8,128)(2,1)S(1)} %get-tuple-element.68.seen.half5), channel_id=1, source_target_pairs={{0,8},{4,12},{8,0},{12,4},{1,9},{5,13},{9,1},{13,5},{2,10},{6,14},... | collective-permute-start | bytes 196616 | tf_op jit(solution)/shard_map/ppermute | solution.py:17
  38.0 3.0 %collective-permute-done.15.half5_far = bf16[128,256]{1,0:T(8,128)(2,1)S(1)} collective-permute-done((bf16[128,256]{1,0:T(8,128)(2,1)S(1)}, bf16[128,256]{1,0:T(8,128)(2,1)S(1)}, u32[]{:S(2)}, u32[]{:S(2)}) %collective-permute-start.15) | collective-permute-done | bytes 65568 | tf_op jit(solution)/shard_map/ppermute | solution.py:17
  41.0 1.5 %shard_map.97 = f32[1,640,256]{2,1,0:T(8,128)} custom-call(f32[640,256]{1,0:T(8,128)S(1)} %get-tuple-element.69.out3, bf16[640,512]{1,0:T(8,128)(2,1)S(1)} %get-tuple-element.59.under, bf16[128,256]{1,0:T(8,128)(2,1)S(1)} %get-tuple-element.68.seen.half5, bf16[128,256]{1,0:T(8,128)(2,1)S(1)} %collective-permute-done.15.half5_far, ...), custom_call_target="tpu_custom_call" | custom-call | flops 1000000000 | tf_op jit(solution)/shard_map/pallas_call | solution.py:88
  (26 shorter events, 3.4 us)
Async XLA Ops:
  2.1 3.2 %collective-permute-start.1 = (bf16[128,256]{1,0:T(8,128)(2,1)S(1)}, bf16[128,256]{1,0:T(8,128)(2,1)S(1)}, u32[]{:S(2)}, u32[]{:S(2)}) collective-permute-start(bf16[128,256]{1,0:T(8,128)(2,1)S(1)} %get-tuple-element.39.p), channel_id=1, source_target_pairs={{0,1},{1,0},{2,3},{3,2},{4,5},{5,4},{6,7},{7,6},{8,9},{9,8},{10,11... | collective-permute-start | bytes 196616 | tf_op jit(solution)/shard_map/ppermute | solution.py:17
  2.6 5.3 %collective-permute-start = (bf16[128,256]{1,0:T(8,128)(2,1)S(1)}, bf16[128,256]{1,0:T(8,128)(2,1)S(1)}, u32[]{:S(2)}, u32[]{:S(2)}) collective-permute-start(bf16[128,256]{1,0:T(8,128)(2,1)S(1)} %get-tuple-element.39.p), channel_id=1, source_target_pairs={{0,4},{4,0},{8,12},{12,8},{1,5},{5,1},{9,13},{13,9},{2,6},{6,2},{1... | collective-permute-start | bytes 196616 | tf_op jit(solution)/shard_map/ppermute | solution.py:17
  5.9 4.9 %collective-permute-start.3 = (bf16[128,384]{1,0:T(8,128)(2,1)S(1)}, bf16[128,384]{1,0:T(8,128)(2,1)S(1)}, u32[]{:S(2)}, u32[]{:S(2)}) collective-permute-start(bf16[128,384]{1,0:T(8,128)(2,1)S(1)} %get-tuple-element.45.seen.own), channel_id=1, source_target_pairs={{0,4},{4,0},{8,12},{12,8},{1,5},{5,1},{9,13},{13,9},{2,6},{6,2},{1... | collective-permute-start | bytes 294920 | tf_op jit(solution)/shard_map/ppermute | solution.py:17
  8.7 5.4 %collective-permute-start.2 = (bf16[128,512]{1,0:T(8,128)(2,1)S(1)}, bf16[128,512]{1,0:T(8,128)(2,1)S(1)}, u32[]{:S(2)}, u32[]{:S(2)}) collective-permute-start(bf16[128,512]{1,0:T(8,128)(2,1)S(1)} %get-tuple-element.49), channel_id=1, source_target_pairs={{0,4},{4,0},{8,12},{12,8},{1,5},{5,1},{9,13},{13,9},{2,6},{6,2},{1... | collective-permute-start | bytes 393224 | tf_op jit(solution)/shard_map/ppermute | solution.py:17
  10.9 7.0 %collective-permute-start.5 = (bf16[128,256]{1,0:T(8,128)(2,1)S(1)}, bf16[128,256]{1,0:T(8,128)(2,1)S(1)}, u32[]{:S(2)}, u32[]{:S(2)}) collective-permute-start(bf16[128,256]{1,0:T(8,128)(2,1)S(1)} %get-tuple-element.55), channel_id=1, source_target_pairs={{0,12},{4,8},{8,4},{12,0},{1,13},{5,9},{9,5},{13,1},{2,14},{6,10},... | collective-permute-start | bytes 196616 | tf_op jit(solution)/shard_map/ppermute | solution.py:17
  14.3 4.5 %copy-start = (bf16[128,512]{1,0:T(8,128)(2,1)S(1)}, bf16[128,512]{1,0:T(8,128)(2,1)}, u32[]{:S(2)}) copy-start(bf16[128,512]{1,0:T(8,128)(2,1)} %caps.3) | copy-start | bytes 393220
  14.3 8.1 %collective-permute-start.4 = (bf16[128,512]{1,0:T(8,128)(2,1)S(1)}, bf16[128,512]{1,0:T(8,128)(2,1)S(1)}, u32[]{:S(2)}, u32[]{:S(2)}) collective-permute-start(bf16[128,512]{1,0:T(8,128)(2,1)S(1)} %get-tuple-element.52.seen.send), channel_id=1, source_target_pairs={{0,12},{4,8},{8,4},{12,0},{1,13},{5,9},{9,5},{13,1},{2,14},{6,10},... | collective-permute-start | bytes 393224 | tf_op jit(solution)/shard_map/ppermute | solution.py:17
  18.4 8.4 %collective-permute-start.6 = (bf16[128,768]{1,0:T(8,128)(2,1)S(1)}, bf16[128,768]{1,0:T(8,128)(2,1)S(1)}, u32[]{:S(2)}, u32[]{:S(2)}) collective-permute-start(bf16[128,768]{1,0:T(8,128)(2,1)S(1)} %shard_map.88.seen.late), channel_id=1, source_target_pairs={{0,4},{4,0},{8,12},{12,8},{1,5},{5,1},{9,13},{13,9},{2,6},{6,2},{1... | collective-permute-start | bytes 589832 | tf_op jit(solution)/shard_map/ppermute | solution.py:17
  18.9 6.4 %collective-permute-start.11 = (bf16[128,512]{1,0:T(8,128)(2,1)S(1)}, bf16[128,512]{1,0:T(8,128)(2,1)S(1)}, u32[]{:S(2)}, u32[]{:S(2)}) collective-permute-start(bf16[128,512]{1,0:T(8,128)(2,1)S(1)} %shard_map.92.a), channel_id=1, source_target_pairs={{0,2},{1,3},{2,0},{3,1},{4,6},{5,7},{6,4},{7,5},{8,10},{9,11},{10,... | collective-permute-start | bytes 393224 | tf_op jit(solution)/shard_map/ppermute | solution.py:17
  22.5 4.3 %collective-permute-start.8 = (bf16[128,256]{1,0:T(8,128)(2,1)S(1)}, bf16[128,256]{1,0:T(8,128)(2,1)S(1)}, u32[]{:S(2)}, u32[]{:S(2)}) collective-permute-start(bf16[128,256]{1,0:T(8,128)(2,1)S(1)} %shard_map.89.seen.a), channel_id=1, source_target_pairs={{0,2},{1,3},{2,0},{3,1},{4,6},{5,7},{6,4},{7,5},{8,10},{9,11},{10,... | collective-permute-start | bytes 196616 | tf_op jit(solution)/shard_map/ppermute | solution.py:17
  24.1 4.2 %collective-permute-start.10 = (bf16[128,512]{1,0:T(8,128)(2,1)S(1)}, bf16[128,512]{1,0:T(8,128)(2,1)S(1)}, u32[]{:S(2)}, u32[]{:S(2)}) collective-permute-start(bf16[128,512]{1,0:T(8,128)(2,1)S(1)} %shard_map.92.a), channel_id=1, source_target_pairs={{0,1},{1,0},{2,3},{3,2},{4,5},{5,4},{6,7},{7,6},{8,9},{9,8},{10,11... | collective-permute-start | bytes 393224 | tf_op jit(solution)/shard_map/ppermute | solution.py:17
  24.8 3.6 %collective-permute-start.7 = (bf16[128,256]{1,0:T(8,128)(2,1)S(1)}, bf16[128,256]{1,0:T(8,128)(2,1)S(1)}, u32[]{:S(2)}, u32[]{:S(2)}) collective-permute-start(bf16[128,256]{1,0:T(8,128)(2,1)S(1)} %shard_map.89.seen.a), channel_id=1, source_target_pairs={{0,1},{1,0},{2,3},{3,2},{4,5},{5,4},{6,7},{7,6},{8,9},{9,8},{10,11... | collective-permute-start | bytes 196616 | tf_op jit(solution)/shard_map/ppermute | solution.py:17
  25.4 5.5 %collective-permute-start.14 = (bf16[128,512]{1,0:T(8,128)(2,1)S(1)}, bf16[128,512]{1,0:T(8,128)(2,1)S(1)}, u32[]{:S(2)}, u32[]{:S(2)}) collective-permute-start(bf16[128,512]{1,0:T(8,128)(2,1)S(1)} %get-tuple-element.66.z), channel_id=1, source_target_pairs={{0,4},{4,0},{8,12},{12,8},{1,5},{5,1},{9,13},{13,9},{2,6},{6,2},{1... | collective-permute-start | bytes 393224 | tf_op jit(solution)/shard_map/ppermute | solution.py:17
  26.9 1.4 %collective-permute-start.12 = (bf16[128,512]{1,0:T(8,128)(2,1)S(1)}, bf16[128,512]{1,0:T(8,128)(2,1)S(1)}, u32[]{:S(2)}, u32[]{:S(2)}) collective-permute-start(bf16[128,512]{1,0:T(8,128)(2,1)S(1)} %collective-permute-done.11.c), channel_id=1, source_target_pairs={{0,1},{1,0},{2,3},{3,2},{4,5},{5,4},{6,7},{7,6},{8,9},{9,8},{10,11... | collective-permute-start | bytes 393224 | tf_op jit(solution)/shard_map/ppermute | solution.py:17
  26.9 1.5 %collective-permute-start.9 = (bf16[128,256]{1,0:T(8,128)(2,1)S(1)}, bf16[128,256]{1,0:T(8,128)(2,1)S(1)}, u32[]{:S(2)}, u32[]{:S(2)}) collective-permute-start(bf16[128,256]{1,0:T(8,128)(2,1)S(1)} %collective-permute-done.8.c), channel_id=1, source_target_pairs={{0,1},{1,0},{2,3},{3,2},{4,5},{5,4},{6,7},{7,6},{8,9},{9,8},{10,11... | collective-permute-start | bytes 196616 | tf_op jit(solution)/shard_map/ppermute | solution.py:17
  29.0 5.7 %collective-permute-start.13 = (bf16[128,512]{1,0:T(8,128)(2,1)S(1)}, bf16[128,512]{1,0:T(8,128)(2,1)S(1)}, u32[]{:S(2)}, u32[]{:S(2)}) collective-permute-start(bf16[128,512]{1,0:T(8,128)(2,1)S(1)} %shard_map.94.back), channel_id=1, source_target_pairs={{0,4},{4,0},{8,12},{12,8},{1,5},{5,1},{9,13},{13,9},{2,6},{6,2},{1... | collective-permute-start | bytes 393224 | tf_op jit(solution)/shard_map/ppermute | solution.py:17
  34.8 6.2 %collective-permute-start.15 = (bf16[128,256]{1,0:T(8,128)(2,1)S(1)}, bf16[128,256]{1,0:T(8,128)(2,1)S(1)}, u32[]{:S(2)}, u32[]{:S(2)}) collective-permute-start(bf16[128,256]{1,0:T(8,128)(2,1)S(1)} %get-tuple-element.68.seen.half5), channel_id=1, source_target_pairs={{0,8},{4,12},{8,0},{12,4},{1,9},{5,13},{9,1},{13,5},{2,10},{6,14},... | collective-permute-start | bytes 196616 | tf_op jit(solution)/shard_map/ppermute | solution.py:17
